TPU v7x, 512 devices: a whole 4x8x8 slice. The times are simulated.
512 devices in a mesh: ent: 128 (over y, z, core), rep: 4 (over x).
Axes of the slice: x: 4, y: 8, z: 8, core: 2. Of those that a mesh axis runs over, the one named last changes fastest.
Arguments:
- item_factors: bfloat16 [524288, 128], P(('ent', 'rep')), may hold values from -0.1 to 0.1
- tile_items: int32 [128, 4, 256, 32], P('ent', 'rep'), may hold values from 0 to 1023
- send_tiles: int32 [128, 4, 128], P('ent', 'rep'), may hold values from 1 to 2, as said below
- tile_users: int32 [128, 4, 256, 1], P('ent', 'rep'), may hold values from 0 to 7
- tile_counts: int32 [128, 4, 256, 32], P('ent', 'rep'), may hold values from 0 to 31
- recv_tiles: int32 [128, 4, 128], P('ent', 'rep'), may hold values from 1 to 2, as said below
Outputs:
- user_factors: float32 [1024, 128], P(('ent', 'rep'))
- item_rhs: float32 [524288, 128], P(('ent', 'rep'))
Inputs may be any that keep to these rules, and one draw needn't show every extreme that they name: send_tiles[e, r, p] counts the leading tile slots p * 2 to p * 2 + 1 of device (e, r) that are live; every device sends 2 tiles to some peer and receives 2 tiles from some peer. recv_tiles[p, r, e] equals send_tiles[e, r, p].
All inputs are finite; a program needn't handle non-finite values.
Results may differ from a plain program's by a relative error of at most 0.0009.
The roundings to bfloat16 on the way count: a program that leaves them out, or rounds other values in their place, can miss the bound.
Values may be sent and summed in bfloat16 or wider, within the bound.
A program may use at most 64 MiB of HBM per device.

v0:
```python
import jax
import jax.numpy as jnp
from jax import lax
from jax.sharding import PartitionSpec as P

U_DEV = 2


ALPHA = 40.0
RIDGE = 1.0
RHS_SCALE = 1.0 / 640.0


def solve_users(gram, rhs):
    lower = jnp.linalg.cholesky(gram)
    halfway = lax.linalg.triangular_solve(lower, rhs[..., None], left_side=True, lower=True)
    result = lax.linalg.triangular_solve(
        lower, halfway, left_side=True, lower=True, transpose_a=True
    )
    return result[..., 0]


def shards(item_factors, tile_items, send_tiles, tile_users, tile_counts, recv_tiles):
    highest = lax.Precision.HIGHEST
    rank_width = item_factors.shape[1]
    item_count = item_factors.shape[0]
    n_ent = lax.axis_size("ent")
    tile_slots = tile_items.shape[2]
    tile_rows = tile_items.shape[3]
    seg_count = tile_users.shape[3]
    seg_length = tile_rows // seg_count
    slot_cap = tile_slots // n_ent
    user_block = U_DEV * lax.axis_size("rep")
    item_ids = tile_items.reshape(tile_slots, tile_rows)
    slot_pos = jnp.arange(tile_slots, dtype=jnp.int32) % slot_cap
    live_send = slot_pos < jnp.repeat(send_tiles.reshape(n_ent), slot_cap)
    live_recv = slot_pos < jnp.repeat(recv_tiles.reshape(n_ent), slot_cap)
    partial_gram = lax.dot_general(
        item_factors, item_factors, (((0,), (0,)), ((), ())), preferred_element_type=jnp.float32
    )
    picked = jnp.take(item_factors, item_ids.reshape(-1), axis=0).reshape(
        tile_slots, tile_rows, rank_width
    )
    picked = jnp.where(live_send[:, None, None], picked, jnp.zeros((), jnp.bfloat16))
    incoming = lax.all_to_all(
        picked.reshape(n_ent, slot_cap * tile_rows, rank_width),
        "ent",
        split_axis=0,
        concat_axis=0,
        tiled=True,
    )
    counts_int = tile_counts.reshape(tile_slots, tile_rows)
    counts_f = counts_int.astype(jnp.float32)
    gram_weight = ALPHA * counts_f
    rhs_weight = jnp.where(
        live_recv[:, None] & (counts_int > 0), 1.0 + ALPHA * counts_f, jnp.float32(0.0)
    )
    owners = tile_users.reshape(tile_slots * seg_count)
    selector = owners[None, :] == jnp.arange(user_block, dtype=jnp.int32)[:, None]
    selector_f = selector.astype(jnp.float32)
    src_group = 1
    while (
        src_group * 2 <= n_ent
        and n_ent % (src_group * 2) == 0
        and (src_group * 2 * slot_cap * tile_rows <= 4096)
    ):
        src_group = src_group * 2
    tiles_blk = src_group * slot_cap
    block_count = tile_slots // tiles_blk
    runs_blk = tiles_blk * seg_count

    def accumulate(state_pair, pieces):
        gram_run, rhs_run = state_pair
        rows_blk, gram_blk, rhs_blk, select_blk = pieces
        weighted = (gram_blk[:, :, None] * rows_blk).astype(jnp.bfloat16)
        rows_seg = rows_blk.reshape(tiles_blk, seg_count, seg_length, rank_width)
        weighted = weighted.reshape(tiles_blk, seg_count, seg_length, rank_width)
        run_gram = jnp.einsum(
            "tsri,tsrj->tsij", weighted, rows_seg, preferred_element_type=jnp.float32
        )
        run_gram = run_gram.reshape(runs_blk, rank_width * rank_width)
        run_rhs = jnp.einsum(
            "tsr,tsri->tsi",
            rhs_blk.reshape(tiles_blk, seg_count, seg_length),
            rows_seg.astype(jnp.float32),
            precision=highest,
        )
        run_rhs = run_rhs.reshape(runs_blk, rank_width)
        gram_run = gram_run + jnp.dot(select_blk, run_gram, precision=highest)
        rhs_run = rhs_run + jnp.dot(select_blk, run_rhs, precision=highest)
        return ((gram_run, rhs_run), None)

    block_pieces = (
        incoming.reshape(block_count, tiles_blk, tile_rows, rank_width),
        gram_weight.reshape(block_count, tiles_blk, tile_rows),
        rhs_weight.reshape(block_count, tiles_blk, tile_rows),
        jnp.transpose(selector_f.reshape(user_block, block_count, runs_blk), (1, 0, 2)),
    )
    start_pair = (
        jnp.zeros((user_block, rank_width * rank_width), jnp.float32),
        jnp.zeros((user_block, rank_width), jnp.float32),
    )
    (gram_acc, rhs_acc), _ = lax.scan(accumulate, start_pair, block_pieces)
    identity_mat = jnp.eye(rank_width, dtype=jnp.float32)
    added_term = lax.psum(partial_gram, ("ent", "rep")) + RIDGE * identity_mat
    own_gram, own_rhs = (
        lax.psum_scatter(gram_acc, "rep", scatter_dimension=0, tiled=True),
        lax.psum_scatter(rhs_acc, "rep", scatter_dimension=0, tiled=True),
    )
    own_factors = solve_users(own_gram.reshape(-1, rank_width, rank_width) + added_term, own_rhs)
    solved = lax.all_gather(own_factors.astype(jnp.bfloat16), "rep", axis=0, tiled=True)
    run_factor = lax.dot_general(
        selector.astype(jnp.bfloat16),
        solved,
        (((0,), (0,)), ((), ())),
        preferred_element_type=jnp.float32,
    )
    back_factor, back_weight = (
        lax.all_to_all(
            run_factor.reshape(n_ent, slot_cap, seg_count * rank_width),
            "ent",
            split_axis=0,
            concat_axis=0,
            tiled=True,
        ),
        lax.all_to_all(
            rhs_weight.reshape(n_ent, slot_cap, tile_rows),
            "ent",
            split_axis=0,
            concat_axis=0,
            tiled=True,
        ),
    )

    def spread(running, pieces):
        factor_blk, weight_blk, item_blk = pieces
        contrib = (weight_blk[:, :, :, None] * factor_blk[:, :, None, :]).reshape(-1, rank_width)
        return (
            running + jax.ops.segment_sum(contrib, item_blk.reshape(-1), num_segments=item_count),
            None,
        )

    spread_pieces = (
        back_factor.reshape(block_count, tiles_blk, seg_count, rank_width),
        back_weight.reshape(block_count, tiles_blk, seg_count, seg_length),
        item_ids.reshape(block_count, tiles_blk, tile_rows),
    )
    item_rhs, _ = lax.scan(spread, jnp.zeros((item_count, rank_width), jnp.float32), spread_pieces)
    return (own_factors, item_rhs * RHS_SCALE)


def solution(mesh):
    in_specs = (
        P(("ent", "rep"), None),
        P("ent", "rep", None, None),
        P("ent", "rep", None),
        P("ent", "rep", None, None),
        P("ent", "rep", None, None),
        P("ent", "rep", None),
    )
    out_specs = (P(("ent", "rep"), None), P(("ent", "rep"), None))
    return jax.shard_map(shards, mesh=mesh, in_specs=in_specs, out_specs=out_specs, check_vma=False)
```

profile of v0, /device:TPU:1, one launch (start us, length us, event | category | flops | bytes accessed | tf_op | source)
XLA Modules:
  0.0 525.9 jit_solution(16828590585126697929)
XLA Ops:
  7.2 0.9 copy.43
  8.4 0.7 broadcast_compare_fusion.2
  9.2 24.0 %gather_fusion = bf16[8192,128]{1,0:T(8,128)(2,1)S(1)} fusion(bf16[1024,128]{1,0:T(8,128)(2,1)S(1)} %copy-done, s32[8192]{0:T(1024)S(1)} %broadcast_clamp_fusion), kind=kCustom, calls=%fused_computation | custom fusion | bytes 4227072 | tf_op jit(solution)/shard_map/jit(_take)/gather | solution.py:41
  33.2 4.6 select_select_fusion
  37.8 18.6 %all-to-all-start = ((bf16[128,64,128]{2,1,0:T(8,128)(2,1)}), bf16[128,64,128]{2,1,0:T(8,128)(2,1)S(1)}, u32[]{:S(2)}, u32[]{:S(2)}) async-start(bf16[128,64,128]{2,1,0:T(8,128)(2,1)} %select_select_fusion), calls=%async_computation | async-start | bytes 4194304 | tf_op jit(solution)/shard_map/all_to_all | solution.py:45
  56.4 0.9 fusion.25
  57.9 0.7 reduce.9
  59.4 1.3 dynamic-slice
  61.5 0.9 and_select_fusion
  62.4 46.3 %all-to-all-done = bf16[128,64,128]{2,1,0:T(8,128)(2,1)S(1)} async-done(((bf16[128,64,128]{2,1,0:T(8,128)(2,1)}), bf16[128,64,128]{2,1,0:T(8,128)(2,1)S(1)}, u32[]{:S(2)}, u32[]{:S(2)}) %all-to-all-start) | async-done | bytes 2097184 | tf_op jit(solution)/shard_map/all_to_all | solution.py:45
  108.7 7.6 %all-to-all-start.1 = ((f32[128,2,32]{2,1,0:T(2,128)}), f32[128,2,32]{2,1,0:T(2,128)S(1)}, u32[]{:S(2)}, u32[]{:S(2)}) async-start(f32[128,2,32]{2,1,0:T(2,128)} %and_select_fusion), calls=%async_computation.1 | async-start | bytes 262144 | tf_op jit(solution)/shard_map/all_to_all | solution.py:126
  116.5 37.8 %while.24 = (s32[]{:T(128)}, f32[8,16384]{1,0:T(8,128)S(1)}, f32[8,128]{1,0:T(8,128)S(1)}, f32[2,8,128]{2,1,0:T(8,128)S(1)}, f32[2,128,32]{2,1,0:T(8,128)S(1)}, ...) while((s32[]{:T(128)}, f32[8,16384]{1,0:T(8,128)S(1)}, ...), condition=%wide.region_1.2_spmd.clone, body=%wide.region_0.1_spmd.clone.sunk | while | flops 345245696 | bytes 21267580 | solution.py:103
  116.5 5.2 fusion.49
  121.7 12.5 %convolution_add_fusion.4 = f32[8,16384]{1,0:T(8,128)S(1)} fusion(f32[16,8,128,128]{3,2,1,0:T(8,128)} %bitcast.121, f32[8,16384]{1,0:T(8,128)S(1)} %get-tuple-element.219, pred[]{:T(512)S(6)} %compare.15, f32[2,8,128]{2,1,0:T(8,128)S(1)} %get-tuple-element.230, s32[]{:T(128)} %get-tuple-element.218), kind=kOutput, calls=%fused_computation.6.clone.1 | convolution fusion | flops 201588736 | bytes 9441285 | tf_op jit(solution)/shard_map/while/body/eval_jaxpr/dot_general | solution.py:89
  134.3 0.9 fusion.50
  135.4 5.2 fusion.49
  140.6 12.5 %convolution_add_fusion.4 = f32[8,16384]{1,0:T(8,128)S(1)} fusion(f32[16,8,128,128]{3,2,1,0:T(8,128)} %bitcast.121, f32[8,16384]{1,0:T(8,128)S(1)} %get-tuple-element.219, pred[]{:T(512)S(6)} %compare.15, f32[2,8,128]{2,1,0:T(8,128)S(1)} %get-tuple-element.230, s32[]{:T(128)} %get-tuple-element.218), kind=kOutput, calls=%fused_computation.6.clone.1 | convolution fusion | flops 201588736 | bytes 9441285 | tf_op jit(solution)/shard_map/while/body/eval_jaxpr/dot_general | solution.py:89
  153.2 0.9 fusion.50
  154.3 0.8 copy-done.1
  155.2 186.9 %all-reduce.5.cloned.1.call-done = f32[128,128]{1,0:T(8,128)} async-done(((f32[128,128]{1,0:T(8,128)}), f32[128,128]{1,0:T(8,128)}) %all-reduce.5.cloned.1.call-update) | async-done | bytes 65552 | tf_op jit(solution)/shard_map/psum | solution.py:105
  342.0 0.9 convert_add_fusion
  343.0 8.1 %all-reduce.1 = f32[8,128]{1,0:T(8,128)S(1)} all-reduce(f32[8,128]{1,0:T(8,128)S(1)} %get-tuple-element.68), channel_id=3, replica_groups=mesh['ent'=128,'rep'=4] {'rep'}, use_global_device_ids=true, to_apply=%region_6.7.clone | all-reduce | flops 1024 | bytes 8192
  351.0 37.3 %all-reduce.7.cloned.1.call-done = f32[8,16384]{1,0:T(8,128)} async-done(((f32[8,16384]{1,0:T(8,128)}), f32[8,16384]{1,0:T(8,128)}) %all-reduce.7.cloned.1.call-update) | async-done | bytes 524304
  388.4 1.1 dynamic-slice_bitcast_fusion.2
  389.7 23.5 %custom-call.9 = f32[2,128,128]{2,1,0:T(8,128)S(1)} custom-call(f32[2,128,128]{2,1,0:T(8,128)S(1)} %fusion.20), custom_call_target="Cholesky" | custom-call | tf_op jit(solution)/shard_map/jit(cholesky)/cholesky | solution.py:15
  413.4 19.7 %custom-call.10 = f32[2,1,128,128]{2,3,1,0:T(8,128)S(1)} custom-call(f32[2,1,128,128]{3,2,1,0:T(8,128)S(1)} %select_bitcast_fusion), custom_call_target="InvertDiagBlocksLowerTriangular" | custom-call | tf_op jit(solution)/shard_map/triangular_solve | solution.py:17
  433.7 6.8 %all-gather = bf16[4,2,128]{2,1,0:T(2,128)(2,1)S(1)} all-gather(bf16[1,2,128]{2,1,0:T(2,128)(2,1)S(1)} %convert_bitcast_fusion), channel_id=1, replica_groups=mesh['ent'=128,'rep'=4] {'rep'}, dimensions={0}, use_global_device_ids=true | all-gather | bytes 2560 | tf_op jit(solution)/shard_map/all_gather | solution.py:111
  440.7 30.5 %all_to_all.15 = f32[128,2,128]{2,1,0:T(2,128)S(1)} all-to-all(f32[128,2,128]{2,1,0:T(2,128)S(1)} %bitcast.132), channel_id=1, replica_groups=mesh['ent'=128,'rep'=4] {'ent'}, dimensions={0} | all-to-all | bytes 262144 | tf_op jit(solution)/shard_map/all_to_all | solution.py:119
  471.3 46.8 %while.23 = (s32[]{:T(128)}, f32[1024,128]{1,0:T(8,128)S(1)}, s32[2,128,32]{2,1,0:T(8,128)S(1)}, f32[2,128,1,32]{3,1,2,0:T(8,128)S(1)}, f32[2,128,1,128]{3,1,2,0:T(8,128)S(1)}, /*index=5*/s32[]{:T(128)}) while((s32[]{:T(128)}, f32[1024,128]{1,0:T(8,128)S(1)}, s32[2,128,32]{2,1,0:T(8,128)S(1)}, f32[2,128,1,32]{3,1,2,0:T(8,128)S(1)}, ...), condition=%wide.region_9.10_spmd, body=%wide.region_7.9_spmd.sunk | while | flops 1048578 | bytes 8749137 | solution.py:148
  472.2 22.6 %scatter_fusion = f32[1024,128]{1,0:T(8,128)S(1)} fusion(f32[1024,128]{1,0:T(8,128)S(1)} %get-tuple-element.243, s32[4096]{0:T(1024)S(1)} %reshape.259, f32[4096,128]{1,0:T(8,128)S(1)} %bitcast_multiply_fusion.2), kind=kCustom, calls=%fused_computation.1.clone.1 | custom fusion | flops 524288 | bytes 6307840 | tf_op jit(solution)/shard_map/while/body/eval_jaxpr/scatter-add | solution.py:139
  495.6 22.6 %scatter_fusion = f32[1024,128]{1,0:T(8,128)S(1)} fusion(f32[1024,128]{1,0:T(8,128)S(1)} %get-tuple-element.243, s32[4096]{0:T(1024)S(1)} %reshape.259, f32[4096,128]{1,0:T(8,128)S(1)} %bitcast_multiply_fusion.2), kind=kCustom, calls=%fused_computation.1.clone.1 | custom fusion | flops 524288 | bytes 6307840 | tf_op jit(solution)/shard_map/while/body/eval_jaxpr/scatter-add | solution.py:139
  518.2 0.8 broadcast_multiply_fusion
  (75 shorter events, 5.6 us)
Async XLA Ops:
  7.2 2.0 copy-start
  37.8 20.1 %copy-start.5 = (s32[1,1,128]{2,1,0:T(1,128)S(1)}, s32[1,1,128]{2,1,0:T(1,128)}, u32[]{:S(2)}) copy-start(s32[1,1,128]{2,1,0:T(1,128)} %param.15) | copy-start | bytes 1540
  37.8 21.1 %copy-start.2 = (s32[1,1,256,32]{2,3,1,0:T(8,128)S(1)}, s32[1,1,256,32]{2,3,1,0:T(8,128)}, u32[]{:S(2)}) copy-start(s32[1,1,256,32]{2,3,1,0:T(8,128)} %param.14) | copy-start | bytes 98308
  37.8 23.6 %copy-start.3 = (s32[1,1,256,1]{2,3,1,0:T(1,128)S(1)}, s32[1,1,256,1]{2,3,1,0:T(1,128)}, u32[]{:S(2)}) copy-start(s32[1,1,256,1]{2,3,1,0:T(1,128)} %param.13) | copy-start | bytes 3076
  37.8 70.9 %all-to-all-start = ((bf16[128,64,128]{2,1,0:T(8,128)(2,1)}), bf16[128,64,128]{2,1,0:T(8,128)(2,1)S(1)}, u32[]{:S(2)}, u32[]{:S(2)}) async-start(bf16[128,64,128]{2,1,0:T(8,128)(2,1)} %select_select_fusion), calls=%async_computation | async-start | bytes 4194304 | tf_op jit(solution)/shard_map/all_to_all | solution.py:45
  56.4 285.6 %all-reduce.5.cloned.1.call-start = ((), (), s32[]{:S(2)}) async-start(), calls=%async_computation.3 | async-start | bytes 131072 | tf_op jit(solution)/shard_map/psum | solution.py:105
  108.7 332.1 %all-to-all-start.1 = ((f32[128,2,32]{2,1,0:T(2,128)}), f32[128,2,32]{2,1,0:T(2,128)S(1)}, u32[]{:S(2)}, u32[]{:S(2)}) async-start(f32[128,2,32]{2,1,0:T(2,128)} %and_select_fusion), calls=%async_computation.1 | async-start | bytes 262144 | tf_op jit(solution)/shard_map/all_to_all | solution.py:126
  116.3 272.1 %all-reduce.7.cloned.1.call-start = ((), (), s32[]{:S(2)}) async-start(), calls=%async_computation.4 | async-start | bytes 1048576
  154.3 0.8 copy-start.1
  433.7 37.7 %copy-start.4 = (f32[2,1,128]{2,1,0:T(1,128)}, f32[2,1,128]{2,1,0:T(1,128)S(1)}, u32[]{:S(2)}) copy-start(f32[2,1,128]{2,1,0:T(1,128)S(1)} %fusion.17) | copy-start | bytes 3076
Sparse Core Ops, SparseCore 0:
  62.2 279.7 all-reduce.4
  345.0 43.2 all-reduce.6
where the time goes:
time: 526 us
  waiting for transfers between devices  271 us (52%)
  other arithmetic  98.5 us (19%)
  blocking collectives  45.4 us (9%)
  matrix products  39.3 us (7%)
  local copies, waits for them, and re-layouts  30.6 us (6%)
  starting transfers between devices  26.4 us (5%)
  between operations  15 us (3%)
    psum x1, waiting for transfers between devices, shards(): added_term = lax.psum(partial_gram, ('ent', 'rep')) + RIDGE * identity_mat  187 us
    all_to_all x1, waiting for transfers between devices, shards(): lax.all_to_all(picked.reshape(n_ent, slot_cap * tile_rows, rank_width), '...  46.3 us
    scatter-add x2, other arithmetic, spread(): jax.ops.segment_sum(contrib, item_blk.reshape(-1), num_segments=item_count)  45.1 us
    unnamed x3, waiting for transfers between devices  37.4 us
    all_to_all x1, blocking collectives, shards(): lax.all_to_all(run_factor.reshape(n_ent, slot_cap, seg_count * rank_width...  30.5 us
    dot_general x2, matrix products, accumulate(): gram_run = gram_run + jnp.dot(select_blk, run_gram, precision=highest)  25 us
    gather x1, local copies, waits for them, and re-layouts, shards(): jnp.take(item_factors, item_ids.reshape(-1), axis=0)  24 us
    another operation x4, other arithmetic, solve_users(): lower = jnp.linalg.cholesky(gram)  23.6 us
  transfers between devices with their start and end apart: 4, of which 3 were waited for; matrix products, arithmetic and copies ran while one was open for 17% of the time, Pallas kernels for 0%

commit v1 on v0

--- a/solution.py
+++ b/solution.py
@@ -20,11 +20,44 @@
     return result[..., 0]
 
 
+def tree_sum(value, count):
+    bits = count.bit_length() - 1
+    for bit in range(bits):
+        step = 1 << bit
+        pairs = [(i, i ^ step) for i in range(count)]
+        value = value + lax.ppermute(value, ("ent", "rep"), pairs)
+    return value
+
+
+def rep_scatter_sum(acc, n_rep, per_dev):
+    me = lax.axis_index("rep")
+    total = lax.dynamic_slice_in_dim(acc, me * per_dev, per_dev, 0)
+    for shift in range(1, n_rep):
+        dest = (me + shift) % n_rep
+        piece = lax.dynamic_slice_in_dim(acc, dest * per_dev, per_dev, 0)
+        pairs = [(i, (i + shift) % n_rep) for i in range(n_rep)]
+        total = total + lax.ppermute(piece, "rep", pairs)
+    width = acc.shape[1]
+    return total[:, : width - 128], total[:, width - 128 :]
+
+
+def rep_gather(value, n_rep):
+    me = lax.axis_index("rep")
+    got = [value]
+    for shift in range(1, n_rep):
+        pairs = [(i, (i + shift) % n_rep) for i in range(n_rep)]
+        got.append(lax.ppermute(value, "rep", pairs))
+    stacked = jnp.stack(got)
+    order = (me - jnp.arange(n_rep)) % n_rep
+    return jnp.take(stacked, order, axis=0).reshape(-1, value.shape[-1])
+
+
 def shards(item_factors, tile_items, send_tiles, tile_users, tile_counts, recv_tiles):
     highest = lax.Precision.HIGHEST
     rank_width = item_factors.shape[1]
     item_count = item_factors.shape[0]
     n_ent = lax.axis_size("ent")
+    n_rep = lax.axis_size("rep")
     tile_slots = tile_items.shape[2]
     tile_rows = tile_items.shape[3]
     seg_count = tile_users.shape[3]
@@ -102,13 +135,12 @@
     )
     (gram_acc, rhs_acc), _ = lax.scan(accumulate, start_pair, block_pieces)
     identity_mat = jnp.eye(rank_width, dtype=jnp.float32)
-    added_term = lax.psum(partial_gram, ("ent", "rep")) + RIDGE * identity_mat
-    own_gram, own_rhs = (
-        lax.psum_scatter(gram_acc, "rep", scatter_dimension=0, tiled=True),
-        lax.psum_scatter(rhs_acc, "rep", scatter_dimension=0, tiled=True),
+    added_term = tree_sum(partial_gram, n_ent * n_rep) + RIDGE * identity_mat
+    own_gram, own_rhs = rep_scatter_sum(
+        jnp.concatenate([gram_acc, rhs_acc], axis=1), n_rep, U_DEV
     )
     own_factors = solve_users(own_gram.reshape(-1, rank_width, rank_width) + added_term, own_rhs)
-    solved = lax.all_gather(own_factors.astype(jnp.bfloat16), "rep", axis=0, tiled=True)
+    solved = rep_gather(own_factors.astype(jnp.bfloat16), n_rep)
     run_factor = lax.dot_general(
         selector.astype(jnp.bfloat16),
         solved,

time: 526 us -> 332 us (0.63)
  waiting for transfers between devices: 271 us -> 53.8 us
  starting transfers between devices: 26.4 us -> 80 us
  blocking collectives: 45.4 us -> 28.2 us
  between operations: 15 us -> 1.25 us
    psum x1 -> x0, waiting for transfers between devices: 187 us -> none  [shards(): added_term = lax.psum(partial_gram, ('ent', 'rep')) + RIDGE * identity_mat]
    ppermute x0 -> x15, waiting for transfers between devices: none -> 53.8 us  [the longest x9 44.7 us: tree_sum(): value = value + lax.ppermute(value, ('ent', 'rep'), pairs)]
    ppermute x0 -> x15, starting transfers between devices: none -> 46.6 us  [the longest x9 29.8 us: tree_sum(): value = value + lax.ppermute(value, ('ent', 'rep'), pairs)]
    all_to_all x1, waiting for transfers between devices: 46.3 us -> 0.01 us  [shards(): lax.all_to_all(picked.reshape(n_ent, slot_cap * tile_rows, rank_width), '...]
    unnamed x3 -> x0, waiting for transfers between devices: 37.4 us -> none
    unnamed x1 -> x0, blocking collectives: 8.06 us -> none
    all_to_all x1, starting transfers between devices: 7.61 us -> 14.8 us  [shards(): lax.all_to_all(rhs_weight.reshape(n_ent, slot_cap, tile_rows), 'ent', spl...]
    all_gather x1 -> x0, blocking collectives: 6.82 us -> none  [shards(): lax.all_gather(own_factors.astype(jnp.bfloat16), 'rep', axis=0, tiled=True)]
  transfers between devices with their start and end apart: 4 -> 17, of which waited for: 3 -> 10; matrix products, arithmetic and copies ran while one was open for 17% -> 27% of each run, Pallas kernels for 0% -> 0%
where the time goes in v1:
time: 332 us; the launch traced here: 331 us
  other arithmetic  100 us (30%)
  starting transfers between devices  80 us (24%)
  waiting for transfers between devices  53.8 us (16%)
  matrix products  38.7 us (12%)
  local copies, waits for them, and re-layouts  29.1 us (9%)
  blocking collectives  28.2 us (8%)
    scatter-add x2, other arithmetic, spread(): jax.ops.segment_sum(contrib, item_blk.reshape(-1), num_segments=item_count)  45.1 us
    ppermute x9, waiting for transfers between devices, tree_sum(): value = value + lax.ppermute(value, ('ent', 'rep'), pairs)  44.7 us
    ppermute x9, starting transfers between devices, tree_sum(): value = value + lax.ppermute(value, ('ent', 'rep'), pairs)  29.8 us
    all_to_all x1, blocking collectives, shards(): lax.all_to_all(run_factor.reshape(n_ent, slot_cap, seg_count * rank_width...  28.2 us
    dot_general x2, matrix products, accumulate(): gram_run = gram_run + jnp.dot(select_blk, run_gram, precision=highest)  25 us
    another operation x4, other arithmetic, solve_users(): lower = jnp.linalg.cholesky(gram)  24.2 us
    gather x1, local copies, waits for them, and re-layouts, shards(): jnp.take(item_factors, item_ids.reshape(-1), axis=0)  24 us
    another operation x3, other arithmetic, solve_users(): lax.linalg.triangular_solve(lower, halfway, left_side=True, lower=True, t...  20.4 us
  transfers between devices with their start and end apart: 17, of which 10 were waited for; matrix products, arithmetic and copies ran while one was open for 27% of the time, Pallas kernels for 0%

profile of v1, /device:TPU:1, one launch (start us, length us, event | category | flops | bytes accessed | tf_op | source)
XLA Modules:
  0.0 331.3 jit_solution(6432870845083060427)
XLA Ops:
  2.7 24.0 %gather_fusion = bf16[8192,128]{1,0:T(8,128)(2,1)S(1)} fusion(bf16[1024,128]{1,0:T(8,128)(2,1)S(1)} %copy-done, s32[8192]{0:T(1024)S(1)} %broadcast_clamp_fusion), kind=kCustom, calls=%fused_computation | custom fusion | bytes 4227072 | tf_op jit(solution)/shard_map/jit(_take)/gather | solution.py:74
  26.7 4.6 %select_select_fusion = bf16[128,64,128]{2,1,0:T(8,128)(2,1)} fusion(bf16[128,64,128]{2,1,0:T(8,128)(2,1)S(1)} %bitcast.133, pred[128,64]{1,0:T(8,128)(4,1)S(1)} %compare_and_fusion, pred[128,64]{1,0:T(8,128)(4,1)S(1)} %copy.49), kind=kLoop, calls=%fused_computation.29 | loop fusion | flops 2097152 | bytes 4210688 | tf_op jit(solution)/shard_map/jit(_where)/select_n | solution.py:77
  31.3 18.6 %all-to-all-start = ((bf16[128,64,128]{2,1,0:T(8,128)(2,1)}), bf16[128,64,128]{2,1,0:T(8,128)(2,1)S(1)}, u32[]{:S(2)}, u32[]{:S(2)}) async-start(bf16[128,64,128]{2,1,0:T(8,128)(2,1)} %select_select_fusion), calls=%async_computation | async-start | bytes 4194304 | tf_op jit(solution)/shard_map/all_to_all | solution.py:78
  50.1 3.1 collective-permute-start.3
  56.1 4.4 %collective-permute-start.4 = (f32[128,128]{1,0:T(8,128)S(1)}, f32[128,128]{1,0:T(8,128)S(1)}, u32[]{:S(2)}, u32[]{:S(2)}) collective-permute-start(f32[128,128]{1,0:T(8,128)S(1)} %add.219), channel_id=1, source_target_pairs={{0,2},{1,3},{2,0},{3,1},{4,6},{5,7},{6,4},{7,5},{8,10},{9,11},{10,... | collective-permute-start | bytes 196616 | tf_op jit(solution)/shard_map/ppermute | solution.py:28
  63.0 3.9 %collective-permute-start.5 = (f32[128,128]{1,0:T(8,128)S(1)}, f32[128,128]{1,0:T(8,128)S(1)}, u32[]{:S(2)}, u32[]{:S(2)}) collective-permute-start(f32[128,128]{1,0:T(8,128)S(1)} %add.220), channel_id=1, source_target_pairs={{0,4},{1,5},{2,6},{3,7},{4,0},{5,1},{6,2},{7,3},{8,12},{9,13},{10,... | collective-permute-start | bytes 196616 | tf_op jit(solution)/shard_map/ppermute | solution.py:28
  68.4 2.8 collective-permute-start.6
  71.8 19.5 %collective-permute-done.6 = f32[128,128]{1,0:T(8,128)S(1)} collective-permute-done((f32[128,128]{1,0:T(8,128)S(1)}, f32[128,128]{1,0:T(8,128)S(1)}, u32[]{:S(2)}, u32[]{:S(2)}) %collective-permute-start.6) | collective-permute-done | bytes 65568 | tf_op jit(solution)/shard_map/ppermute | solution.py:28
  93.9 10.1 %collective-permute-done.7 = f32[128,128]{1,0:T(8,128)S(1)} collective-permute-done((f32[128,128]{1,0:T(8,128)S(1)}, f32[128,128]{1,0:T(8,128)S(1)}, u32[]{:S(2)}, u32[]{:S(2)}) %collective-permute-start.7) | collective-permute-done | bytes 65568 | tf_op jit(solution)/shard_map/ppermute | solution.py:28
  106.2 7.1 %collective-permute-done.8 = f32[128,128]{1,0:T(8,128)S(1)} collective-permute-done((f32[128,128]{1,0:T(8,128)S(1)}, f32[128,128]{1,0:T(8,128)S(1)}, u32[]{:S(2)}, u32[]{:S(2)}) %collective-permute-start.8) | collective-permute-done | bytes 65568 | tf_op jit(solution)/shard_map/ppermute | solution.py:28
  115.3 3.1 collective-permute-done.9
  118.4 3.6 %collective-permute-start.10 = (f32[128,128]{1,0:T(8,128)S(1)}, f32[128,128]{1,0:T(8,128)S(1)}, u32[]{:S(2)}, u32[]{:S(2)}) collective-permute-start(f32[128,128]{1,0:T(8,128)S(1)} %add.225), channel_id=1, source_target_pairs={{0,128},{1,129},{2,130},{3,131},{4,132},{5,133},{6,134},{7,135},{8... | collective-permute-start | bytes 196616 | tf_op jit(solution)/shard_map/ppermute | solution.py:28
  122.5 2.5 collective-permute-done.10
  125.0 5.9 %collective-permute-start.11 = (f32[128,128]{1,0:T(8,128)S(1)}, f32[128,128]{1,0:T(8,128)S(1)}, u32[]{:S(2)}, u32[]{:S(2)}) collective-permute-start(f32[128,128]{1,0:T(8,128)S(1)} %add.226), channel_id=1, source_target_pairs={{0,256},{1,257},{2,258},{3,259},{4,260},{5,261},{6,262},{7,263},{8... | collective-permute-start | bytes 196616 | tf_op jit(solution)/shard_map/ppermute | solution.py:28
  131.0 14.8 %all-to-all-start.1 = ((f32[128,2,32]{2,1,0:T(2,128)}), f32[128,2,32]{2,1,0:T(2,128)S(1)}, u32[]{:S(2)}, u32[]{:S(2)}) async-start(f32[128,2,32]{2,1,0:T(2,128)} %and_select_fusion), calls=%async_computation.1 | async-start | bytes 262144 | tf_op jit(solution)/shard_map/all_to_all | solution.py:158
  145.7 37.7 %while.24 = (s32[]{:T(128)}, f32[8,16384]{1,0:T(8,128)S(1)}, f32[8,128]{1,0:T(8,128)S(1)}, f32[2,8,128]{2,1,0:T(8,128)S(1)}, f32[2,128,32]{2,1,0:T(8,128)S(1)}, ...) while((s32[]{:T(128)}, f32[8,16384]{1,0:T(8,128)S(1)}, ...), condition=%wide.region_1.2_spmd.clone, body=%wide.region_0.1_spmd.clone.sunk | while | flops 345245696 | bytes 21267588 | solution.py:136
  145.8 5.2 %fusion.54 = f32[128,128,128]{2,1,0:T(8,128)} fusion(f32[128,32]{1,0:T(8,128)S(1)} %dynamic-slice_bitcast_fusion.5, bf16[2,128,32,128]{3,2,1,0:T(8,128)(2,1)S(1)} %get-tuple-element.237, s32[]{:T(128)S(6)} %copy.84), kind=kOutput, calls=%fused_computation.11.clone.1 | convolution fusion | flops 135790592 | bytes 10503168 | tf_op jit(solution)/shard_map/while/body/eval_jaxpr/tsri,tsrj->tsij/dot_general | solution.py:111
  151.0 12.5 %convolution_add_fusion.4 = f32[8,16384]{1,0:T(8,128)S(1)} fusion(f32[16,8,128,128]{3,2,1,0:T(8,128)} %bitcast.131, f32[8,16384]{1,0:T(8,128)S(1)} %get-tuple-element.224, pred[]{:T(512)S(6)} %compare.26, f32[2,8,128]{2,1,0:T(8,128)S(1)} %get-tuple-element.235, s32[]{:T(128)S(6)} %copy.84), kind=kOutput, calls=%fused_computation.7.clone.1 | convolution fusion | flops 201588736 | bytes 9441285 | tf_op jit(solution)/shard_map/while/body/eval_jaxpr/dot_general | solution.py:122
  164.6 5.2 %fusion.54 = f32[128,128,128]{2,1,0:T(8,128)} fusion(f32[128,32]{1,0:T(8,128)S(1)} %dynamic-slice_bitcast_fusion.5, bf16[2,128,32,128]{3,2,1,0:T(8,128)(2,1)S(1)} %get-tuple-element.237, s32[]{:T(128)S(6)} %copy.84), kind=kOutput, calls=%fused_computation.11.clone.1 | convolution fusion | flops 135790592 | bytes 10503168 | tf_op jit(solution)/shard_map/while/body/eval_jaxpr/tsri,tsrj->tsij/dot_general | solution.py:111
  169.9 12.5 %convolution_add_fusion.4 = f32[8,16384]{1,0:T(8,128)S(1)} fusion(f32[16,8,128,128]{3,2,1,0:T(8,128)} %bitcast.131, f32[8,16384]{1,0:T(8,128)S(1)} %get-tuple-element.224, pred[]{:T(512)S(6)} %compare.26, f32[2,8,128]{2,1,0:T(8,128)S(1)} %get-tuple-element.235, s32[]{:T(128)S(6)} %copy.84), kind=kOutput, calls=%fused_computation.7.clone.1 | convolution fusion | flops 201588736 | bytes 9441285 | tf_op jit(solution)/shard_map/while/body/eval_jaxpr/dot_general | solution.py:122
  183.7 4.5 %collective-permute-start.2 = (f32[2,16512]{1,0:T(2,128)S(1)}, f32[2,16512]{1,0:T(2,128)S(1)}, u32[]{:S(2)}, u32[]{:S(2)}) collective-permute-start(f32[2,16512]{1,0:T(2,128)S(1)} %get-tuple-element.134), channel_id=1, source_target_pairs={{0,3},{1,0},{2,1},{3,2},{4,7},{5,4},{6,5},{7,6},{8,11},{9,8},{10,9... | collective-permute-start | bytes 396296 | tf_op jit(solution)/shard_map/ppermute | solution.py:39
  188.2 2.4 collective-permute-start.1
  190.7 2.7 collective-permute-start
  195.5 3.9 %collective-permute-done = f32[2,16512]{1,0:T(2,128)S(1)} collective-permute-done((f32[2,16512]{1,0:T(2,128)S(1)}, f32[2,16512]{1,0:T(2,128)S(1)}, u32[]{:S(2)}, u32[]{:S(2)}) %collective-permute-start) | collective-permute-done | bytes 132128 | tf_op jit(solution)/shard_map/ppermute | solution.py:39
  199.8 23.5 %custom-call.9 = f32[2,128,128]{2,1,0:T(8,128)S(1)} custom-call(f32[2,128,128]{2,1,0:T(8,128)S(1)} %fusion.20), custom_call_target="Cholesky" | custom-call | tf_op jit(solution)/shard_map/jit(cholesky)/cholesky | solution.py:15
  223.6 19.7 %custom-call.10 = f32[2,1,128,128]{2,3,1,0:T(8,128)S(1)} custom-call(f32[2,1,128,128]{3,2,1,0:T(8,128)S(1)} %select_bitcast_fusion), custom_call_target="InvertDiagBlocksLowerTriangular" | custom-call | tf_op jit(solution)/shard_map/triangular_solve | solution.py:17
  247.7 3.3 collective-permute-start.12
  251.5 2.8 collective-permute-done.12
  255.4 28.2 %all_to_all.15 = f32[128,2,128]{2,1,0:T(2,128)S(1)} all-to-all(f32[128,2,128]{2,1,0:T(2,128)S(1)} %copy.61), channel_id=1, replica_groups=mesh['ent'=128,'rep'=4] {'ent'}, dimensions={0} | all-to-all | bytes 262144 | tf_op jit(solution)/shard_map/all_to_all | solution.py:151
  283.6 46.8 %while.23 = (s32[]{:T(128)}, f32[1024,128]{1,0:T(8,128)S(1)}, s32[2,128,32]{2,1,0:T(8,128)S(1)}, f32[2,128,1,32]{3,1,2,0:T(8,128)S(1)}, f32[2,128,1,128]{3,1,2,0:T(8,128)S(1)}, /*index=5*/s32[]{:T(128)}) while((s32[]{:T(128)}, f32[1024,128]{1,0:T(8,128)S(1)}, s32[2,128,32]{2,1,0:T(8,128)S(1)}, f32[2,128,1,32]{3,1,2,0:T(8,128)S(1)}, ...), condition=%wide.region_6.7_spmd, body=%wide.region_4.6_spmd.sunk | while | flops 1048578 | bytes 8749145 | solution.py:180
  284.5 22.6 %scatter_fusion = f32[1024,128]{1,0:T(8,128)S(1)} fusion(f32[1024,128]{1,0:T(8,128)S(1)} %get-tuple-element.248, s32[4096]{0:T(1024)S(1)} %reshape.373, f32[4096,128]{1,0:T(8,128)S(1)} %bitcast_multiply_fusion.2), kind=kCustom, calls=%fused_computation.2.clone.1 | custom fusion | flops 524288 | bytes 6307840 | tf_op jit(solution)/shard_map/while/body/eval_jaxpr/scatter-add | solution.py:171
  307.9 22.6 %scatter_fusion = f32[1024,128]{1,0:T(8,128)S(1)} fusion(f32[1024,128]{1,0:T(8,128)S(1)} %get-tuple-element.248, s32[4096]{0:T(1024)S(1)} %reshape.373, f32[4096,128]{1,0:T(8,128)S(1)} %bitcast_multiply_fusion.2), kind=kCustom, calls=%fused_computation.2.clone.1 | custom fusion | flops 524288 | bytes 6307840 | tf_op jit(solution)/shard_map/while/body/eval_jaxpr/scatter-add | solution.py:171
  (124 shorter events, 30.3 us)
Async XLA Ops:
  0.6 2.0 copy-start
  31.3 22.0 %copy-start.1 = (s32[1,1,256,32]{2,3,1,0:T(8,128)S(1)}, s32[1,1,256,32]{2,3,1,0:T(8,128)}, u32[]{:S(2)}) copy-start(s32[1,1,256,32]{2,3,1,0:T(8,128)} %param.14) | copy-start | bytes 98308
  31.3 22.6 %copy-start.8 = (s32[1,1,128]{2,1,0:T(1,128)S(1)}, s32[1,1,128]{2,1,0:T(1,128)}, u32[]{:S(2)}) copy-start(s32[1,1,128]{2,1,0:T(1,128)} %param.15) | copy-start | bytes 1540
  31.3 99.7 %all-to-all-start = ((bf16[128,64,128]{2,1,0:T(8,128)(2,1)}), bf16[128,64,128]{2,1,0:T(8,128)(2,1)S(1)}, u32[]{:S(2)}, u32[]{:S(2)}) async-start(bf16[128,64,128]{2,1,0:T(8,128)(2,1)} %select_select_fusion), calls=%async_computation | async-start | bytes 4194304 | tf_op jit(solution)/shard_map/all_to_all | solution.py:78
  49.8 17.1 %copy-start.5 = (s32[1,1,256,1]{2,3,1,0:T(1,128)S(1)}, s32[1,1,256,1]{2,3,1,0:T(1,128)}, u32[]{:S(2)}) copy-start(s32[1,1,256,1]{2,3,1,0:T(1,128)} %param.13) | copy-start | bytes 3076
  50.1 6.0 %collective-permute-start.3 = (f32[128,128]{1,0:T(8,128)S(1)}, f32[128,128]{1,0:T(8,128)S(1)}, u32[]{:S(2)}, u32[]{:S(2)}) collective-permute-start(f32[128,128]{1,0:T(8,128)S(1)} %fusion.30), channel_id=1, source_target_pairs={{0,1},{1,0},{2,3},{3,2},{4,5},{5,4},{6,7},{7,6},{8,9},{9,8},{10,11... | collective-permute-start | bytes 196616 | tf_op jit(solution)/shard_map/ppermute | solution.py:28
  56.1 6.8 %collective-permute-start.4 = (f32[128,128]{1,0:T(8,128)S(1)}, f32[128,128]{1,0:T(8,128)S(1)}, u32[]{:S(2)}, u32[]{:S(2)}) collective-permute-start(f32[128,128]{1,0:T(8,128)S(1)} %add.219), channel_id=1, source_target_pairs={{0,2},{1,3},{2,0},{3,1},{4,6},{5,7},{6,4},{7,5},{8,10},{9,11},{10,... | collective-permute-start | bytes 196616 | tf_op jit(solution)/shard_map/ppermute | solution.py:28
  63.0 5.4 %collective-permute-start.5 = (f32[128,128]{1,0:T(8,128)S(1)}, f32[128,128]{1,0:T(8,128)S(1)}, u32[]{:S(2)}, u32[]{:S(2)}) collective-permute-start(f32[128,128]{1,0:T(8,128)S(1)} %add.220), channel_id=1, source_target_pairs={{0,4},{1,5},{2,6},{3,7},{4,0},{5,1},{6,2},{7,3},{8,12},{9,13},{10,... | collective-permute-start | bytes 196616 | tf_op jit(solution)/shard_map/ppermute | solution.py:28
  68.4 22.9 %collective-permute-start.6 = (f32[128,128]{1,0:T(8,128)S(1)}, f32[128,128]{1,0:T(8,128)S(1)}, u32[]{:S(2)}, u32[]{:S(2)}) collective-permute-start(f32[128,128]{1,0:T(8,128)S(1)} %add.221), channel_id=1, source_target_pairs={{0,8},{1,9},{2,10},{3,11},{4,12},{5,13},{6,14},{7,15},{8,0},{9,1},... | collective-permute-start | bytes 196616 | tf_op jit(solution)/shard_map/ppermute | solution.py:28
  91.3 12.6 %collective-permute-start.7 = (f32[128,128]{1,0:T(8,128)S(1)}, f32[128,128]{1,0:T(8,128)S(1)}, u32[]{:S(2)}, u32[]{:S(2)}) collective-permute-start(f32[128,128]{1,0:T(8,128)S(1)} %add.222), channel_id=1, source_target_pairs={{0,16},{1,17},{2,18},{3,19},{4,20},{5,21},{6,22},{7,23},{8,24},{9,... | collective-permute-start | bytes 196616 | tf_op jit(solution)/shard_map/ppermute | solution.py:28
  103.9 9.4 %collective-permute-start.8 = (f32[128,128]{1,0:T(8,128)S(1)}, f32[128,128]{1,0:T(8,128)S(1)}, u32[]{:S(2)}, u32[]{:S(2)}) collective-permute-start(f32[128,128]{1,0:T(8,128)S(1)} %add.223), channel_id=1, source_target_pairs={{0,32},{1,33},{2,34},{3,35},{4,36},{5,37},{6,38},{7,39},{8,40},{9,... | collective-permute-start | bytes 196616 | tf_op jit(solution)/shard_map/ppermute | solution.py:28
  113.4 5.0 %collective-permute-start.9 = (f32[128,128]{1,0:T(8,128)S(1)}, f32[128,128]{1,0:T(8,128)S(1)}, u32[]{:S(2)}, u32[]{:S(2)}) collective-permute-start(f32[128,128]{1,0:T(8,128)S(1)} %add.224), channel_id=1, source_target_pairs={{0,64},{1,65},{2,66},{3,67},{4,68},{5,69},{6,70},{7,71},{8,72},{9,... | collective-permute-start | bytes 196616 | tf_op jit(solution)/shard_map/ppermute | solution.py:28
  118.4 6.6 %collective-permute-start.10 = (f32[128,128]{1,0:T(8,128)S(1)}, f32[128,128]{1,0:T(8,128)S(1)}, u32[]{:S(2)}, u32[]{:S(2)}) collective-permute-start(f32[128,128]{1,0:T(8,128)S(1)} %add.225), channel_id=1, source_target_pairs={{0,128},{1,129},{2,130},{3,131},{4,132},{5,133},{6,134},{7,135},{8... | collective-permute-start | bytes 196616 | tf_op jit(solution)/shard_map/ppermute | solution.py:28
  125.0 68.4 %collective-permute-start.11 = (f32[128,128]{1,0:T(8,128)S(1)}, f32[128,128]{1,0:T(8,128)S(1)}, u32[]{:S(2)}, u32[]{:S(2)}) collective-permute-start(f32[128,128]{1,0:T(8,128)S(1)} %add.226), channel_id=1, source_target_pairs={{0,256},{1,257},{2,258},{3,259},{4,260},{5,261},{6,262},{7,263},{8... | collective-permute-start | bytes 196616 | tf_op jit(solution)/shard_map/ppermute | solution.py:28
  131.0 124.4 %all-to-all-start.1 = ((f32[128,2,32]{2,1,0:T(2,128)}), f32[128,2,32]{2,1,0:T(2,128)S(1)}, u32[]{:S(2)}, u32[]{:S(2)}) async-start(f32[128,2,32]{2,1,0:T(2,128)} %and_select_fusion), calls=%async_computation.1 | async-start | bytes 262144 | tf_op jit(solution)/shard_map/all_to_all | solution.py:158
  183.5 39.8 %copy-start.2 = (pred[128,128]{1,0:T(8,128)(4,1)S(1)}, pred[128,128]{1,0:T(8,128)(4,1)}, u32[]{:S(2)}) copy-start(pred[128,128]{1,0:T(8,128)(4,1)} %iota_compare_fusion) | copy-start | bytes 49156
  183.5 39.9 %copy-start.3 = (pred[128,128]{1,0:T(8,128)(4,1)S(1)}, pred[128,128]{1,0:T(8,128)(4,1)}, u32[]{:S(2)}) copy-start(pred[128,128]{1,0:T(8,128)(4,1)} %iota_compare_fusion.1) | copy-start | bytes 49156
  183.6 71.3 %copy-start.7 = (pred[4]{0:T(512)(128)(4,1)S(1)}, pred[4]{0:T(512)(128)(4,1)}, u32[]{:S(2)}) copy-start(pred[4]{0:T(512)(128)(4,1)} %compare_and_fusion.1) | copy-start | bytes 16
  183.6 71.4 %copy-start.4 = (s32[128,2]{0,1:T(2,128)S(1)}, s32[128,2]{0,1:T(2,128)}, u32[]{:S(2)}) copy-start(s32[128,2]{0,1:T(2,128)} %copy.60) | copy-start | bytes 3076
  183.7 9.8 %collective-permute-start.2 = (f32[2,16512]{1,0:T(2,128)S(1)}, f32[2,16512]{1,0:T(2,128)S(1)}, u32[]{:S(2)}, u32[]{:S(2)}) collective-permute-start(f32[2,16512]{1,0:T(2,128)S(1)} %get-tuple-element.134), channel_id=1, source_target_pairs={{0,3},{1,0},{2,1},{3,2},{4,7},{5,4},{6,5},{7,6},{8,11},{9,8},{10,9... | collective-permute-start | bytes 396296 | tf_op jit(solution)/shard_map/ppermute | solution.py:39
  188.2 7.2 %collective-permute-start.1 = (f32[2,16512]{1,0:T(2,128)S(1)}, f32[2,16512]{1,0:T(2,128)S(1)}, u32[]{:S(2)}, u32[]{:S(2)}) collective-permute-start(f32[2,16512]{1,0:T(2,128)S(1)} %get-tuple-element.135), channel_id=1, source_target_pairs={{0,2},{1,3},{2,0},{3,1},{4,6},{5,7},{6,4},{7,5},{8,10},{9,11},{10,... | collective-permute-start | bytes 396296 | tf_op jit(solution)/shard_map/ppermute | solution.py:39
  190.7 8.7 %collective-permute-start = (f32[2,16512]{1,0:T(2,128)S(1)}, f32[2,16512]{1,0:T(2,128)S(1)}, u32[]{:S(2)}, u32[]{:S(2)}) collective-permute-start(f32[2,16512]{1,0:T(2,128)S(1)} %get-tuple-element.133), channel_id=1, source_target_pairs={{0,1},{1,2},{2,3},{3,0},{4,5},{5,6},{6,7},{7,4},{8,9},{9,10},{10,1... | collective-permute-start | bytes 396296 | tf_op jit(solution)/shard_map/ppermute | solution.py:39
  243.8 39.8 %copy-start.6 = (f32[2,1,128]{2,1,0:T(1,128)}, f32[2,1,128]{2,1,0:T(1,128)S(1)}, u32[]{:S(2)}) copy-start(f32[2,1,128]{2,1,0:T(1,128)S(1)} %fusion.17) | copy-start | bytes 3076
  243.8 7.2 %collective-permute-start.14 = (bf16[2,128]{1,0:T(2,128)(2,1)S(1)}, bf16[2,128]{1,0:T(2,128)(2,1)S(1)}, u32[]{:S(2)}, u32[]{:S(2)}) collective-permute-start(bf16[2,128]{1,0:T(2,128)(2,1)S(1)} %convert_element_type.34), channel_id=1, source_target_pairs={{0,3},{1,0},{2,1},{3,2},{4,7},{5,4},{6,5},{7,6},{8,11},{9,8},{10,9... | collective-permute-start | bytes 1544 | tf_op jit(solution)/shard_map/ppermute | solution.py:49
  245.7 5.8 %collective-permute-start.13 = (bf16[2,128]{1,0:T(2,128)(2,1)S(1)}, bf16[2,128]{1,0:T(2,128)(2,1)S(1)}, u32[]{:S(2)}, u32[]{:S(2)}) collective-permute-start(bf16[2,128]{1,0:T(2,128)(2,1)S(1)} %convert_element_type.34), channel_id=1, source_target_pairs={{0,2},{1,3},{2,0},{3,1},{4,6},{5,7},{6,4},{7,5},{8,10},{9,11},{10,... | collective-permute-start | bytes 1544 | tf_op jit(solution)/shard_map/ppermute | solution.py:49
  247.7 6.6 %collective-permute-start.12 = (bf16[2,128]{1,0:T(2,128)(2,1)S(1)}, bf16[2,128]{1,0:T(2,128)(2,1)S(1)}, u32[]{:S(2)}, u32[]{:S(2)}) collective-permute-start(bf16[2,128]{1,0:T(2,128)(2,1)S(1)} %convert_element_type.34), channel_id=1, source_target_pairs={{0,1},{1,2},{2,3},{3,0},{4,5},{5,6},{6,7},{7,4},{8,9},{9,10},{10,1... | collective-permute-start | bytes 1544 | tf_op jit(solution)/shard_map/ppermute | solution.py:49

commit v2 on v1

--- a/solution.py
+++ b/solution.py
@@ -91,49 +91,25 @@
     owners = tile_users.reshape(tile_slots * seg_count)
     selector = owners[None, :] == jnp.arange(user_block, dtype=jnp.int32)[:, None]
     selector_f = selector.astype(jnp.float32)
-    src_group = 1
-    while (
-        src_group * 2 <= n_ent
-        and n_ent % (src_group * 2) == 0
-        and (src_group * 2 * slot_cap * tile_rows <= 4096)
-    ):
-        src_group = src_group * 2
-    tiles_blk = src_group * slot_cap
-    block_count = tile_slots // tiles_blk
-    runs_blk = tiles_blk * seg_count
-
-    def accumulate(state_pair, pieces):
-        gram_run, rhs_run = state_pair
-        rows_blk, gram_blk, rhs_blk, select_blk = pieces
-        weighted = (gram_blk[:, :, None] * rows_blk).astype(jnp.bfloat16)
-        rows_seg = rows_blk.reshape(tiles_blk, seg_count, seg_length, rank_width)
-        weighted = weighted.reshape(tiles_blk, seg_count, seg_length, rank_width)
-        run_gram = jnp.einsum(
-            "tsri,tsrj->tsij", weighted, rows_seg, preferred_element_type=jnp.float32
-        )
-        run_gram = run_gram.reshape(runs_blk, rank_width * rank_width)
-        run_rhs = jnp.einsum(
-            "tsr,tsri->tsi",
-            rhs_blk.reshape(tiles_blk, seg_count, seg_length),
-            rows_seg.astype(jnp.float32),
-            precision=highest,
-        )
-        run_rhs = run_rhs.reshape(runs_blk, rank_width)
-        gram_run = gram_run + jnp.dot(select_blk, run_gram, precision=highest)
-        rhs_run = rhs_run + jnp.dot(select_blk, run_rhs, precision=highest)
-        return ((gram_run, rhs_run), None)
-
-    block_pieces = (
-        incoming.reshape(block_count, tiles_blk, tile_rows, rank_width),
-        gram_weight.reshape(block_count, tiles_blk, tile_rows),
-        rhs_weight.reshape(block_count, tiles_blk, tile_rows),
-        jnp.transpose(selector_f.reshape(user_block, block_count, runs_blk), (1, 0, 2)),
+    rows_all = incoming.reshape(tile_slots * tile_rows, rank_width)
+    weighted = (gram_weight.reshape(-1, 1) * rows_all.astype(jnp.float32)).astype(jnp.bfloat16)
+    row_owner = jnp.repeat(owners, seg_length)
+    row_select = row_owner[:, None] == jnp.arange(user_block, dtype=jnp.int32)[None, :]
+    masked = jnp.where(row_select[:, :, None], weighted[:, None, :], jnp.zeros((), jnp.bfloat16))
+    gram_acc = lax.dot_general(
+        masked.reshape(-1, user_block * rank_width),
+        rows_all,
+        (((0,), (0,)), ((), ())),
+        preferred_element_type=jnp.float32,
+    ).reshape(user_block, rank_width * rank_width)
+    rhs_rows = jnp.where(row_select, rhs_weight.reshape(-1, 1), 0.0)
+    rhs_acc = lax.dot_general(
+        rhs_rows,
+        rows_all.astype(jnp.float32),
+        (((0,), (0,)), ((), ())),
+        precision=highest,
+        preferred_element_type=jnp.float32,
     )
-    start_pair = (
-        jnp.zeros((user_block, rank_width * rank_width), jnp.float32),
-        jnp.zeros((user_block, rank_width), jnp.float32),
-    )
-    (gram_acc, rhs_acc), _ = lax.scan(accumulate, start_pair, block_pieces)
     identity_mat = jnp.eye(rank_width, dtype=jnp.float32)
     added_term = tree_sum(partial_gram, n_ent * n_rep) + RIDGE * identity_mat
     own_gram, own_rhs = rep_scatter_sum(
@@ -146,7 +122,7 @@
         solved,
         (((0,), (0,)), ((), ())),
         preferred_element_type=jnp.float32,
-    )
+    ).astype(jnp.bfloat16)
     back_factor, back_weight = (
         lax.all_to_all(
             run_factor.reshape(n_ent, slot_cap, seg_count * rank_width),
@@ -163,21 +139,17 @@
             tiled=True,
         ),
     )
-
-    def spread(running, pieces):
-        factor_blk, weight_blk, item_blk = pieces
-        contrib = (weight_blk[:, :, :, None] * factor_blk[:, :, None, :]).reshape(-1, rank_width)
-        return (
-            running + jax.ops.segment_sum(contrib, item_blk.reshape(-1), num_segments=item_count),
-            None,
-        )
-
-    spread_pieces = (
-        back_factor.reshape(block_count, tiles_blk, seg_count, rank_width),
-        back_weight.reshape(block_count, tiles_blk, seg_count, seg_length),
-        item_ids.reshape(block_count, tiles_blk, tile_rows),
+    item_hot = item_ids[:, :, None] == jnp.arange(item_count, dtype=jnp.int32)[None, None, :]
+    run_weight = back_weight.reshape(tile_slots * seg_count, seg_length)
+    hot_runs = item_hot.reshape(tile_slots * seg_count, seg_length, item_count)
+    spread_mat = jnp.sum(jnp.where(hot_runs, run_weight[:, :, None], 0.0), axis=1)
+    item_rhs = lax.dot_general(
+        spread_mat,
+        back_factor.reshape(tile_slots * seg_count, rank_width).astype(jnp.float32),
+        (((0,), (0,)), ((), ())),
+        precision=highest,
+        preferred_element_type=jnp.float32,
     )
-    item_rhs, _ = lax.scan(spread, jnp.zeros((item_count, rank_width), jnp.float32), spread_pieces)
     return (own_factors, item_rhs * RHS_SCALE)
 
 

time: 332 us -> 272 us (0.82)
  blocking collectives: 28.2 us -> 0 us
  matrix products: 38.7 us -> 10.6 us
  other arithmetic: 100 us -> 74.8 us
  starting transfers between devices: 80 us -> 102 us
  waiting for transfers between devices: 53.8 us -> 50.3 us
    scatter-add x2 -> x0, other arithmetic: 45.1 us -> none  [spread(): jax.ops.segment_sum(contrib, item_blk.reshape(-1), num_segments=item_count)]
    dot_general x8 -> x3, matrix products: 37.6 us -> 8.89 us  [the longest x1 5.39 us: shards(): lax.dot_general(masked.reshape(-1, user_block * rank_width), rows_all, ((...]
    all_to_all x1 -> x0, blocking collectives: 28.2 us -> none  [shards(): lax.all_to_all(run_factor.reshape(n_ent, slot_cap, seg_count * rank_width...]
    all_to_all x0 -> x1, starting transfers between devices: none -> 15.9 us  [shards(): lax.all_to_all(run_factor.reshape(n_ent, slot_cap, seg_count * rank_width...]
    select_n x0 -> x1, other arithmetic: none -> 11.2 us  [shards(): jnp.where(row_select[:, :, None], weighted[:, None, :], jnp.zeros((), jnp...]
    reduce_sum x0 -> x1, other arithmetic: none -> 7.37 us  [shards(): jnp.sum(jnp.where(hot_runs, run_weight[:, :, None], 0.0), axis=1)]
    ppermute x9, starting transfers between devices: 29.8 us -> 37.1 us  [tree_sum(): value = value + lax.ppermute(value, ('ent', 'rep'), pairs)]
    ppermute x9, waiting for transfers between devices: 44.7 us -> 38 us  [tree_sum(): value = value + lax.ppermute(value, ('ent', 'rep'), pairs)]
  transfers between devices with their start and end apart: 17 -> 18, of which waited for: 10 -> 12; matrix products, arithmetic and copies ran while one was open for 27% -> 31% of each run, Pallas kernels for 0% -> 0%
where the time goes in v2:
time: 272 us; the launch traced here: 271 us
  starting transfers between devices  102 us (38%)
  other arithmetic  74.8 us (28%)
  waiting for transfers between devices  50.3 us (18%)
  local copies, waits for them, and re-layouts  31.5 us (12%)
  matrix products  10.6 us (4%)
    ppermute x9, waiting for transfers between devices, tree_sum(): value = value + lax.ppermute(value, ('ent', 'rep'), pairs)  38 us
    ppermute x9, starting transfers between devices, tree_sum(): value = value + lax.ppermute(value, ('ent', 'rep'), pairs)  37.1 us
    gather x1, local copies, waits for them, and re-layouts, shards(): jnp.take(item_factors, item_ids.reshape(-1), axis=0)  24 us
    another operation x4, other arithmetic, solve_users(): lower = jnp.linalg.cholesky(gram)  23.6 us
    another operation x3, other arithmetic, solve_users(): lax.linalg.triangular_solve(lower, halfway, left_side=True, lower=True, t...  20.4 us
    all_to_all x1, starting transfers between devices, shards(): lax.all_to_all(picked.reshape(n_ent, slot_cap * tile_rows, rank_width), '...  18.5 us
    all_to_all x1, starting transfers between devices, shards(): lax.all_to_all(run_factor.reshape(n_ent, slot_cap, seg_count * rank_width...  15.9 us
    all_to_all x1, starting transfers between devices, shards(): lax.all_to_all(rhs_weight.reshape(n_ent, slot_cap, tile_rows), 'ent', spl...  13.7 us
  transfers between devices with their start and end apart: 18, of which 12 were waited for; matrix products, arithmetic and copies ran while one was open for 31% of the time, Pallas kernels for 0%

profile of v2, /device:TPU:1, one launch (start us, length us, event | category | flops | bytes accessed | tf_op | source)
XLA Modules:
  0.0 270.6 jit_solution(2329472332838331212)
XLA Ops:
  2.7 24.0 %gather_fusion = bf16[8192,128]{1,0:T(8,128)(2,1)S(1)} fusion(bf16[1024,128]{1,0:T(8,128)(2,1)S(1)} %copy-done, s32[8192]{0:T(1024)S(1)} %broadcast_clamp_fusion), kind=kCustom, calls=%fused_computation | custom fusion | bytes 4227072 | tf_op jit(solution)/shard_map/jit(_take)/gather | solution.py:74
  26.7 4.5 %select_select_fusion = bf16[128,64,128]{2,1,0:T(8,128)(2,1)} fusion(bf16[128,64,128]{2,1,0:T(8,128)(2,1)S(1)} %bitcast.73, pred[128,64]{1,0:T(8,128)(4,1)S(1)} %compare_and_fusion, pred[128,64]{1,0:T(8,128)(4,1)S(1)} %copy.39), kind=kLoop, calls=%fused_computation.9 | loop fusion | flops 2097152 | bytes 4210688 | tf_op jit(solution)/shard_map/jit(_where)/select_n | solution.py:77
  31.3 18.5 %all-to-all-start = ((bf16[128,64,128]{2,1,0:T(8,128)(2,1)}), bf16[128,64,128]{2,1,0:T(8,128)(2,1)S(1)}, u32[]{:S(2)}, u32[]{:S(2)}) async-start(bf16[128,64,128]{2,1,0:T(8,128)(2,1)} %select_select_fusion), calls=%async_computation | async-start | bytes 4194304 | tf_op jit(solution)/shard_map/all_to_all | solution.py:78
  50.1 3.1 %collective-permute-start.3 = (f32[128,128]{1,0:T(8,128)S(1)}, f32[128,128]{1,0:T(8,128)S(1)}, u32[]{:S(2)}, u32[]{:S(2)}) collective-permute-start(f32[128,128]{1,0:T(8,128)S(1)} %fusion.28), channel_id=1, source_target_pairs={{0,1},{1,0},{2,3},{3,2},{4,5},{5,4},{6,7},{7,6},{8,9},{9,8},{10,11... | collective-permute-start | bytes 196616 | tf_op jit(solution)/shard_map/ppermute | solution.py:28
  55.4 4.7 %collective-permute-start.4 = (f32[128,128]{1,0:T(8,128)S(1)}, f32[128,128]{1,0:T(8,128)S(1)}, u32[]{:S(2)}, u32[]{:S(2)}) collective-permute-start(f32[128,128]{1,0:T(8,128)S(1)} %add.205), channel_id=1, source_target_pairs={{0,2},{1,3},{2,0},{3,1},{4,6},{5,7},{6,4},{7,5},{8,10},{9,11},{10,... | collective-permute-start | bytes 196616 | tf_op jit(solution)/shard_map/ppermute | solution.py:28
  62.2 4.5 %collective-permute-start.5 = (f32[128,128]{1,0:T(8,128)S(1)}, f32[128,128]{1,0:T(8,128)S(1)}, u32[]{:S(2)}, u32[]{:S(2)}) collective-permute-start(f32[128,128]{1,0:T(8,128)S(1)} %add.206), channel_id=1, source_target_pairs={{0,4},{1,5},{2,6},{3,7},{4,0},{5,1},{6,2},{7,3},{8,12},{9,13},{10,... | collective-permute-start | bytes 196616 | tf_op jit(solution)/shard_map/ppermute | solution.py:28
  67.4 2.0 copy.37
  69.5 2.8 %collective-permute-start.6 = (f32[128,128]{1,0:T(8,128)S(1)}, f32[128,128]{1,0:T(8,128)S(1)}, u32[]{:S(2)}, u32[]{:S(2)}) collective-permute-start(f32[128,128]{1,0:T(8,128)S(1)} %add.207), channel_id=1, source_target_pairs={{0,8},{1,9},{2,10},{3,11},{4,12},{5,13},{6,14},{7,15},{8,0},{9,1},... | collective-permute-start | bytes 196616 | tf_op jit(solution)/shard_map/ppermute | solution.py:28
  73.1 18.2 %collective-permute-done.6 = f32[128,128]{1,0:T(8,128)S(1)} collective-permute-done((f32[128,128]{1,0:T(8,128)S(1)}, f32[128,128]{1,0:T(8,128)S(1)}, u32[]{:S(2)}, u32[]{:S(2)}) %collective-permute-start.6) | collective-permute-done | bytes 65568 | tf_op jit(solution)/shard_map/ppermute | solution.py:28
  91.3 5.7 %collective-permute-start.7 = (f32[128,128]{1,0:T(8,128)S(1)}, f32[128,128]{1,0:T(8,128)S(1)}, u32[]{:S(2)}, u32[]{:S(2)}) collective-permute-start(f32[128,128]{1,0:T(8,128)S(1)} %add.208), channel_id=1, source_target_pairs={{0,16},{1,17},{2,18},{3,19},{4,20},{5,21},{6,22},{7,23},{8,24},{9,... | collective-permute-start | bytes 196616 | tf_op jit(solution)/shard_map/ppermute | solution.py:28
  97.0 6.9 %collective-permute-done.7 = f32[128,128]{1,0:T(8,128)S(1)} collective-permute-done((f32[128,128]{1,0:T(8,128)S(1)}, f32[128,128]{1,0:T(8,128)S(1)}, u32[]{:S(2)}, u32[]{:S(2)}) %collective-permute-start.7) | collective-permute-done | bytes 65568 | tf_op jit(solution)/shard_map/ppermute | solution.py:28
  103.9 2.2 collective-permute-start.8
  106.8 6.2 %collective-permute-done.8 = f32[128,128]{1,0:T(8,128)S(1)} collective-permute-done((f32[128,128]{1,0:T(8,128)S(1)}, f32[128,128]{1,0:T(8,128)S(1)}, u32[]{:S(2)}, u32[]{:S(2)}) %collective-permute-start.8) | collective-permute-done | bytes 65568 | tf_op jit(solution)/shard_map/ppermute | solution.py:28
  114.9 3.1 %collective-permute-done.9 = f32[128,128]{1,0:T(8,128)S(1)} collective-permute-done((f32[128,128]{1,0:T(8,128)S(1)}, f32[128,128]{1,0:T(8,128)S(1)}, u32[]{:S(2)}, u32[]{:S(2)}) %collective-permute-start.9) | collective-permute-done | bytes 65568 | tf_op jit(solution)/shard_map/ppermute | solution.py:28
  118.0 7.8 %collective-permute-start.10 = (f32[128,128]{1,0:T(8,128)S(1)}, f32[128,128]{1,0:T(8,128)S(1)}, u32[]{:S(2)}, u32[]{:S(2)}) collective-permute-start(f32[128,128]{1,0:T(8,128)S(1)} %add.211), channel_id=1, source_target_pairs={{0,128},{1,129},{2,130},{3,131},{4,132},{5,133},{6,134},{7,135},{8... | collective-permute-start | bytes 196616 | tf_op jit(solution)/shard_map/ppermute | solution.py:28
  128.1 4.5 %collective-permute-start.11 = (f32[128,128]{1,0:T(8,128)}, f32[128,128]{1,0:T(8,128)}, u32[]{:S(2)}, u32[]{:S(2)}) collective-permute-start(f32[128,128]{1,0:T(8,128)} %add.212), channel_id=1, source_target_pairs={{0,256},{1,257},{2,258},{3,259},{4,260},{5,261},{6,262},{7,263},{8... | collective-permute-start | bytes 196616 | tf_op jit(solution)/shard_map/ppermute | solution.py:28
  132.6 13.7 %all-to-all-start.1 = ((f32[128,2,32]{2,1,0:T(2,128)}), f32[128,2,32]{2,1,0:T(2,128)S(1)}, u32[]{:S(2)}, u32[]{:S(2)}) async-start(f32[128,2,32]{2,1,0:T(2,128)} %and_select_fusion), calls=%async_computation.1 | async-start | bytes 262144 | tf_op jit(solution)/shard_map/all_to_all | solution.py:134
  146.3 3.5 %multiply_convert_fusion = bf16[8192,128]{1,0:T(8,128)(2,1)S(1)} fusion(f32[8192]{0:T(1024)S(1)} %mul.47, bf16[128,64,128]{2,1,0:T(8,128)(2,1)S(1)} %all-to-all-done), kind=kLoop, calls=%fused_computation.8 | loop fusion | flops 3145728 | bytes 4227072 | tf_op jit(solution)/shard_map/convert_element_type | solution.py:95
  149.8 11.2 %broadcast_select_fusion = bf16[8192,8,128]{2,1,0:T(8,128)(2,1)S(1)} fusion(pred[8192,8]{1,0:T(8,128)(4,1)S(1)} %copy-done.1, bf16[8192,128]{1,0:T(8,128)(2,1)S(1)} %multiply_convert_fusion), kind=kLoop, calls=%fused_computation.7 | loop fusion | flops 8388608 | bytes 18939904 | tf_op jit(solution)/shard_map/jit(_where)/select_n | solution.py:98
  161.0 5.4 %fusion = f32[1024,128]{1,0:T(8,128)} fusion(bf16[8192,128]{1,0:T(8,128)(2,1)S(1)} %bitcast.70, bf16[1024,8,8,128]{3,2,1,0:T(8,128)(2,1)S(1)} %bitcast.72), kind=kOutput, calls=%fused_computation.4 | convolution fusion | flops 2147483648 | bytes 19398656 | tf_op jit(solution)/shard_map/dot_general | solution.py:99
  169.5 4.4 %collective-permute-start.2 = (f32[2,16512]{1,0:T(2,128)S(1)}, f32[2,16512]{1,0:T(2,128)S(1)}, u32[]{:S(2)}, u32[]{:S(2)}) collective-permute-start(f32[2,16512]{1,0:T(2,128)S(1)} %get-tuple-element.4), channel_id=1, source_target_pairs={{0,3},{1,0},{2,1},{3,2},{4,7},{5,4},{6,5},{7,6},{8,11},{9,8},{10,9... | collective-permute-start | bytes 396296 | tf_op jit(solution)/shard_map/ppermute | solution.py:39
  173.8 2.4 collective-permute-start.1
  176.3 2.7 %collective-permute-start = (f32[2,16512]{1,0:T(2,128)S(1)}, f32[2,16512]{1,0:T(2,128)S(1)}, u32[]{:S(2)}, u32[]{:S(2)}) collective-permute-start(f32[2,16512]{1,0:T(2,128)S(1)} %get-tuple-element.2), channel_id=1, source_target_pairs={{0,1},{1,2},{2,3},{3,0},{4,5},{5,6},{6,7},{7,4},{8,9},{9,10},{10,1... | collective-permute-start | bytes 396296 | tf_op jit(solution)/shard_map/ppermute | solution.py:39
  181.1 3.9 %collective-permute-done = f32[2,16512]{1,0:T(2,128)S(1)} collective-permute-done((f32[2,16512]{1,0:T(2,128)S(1)}, f32[2,16512]{1,0:T(2,128)S(1)}, u32[]{:S(2)}, u32[]{:S(2)}) %collective-permute-start) | collective-permute-done | bytes 132128 | tf_op jit(solution)/shard_map/ppermute | solution.py:39
  185.4 23.5 %custom-call.9 = f32[2,128,128]{2,1,0:T(8,128)S(1)} custom-call(f32[2,128,128]{2,1,0:T(8,128)S(1)} %fusion.15), custom_call_target="Cholesky" | custom-call | tf_op jit(solution)/shard_map/jit(cholesky)/cholesky | solution.py:15
  209.2 19.7 %custom-call.10 = f32[2,1,128,128]{2,3,1,0:T(8,128)S(1)} custom-call(f32[2,1,128,128]{3,2,1,0:T(8,128)S(1)} %select_bitcast_fusion), custom_call_target="InvertDiagBlocksLowerTriangular" | custom-call | tf_op jit(solution)/shard_map/triangular_solve | solution.py:17
  231.3 2.0 collective-permute-start.13
  233.3 3.3 %collective-permute-start.12 = (bf16[2,128]{1,0:T(2,128)(2,1)S(1)}, bf16[2,128]{1,0:T(2,128)(2,1)S(1)}, u32[]{:S(2)}, u32[]{:S(2)}) collective-permute-start(bf16[2,128]{1,0:T(2,128)(2,1)S(1)} %convert_element_type.43), channel_id=1, source_target_pairs={{0,1},{1,2},{2,3},{3,0},{4,5},{5,6},{6,7},{7,4},{8,9},{9,10},{10,1... | collective-permute-start | bytes 1544 | tf_op jit(solution)/shard_map/ppermute | solution.py:49
  237.1 2.8 %collective-permute-done.12 = bf16[2,128]{1,0:T(2,128)(2,1)S(1)} collective-permute-done((bf16[2,128]{1,0:T(2,128)(2,1)S(1)}, bf16[2,128]{1,0:T(2,128)(2,1)S(1)}, u32[]{:S(2)}, u32[]{:S(2)}) %collective-permute-start.12) | collective-permute-done | bytes 544 | tf_op jit(solution)/shard_map/ppermute | solution.py:49
  241.4 15.9 %all-to-all-start.2 = ((bf16[128,2,128]{2,1,0:T(2,128)(2,1)}), bf16[128,2,128]{2,1,0:T(2,128)(2,1)S(1)}, u32[]{:S(2)}, u32[]{:S(2)}) async-start(bf16[128,2,128]{2,1,0:T(2,128)(2,1)} %bitcast.27), calls=%async_computation.2 | async-start | bytes 131072 | tf_op jit(solution)/shard_map/all_to_all | solution.py:127
  257.3 7.4 %select_reduce_fusion = f32[256,1024]{1,0:T(8,128)S(1)} fusion(f32[256,32]{1,0:T(8,128)S(1)} %bitcast.74, s32[256,32]{1,0:T(8,128)S(1)} %copy.47), kind=kLoop, calls=%fused_computation.2 | loop fusion | flops 24903680 | bytes 1114112 | tf_op jit(solution)/shard_map/reduce_sum | solution.py:145
  264.7 4.1 %all-to-all-done.2 = bf16[128,2,128]{2,1,0:T(2,128)(2,1)S(1)} async-done(((bf16[128,2,128]{2,1,0:T(2,128)(2,1)}), bf16[128,2,128]{2,1,0:T(2,128)(2,1)S(1)}, u32[]{:S(2)}, u32[]{:S(2)}) %all-to-all-start.2) | async-done | bytes 65568 | tf_op jit(solution)/shard_map/all_to_all | solution.py:127
  (102 shorter events, 24.7 us)
Async XLA Ops:
  0.6 2.0 copy-start
  31.2 22.0 %copy-start.6 = (s32[1,1,256,1]{2,3,1,0:T(1,128)S(1)}, s32[1,1,256,1]{2,3,1,0:T(1,128)}, u32[]{:S(2)}) copy-start(s32[1,1,256,1]{2,3,1,0:T(1,128)} %param.9) | copy-start | bytes 3076
  31.3 22.2 %copy-start.3 = (s32[1,1,256,32]{2,3,1,0:T(8,128)S(1)}, s32[1,1,256,32]{2,3,1,0:T(8,128)}, u32[]{:S(2)}) copy-start(s32[1,1,256,32]{2,3,1,0:T(8,128)} %param.10) | copy-start | bytes 98308
  31.3 23.6 %copy-start.7 = (s32[1,1,128]{2,1,0:T(1,128)S(1)}, s32[1,1,128]{2,1,0:T(1,128)}, u32[]{:S(2)}) copy-start(s32[1,1,128]{2,1,0:T(1,128)} %param.11) | copy-start | bytes 1540
  31.3 101.3 %all-to-all-start = ((bf16[128,64,128]{2,1,0:T(8,128)(2,1)}), bf16[128,64,128]{2,1,0:T(8,128)(2,1)S(1)}, u32[]{:S(2)}, u32[]{:S(2)}) async-start(bf16[128,64,128]{2,1,0:T(8,128)(2,1)} %select_select_fusion), calls=%async_computation | async-start | bytes 4194304 | tf_op jit(solution)/shard_map/all_to_all | solution.py:78
  49.8 19.6 %copy-start.4 = (s32[1,1,256,32]{2,3,1,0:T(8,128)S(1)}, s32[1,1,256,32]{2,3,1,0:T(8,128)}, u32[]{:S(2)}) copy-start(s32[1,1,256,32]{2,3,1,0:T(8,128)} %param.7) | copy-start | bytes 98308
  50.1 5.3 %collective-permute-start.3 = (f32[128,128]{1,0:T(8,128)S(1)}, f32[128,128]{1,0:T(8,128)S(1)}, u32[]{:S(2)}, u32[]{:S(2)}) collective-permute-start(f32[128,128]{1,0:T(8,128)S(1)} %fusion.28), channel_id=1, source_target_pairs={{0,1},{1,0},{2,3},{3,2},{4,5},{5,4},{6,7},{7,6},{8,9},{9,8},{10,11... | collective-permute-start | bytes 196616 | tf_op jit(solution)/shard_map/ppermute | solution.py:28
  53.4 92.9 %copy-start.2 = (s32[8192]{0:T(1024)}, s32[8192]{0:T(1024)S(1)}, u32[]{:S(2)}) copy-start(s32[8192]{0:T(1024)S(1)} %eq.56) | copy-start | bytes 98308
  55.4 6.8 %collective-permute-start.4 = (f32[128,128]{1,0:T(8,128)S(1)}, f32[128,128]{1,0:T(8,128)S(1)}, u32[]{:S(2)}, u32[]{:S(2)}) collective-permute-start(f32[128,128]{1,0:T(8,128)S(1)} %add.205), channel_id=1, source_target_pairs={{0,2},{1,3},{2,0},{3,1},{4,6},{5,7},{6,4},{7,5},{8,10},{9,11},{10,... | collective-permute-start | bytes 196616 | tf_op jit(solution)/shard_map/ppermute | solution.py:28
  62.2 7.3 %collective-permute-start.5 = (f32[128,128]{1,0:T(8,128)S(1)}, f32[128,128]{1,0:T(8,128)S(1)}, u32[]{:S(2)}, u32[]{:S(2)}) collective-permute-start(f32[128,128]{1,0:T(8,128)S(1)} %add.206), channel_id=1, source_target_pairs={{0,4},{1,5},{2,6},{3,7},{4,0},{5,1},{6,2},{7,3},{8,12},{9,13},{10,... | collective-permute-start | bytes 196616 | tf_op jit(solution)/shard_map/ppermute | solution.py:28
  69.5 21.7 %collective-permute-start.6 = (f32[128,128]{1,0:T(8,128)S(1)}, f32[128,128]{1,0:T(8,128)S(1)}, u32[]{:S(2)}, u32[]{:S(2)}) collective-permute-start(f32[128,128]{1,0:T(8,128)S(1)} %add.207), channel_id=1, source_target_pairs={{0,8},{1,9},{2,10},{3,11},{4,12},{5,13},{6,14},{7,15},{8,0},{9,1},... | collective-permute-start | bytes 196616 | tf_op jit(solution)/shard_map/ppermute | solution.py:28
  91.3 12.6 %collective-permute-start.7 = (f32[128,128]{1,0:T(8,128)S(1)}, f32[128,128]{1,0:T(8,128)S(1)}, u32[]{:S(2)}, u32[]{:S(2)}) collective-permute-start(f32[128,128]{1,0:T(8,128)S(1)} %add.208), channel_id=1, source_target_pairs={{0,16},{1,17},{2,18},{3,19},{4,20},{5,21},{6,22},{7,23},{8,24},{9,... | collective-permute-start | bytes 196616 | tf_op jit(solution)/shard_map/ppermute | solution.py:28
  103.9 9.1 %collective-permute-start.8 = (f32[128,128]{1,0:T(8,128)S(1)}, f32[128,128]{1,0:T(8,128)S(1)}, u32[]{:S(2)}, u32[]{:S(2)}) collective-permute-start(f32[128,128]{1,0:T(8,128)S(1)} %add.209), channel_id=1, source_target_pairs={{0,32},{1,33},{2,34},{3,35},{4,36},{5,37},{6,38},{7,39},{8,40},{9,... | collective-permute-start | bytes 196616 | tf_op jit(solution)/shard_map/ppermute | solution.py:28
  113.0 5.0 %collective-permute-start.9 = (f32[128,128]{1,0:T(8,128)S(1)}, f32[128,128]{1,0:T(8,128)S(1)}, u32[]{:S(2)}, u32[]{:S(2)}) collective-permute-start(f32[128,128]{1,0:T(8,128)S(1)} %add.210), channel_id=1, source_target_pairs={{0,64},{1,65},{2,66},{3,67},{4,68},{5,69},{6,70},{7,71},{8,72},{9,... | collective-permute-start | bytes 196616 | tf_op jit(solution)/shard_map/ppermute | solution.py:28
  118.0 9.4 %collective-permute-start.10 = (f32[128,128]{1,0:T(8,128)S(1)}, f32[128,128]{1,0:T(8,128)S(1)}, u32[]{:S(2)}, u32[]{:S(2)}) collective-permute-start(f32[128,128]{1,0:T(8,128)S(1)} %add.211), channel_id=1, source_target_pairs={{0,128},{1,129},{2,130},{3,131},{4,132},{5,133},{6,134},{7,135},{8... | collective-permute-start | bytes 196616 | tf_op jit(solution)/shard_map/ppermute | solution.py:28
  128.1 51.0 %collective-permute-start.11 = (f32[128,128]{1,0:T(8,128)}, f32[128,128]{1,0:T(8,128)}, u32[]{:S(2)}, u32[]{:S(2)}) collective-permute-start(f32[128,128]{1,0:T(8,128)} %add.212), channel_id=1, source_target_pairs={{0,256},{1,257},{2,258},{3,259},{4,260},{5,261},{6,262},{7,263},{8... | collective-permute-start | bytes 196616 | tf_op jit(solution)/shard_map/ppermute | solution.py:28
  132.6 108.8 %all-to-all-start.1 = ((f32[128,2,32]{2,1,0:T(2,128)}), f32[128,2,32]{2,1,0:T(2,128)S(1)}, u32[]{:S(2)}, u32[]{:S(2)}) async-start(f32[128,2,32]{2,1,0:T(2,128)} %and_select_fusion), calls=%async_computation.1 | async-start | bytes 262144 | tf_op jit(solution)/shard_map/all_to_all | solution.py:134
  146.3 3.5 %copy-start.1 = (pred[8192,8]{1,0:T(8,128)(4,1)S(1)}, pred[8192,8]{1,0:T(8,128)(4,1)}, u32[]{:S(2)}) copy-start(pred[8192,8]{1,0:T(8,128)(4,1)} %copy.37) | copy-start | bytes 196612
  169.3 39.8 %copy-start.5 = (pred[128,128]{1,0:T(8,128)(4,1)S(1)}, pred[128,128]{1,0:T(8,128)(4,1)}, u32[]{:S(2)}) copy-start(pred[128,128]{1,0:T(8,128)(4,1)} %iota_compare_fusion.3) | copy-start | bytes 49156
  169.4 71.1 %copy-start.9 = (pred[8]{0:T(512)(128)(4,1)S(1)}, pred[8]{0:T(512)(128)(4,1)}, u32[]{:S(2)}) copy-start(pred[8]{0:T(512)(128)(4,1)} %broadcast_in_dim.134) | copy-start | bytes 28
  169.5 10.6 %collective-permute-start.2 = (f32[2,16512]{1,0:T(2,128)S(1)}, f32[2,16512]{1,0:T(2,128)S(1)}, u32[]{:S(2)}, u32[]{:S(2)}) collective-permute-start(f32[2,16512]{1,0:T(2,128)S(1)} %get-tuple-element.4), channel_id=1, source_target_pairs={{0,3},{1,0},{2,1},{3,2},{4,7},{5,4},{6,5},{7,6},{8,11},{9,8},{10,9... | collective-permute-start | bytes 396296 | tf_op jit(solution)/shard_map/ppermute | solution.py:39
  173.8 7.2 %collective-permute-start.1 = (f32[2,16512]{1,0:T(2,128)S(1)}, f32[2,16512]{1,0:T(2,128)S(1)}, u32[]{:S(2)}, u32[]{:S(2)}) collective-permute-start(f32[2,16512]{1,0:T(2,128)S(1)} %get-tuple-element.3), channel_id=1, source_target_pairs={{0,2},{1,3},{2,0},{3,1},{4,6},{5,7},{6,4},{7,5},{8,10},{9,11},{10,... | collective-permute-start | bytes 396296 | tf_op jit(solution)/shard_map/ppermute | solution.py:39
  176.3 8.7 %collective-permute-start = (f32[2,16512]{1,0:T(2,128)S(1)}, f32[2,16512]{1,0:T(2,128)S(1)}, u32[]{:S(2)}, u32[]{:S(2)}) collective-permute-start(f32[2,16512]{1,0:T(2,128)S(1)} %get-tuple-element.2), channel_id=1, source_target_pairs={{0,1},{1,2},{2,3},{3,0},{4,5},{5,6},{6,7},{7,4},{8,9},{9,10},{10,1... | collective-permute-start | bytes 396296 | tf_op jit(solution)/shard_map/ppermute | solution.py:39
  229.4 41.2 %copy-start.8 = (f32[2,1,128]{2,1,0:T(1,128)}, f32[2,1,128]{2,1,0:T(1,128)S(1)}, u32[]{:S(2)}) copy-start(f32[2,1,128]{2,1,0:T(1,128)S(1)} %fusion.12) | copy-start | bytes 3076
  229.4 7.2 %collective-permute-start.14 = (bf16[2,128]{1,0:T(2,128)(2,1)S(1)}, bf16[2,128]{1,0:T(2,128)(2,1)S(1)}, u32[]{:S(2)}, u32[]{:S(2)}) collective-permute-start(bf16[2,128]{1,0:T(2,128)(2,1)S(1)} %convert_element_type.43), channel_id=1, source_target_pairs={{0,3},{1,0},{2,1},{3,2},{4,7},{5,4},{6,5},{7,6},{8,11},{9,8},{10,9... | collective-permute-start | bytes 1544 | tf_op jit(solution)/shard_map/ppermute | solution.py:49
  231.3 5.8 %collective-permute-start.13 = (bf16[2,128]{1,0:T(2,128)(2,1)S(1)}, bf16[2,128]{1,0:T(2,128)(2,1)S(1)}, u32[]{:S(2)}, u32[]{:S(2)}) collective-permute-start(bf16[2,128]{1,0:T(2,128)(2,1)S(1)} %convert_element_type.43), channel_id=1, source_target_pairs={{0,2},{1,3},{2,0},{3,1},{4,6},{5,7},{6,4},{7,5},{8,10},{9,11},{10,... | collective-permute-start | bytes 1544 | tf_op jit(solution)/shard_map/ppermute | solution.py:49
  233.3 6.6 %collective-permute-start.12 = (bf16[2,128]{1,0:T(2,128)(2,1)S(1)}, bf16[2,128]{1,0:T(2,128)(2,1)S(1)}, u32[]{:S(2)}, u32[]{:S(2)}) collective-permute-start(bf16[2,128]{1,0:T(2,128)(2,1)S(1)} %convert_element_type.43), channel_id=1, source_target_pairs={{0,1},{1,2},{2,3},{3,0},{4,5},{5,6},{6,7},{7,4},{8,9},{9,10},{10,1... | collective-permute-start | bytes 1544 | tf_op jit(solution)/shard_map/ppermute | solution.py:49
  241.4 27.4 %all-to-all-start.2 = ((bf16[128,2,128]{2,1,0:T(2,128)(2,1)}), bf16[128,2,128]{2,1,0:T(2,128)(2,1)S(1)}, u32[]{:S(2)}, u32[]{:S(2)}) async-start(bf16[128,2,128]{2,1,0:T(2,128)(2,1)} %bitcast.27), calls=%async_computation.2 | async-start | bytes 131072 | tf_op jit(solution)/shard_map/all_to_all | solution.py:127

commit v3 on v2

--- a/solution.py
+++ b/solution.py
@@ -1,7 +1,13 @@
+import functools
+
 import jax
 import jax.numpy as jnp
 from jax import lax
+from jax.experimental import pallas as pl
+from jax.experimental.pallas import tpu as pltpu
 from jax.sharding import PartitionSpec as P
+
+MESH_ID = pl.DeviceIdType.MESH
 
 U_DEV = 2
 
@@ -20,13 +26,49 @@
     return result[..., 0]
 
 
+def doubling_kernel(n_rep, rounds, x_ref, o_ref, recv, send_sem, recv_sem):
+    flat = lax.axis_index("ent") * n_rep + lax.axis_index("rep")
+    partners = []
+    for bit in range(rounds):
+        step = 1 << bit
+        upper = (flat // step) % 2
+        peer = flat + step - 2 * step * upper
+        partners.append((peer // n_rep, peer % n_rep))
+    barrier = pltpu.get_barrier_semaphore()
+    for peer in partners:
+        pl.semaphore_signal(barrier, inc=1, device_id=peer, device_id_type=MESH_ID)
+    pl.semaphore_wait(barrier, rounds)
+    o_ref[...] = x_ref[...]
+    for bit in range(rounds):
+        copy = pltpu.make_async_remote_copy(
+            src_ref=o_ref,
+            dst_ref=recv.at[bit],
+            send_sem=send_sem.at[bit],
+            recv_sem=recv_sem.at[bit],
+            device_id=partners[bit],
+            device_id_type=MESH_ID,
+        )
+        copy.start()
+        copy.wait_recv()
+        copy.wait_send()
+        o_ref[...] = o_ref[...] + recv[bit]
+
+
 def tree_sum(value, count):
-    bits = count.bit_length() - 1
-    for bit in range(bits):
-        step = 1 << bit
-        pairs = [(i, i ^ step) for i in range(count)]
-        value = value + lax.ppermute(value, ("ent", "rep"), pairs)
-    return value
+    rounds = count.bit_length() - 1
+    n_rep = lax.axis_size("rep")
+    return pl.pallas_call(
+        functools.partial(doubling_kernel, n_rep, rounds),
+        out_shape=jax.ShapeDtypeStruct(value.shape, value.dtype),
+        in_specs=[pl.BlockSpec(memory_space=pltpu.VMEM)],
+        out_specs=pl.BlockSpec(memory_space=pltpu.VMEM),
+        scratch_shapes=[
+            pltpu.VMEM((rounds,) + value.shape, value.dtype),
+            pltpu.SemaphoreType.DMA((rounds,)),
+            pltpu.SemaphoreType.DMA((rounds,)),
+        ],
+        compiler_params=pltpu.CompilerParams(collective_id=0, has_side_effects=True),
+    )(value)
 
 
 def rep_scatter_sum(acc, n_rep, per_dev):

time: 272 us -> 300 us (1.10)
  Pallas kernels: 0 us -> 60.2 us
  waiting for transfers between devices: 50.3 us -> 13 us
  starting transfers between devices: 102 us -> 67.1 us
  other arithmetic: 74.8 us -> 108 us
  matrix products: 10.6 us -> 14.1 us
  local copies, waits for them, and re-layouts: 31.5 us -> 34.8 us
    pallas_call x0 -> x1, Pallas kernels: none -> 60.2 us  [tree_sum(): pl.pallas_call(functools.partial(doubling_kernel, n_rep, rounds), out_sha...]
    ppermute x9 -> x0, waiting for transfers between devices: 38 us -> none  [tree_sum(): value = value + lax.ppermute(value, ('ent', 'rep'), pairs)]
    ppermute x9 -> x0, starting transfers between devices: 37.1 us -> none  [tree_sum(): value = value + lax.ppermute(value, ('ent', 'rep'), pairs)]
    select_n x1, other arithmetic: 11.2 us -> 41.6 us  [shards(): jnp.where(row_select[:, :, None], weighted[:, None, :], jnp.zeros((), jnp...]
  transfers between devices with their start and end apart: 18 -> 9, of which waited for: 12 -> 5; matrix products, arithmetic and copies ran while one was open for 31% -> 42% of each run, Pallas kernels for 0% -> 20%
where the time goes in v3:
time: 300 us; the launch traced here: 299 us
  other arithmetic  108 us (36%)
  starting transfers between devices  67.1 us (22%)
  Pallas kernels  60.2 us (20%)
  local copies, waits for them, and re-layouts  34.8 us (12%)
  matrix products  14.1 us (5%)
  waiting for transfers between devices  13 us (4%)
    pallas_call x1, Pallas kernels, tree_sum(): pl.pallas_call(functools.partial(doubling_kernel, n_rep, rounds), out_sha...  60.2 us
    select_n x1, other arithmetic, shards(): jnp.where(row_select[:, :, None], weighted[:, None, :], jnp.zeros((), jnp...  41.6 us
    gather x1, local copies, waits for them, and re-layouts, shards(): jnp.take(item_factors, item_ids.reshape(-1), axis=0)  24 us
    another operation x4, other arithmetic, solve_users(): lower = jnp.linalg.cholesky(gram)  23.6 us
    another operation x3, other arithmetic, solve_users(): lax.linalg.triangular_solve(lower, halfway, left_side=True, lower=True, t...  19.8 us
    all_to_all x1, starting transfers between devices, shards(): lax.all_to_all(picked.reshape(n_ent, slot_cap * tile_rows, rank_width), '...  18.6 us
    all_to_all x1, starting transfers between devices, shards(): lax.all_to_all(rhs_weight.reshape(n_ent, slot_cap, tile_rows), 'ent', spl...  16.5 us
    all_to_all x1, starting transfers between devices, shards(): lax.all_to_all(run_factor.reshape(n_ent, slot_cap, seg_count * rank_width...  15.8 us
  transfers between devices with their start and end apart: 9, of which 5 were waited for; matrix products, arithmetic and copies ran while one was open for 42% of the time, Pallas kernels for 20%

profile of v3, /device:TPU:1, one launch (start us, length us, event | category | flops | bytes accessed | tf_op | source)
XLA Modules:
  0.0 298.7 jit_solution(8503616841106150250)
XLA Ops:
  0.6 0.9 copy.40
  2.7 24.0 %gather_fusion = bf16[8192,128]{1,0:T(8,128)(2,1)S(1)} fusion(bf16[1024,128]{1,0:T(8,128)(2,1)S(1)} %copy-done, s32[8192]{0:T(1024)S(1)} %broadcast_clamp_fusion), kind=kCustom, calls=%fused_computation | custom fusion | bytes 4227072 | tf_op jit(solution)/shard_map/jit(_take)/gather | solution.py:116
  26.7 4.6 %select_select_fusion = bf16[128,64,128]{2,1,0:T(8,128)(2,1)} fusion(bf16[128,64,128]{2,1,0:T(8,128)(2,1)S(1)} %bitcast.73, pred[128,64]{1,0:T(8,128)(4,1)S(1)} %compare_and_fusion, pred[128,64]{1,0:T(8,128)(4,1)S(1)} %copy.39), kind=kLoop, calls=%fused_computation.9 | loop fusion | flops 2097152 | bytes 4210688 | tf_op jit(solution)/shard_map/jit(_where)/select_n | solution.py:119
  31.3 18.6 %all-to-all-start = ((bf16[128,64,128]{2,1,0:T(8,128)(2,1)}), bf16[128,64,128]{2,1,0:T(8,128)(2,1)S(1)}, u32[]{:S(2)}, u32[]{:S(2)}) async-start(bf16[128,64,128]{2,1,0:T(8,128)(2,1)} %select_select_fusion), calls=%async_computation | async-start | bytes 4194304 | tf_op jit(solution)/shard_map/all_to_all | solution.py:120
  52.3 1.7 copy.37
  54.0 1.4 broadcast_add_fusion.1
  58.0 0.9 fusion.28.x_ref
  58.9 60.2 %shard_map.77 = f32[128,128]{1,0:T(8,128)} custom-call(f32[128,128]{1,0:T(8,128)} %fusion.28.x_ref), custom_call_target="tpu_custom_call" | custom-call | tf_op jit(solution)/shard_map/pallas_call | solution.py:60
  121.3 1.4 add_select_fusion
  122.7 1.5 convert_add_fusion
  124.2 1.7 and_select_fusion
  125.9 16.5 %all-to-all-start.1 = ((f32[128,2,32]{2,1,0:T(2,128)}), f32[128,2,32]{2,1,0:T(2,128)S(1)}, u32[]{:S(2)}, u32[]{:S(2)}) async-start(f32[128,2,32]{2,1,0:T(2,128)} %and_select_fusion), calls=%async_computation.1 | async-start | bytes 262144 | tf_op jit(solution)/shard_map/all_to_all | solution.py:176
  142.4 3.7 %multiply_convert_fusion = bf16[8192,128]{1,0:T(8,128)(2,1)S(1)} fusion(f32[8192]{0:T(1024)} %mul.47, bf16[128,64,128]{2,1,0:T(8,128)(2,1)S(1)} %all-to-all-done), kind=kLoop, calls=%fused_computation.8 | loop fusion | flops 3145728 | bytes 4227072 | tf_op jit(solution)/shard_map/convert_element_type | solution.py:137
  146.1 41.6 %broadcast_select_fusion = bf16[8192,8,128]{2,1,0:T(8,128)(2,1)} fusion(pred[8192,8]{1,0:T(8,128)(4,1)S(1)} %copy.37, bf16[8192,128]{1,0:T(8,128)(2,1)S(1)} %multiply_convert_fusion), kind=kLoop, calls=%fused_computation.7 | loop fusion | flops 8388608 | bytes 18939904 | tf_op jit(solution)/shard_map/jit(_where)/select_n | solution.py:140
  187.7 8.2 %fusion = f32[1024,128]{1,0:T(8,128)S(1)} fusion(bf16[8192,128]{1,0:T(8,128)(2,1)S(1)} %bitcast.70, bf16[1024,8,8,128]{3,2,1,0:T(8,128)(2,1)} %bitcast.72), kind=kOutput, calls=%fused_computation.4 | convolution fusion | flops 2147483648 | bytes 19398656 | tf_op jit(solution)/shard_map/dot_general | solution.py:141
  196.1 1.7 fusion.3
  198.0 3.9 %collective-permute-start.2 = (f32[2,16512]{1,0:T(2,128)S(1)}, f32[2,16512]{1,0:T(2,128)S(1)}, u32[]{:S(2)}, u32[]{:S(2)}) collective-permute-start(f32[2,16512]{1,0:T(2,128)S(1)} %get-tuple-element.4), channel_id=1, source_target_pairs={{0,3},{1,0},{2,1},{3,2},{4,7},{5,4},{6,5},{7,6},{8,11},{9,8},{10,9... | collective-permute-start | bytes 396296 | tf_op jit(solution)/shard_map/ppermute | solution.py:81
  201.9 2.2 collective-permute-start.1
  204.1 3.0 collective-permute-start
  207.5 1.6 collective-permute-done.1
  209.1 3.9 %collective-permute-done = f32[2,16512]{1,0:T(2,128)S(1)} collective-permute-done((f32[2,16512]{1,0:T(2,128)S(1)}, f32[2,16512]{1,0:T(2,128)S(1)}, u32[]{:S(2)}, u32[]{:S(2)}) %collective-permute-start) | collective-permute-done | bytes 132128 | tf_op jit(solution)/shard_map/ppermute | solution.py:81
  213.5 23.5 %custom-call.9 = f32[2,128,128]{2,1,0:T(8,128)S(1)} custom-call(f32[2,128,128]{2,1,0:T(8,128)S(1)} %fusion.15), custom_call_target="Cholesky" | custom-call | tf_op jit(solution)/shard_map/jit(cholesky)/cholesky | solution.py:21
  237.2 19.7 %custom-call.10 = f32[2,1,128,128]{2,3,1,0:T(8,128)S(1)} custom-call(f32[2,1,128,128]{3,2,1,0:T(8,128)S(1)} %select_bitcast_fusion), custom_call_target="InvertDiagBlocksLowerTriangular" | custom-call | tf_op jit(solution)/shard_map/triangular_solve | solution.py:23
  257.5 1.9 collective-permute-start.5
  259.4 1.9 collective-permute-start.4
  261.3 3.4 %collective-permute-start.3 = (bf16[2,128]{1,0:T(2,128)(2,1)S(1)}, bf16[2,128]{1,0:T(2,128)(2,1)S(1)}, u32[]{:S(2)}, u32[]{:S(2)}) collective-permute-start(bf16[2,128]{1,0:T(2,128)(2,1)S(1)} %convert_element_type.43), channel_id=1, source_target_pairs={{0,1},{1,2},{2,3},{3,0},{4,5},{5,6},{6,7},{7,4},{8,9},{9,10},{10,1... | collective-permute-start | bytes 1544 | tf_op jit(solution)/shard_map/ppermute | solution.py:91
  265.2 2.8 collective-permute-done.3
  268.7 0.9 convolution_convert_fusion
  269.6 15.8 %all-to-all-start.2 = ((bf16[128,2,128]{2,1,0:T(2,128)(2,1)}), bf16[128,2,128]{2,1,0:T(2,128)(2,1)S(1)}, u32[]{:S(2)}, u32[]{:S(2)}) async-start(bf16[128,2,128]{2,1,0:T(2,128)(2,1)} %bitcast.27), calls=%async_computation.2 | async-start | bytes 131072 | tf_op jit(solution)/shard_map/all_to_all | solution.py:169
  285.4 7.4 %select_reduce_fusion = f32[256,1024]{1,0:T(8,128)S(1)} fusion(f32[256,32]{1,0:T(8,128)S(1)} %bitcast.74, s32[256,32]{1,0:T(8,128)S(1)} %copy.47), kind=kLoop, calls=%fused_computation.2 | loop fusion | flops 24903680 | bytes 1114112 | tf_op jit(solution)/shard_map/reduce_sum | solution.py:187
  292.8 4.2 %all-to-all-done.2 = bf16[128,2,128]{2,1,0:T(2,128)(2,1)S(1)} async-done(((bf16[128,2,128]{2,1,0:T(2,128)(2,1)}), bf16[128,2,128]{2,1,0:T(2,128)(2,1)S(1)}, u32[]{:S(2)}, u32[]{:S(2)}) %all-to-all-start.2) | async-done | bytes 65568 | tf_op jit(solution)/shard_map/all_to_all | solution.py:169
  296.9 1.8 convolution_multiply_fusion
  (75 shorter events, 11.3 us)
Async XLA Ops:
  0.6 2.0 copy-start
  31.3 18.6 %copy-start.3 = (s32[1,1,256,32]{2,3,1,0:T(8,128)S(1)}, s32[1,1,256,32]{2,3,1,0:T(8,128)}, u32[]{:S(2)}) copy-start(s32[1,1,256,32]{2,3,1,0:T(8,128)} %param.10) | copy-start | bytes 98308
  31.3 20.2 %copy-start.5 = (s32[1,1,256,1]{2,3,1,0:T(1,128)S(1)}, s32[1,1,256,1]{2,3,1,0:T(1,128)}, u32[]{:S(2)}) copy-start(s32[1,1,256,1]{2,3,1,0:T(1,128)} %param.9) | copy-start | bytes 3076
  31.3 94.6 %all-to-all-start = ((bf16[128,64,128]{2,1,0:T(8,128)(2,1)}), bf16[128,64,128]{2,1,0:T(8,128)(2,1)S(1)}, u32[]{:S(2)}, u32[]{:S(2)}) async-start(bf16[128,64,128]{2,1,0:T(8,128)(2,1)} %select_select_fusion), calls=%async_computation | async-start | bytes 4194304 | tf_op jit(solution)/shard_map/all_to_all | solution.py:120
  49.9 7.1 %copy-start.7 = (s32[1,1,128]{2,1,0:T(1,128)S(1)}, s32[1,1,128]{2,1,0:T(1,128)}, u32[]{:S(2)}) copy-start(s32[1,1,128]{2,1,0:T(1,128)} %param.11) | copy-start | bytes 1540
  51.7 0.6 copy-start.1
  125.9 143.7 %all-to-all-start.1 = ((f32[128,2,32]{2,1,0:T(2,128)}), f32[128,2,32]{2,1,0:T(2,128)S(1)}, u32[]{:S(2)}, u32[]{:S(2)}) async-start(f32[128,2,32]{2,1,0:T(2,128)} %and_select_fusion), calls=%async_computation.1 | async-start | bytes 262144 | tf_op jit(solution)/shard_map/all_to_all | solution.py:176
  196.0 11.1 %copy-start.2 = (f32[128,128]{1,0:T(8,128)S(1)}, f32[128,128]{1,0:T(8,128)}, u32[]{:S(2)}) copy-start(f32[128,128]{1,0:T(8,128)} %convert_add_fusion) | copy-start | bytes 196612
  196.1 11.2 %copy-start.4 = (s32[1,1,256,32]{2,3,1,0:T(8,128)S(1)}, s32[1,1,256,32]{2,3,1,0:T(8,128)}, u32[]{:S(2)}) copy-start(s32[1,1,256,32]{2,3,1,0:T(8,128)} %param.7) | copy-start | bytes 98308
  198.0 70.7 %copy-start.6 = (s32[1,1,256,1]{2,3,1,0:T(1,128)S(1)}, s32[1,1,256,1]{2,3,1,0:T(1,128)}, u32[]{:S(2)}) copy-start(s32[1,1,256,1]{2,3,1,0:T(1,128)} %param.9) | copy-start | bytes 3076
  198.0 9.5 %collective-permute-start.2 = (f32[2,16512]{1,0:T(2,128)S(1)}, f32[2,16512]{1,0:T(2,128)S(1)}, u32[]{:S(2)}, u32[]{:S(2)}) collective-permute-start(f32[2,16512]{1,0:T(2,128)S(1)} %get-tuple-element.4), channel_id=1, source_target_pairs={{0,3},{1,0},{2,1},{3,2},{4,7},{5,4},{6,5},{7,6},{8,11},{9,8},{10,9... | collective-permute-start | bytes 396296 | tf_op jit(solution)/shard_map/ppermute | solution.py:81
  201.9 7.2 %collective-permute-start.1 = (f32[2,16512]{1,0:T(2,128)S(1)}, f32[2,16512]{1,0:T(2,128)S(1)}, u32[]{:S(2)}, u32[]{:S(2)}) collective-permute-start(f32[2,16512]{1,0:T(2,128)S(1)} %get-tuple-element.3), channel_id=1, source_target_pairs={{0,2},{1,3},{2,0},{3,1},{4,6},{5,7},{6,4},{7,5},{8,10},{9,11},{10,... | collective-permute-start | bytes 396296 | tf_op jit(solution)/shard_map/ppermute | solution.py:81
  204.1 9.0 %collective-permute-start = (f32[2,16512]{1,0:T(2,128)S(1)}, f32[2,16512]{1,0:T(2,128)S(1)}, u32[]{:S(2)}, u32[]{:S(2)}) collective-permute-start(f32[2,16512]{1,0:T(2,128)S(1)} %get-tuple-element.2), channel_id=1, source_target_pairs={{0,1},{1,2},{2,3},{3,0},{4,5},{5,6},{6,7},{7,4},{8,9},{9,10},{10,1... | collective-permute-start | bytes 396296 | tf_op jit(solution)/shard_map/ppermute | solution.py:81
  257.5 41.3 %copy-start.8 = (f32[2,1,128]{2,1,0:T(1,128)}, f32[2,1,128]{2,1,0:T(1,128)S(1)}, u32[]{:S(2)}) copy-start(f32[2,1,128]{2,1,0:T(1,128)S(1)} %fusion.12) | copy-start | bytes 3076
  257.5 7.2 %collective-permute-start.5 = (bf16[2,128]{1,0:T(2,128)(2,1)S(1)}, bf16[2,128]{1,0:T(2,128)(2,1)S(1)}, u32[]{:S(2)}, u32[]{:S(2)}) collective-permute-start(bf16[2,128]{1,0:T(2,128)(2,1)S(1)} %convert_element_type.43), channel_id=1, source_target_pairs={{0,3},{1,0},{2,1},{3,2},{4,7},{5,4},{6,5},{7,6},{8,11},{9,8},{10,9... | collective-permute-start | bytes 1544 | tf_op jit(solution)/shard_map/ppermute | solution.py:91
  259.4 5.8 %collective-permute-start.4 = (bf16[2,128]{1,0:T(2,128)(2,1)S(1)}, bf16[2,128]{1,0:T(2,128)(2,1)S(1)}, u32[]{:S(2)}, u32[]{:S(2)}) collective-permute-start(bf16[2,128]{1,0:T(2,128)(2,1)S(1)} %convert_element_type.43), channel_id=1, source_target_pairs={{0,2},{1,3},{2,0},{3,1},{4,6},{5,7},{6,4},{7,5},{8,10},{9,11},{10,... | collective-permute-start | bytes 1544 | tf_op jit(solution)/shard_map/ppermute | solution.py:91
  261.3 6.7 %collective-permute-start.3 = (bf16[2,128]{1,0:T(2,128)(2,1)S(1)}, bf16[2,128]{1,0:T(2,128)(2,1)S(1)}, u32[]{:S(2)}, u32[]{:S(2)}) collective-permute-start(bf16[2,128]{1,0:T(2,128)(2,1)S(1)} %convert_element_type.43), channel_id=1, source_target_pairs={{0,1},{1,2},{2,3},{3,0},{4,5},{5,6},{6,7},{7,4},{8,9},{9,10},{10,1... | collective-permute-start | bytes 1544 | tf_op jit(solution)/shard_map/ppermute | solution.py:91
  269.6 27.3 %all-to-all-start.2 = ((bf16[128,2,128]{2,1,0:T(2,128)(2,1)}), bf16[128,2,128]{2,1,0:T(2,128)(2,1)S(1)}, u32[]{:S(2)}, u32[]{:S(2)}) async-start(bf16[128,2,128]{2,1,0:T(2,128)(2,1)} %bitcast.27), calls=%async_computation.2 | async-start | bytes 131072 | tf_op jit(solution)/shard_map/all_to_all | solution.py:169

commit v4 on v3

--- a/solution.py
+++ b/solution.py
@@ -94,6 +94,85 @@
     return jnp.take(stacked, order, axis=0).reshape(-1, value.shape[-1])
 
 
+def gather_kernel(idx_ref, table_ref, out_ref):
+    picks = idx_ref[...] == lax.broadcasted_iota(jnp.int32, (idx_ref.shape[0], table_ref.shape[0]), 1)
+    out_ref[...] = jnp.dot(
+        picks.astype(jnp.bfloat16), table_ref[...], preferred_element_type=jnp.float32
+    ).astype(out_ref.dtype)
+
+
+def gather_rows(table, idx_col, chunk=512):
+    count = idx_col.shape[0]
+    return pl.pallas_call(
+        gather_kernel,
+        out_shape=jax.ShapeDtypeStruct((count, table.shape[1]), table.dtype),
+        grid=(count // chunk,),
+        in_specs=[
+            pl.BlockSpec((chunk, 1), lambda i: (i, 0)),
+            pl.BlockSpec(table.shape, lambda i: (0, 0)),
+        ],
+        out_specs=pl.BlockSpec((chunk, table.shape[1]), lambda i: (i, 0)),
+        cost_estimate=pl.CostEstimate(
+            flops=2 * count * table.shape[0] * table.shape[1],
+            transcendentals=0,
+            bytes_accessed=count * 4 + table.size * 2 + count * table.shape[1] * 2,
+        ),
+    )(idx_col, table)
+
+
+def gram_kernel(n_user, rows_ref, gw_ref, user_ref, rw_ref, gram_ref, rhs_ref):
+    step = pl.program_id(0)
+
+    @pl.when(step == 0)
+    def _():
+        gram_ref[...] = jnp.zeros_like(gram_ref)
+        rhs_ref[...] = jnp.zeros_like(rhs_ref)
+
+    rows = rows_ref[...]
+    rows_t = rows.astype(jnp.float32).T
+    weights_t = (rows_t * gw_ref[pl.ds(step, 1), :]).astype(jnp.bfloat16)
+    users = user_ref[pl.ds(step, 1), :]
+    zero = jnp.zeros((), jnp.bfloat16)
+    for user in range(n_user):
+        picked = jnp.where(users == user, weights_t, zero)
+        gram_ref[user] += jnp.dot(picked, rows, preferred_element_type=jnp.float32)
+    slots = lax.broadcasted_iota(jnp.int32, (n_user, users.shape[1]), 0)
+    per_user = jnp.where(users == slots, rw_ref[pl.ds(step, 1), :], 0.0)
+    high = per_user.astype(jnp.bfloat16)
+    low = (per_user - high.astype(jnp.float32)).astype(jnp.bfloat16)
+    rhs_ref[...] += jnp.dot(high, rows, preferred_element_type=jnp.float32) + jnp.dot(
+        low, rows, preferred_element_type=jnp.float32
+    )
+
+
+def user_grams(rows, gw_lanes, user_lanes, rw_lanes, n_user):
+    chunks, chunk = gw_lanes.shape
+    width = rows.shape[1]
+    return pl.pallas_call(
+        functools.partial(gram_kernel, n_user),
+        out_shape=(
+            jax.ShapeDtypeStruct((n_user, width, width), jnp.float32),
+            jax.ShapeDtypeStruct((n_user, width), jnp.float32),
+        ),
+        grid=(chunks,),
+        in_specs=[
+            pl.BlockSpec((chunk, width), lambda i: (i, 0)),
+            pl.BlockSpec((chunks, chunk), lambda i: (0, 0)),
+            pl.BlockSpec((chunks, chunk), lambda i: (0, 0)),
+            pl.BlockSpec((chunks, chunk), lambda i: (0, 0)),
+        ],
+        out_specs=(
+            pl.BlockSpec((n_user, width, width), lambda i: (0, 0, 0)),
+            pl.BlockSpec((n_user, width), lambda i: (0, 0)),
+        ),
+        cost_estimate=pl.CostEstimate(
+            flops=2 * rows.shape[0] * width * width * (n_user + 2),
+            transcendentals=0,
+            bytes_accessed=rows.size * 2 + 12 * rows.shape[0] + n_user * width * (width + 1) * 4,
+        ),
+    )(rows, gw_lanes, user_lanes, rw_lanes)
+
+
 def shards(item_factors, tile_items, send_tiles, tile_users, tile_counts, recv_tiles):
     highest = lax.Precision.HIGHEST
     rank_width = item_factors.shape[1]
@@ -113,10 +192,9 @@
     partial_gram = lax.dot_general(
         item_factors, item_factors, (((0,), (0,)), ((), ())), preferred_element_type=jnp.float32
     )
-    picked = jnp.take(item_factors, item_ids.reshape(-1), axis=0).reshape(
-        tile_slots, tile_rows, rank_width
-    )
-    picked = jnp.where(live_send[:, None, None], picked, jnp.zeros((), jnp.bfloat16))
+    live_rows = jnp.repeat(live_send, tile_rows)
+    idx_col = jnp.where(live_rows, item_ids.reshape(-1), -1).reshape(-1, 1)
+    picked = gather_rows(item_factors, idx_col)
     incoming = lax.all_to_all(
         picked.reshape(n_ent, slot_cap * tile_rows, rank_width),
         "ent",
@@ -134,24 +212,16 @@
     selector = owners[None, :] == jnp.arange(user_block, dtype=jnp.int32)[:, None]
     selector_f = selector.astype(jnp.float32)
     rows_all = incoming.reshape(tile_slots * tile_rows, rank_width)
-    weighted = (gram_weight.reshape(-1, 1) * rows_all.astype(jnp.float32)).astype(jnp.bfloat16)
+    lane_chunk = 1024
     row_owner = jnp.repeat(owners, seg_length)
-    row_select = row_owner[:, None] == jnp.arange(user_block, dtype=jnp.int32)[None, :]
-    masked = jnp.where(row_select[:, :, None], weighted[:, None, :], jnp.zeros((), jnp.bfloat16))
-    gram_acc = lax.dot_general(
-        masked.reshape(-1, user_block * rank_width),
+    gram_acc, rhs_acc = user_grams(
         rows_all,
-        (((0,), (0,)), ((), ())),
-        preferred_element_type=jnp.float32,
-    ).reshape(user_block, rank_width * rank_width)
-    rhs_rows = jnp.where(row_select, rhs_weight.reshape(-1, 1), 0.0)
-    rhs_acc = lax.dot_general(
-        rhs_rows,
-        rows_all.astype(jnp.float32),
-        (((0,), (0,)), ((), ())),
-        precision=highest,
-        preferred_element_type=jnp.float32,
-    )
+        gram_weight.reshape(-1, lane_chunk),
+        row_owner.reshape(-1, lane_chunk),
+        rhs_weight.reshape(-1, lane_chunk),
+        user_block,
+    )
+    gram_acc = gram_acc.reshape(user_block, rank_width * rank_width)
     identity_mat = jnp.eye(rank_width, dtype=jnp.float32)
     added_term = tree_sum(partial_gram, n_ent * n_rep) + RIDGE * identity_mat
     own_gram, own_rhs = rep_scatter_sum(

time: 300 us -> 251 us (0.84)
  other arithmetic: 108 us -> 59.3 us
  Pallas kernels: 60.2 us -> 87.1 us
  local copies, waits for them, and re-layouts: 34.8 us -> 17.9 us
  matrix products: 14.1 us -> 4.13 us
    select_n x3 -> x1, other arithmetic: 46.3 us -> 4.53 us  [shards(): idx_col = jnp.where(live_rows, item_ids.reshape(-1), -1).reshape(-1, 1)]
    gather x1 -> x0, local copies, waits for them, and re-layouts: 24 us -> none  [shards(): jnp.take(item_factors, item_ids.reshape(-1), axis=0)]
    pallas_call x0 -> x2, Pallas kernels: none -> 23.1 us  [the longest x1 14.4 us: gather_rows(): pl.pallas_call(gather_kernel, out_shape=jax.ShapeDtypeStruct((count, tabl...]
    dot_general x2 -> x0, matrix products: 9.96 us -> none  [the longest x1 8.23 us: shards(): lax.dot_general(masked.reshape(-1, user_block * rank_width), rows_all, ((...]
    another operation x2 -> x1, local copies, waits for them, and re-layouts: 0.2 us -> 5.65 us  [shards(): idx_col = jnp.where(live_rows, item_ids.reshape(-1), -1).reshape(-1, 1)]
    reshape x2, local copies, waits for them, and re-layouts: 0.25 us -> 4.74 us  [the longest x1 4.59 us: shards(): live_rows = jnp.repeat(live_send, tile_rows)]
    pallas_call x1, Pallas kernels: 60.2 us -> 64 us  [tree_sum(): pl.pallas_call(functools.partial(doubling_kernel, n_rep, rounds), out_sha...]
    convert_element_type x1 -> x0, other arithmetic: 3.69 us -> none  [shards(): (gram_weight.reshape(-1, 1) * rows_all.astype(jnp.float32)).astype(jnp.bf...]
  transfers between devices with their start and end apart: 9 -> 9, of which waited for: 5 -> 5; matrix products, arithmetic and copies ran while one was open for 42% -> 25% of each run, Pallas kernels for 20% -> 29%
where the time goes in v4:
time: 251 us; the launch traced here: 250 us
  Pallas kernels  87.1 us (35%)
  starting transfers between devices  67.4 us (27%)
  other arithmetic  59.3 us (24%)
  local copies, waits for them, and re-layouts  17.9 us (7%)
  waiting for transfers between devices  12.7 us (5%)
  matrix products  4.13 us (2%)
    pallas_call x1, Pallas kernels, tree_sum(): pl.pallas_call(functools.partial(doubling_kernel, n_rep, rounds), out_sha...  64 us
    another operation x4, other arithmetic, solve_users(): lower = jnp.linalg.cholesky(gram)  23.6 us
    another operation x3, other arithmetic, solve_users(): lax.linalg.triangular_solve(lower, halfway, left_side=True, lower=True, t...  19.8 us
    all_to_all x1, starting transfers between devices, shards(): lax.all_to_all(picked.reshape(n_ent, slot_cap * tile_rows, rank_width), '...  18.6 us
    all_to_all x1, starting transfers between devices, shards(): lax.all_to_all(rhs_weight.reshape(n_ent, slot_cap, tile_rows), 'ent', spl...  16.8 us
    all_to_all x1, starting transfers between devices, shards(): lax.all_to_all(run_factor.reshape(n_ent, slot_cap, seg_count * rank_width...  16.1 us
    pallas_call x1, Pallas kernels, gather_rows(): pl.pallas_call(gather_kernel, out_shape=jax.ShapeDtypeStruct((count, tabl...  14.4 us
    ppermute x3, starting transfers between devices, rep_scatter_sum(): total = total + lax.ppermute(piece, 'rep', pairs)  8.75 us
  transfers between devices with their start and end apart: 9, of which 5 were waited for; matrix products, arithmetic and copies ran while one was open for 25% of the time, Pallas kernels for 29%

profile of v4, /device:TPU:1, one launch (start us, length us, event | category | flops | bytes accessed | tf_op | source)
XLA Modules:
  0.0 249.6 jit_solution(14670880927120296086)
XLA Ops:
  0.6 0.7 broadcast_in_dim.69
  1.6 4.6 %reshape.204 = pred[8192,1]{1,0:T(8,128)(4,1)S(1)} reshape(pred[256,32]{1,0:T(8,128)(4,1)S(1)} %broadcast_in_dim.70) | data formatting | bytes 16384 | tf_op jit(solution)/shard_map/reshape | solution.py:195
  6.2 0.9 copy.28
  7.1 5.7 %reshape_reshape.5 = s32[8192,1]{1,0:T(8,128)} reshape(s32[1,1,256,32]{3,2,1,0:T(8,128)S(1)} %copy.28) | data formatting | bytes 65536 | tf_op jit(solution)/shard_map/reshape;reshape | solution.py:196
  12.7 4.5 %broadcast_select_fusion.idx_ref = s32[8192,1]{1,0:T(8,128)} fusion(pred[8192,1]{1,0:T(8,128)(4,1)S(1)} %reshape.204, s32[8192,1]{1,0:T(8,128)} %reshape_reshape.5), kind=kLoop, calls=%fused_computation.3 | loop fusion | flops 8192 | bytes 73728 | tf_op jit(solution)/shard_map/jit(_where)/select_n | solution.py:196
  17.3 14.4 %shard_map.77 = bf16[8192,128]{1,0:T(8,128)(2,1)} custom-call(s32[8192,1]{1,0:T(8,128)} %broadcast_select_fusion.idx_ref, bf16[1024,128]{1,0:T(8,128)(2,1)} %table_ref.1), custom_call_target="tpu_custom_call" | custom-call | flops 2147483648 | bytes 2392064 | tf_op jit(solution)/shard_map/pallas_call | solution.py:106
  31.7 18.6 %all-to-all-start = ((bf16[128,64,128]{2,1,0:T(8,128)(2,1)}), bf16[128,64,128]{2,1,0:T(8,128)(2,1)S(1)}, u32[]{:S(2)}, u32[]{:S(2)}) async-start(bf16[128,64,128]{2,1,0:T(8,128)(2,1)} %bitcast.65), calls=%async_computation | async-start | bytes 4194304 | tf_op jit(solution)/shard_map/all_to_all | solution.py:198
  52.2 0.7 broadcast_in_dim.74.user_ref
  54.2 0.9 fusion.21.x_ref
  55.1 64.0 %shard_map.79 = f32[128,128]{1,0:T(8,128)} custom-call(f32[128,128]{1,0:T(8,128)} %fusion.21.x_ref), custom_call_target="tpu_custom_call" | custom-call | tf_op jit(solution)/shard_map/pallas_call | solution.py:60
  119.9 0.9 convert_add_fusion
  120.8 0.9 and_select_fusion
  121.7 16.8 %all-to-all-start.1 = ((f32[128,2,32]{2,1,0:T(2,128)}), f32[128,2,32]{2,1,0:T(2,128)S(1)}, u32[]{:S(2)}, u32[]{:S(2)}) async-start(f32[128,2,32]{2,1,0:T(2,128)} %and_select_fusion), calls=%async_computation.1 | async-start | bytes 262144 | tf_op jit(solution)/shard_map/all_to_all | solution.py:246
  138.5 8.7 %shard_map.78 = (f32[8,128,128]{2,1,0:T(8,128)}, f32[8,128]{1,0:T(8,128)}) custom-call(bf16[8192,128]{1,0:T(8,128)(2,1)} %bitcast.64, f32[8,1024]{1,0:T(8,128)} %copy-done.4, s32[8,1024]{1,0:T(8,128)} %broadcast_in_dim.74.user_ref, f32[8,1024]{1,0:T(8,128)} %add_select_fusion.1.rw_ref), custom_call_target="tpu_custom_call" | custom-call | flops 2684354560 | bytes 2723840 | tf_op jit(solution)/shard_map/pallas_call | solution.py:151
  147.2 1.3 bitcast_dynamic-update-slice_fusion
  148.6 0.7 constant_dynamic-update-slice_fusion
  149.4 3.7 %collective-permute-start.2 = (f32[2,16512]{1,0:T(2,128)S(1)}, f32[2,16512]{1,0:T(2,128)S(1)}, u32[]{:S(2)}, u32[]{:S(2)}) collective-permute-start(f32[2,16512]{1,0:T(2,128)S(1)} %get-tuple-element.7), channel_id=1, source_target_pairs={{0,3},{1,0},{2,1},{3,2},{4,7},{5,4},{6,5},{7,6},{8,11},{9,8},{10,9... | collective-permute-start | bytes 396296 | tf_op jit(solution)/shard_map/ppermute | solution.py:81
  153.0 2.4 collective-permute-start.1
  155.5 2.7 %collective-permute-start = (f32[2,16512]{1,0:T(2,128)S(1)}, f32[2,16512]{1,0:T(2,128)S(1)}, u32[]{:S(2)}, u32[]{:S(2)}) collective-permute-start(f32[2,16512]{1,0:T(2,128)S(1)} %get-tuple-element.6), channel_id=1, source_target_pairs={{0,1},{1,2},{2,3},{3,0},{4,5},{5,6},{6,7},{7,4},{8,9},{9,10},{10,1... | collective-permute-start | bytes 396296 | tf_op jit(solution)/shard_map/ppermute | solution.py:81
  158.6 1.7 collective-permute-done.1
  160.3 3.6 %collective-permute-done = f32[2,16512]{1,0:T(2,128)S(1)} collective-permute-done((f32[2,16512]{1,0:T(2,128)S(1)}, f32[2,16512]{1,0:T(2,128)S(1)}, u32[]{:S(2)}, u32[]{:S(2)}) %collective-permute-start) | collective-permute-done | bytes 132128 | tf_op jit(solution)/shard_map/ppermute | solution.py:81
  164.3 23.5 %custom-call.9 = f32[2,128,128]{2,1,0:T(8,128)S(1)} custom-call(f32[2,128,128]{2,1,0:T(8,128)S(1)} %fusion.3), custom_call_target="Cholesky" | custom-call | tf_op jit(solution)/shard_map/jit(cholesky)/cholesky | solution.py:21
  188.0 19.7 %custom-call.10 = f32[2,1,128,128]{2,3,1,0:T(8,128)S(1)} custom-call(f32[2,1,128,128]{3,2,1,0:T(8,128)S(1)} %select_bitcast_fusion), custom_call_target="InvertDiagBlocksLowerTriangular" | custom-call | tf_op jit(solution)/shard_map/triangular_solve | solution.py:23
  208.3 2.1 collective-permute-start.5
  210.4 2.0 collective-permute-start.4
  212.3 3.2 %collective-permute-start.3 = (bf16[2,128]{1,0:T(2,128)(2,1)S(1)}, bf16[2,128]{1,0:T(2,128)(2,1)S(1)}, u32[]{:S(2)}, u32[]{:S(2)}) collective-permute-start(bf16[2,128]{1,0:T(2,128)(2,1)S(1)} %convert_element_type.21), channel_id=1, source_target_pairs={{0,1},{1,2},{2,3},{3,0},{4,5},{5,6},{6,7},{7,4},{8,9},{9,10},{10,1... | collective-permute-start | bytes 1544 | tf_op jit(solution)/shard_map/ppermute | solution.py:91
  216.2 2.6 %collective-permute-done.3 = bf16[2,128]{1,0:T(2,128)(2,1)S(1)} collective-permute-done((bf16[2,128]{1,0:T(2,128)(2,1)S(1)}, bf16[2,128]{1,0:T(2,128)(2,1)S(1)}, u32[]{:S(2)}, u32[]{:S(2)}) %collective-permute-start.3) | collective-permute-done | bytes 544 | tf_op jit(solution)/shard_map/ppermute | solution.py:91
  219.4 0.9 convolution_convert_fusion
  220.3 16.1 %all-to-all-start.2 = ((bf16[128,2,128]{2,1,0:T(2,128)(2,1)}), bf16[128,2,128]{2,1,0:T(2,128)(2,1)S(1)}, u32[]{:S(2)}, u32[]{:S(2)}) async-start(bf16[128,2,128]{2,1,0:T(2,128)(2,1)} %bitcast.26), calls=%async_computation.2 | async-start | bytes 131072 | tf_op jit(solution)/shard_map/all_to_all | solution.py:239
  236.4 7.4 %select_reduce_fusion = f32[256,1024]{1,0:T(8,128)S(1)} fusion(f32[256,32]{1,0:T(8,128)S(1)} %bitcast.66, s32[256,32]{1,0:T(8,128)S(1)} %copy.38), kind=kLoop, calls=%fused_computation.1 | loop fusion | flops 24903680 | bytes 1114112 | tf_op jit(solution)/shard_map/reduce_sum | solution.py:257
  243.7 4.1 %all-to-all-done.2 = bf16[128,2,128]{2,1,0:T(2,128)(2,1)S(1)} async-done(((bf16[128,2,128]{2,1,0:T(2,128)(2,1)}), bf16[128,2,128]{2,1,0:T(2,128)(2,1)S(1)}, u32[]{:S(2)}, u32[]{:S(2)}) %all-to-all-start.2) | async-done | bytes 65568 | tf_op jit(solution)/shard_map/all_to_all | solution.py:239
  247.8 1.8 convolution_multiply_fusion
  (73 shorter events, 7.1 us)
Async XLA Ops:
  17.3 33.0 %copy-start.2 = (s32[1,1,256,32]{2,3,1,0:T(8,128)S(1)}, s32[1,1,256,32]{2,3,1,0:T(8,128)}, u32[]{:S(2)}) copy-start(s32[1,1,256,32]{2,3,1,0:T(8,128)} %param.10) | copy-start | bytes 98308
  31.7 19.7 %copy-start.5 = (s32[1,1,256,1]{2,3,1,0:T(1,128)S(1)}, s32[1,1,256,1]{2,3,1,0:T(1,128)}, u32[]{:S(2)}) copy-start(s32[1,1,256,1]{2,3,1,0:T(1,128)} %param.9) | copy-start | bytes 3076
  31.7 21.3 %copy-start.7 = (s32[1,1,128]{2,1,0:T(1,128)S(1)}, s32[1,1,128]{2,1,0:T(1,128)}, u32[]{:S(2)}) copy-start(s32[1,1,128]{2,1,0:T(1,128)} %param.11) | copy-start | bytes 1540
  31.7 22.5 %copy-start.1 = (bf16[1024,128]{1,0:T(8,128)(2,1)S(1)}, bf16[1024,128]{1,0:T(8,128)(2,1)}, u32[]{:S(2)}) copy-start(bf16[1024,128]{1,0:T(8,128)(2,1)} %table_ref.1) | copy-start | bytes 786436
  31.7 90.0 %all-to-all-start = ((bf16[128,64,128]{2,1,0:T(8,128)(2,1)}), bf16[128,64,128]{2,1,0:T(8,128)(2,1)S(1)}, u32[]{:S(2)}, u32[]{:S(2)}) async-start(bf16[128,64,128]{2,1,0:T(8,128)(2,1)} %bitcast.65), calls=%async_computation | async-start | bytes 4194304 | tf_op jit(solution)/shard_map/all_to_all | solution.py:198
  50.9 87.6 %copy-start.4 = (f32[8,1024]{1,0:T(8,128)}, f32[8,1024]{1,0:T(8,128)S(1)}, u32[]{:S(2)}) copy-start(f32[8,1024]{1,0:T(8,128)S(1)} %mul.30.gw_ref) | copy-start | bytes 98308
  121.7 16.8 %copy-start = (bf16[128,64,128]{2,1,0:T(8,128)(2,1)}, bf16[128,64,128]{2,1,0:T(8,128)(2,1)S(1)}, u32[]{:S(2)}) copy-start(bf16[128,64,128]{2,1,0:T(8,128)(2,1)S(1)} %all-to-all-done) | copy-start | bytes 6291460
  121.7 98.6 %all-to-all-start.1 = ((f32[128,2,32]{2,1,0:T(2,128)}), f32[128,2,32]{2,1,0:T(2,128)S(1)}, u32[]{:S(2)}, u32[]{:S(2)}) async-start(f32[128,2,32]{2,1,0:T(2,128)} %and_select_fusion), calls=%async_computation.1 | async-start | bytes 262144 | tf_op jit(solution)/shard_map/all_to_all | solution.py:246
  138.4 19.8 %copy-start.3 = (s32[1,1,256,32]{2,3,1,0:T(8,128)S(1)}, s32[1,1,256,32]{2,3,1,0:T(8,128)}, u32[]{:S(2)}) copy-start(s32[1,1,256,32]{2,3,1,0:T(8,128)} %param.7) | copy-start | bytes 98308
  149.4 9.2 %collective-permute-start.2 = (f32[2,16512]{1,0:T(2,128)S(1)}, f32[2,16512]{1,0:T(2,128)S(1)}, u32[]{:S(2)}, u32[]{:S(2)}) collective-permute-start(f32[2,16512]{1,0:T(2,128)S(1)} %get-tuple-element.7), channel_id=1, source_target_pairs={{0,3},{1,0},{2,1},{3,2},{4,7},{5,4},{6,5},{7,6},{8,11},{9,8},{10,9... | collective-permute-start | bytes 396296 | tf_op jit(solution)/shard_map/ppermute | solution.py:81
  153.0 7.2 %collective-permute-start.1 = (f32[2,16512]{1,0:T(2,128)S(1)}, f32[2,16512]{1,0:T(2,128)S(1)}, u32[]{:S(2)}, u32[]{:S(2)}) collective-permute-start(f32[2,16512]{1,0:T(2,128)S(1)} %get-tuple-element.8), channel_id=1, source_target_pairs={{0,2},{1,3},{2,0},{3,1},{4,6},{5,7},{6,4},{7,5},{8,10},{9,11},{10,... | collective-permute-start | bytes 396296 | tf_op jit(solution)/shard_map/ppermute | solution.py:81
  155.5 8.4 %collective-permute-start = (f32[2,16512]{1,0:T(2,128)S(1)}, f32[2,16512]{1,0:T(2,128)S(1)}, u32[]{:S(2)}, u32[]{:S(2)}) collective-permute-start(f32[2,16512]{1,0:T(2,128)S(1)} %get-tuple-element.6), channel_id=1, source_target_pairs={{0,1},{1,2},{2,3},{3,0},{4,5},{5,6},{6,7},{7,4},{8,9},{9,10},{10,1... | collective-permute-start | bytes 396296 | tf_op jit(solution)/shard_map/ppermute | solution.py:81
  208.3 41.4 %copy-start.6 = (f32[2,1,128]{2,1,0:T(1,128)}, f32[2,1,128]{2,1,0:T(1,128)S(1)}, u32[]{:S(2)}) copy-start(f32[2,1,128]{2,1,0:T(1,128)S(1)} %fusion) | copy-start | bytes 3076
  208.3 7.2 %collective-permute-start.5 = (bf16[2,128]{1,0:T(2,128)(2,1)S(1)}, bf16[2,128]{1,0:T(2,128)(2,1)S(1)}, u32[]{:S(2)}, u32[]{:S(2)}) collective-permute-start(bf16[2,128]{1,0:T(2,128)(2,1)S(1)} %convert_element_type.21), channel_id=1, source_target_pairs={{0,3},{1,0},{2,1},{3,2},{4,7},{5,4},{6,5},{7,6},{8,11},{9,8},{10,9... | collective-permute-start | bytes 1544 | tf_op jit(solution)/shard_map/ppermute | solution.py:91
  210.4 5.8 %collective-permute-start.4 = (bf16[2,128]{1,0:T(2,128)(2,1)S(1)}, bf16[2,128]{1,0:T(2,128)(2,1)S(1)}, u32[]{:S(2)}, u32[]{:S(2)}) collective-permute-start(bf16[2,128]{1,0:T(2,128)(2,1)S(1)} %convert_element_type.21), channel_id=1, source_target_pairs={{0,2},{1,3},{2,0},{3,1},{4,6},{5,7},{6,4},{7,5},{8,10},{9,11},{10,... | collective-permute-start | bytes 1544 | tf_op jit(solution)/shard_map/ppermute | solution.py:91
  212.3 6.5 %collective-permute-start.3 = (bf16[2,128]{1,0:T(2,128)(2,1)S(1)}, bf16[2,128]{1,0:T(2,128)(2,1)S(1)}, u32[]{:S(2)}, u32[]{:S(2)}) collective-permute-start(bf16[2,128]{1,0:T(2,128)(2,1)S(1)} %convert_element_type.21), channel_id=1, source_target_pairs={{0,1},{1,2},{2,3},{3,0},{4,5},{5,6},{6,7},{7,4},{8,9},{9,10},{10,1... | collective-permute-start | bytes 1544 | tf_op jit(solution)/shard_map/ppermute | solution.py:91
  220.3 27.5 %all-to-all-start.2 = ((bf16[128,2,128]{2,1,0:T(2,128)(2,1)}), bf16[128,2,128]{2,1,0:T(2,128)(2,1)S(1)}, u32[]{:S(2)}, u32[]{:S(2)}) async-start(bf16[128,2,128]{2,1,0:T(2,128)(2,1)} %bitcast.26), calls=%async_computation.2 | async-start | bytes 131072 | tf_op jit(solution)/shard_map/all_to_all | solution.py:239

commit v5 on v4

--- a/solution.py
+++ b/solution.py
@@ -26,46 +26,104 @@
     return result[..., 0]
 
 
-def doubling_kernel(n_rep, rounds, x_ref, o_ref, recv, send_sem, recv_sem):
+def flip_bits(value, mask, bits):
+    out = value - value % (1 << bits)
+    for bit in range(bits):
+        here = (value // (1 << bit)) % 2
+        out = out + (1 << bit) * ((1 - here) if (mask >> bit) & 1 else here)
+    return out
+
+
+def doubling_kernel(
+    n_rep, low_bits, rounds, x_ref, o_ref, full_recv, piece_recv, piece, gath,
+    sem_a, sem_b, sem_c, sem_d, sem_e, sem_f,
+):
     flat = lax.axis_index("ent") * n_rep + lax.axis_index("rep")
-    partners = []
-    for bit in range(rounds):
+    group = 1 << low_bits
+    rows = x_ref.shape[0] // group
+    slot = flat % group
+
+    def place(p):
+        return (p // n_rep, p % n_rep)
+
+    def flip(bit):
         step = 1 << bit
         upper = (flat // step) % 2
-        peer = flat + step - 2 * step * upper
-        partners.append((peer // n_rep, peer % n_rep))
+        return flat + step - 2 * step * upper
+
+    members = [flip_bits(flat, k, low_bits) for k in range(1, group)]
+    outer = [flip(bit) for bit in range(low_bits, rounds)]
     barrier = pltpu.get_barrier_semaphore()
-    for peer in partners:
-        pl.semaphore_signal(barrier, inc=1, device_id=peer, device_id_type=MESH_ID)
-    pl.semaphore_wait(barrier, rounds)
+    for p in members + outer:
+        pl.semaphore_signal(barrier, inc=1, device_id=place(p), device_id_type=MESH_ID)
+    pl.semaphore_wait(barrier, len(members) + len(outer))
+
     o_ref[...] = x_ref[...]
-    for bit in range(rounds):
+    for bit in range(low_bits):
         copy = pltpu.make_async_remote_copy(
-            src_ref=o_ref,
-            dst_ref=recv.at[bit],
-            send_sem=send_sem.at[bit],
-            recv_sem=recv_sem.at[bit],
-            device_id=partners[bit],
-            device_id_type=MESH_ID,
+            src_ref=o_ref, dst_ref=full_recv.at[bit], send_sem=sem_a.at[bit],
+            recv_sem=sem_b.at[bit], device_id=place(flip(bit)), device_id_type=MESH_ID,
         )
         copy.start()
         copy.wait_recv()
         copy.wait_send()
-        o_ref[...] = o_ref[...] + recv[bit]
+        o_ref[...] = o_ref[...] + full_recv[bit]
+
+    piece[...] = o_ref[pl.ds(pl.multiple_of(slot * rows, rows), rows), :]
+    for index, p in enumerate(outer):
+        copy = pltpu.make_async_remote_copy(
+            src_ref=piece, dst_ref=piece_recv.at[index], send_sem=sem_c.at[index],
+            recv_sem=sem_d.at[index], device_id=place(p), device_id_type=MESH_ID,
+        )
+        copy.start()
+        copy.wait_recv()
+        copy.wait_send()
+        piece[...] = piece[...] + piece_recv[index]
+
+    gath[slot] = piece[...]
+    sends = []
+    for index, p in enumerate(members):
+        copy = pltpu.make_async_remote_copy(
+            src_ref=piece, dst_ref=gath.at[slot], send_sem=sem_e.at[index],
+            recv_sem=sem_f.at[slot], device_id=place(p), device_id_type=MESH_ID,
+        )
+        copy.start()
+        sends.append(copy)
+    for k in range(1, group):
+        source = flip_bits(slot, k, low_bits)
+        pltpu.make_async_remote_copy(
+            src_ref=piece, dst_ref=gath.at[source], send_sem=sem_e.at[k - 1],
+            recv_sem=sem_f.at[source], device_id=place(members[k - 1]), device_id_type=MESH_ID,
+        ).wait_recv()
+    for copy in sends:
+        copy.wait_send()
+    for part in range(group):
+        o_ref[pl.ds(part * rows, rows), :] = gath[part]
 
 
 def tree_sum(value, count):
     rounds = count.bit_length() - 1
     n_rep = lax.axis_size("rep")
+    low_bits = (n_rep * 2).bit_length() - 1
+    group = 1 << low_bits
+    rows = value.shape[0] // group
+    outer = rounds - low_bits
     return pl.pallas_call(
-        functools.partial(doubling_kernel, n_rep, rounds),
+        functools.partial(doubling_kernel, n_rep, low_bits, rounds),
         out_shape=jax.ShapeDtypeStruct(value.shape, value.dtype),
         in_specs=[pl.BlockSpec(memory_space=pltpu.VMEM)],
         out_specs=pl.BlockSpec(memory_space=pltpu.VMEM),
         scratch_shapes=[
-            pltpu.VMEM((rounds,) + value.shape, value.dtype),
-            pltpu.SemaphoreType.DMA((rounds,)),
-            pltpu.SemaphoreType.DMA((rounds,)),
+            pltpu.VMEM((low_bits,) + value.shape, value.dtype),
+            pltpu.VMEM((outer, rows, value.shape[1]), value.dtype),
+            pltpu.VMEM((rows, value.shape[1]), value.dtype),
+            pltpu.VMEM((group, rows, value.shape[1]), value.dtype),
+            pltpu.SemaphoreType.DMA((low_bits,)),
+            pltpu.SemaphoreType.DMA((low_bits,)),
+            pltpu.SemaphoreType.DMA((outer,)),
+            pltpu.SemaphoreType.DMA((outer,)),
+            pltpu.SemaphoreType.DMA((group - 1,)),
+            pltpu.SemaphoreType.DMA((group,)),
         ],
         compiler_params=pltpu.CompilerParams(collective_id=0, has_side_effects=True),
     )(value)

time: 251 us -> 246 us (0.980)
  starting transfers between devices: 67.4 us -> 62.6 us
    all_to_all x1, starting transfers between devices: 16.8 us -> 11 us  [shards(): lax.all_to_all(rhs_weight.reshape(n_ent, slot_cap, tile_rows), 'ent', spl...]
  transfers between devices with their start and end apart: 9 -> 9, of which waited for: 5 -> 4; matrix products, arithmetic and copies ran while one was open for 25% -> 26% of each run, Pallas kernels for 29% -> 30%
where the time goes in v5:
time: 246 us; the launch traced here: 245 us
  Pallas kernels  88.8 us (36%)
  starting transfers between devices  62.6 us (25%)
  other arithmetic  59.3 us (24%)
  local copies, waits for them, and re-layouts  17.9 us (7%)
  waiting for transfers between devices  11.4 us (5%)
  matrix products  4.13 us (2%)
    pallas_call x1, Pallas kernels, tree_sum(): pl.pallas_call(functools.partial(doubling_kernel, n_rep, low_bits, rounds...  65.6 us
    another operation x4, other arithmetic, solve_users(): lower = jnp.linalg.cholesky(gram)  23.6 us
    another operation x3, other arithmetic, solve_users(): lax.linalg.triangular_solve(lower, halfway, left_side=True, lower=True, t...  19.8 us
    all_to_all x1, starting transfers between devices, shards(): lax.all_to_all(picked.reshape(n_ent, slot_cap * tile_rows, rank_width), '...  18.6 us
    all_to_all x1, starting transfers between devices, shards(): lax.all_to_all(run_factor.reshape(n_ent, slot_cap, seg_count * rank_width...  16.4 us
    pallas_call x1, Pallas kernels, gather_rows(): pl.pallas_call(gather_kernel, out_shape=jax.ShapeDtypeStruct((count, tabl...  14.4 us
    all_to_all x1, starting transfers between devices, shards(): lax.all_to_all(rhs_weight.reshape(n_ent, slot_cap, tile_rows), 'ent', spl...  11 us
    pallas_call x1, Pallas kernels, user_grams(): pl.pallas_call(functools.partial(gram_kernel, n_user), out_shape=(jax.Sha...  8.76 us
  transfers between devices with their start and end apart: 9, of which 4 were waited for; matrix products, arithmetic and copies ran while one was open for 26% of the time, Pallas kernels for 30%

profile of v5, /device:TPU:1, one launch (start us, length us, event | category | flops | bytes accessed | tf_op | source)
XLA Modules:
  0.0 245.3 jit_solution(3124458455775714973)
XLA Ops:
  0.6 0.7 broadcast_in_dim.69
  1.6 4.6 %reshape.204 = pred[8192,1]{1,0:T(8,128)(4,1)S(1)} reshape(pred[256,32]{1,0:T(8,128)(4,1)S(1)} %broadcast_in_dim.70) | data formatting | bytes 16384 | tf_op jit(solution)/shard_map/reshape | solution.py:253
  6.2 0.9 copy.28
  7.1 5.7 %reshape_reshape.5 = s32[8192,1]{1,0:T(8,128)} reshape(s32[1,1,256,32]{3,2,1,0:T(8,128)S(1)} %copy.28) | data formatting | bytes 65536 | tf_op jit(solution)/shard_map/reshape;reshape | solution.py:254
  12.7 4.5 %broadcast_select_fusion.idx_ref = s32[8192,1]{1,0:T(8,128)} fusion(pred[8192,1]{1,0:T(8,128)(4,1)S(1)} %reshape.204, s32[8192,1]{1,0:T(8,128)} %reshape_reshape.5), kind=kLoop, calls=%fused_computation.3 | loop fusion | flops 8192 | bytes 73728 | tf_op jit(solution)/shard_map/jit(_where)/select_n | solution.py:254
  17.3 14.4 %shard_map.77 = bf16[8192,128]{1,0:T(8,128)(2,1)} custom-call(s32[8192,1]{1,0:T(8,128)} %broadcast_select_fusion.idx_ref, bf16[1024,128]{1,0:T(8,128)(2,1)} %table_ref.1), custom_call_target="tpu_custom_call" | custom-call | flops 2147483648 | bytes 2392064 | tf_op jit(solution)/shard_map/pallas_call | solution.py:164
  31.7 18.6 %all-to-all-start = ((bf16[128,64,128]{2,1,0:T(8,128)(2,1)}), bf16[128,64,128]{2,1,0:T(8,128)(2,1)S(1)}, u32[]{:S(2)}, u32[]{:S(2)}) async-start(bf16[128,64,128]{2,1,0:T(8,128)(2,1)} %bitcast.65), calls=%async_computation | async-start | bytes 4194304 | tf_op jit(solution)/shard_map/all_to_all | solution.py:256
  52.2 0.7 broadcast_in_dim.74.user_ref
  54.2 0.9 fusion.21.x_ref
  55.1 65.6 %shard_map.79 = f32[128,128]{1,0:T(8,128)} custom-call(f32[128,128]{1,0:T(8,128)} %fusion.21.x_ref), custom_call_target="tpu_custom_call" | custom-call | tf_op jit(solution)/shard_map/pallas_call | solution.py:111
  121.5 0.9 convert_add_fusion
  122.4 0.9 and_select_fusion
  123.3 11.0 %all-to-all-start.1 = ((f32[128,2,32]{2,1,0:T(2,128)}), f32[128,2,32]{2,1,0:T(2,128)S(1)}, u32[]{:S(2)}, u32[]{:S(2)}) async-start(f32[128,2,32]{2,1,0:T(2,128)} %and_select_fusion), calls=%async_computation.1 | async-start | bytes 262144 | tf_op jit(solution)/shard_map/all_to_all | solution.py:304
  134.3 8.8 %shard_map.78 = (f32[8,128,128]{2,1,0:T(8,128)}, f32[8,128]{1,0:T(8,128)}) custom-call(bf16[8192,128]{1,0:T(8,128)(2,1)} %bitcast.64, f32[8,1024]{1,0:T(8,128)} %copy-done.4, s32[8,1024]{1,0:T(8,128)} %broadcast_in_dim.74.user_ref, f32[8,1024]{1,0:T(8,128)} %add_select_fusion.1.rw_ref), custom_call_target="tpu_custom_call" | custom-call | flops 2684354560 | bytes 2723840 | tf_op jit(solution)/shard_map/pallas_call | solution.py:209
  143.1 1.3 bitcast_dynamic-update-slice_fusion
  144.4 0.7 constant_dynamic-update-slice_fusion
  145.3 2.8 %collective-permute-start.2 = (f32[2,16512]{1,0:T(2,128)S(1)}, f32[2,16512]{1,0:T(2,128)S(1)}, u32[]{:S(2)}, u32[]{:S(2)}) collective-permute-start(f32[2,16512]{1,0:T(2,128)S(1)} %get-tuple-element.7), channel_id=1, source_target_pairs={{0,3},{1,0},{2,1},{3,2},{4,7},{5,4},{6,5},{7,6},{8,11},{9,8},{10,9... | collective-permute-start | bytes 396296 | tf_op jit(solution)/shard_map/ppermute | solution.py:139
  148.0 3.2 %collective-permute-start.1 = (f32[2,16512]{1,0:T(2,128)S(1)}, f32[2,16512]{1,0:T(2,128)S(1)}, u32[]{:S(2)}, u32[]{:S(2)}) collective-permute-start(f32[2,16512]{1,0:T(2,128)S(1)} %get-tuple-element.8), channel_id=1, source_target_pairs={{0,2},{1,3},{2,0},{3,1},{4,6},{5,7},{6,4},{7,5},{8,10},{9,11},{10,... | collective-permute-start | bytes 396296 | tf_op jit(solution)/shard_map/ppermute | solution.py:139
  151.2 2.1 collective-permute-start
  153.7 1.5 collective-permute-done.1
  155.3 3.0 %collective-permute-done = f32[2,16512]{1,0:T(2,128)S(1)} collective-permute-done((f32[2,16512]{1,0:T(2,128)S(1)}, f32[2,16512]{1,0:T(2,128)S(1)}, u32[]{:S(2)}, u32[]{:S(2)}) %collective-permute-start) | collective-permute-done | bytes 132128 | tf_op jit(solution)/shard_map/ppermute | solution.py:139
  158.7 23.5 %custom-call.9 = f32[2,128,128]{2,1,0:T(8,128)S(1)} custom-call(f32[2,128,128]{2,1,0:T(8,128)S(1)} %fusion.3), custom_call_target="Cholesky" | custom-call | tf_op jit(solution)/shard_map/jit(cholesky)/cholesky | solution.py:21
  182.5 19.7 %custom-call.10 = f32[2,1,128,128]{2,3,1,0:T(8,128)S(1)} custom-call(f32[2,1,128,128]{3,2,1,0:T(8,128)S(1)} %select_bitcast_fusion), custom_call_target="InvertDiagBlocksLowerTriangular" | custom-call | tf_op jit(solution)/shard_map/triangular_solve | solution.py:23
  202.7 2.3 collective-permute-start.5
  205.0 3.7 %collective-permute-start.4 = (bf16[2,128]{1,0:T(2,128)(2,1)S(1)}, bf16[2,128]{1,0:T(2,128)(2,1)S(1)}, u32[]{:S(2)}, u32[]{:S(2)}) collective-permute-start(bf16[2,128]{1,0:T(2,128)(2,1)S(1)} %convert_element_type.21), channel_id=1, source_target_pairs={{0,2},{1,3},{2,0},{3,1},{4,6},{5,7},{6,4},{7,5},{8,10},{9,11},{10,... | collective-permute-start | bytes 1544 | tf_op jit(solution)/shard_map/ppermute | solution.py:149
  208.7 2.7 %collective-permute-start.3 = (bf16[2,128]{1,0:T(2,128)(2,1)S(1)}, bf16[2,128]{1,0:T(2,128)(2,1)S(1)}, u32[]{:S(2)}, u32[]{:S(2)}) collective-permute-start(bf16[2,128]{1,0:T(2,128)(2,1)S(1)} %convert_element_type.21), channel_id=1, source_target_pairs={{0,1},{1,2},{2,3},{3,0},{4,5},{5,6},{6,7},{7,4},{8,9},{9,10},{10,1... | collective-permute-start | bytes 1544 | tf_op jit(solution)/shard_map/ppermute | solution.py:149
  211.4 2.8 %collective-permute-done.3 = bf16[2,128]{1,0:T(2,128)(2,1)S(1)} collective-permute-done((bf16[2,128]{1,0:T(2,128)(2,1)S(1)}, bf16[2,128]{1,0:T(2,128)(2,1)S(1)}, u32[]{:S(2)}, u32[]{:S(2)}) %collective-permute-start.3) | collective-permute-done | bytes 544 | tf_op jit(solution)/shard_map/ppermute | solution.py:149
  214.7 0.9 convolution_convert_fusion
  215.6 16.4 %all-to-all-start.2 = ((bf16[128,2,128]{2,1,0:T(2,128)(2,1)}), bf16[128,2,128]{2,1,0:T(2,128)(2,1)S(1)}, u32[]{:S(2)}, u32[]{:S(2)}) async-start(bf16[128,2,128]{2,1,0:T(2,128)(2,1)} %bitcast.26), calls=%async_computation.2 | async-start | bytes 131072 | tf_op jit(solution)/shard_map/all_to_all | solution.py:297
  232.0 7.4 %select_reduce_fusion = f32[256,1024]{1,0:T(8,128)S(1)} fusion(f32[256,32]{1,0:T(8,128)S(1)} %bitcast.66, s32[256,32]{1,0:T(8,128)S(1)} %copy.38), kind=kLoop, calls=%fused_computation.1 | loop fusion | flops 24903680 | bytes 1114112 | tf_op jit(solution)/shard_map/reduce_sum | solution.py:315
  239.4 4.1 %all-to-all-done.2 = bf16[128,2,128]{2,1,0:T(2,128)(2,1)S(1)} async-done(((bf16[128,2,128]{2,1,0:T(2,128)(2,1)}), bf16[128,2,128]{2,1,0:T(2,128)(2,1)S(1)}, u32[]{:S(2)}, u32[]{:S(2)}) %all-to-all-start.2) | async-done | bytes 65568 | tf_op jit(solution)/shard_map/all_to_all | solution.py:297
  243.4 1.8 convolution_multiply_fusion
  (73 shorter events, 6.5 us)
Async XLA Ops:
  17.3 33.0 %copy-start.2 = (s32[1,1,256,32]{2,3,1,0:T(8,128)S(1)}, s32[1,1,256,32]{2,3,1,0:T(8,128)}, u32[]{:S(2)}) copy-start(s32[1,1,256,32]{2,3,1,0:T(8,128)} %param.10) | copy-start | bytes 98308
  31.7 19.7 %copy-start.5 = (s32[1,1,256,1]{2,3,1,0:T(1,128)S(1)}, s32[1,1,256,1]{2,3,1,0:T(1,128)}, u32[]{:S(2)}) copy-start(s32[1,1,256,1]{2,3,1,0:T(1,128)} %param.9) | copy-start | bytes 3076
  31.7 21.3 %copy-start.7 = (s32[1,1,128]{2,1,0:T(1,128)S(1)}, s32[1,1,128]{2,1,0:T(1,128)}, u32[]{:S(2)}) copy-start(s32[1,1,128]{2,1,0:T(1,128)} %param.11) | copy-start | bytes 1540
  31.7 22.5 %copy-start.1 = (bf16[1024,128]{1,0:T(8,128)(2,1)S(1)}, bf16[1024,128]{1,0:T(8,128)(2,1)}, u32[]{:S(2)}) copy-start(bf16[1024,128]{1,0:T(8,128)(2,1)} %table_ref.1) | copy-start | bytes 786436
  31.7 91.6 %all-to-all-start = ((bf16[128,64,128]{2,1,0:T(8,128)(2,1)}), bf16[128,64,128]{2,1,0:T(8,128)(2,1)S(1)}, u32[]{:S(2)}, u32[]{:S(2)}) async-start(bf16[128,64,128]{2,1,0:T(8,128)(2,1)} %bitcast.65), calls=%async_computation | async-start | bytes 4194304 | tf_op jit(solution)/shard_map/all_to_all | solution.py:256
  50.9 83.4 %copy-start.4 = (f32[8,1024]{1,0:T(8,128)}, f32[8,1024]{1,0:T(8,128)S(1)}, u32[]{:S(2)}) copy-start(f32[8,1024]{1,0:T(8,128)S(1)} %mul.30.gw_ref) | copy-start | bytes 98308
  123.3 11.0 %copy-start = (bf16[128,64,128]{2,1,0:T(8,128)(2,1)}, bf16[128,64,128]{2,1,0:T(8,128)(2,1)S(1)}, u32[]{:S(2)}) copy-start(bf16[128,64,128]{2,1,0:T(8,128)(2,1)S(1)} %all-to-all-done) | copy-start | bytes 6291460
  123.3 92.4 %all-to-all-start.1 = ((f32[128,2,32]{2,1,0:T(2,128)}), f32[128,2,32]{2,1,0:T(2,128)S(1)}, u32[]{:S(2)}, u32[]{:S(2)}) async-start(f32[128,2,32]{2,1,0:T(2,128)} %and_select_fusion), calls=%async_computation.1 | async-start | bytes 262144 | tf_op jit(solution)/shard_map/all_to_all | solution.py:304
  134.3 19.1 %copy-start.3 = (s32[1,1,256,32]{2,3,1,0:T(8,128)S(1)}, s32[1,1,256,32]{2,3,1,0:T(8,128)}, u32[]{:S(2)}) copy-start(s32[1,1,256,32]{2,3,1,0:T(8,128)} %param.7) | copy-start | bytes 98308
  145.3 8.5 %collective-permute-start.2 = (f32[2,16512]{1,0:T(2,128)S(1)}, f32[2,16512]{1,0:T(2,128)S(1)}, u32[]{:S(2)}, u32[]{:S(2)}) collective-permute-start(f32[2,16512]{1,0:T(2,128)S(1)} %get-tuple-element.7), channel_id=1, source_target_pairs={{0,3},{1,0},{2,1},{3,2},{4,7},{5,4},{6,5},{7,6},{8,11},{9,8},{10,9... | collective-permute-start | bytes 396296 | tf_op jit(solution)/shard_map/ppermute | solution.py:139
  148.0 7.2 %collective-permute-start.1 = (f32[2,16512]{1,0:T(2,128)S(1)}, f32[2,16512]{1,0:T(2,128)S(1)}, u32[]{:S(2)}, u32[]{:S(2)}) collective-permute-start(f32[2,16512]{1,0:T(2,128)S(1)} %get-tuple-element.8), channel_id=1, source_target_pairs={{0,2},{1,3},{2,0},{3,1},{4,6},{5,7},{6,4},{7,5},{8,10},{9,11},{10,... | collective-permute-start | bytes 396296 | tf_op jit(solution)/shard_map/ppermute | solution.py:139
  151.2 7.1 %collective-permute-start = (f32[2,16512]{1,0:T(2,128)S(1)}, f32[2,16512]{1,0:T(2,128)S(1)}, u32[]{:S(2)}, u32[]{:S(2)}) collective-permute-start(f32[2,16512]{1,0:T(2,128)S(1)} %get-tuple-element.6), channel_id=1, source_target_pairs={{0,1},{1,2},{2,3},{3,0},{4,5},{5,6},{6,7},{7,4},{8,9},{9,10},{10,1... | collective-permute-start | bytes 396296 | tf_op jit(solution)/shard_map/ppermute | solution.py:139
  202.7 42.6 %copy-start.6 = (f32[2,1,128]{2,1,0:T(1,128)}, f32[2,1,128]{2,1,0:T(1,128)S(1)}, u32[]{:S(2)}) copy-start(f32[2,1,128]{2,1,0:T(1,128)S(1)} %fusion) | copy-start | bytes 3076
  202.7 8.7 %collective-permute-start.5 = (bf16[2,128]{1,0:T(2,128)(2,1)S(1)}, bf16[2,128]{1,0:T(2,128)(2,1)S(1)}, u32[]{:S(2)}, u32[]{:S(2)}) collective-permute-start(bf16[2,128]{1,0:T(2,128)(2,1)S(1)} %convert_element_type.21), channel_id=1, source_target_pairs={{0,3},{1,0},{2,1},{3,2},{4,7},{5,4},{6,5},{7,6},{8,11},{9,8},{10,9... | collective-permute-start | bytes 1544 | tf_op jit(solution)/shard_map/ppermute | solution.py:149
  205.0 6.4 %collective-permute-start.4 = (bf16[2,128]{1,0:T(2,128)(2,1)S(1)}, bf16[2,128]{1,0:T(2,128)(2,1)S(1)}, u32[]{:S(2)}, u32[]{:S(2)}) collective-permute-start(bf16[2,128]{1,0:T(2,128)(2,1)S(1)} %convert_element_type.21), channel_id=1, source_target_pairs={{0,2},{1,3},{2,0},{3,1},{4,6},{5,7},{6,4},{7,5},{8,10},{9,11},{10,... | collective-permute-start | bytes 1544 | tf_op jit(solution)/shard_map/ppermute | solution.py:149
  208.7 5.5 %collective-permute-start.3 = (bf16[2,128]{1,0:T(2,128)(2,1)S(1)}, bf16[2,128]{1,0:T(2,128)(2,1)S(1)}, u32[]{:S(2)}, u32[]{:S(2)}) collective-permute-start(bf16[2,128]{1,0:T(2,128)(2,1)S(1)} %convert_element_type.21), channel_id=1, source_target_pairs={{0,1},{1,2},{2,3},{3,0},{4,5},{5,6},{6,7},{7,4},{8,9},{9,10},{10,1... | collective-permute-start | bytes 1544 | tf_op jit(solution)/shard_map/ppermute | solution.py:149
  215.6 27.8 %all-to-all-start.2 = ((bf16[128,2,128]{2,1,0:T(2,128)(2,1)}), bf16[128,2,128]{2,1,0:T(2,128)(2,1)S(1)}, u32[]{:S(2)}, u32[]{:S(2)}) async-start(bf16[128,2,128]{2,1,0:T(2,128)(2,1)} %bitcast.26), calls=%async_computation.2 | async-start | bytes 131072 | tf_op jit(solution)/shard_map/all_to_all | solution.py:297

commit v6 on v5

--- a/solution.py
+++ b/solution.py
@@ -152,22 +152,24 @@
     return jnp.take(stacked, order, axis=0).reshape(-1, value.shape[-1])
 
 
-def gather_kernel(idx_ref, table_ref, out_ref):
-    picks = idx_ref[...] == lax.broadcasted_iota(jnp.int32, (idx_ref.shape[0], table_ref.shape[0]), 1)
-    out_ref[...] = jnp.dot(
-        picks.astype(jnp.bfloat16), table_ref[...], preferred_element_type=jnp.float32
-    ).astype(out_ref.dtype)
-
-
-def gather_rows(table, idx_col, chunk=512):
-    count = idx_col.shape[0]
+def gather_kernel(idx_ref, table_t_ref, out_ref):
+    step = pl.program_id(0)
+    idx = idx_ref[pl.ds(step, 1), :]
+    picks = lax.broadcasted_iota(jnp.int32, (table_t_ref.shape[1], idx.shape[1]), 0) == idx
+    rows_t = jnp.dot(table_t_ref[...], picks.astype(jnp.bfloat16), preferred_element_type=jnp.float32)
+    out_ref[...] = rows_t.T.astype(out_ref.dtype)
+
+
+def gather_rows(table, idx, chunk=512):
+    count = idx.shape[0]
+    idx_lanes = idx.reshape(count // chunk, chunk)
     return pl.pallas_call(
         gather_kernel,
         out_shape=jax.ShapeDtypeStruct((count, table.shape[1]), table.dtype),
         grid=(count // chunk,),
         in_specs=[
-            pl.BlockSpec((chunk, 1), lambda i: (i, 0)),
-            pl.BlockSpec(table.shape, lambda i: (0, 0)),
+            pl.BlockSpec(idx_lanes.shape, lambda i: (0, 0)),
+            pl.BlockSpec((table.shape[1], table.shape[0]), lambda i: (0, 0)),
         ],
         out_specs=pl.BlockSpec((chunk, table.shape[1]), lambda i: (i, 0)),
         cost_estimate=pl.CostEstimate(
@@ -175,7 +177,7 @@
             transcendentals=0,
             bytes_accessed=count * 4 + table.size * 2 + count * table.shape[1] * 2,
         ),
-    )(idx_col, table)
+    )(idx_lanes, table.T)
 
 
 def gram_kernel(n_user, rows_ref, gw_ref, user_ref, rw_ref, gram_ref, rhs_ref):
@@ -251,8 +253,7 @@
         item_factors, item_factors, (((0,), (0,)), ((), ())), preferred_element_type=jnp.float32
     )
     live_rows = jnp.repeat(live_send, tile_rows)
-    idx_col = jnp.where(live_rows, item_ids.reshape(-1), -1).reshape(-1, 1)
-    picked = gather_rows(item_factors, idx_col)
+    picked = gather_rows(item_factors, jnp.where(live_rows, item_ids.reshape(-1), -1))
     incoming = lax.all_to_all(
         picked.reshape(n_ent, slot_cap * tile_rows, rank_width),
         "ent",
@@ -293,21 +294,20 @@
         (((0,), (0,)), ((), ())),
         preferred_element_type=jnp.float32,
     ).astype(jnp.bfloat16)
-    back_factor, back_weight = (
-        lax.all_to_all(
-            run_factor.reshape(n_ent, slot_cap, seg_count * rank_width),
-            "ent",
-            split_axis=0,
-            concat_axis=0,
-            tiled=True,
-        ),
-        lax.all_to_all(
-            rhs_weight.reshape(n_ent, slot_cap, tile_rows),
-            "ent",
-            split_axis=0,
-            concat_axis=0,
-            tiled=True,
-        ),
+    back_load = jnp.concatenate(
+        [
+            run_factor.reshape(tile_slots, seg_count * rank_width),
+            counts_int.astype(jnp.bfloat16),
+        ],
+        axis=1,
+    )
+    back_load = lax.all_to_all(
+        back_load.reshape(n_ent, slot_cap, -1), "ent", split_axis=0, concat_axis=0, tiled=True
+    ).reshape(tile_slots, -1)
+    back_factor = back_load[:, : seg_count * rank_width]
+    back_counts = back_load[:, seg_count * rank_width :].astype(jnp.float32)
+    back_weight = jnp.where(
+        live_send[:, None] & (back_counts > 0), 1.0 + ALPHA * back_counts, jnp.float32(0.0)
     )
     item_hot = item_ids[:, :, None] == jnp.arange(item_count, dtype=jnp.int32)[None, None, :]
     run_weight = back_weight.reshape(tile_slots * seg_count, seg_length)

time: 246 us -> 226 us (0.919)
  starting transfers between devices: 62.6 us -> 48.8 us
  waiting for transfers between devices: 11.4 us -> 19.1 us
  local copies, waits for them, and re-layouts: 17.9 us -> 11.4 us
  Pallas kernels: 88.8 us -> 84.8 us
  other arithmetic: 59.3 us -> 56 us
    all_to_all x2 -> x1, starting transfers between devices: 27.4 us -> 13.6 us  [shards(): lax.all_to_all(back_load.reshape(n_ent, slot_cap, -1), 'ent', split_axis=...]
    all_to_all x2 -> x1, waiting for transfers between devices: 4.08 us -> 12.2 us  [shards(): lax.all_to_all(back_load.reshape(n_ent, slot_cap, -1), 'ent', split_axis=...]
    another operation x1, local copies, waits for them, and re-layouts: 5.65 us -> 0.1 us  [shards(): item_ids.reshape(-1)]
    pallas_call x1, Pallas kernels: 14.4 us -> 9.63 us  [gather_rows(): pl.pallas_call(gather_kernel, out_shape=jax.ShapeDtypeStruct((count, tabl...]
    select_n x1 -> x2, other arithmetic: 4.53 us -> 0.71 us  [the longest x1 0.6 us: shards(): jnp.where(live_rows, item_ids.reshape(-1), -1)]
    reshape x1 -> x2, local copies, waits for them, and re-layouts: 4.59 us -> 0.85 us  [the longest x1 0.73 us: shards(): back_load.reshape(n_ent, slot_cap, -1)]
    unnamed x21 -> x24, local copies, waits for them, and re-layouts: 2.78 us -> 5.89 us
  transfers between devices with their start and end apart: 9 -> 8, of which waited for: 4 -> 4; matrix products, arithmetic and copies ran while one was open for 26% -> 3% of each run, Pallas kernels for 30% -> 30%
where the time goes in v6:
time: 226 us; the launch traced here: 225 us
  Pallas kernels  84.8 us (38%)
  other arithmetic  56 us (25%)
  starting transfers between devices  48.8 us (22%)
  waiting for transfers between devices  19.1 us (8%)
  local copies, waits for them, and re-layouts  11.4 us (5%)
  matrix products  3.54 us (2%)
    pallas_call x1, Pallas kernels, tree_sum(): pl.pallas_call(functools.partial(doubling_kernel, n_rep, low_bits, rounds...  66.4 us
    another operation x4, other arithmetic, solve_users(): lower = jnp.linalg.cholesky(gram)  23.6 us
    another operation x3, other arithmetic, solve_users(): lax.linalg.triangular_solve(lower, halfway, left_side=True, lower=True, t...  19.8 us
    all_to_all x1, starting transfers between devices, shards(): lax.all_to_all(picked.reshape(n_ent, slot_cap * tile_rows, rank_width), '...  18.6 us
    all_to_all x1, starting transfers between devices, shards(): lax.all_to_all(back_load.reshape(n_ent, slot_cap, -1), 'ent', split_axis=...  13.6 us
    all_to_all x1, waiting for transfers between devices, shards(): lax.all_to_all(back_load.reshape(n_ent, slot_cap, -1), 'ent', split_axis=...  12.2 us
    pallas_call x1, Pallas kernels, gather_rows(): pl.pallas_call(gather_kernel, out_shape=jax.ShapeDtypeStruct((count, tabl...  9.63 us
    ppermute x3, starting transfers between devices, rep_gather(): got.append(lax.ppermute(value, 'rep', pairs))  8.82 us
  transfers between devices with their start and end apart: 8, of which 4 were waited for; matrix products, arithmetic and copies ran while one was open for 3% of the time, Pallas kernels for 30%

profile of v6, /device:TPU:1, one launch (start us, length us, event | category | flops | bytes accessed | tf_op | source)
XLA Modules:
  0.0 224.7 jit_solution(1677801634630210730)
XLA Ops:
  1.1 1.3 reduce.15
  3.0 0.9 copy.31
  3.9 1.8 copy.32
  6.3 9.6 %shard_map.77 = bf16[8192,128]{1,0:T(8,128)(2,1)} custom-call(s32[16,512]{1,0:T(8,128)} %broadcast_select_fusion.idx_ref, bf16[128,1024]{1,0:T(8,128)(2,1)} %bitcast.64), custom_call_target="tpu_custom_call" | custom-call | flops 2147483648 | bytes 2392064 | tf_op jit(solution)/shard_map/pallas_call | solution.py:166
  16.0 18.6 %all-to-all-start = ((bf16[128,64,128]{2,1,0:T(8,128)(2,1)}), bf16[128,64,128]{2,1,0:T(8,128)(2,1)S(1)}, u32[]{:S(2)}, u32[]{:S(2)}) async-start(bf16[128,64,128]{2,1,0:T(8,128)(2,1)} %bitcast.61), calls=%async_computation | async-start | bytes 4194304 | tf_op jit(solution)/shard_map/all_to_all | solution.py:257
  34.8 0.7 reduce.16
  35.7 0.7 broadcast_in_dim.84.user_ref
  36.4 0.7 reduce.17
  37.9 0.9 fusion.25.x_ref
  38.8 66.4 %shard_map.79 = f32[128,128]{1,0:T(8,128)} custom-call(f32[128,128]{1,0:T(8,128)} %fusion.25.x_ref), custom_call_target="tpu_custom_call" | custom-call | tf_op jit(solution)/shard_map/pallas_call | solution.py:111
  105.3 0.6 add_select_fusion.rw_ref
  105.9 0.9 convert_add_fusion
  106.7 1.3 copy-done.1
  108.1 8.8 %shard_map.78 = (f32[8,128,128]{2,1,0:T(8,128)}, f32[8,128]{1,0:T(8,128)}) custom-call(bf16[8192,128]{1,0:T(8,128)(2,1)} %bitcast.60, f32[8,1024]{1,0:T(8,128)} %copy-done.4, s32[8,1024]{1,0:T(8,128)} %broadcast_in_dim.84.user_ref, f32[8,1024]{1,0:T(8,128)} %add_select_fusion.rw_ref), custom_call_target="tpu_custom_call" | custom-call | flops 2684354560 | bytes 2723840 | tf_op jit(solution)/shard_map/pallas_call | solution.py:211
  116.8 1.4 bitcast_dynamic-update-slice_fusion
  118.2 0.7 constant_dynamic-update-slice_fusion
  119.0 2.5 %collective-permute-start.2 = (f32[2,16512]{1,0:T(2,128)S(1)}, f32[2,16512]{1,0:T(2,128)S(1)}, u32[]{:S(2)}, u32[]{:S(2)}) collective-permute-start(f32[2,16512]{1,0:T(2,128)S(1)} %get-tuple-element.7), channel_id=1, source_target_pairs={{0,3},{1,0},{2,1},{3,2},{4,7},{5,4},{6,5},{7,6},{8,11},{9,8},{10,9... | collective-permute-start | bytes 396296 | tf_op jit(solution)/shard_map/ppermute | solution.py:139
  121.6 3.2 %collective-permute-start.1 = (f32[2,16512]{1,0:T(2,128)S(1)}, f32[2,16512]{1,0:T(2,128)S(1)}, u32[]{:S(2)}, u32[]{:S(2)}) collective-permute-start(f32[2,16512]{1,0:T(2,128)S(1)} %get-tuple-element.8), channel_id=1, source_target_pairs={{0,2},{1,3},{2,0},{3,1},{4,6},{5,7},{6,4},{7,5},{8,10},{9,11},{10,... | collective-permute-start | bytes 396296 | tf_op jit(solution)/shard_map/ppermute | solution.py:139
  124.8 2.1 collective-permute-start
  127.6 1.8 collective-permute-done.1
  129.3 2.4 %collective-permute-done = f32[2,16512]{1,0:T(2,128)S(1)} collective-permute-done((f32[2,16512]{1,0:T(2,128)S(1)}, f32[2,16512]{1,0:T(2,128)S(1)}, u32[]{:S(2)}, u32[]{:S(2)}) %collective-permute-start) | collective-permute-done | bytes 132128 | tf_op jit(solution)/shard_map/ppermute | solution.py:139
  132.2 23.5 %custom-call.9 = f32[2,128,128]{2,1,0:T(8,128)S(1)} custom-call(f32[2,128,128]{2,1,0:T(8,128)S(1)} %fusion.5), custom_call_target="Cholesky" | custom-call | tf_op jit(solution)/shard_map/jit(cholesky)/cholesky | solution.py:21
  155.9 19.7 %custom-call.10 = f32[2,1,128,128]{2,3,1,0:T(8,128)S(1)} custom-call(f32[2,1,128,128]{3,2,1,0:T(8,128)S(1)} %select_bitcast_fusion), custom_call_target="InvertDiagBlocksLowerTriangular" | custom-call | tf_op jit(solution)/shard_map/triangular_solve | solution.py:23
  176.1 2.6 %collective-permute-start.5 = (bf16[2,128]{1,0:T(2,128)(2,1)S(1)}, bf16[2,128]{1,0:T(2,128)(2,1)S(1)}, u32[]{:S(2)}, u32[]{:S(2)}) collective-permute-start(bf16[2,128]{1,0:T(2,128)(2,1)S(1)} %convert_element_type.28), channel_id=1, source_target_pairs={{0,3},{1,0},{2,1},{3,2},{4,7},{5,4},{6,5},{7,6},{8,11},{9,8},{10,9... | collective-permute-start | bytes 1544 | tf_op jit(solution)/shard_map/ppermute | solution.py:149
  178.7 3.5 %collective-permute-start.4 = (bf16[2,128]{1,0:T(2,128)(2,1)S(1)}, bf16[2,128]{1,0:T(2,128)(2,1)S(1)}, u32[]{:S(2)}, u32[]{:S(2)}) collective-permute-start(bf16[2,128]{1,0:T(2,128)(2,1)S(1)} %convert_element_type.28), channel_id=1, source_target_pairs={{0,2},{1,3},{2,0},{3,1},{4,6},{5,7},{6,4},{7,5},{8,10},{9,11},{10,... | collective-permute-start | bytes 1544 | tf_op jit(solution)/shard_map/ppermute | solution.py:149
  182.2 2.7 %collective-permute-start.3 = (bf16[2,128]{1,0:T(2,128)(2,1)S(1)}, bf16[2,128]{1,0:T(2,128)(2,1)S(1)}, u32[]{:S(2)}, u32[]{:S(2)}) collective-permute-start(bf16[2,128]{1,0:T(2,128)(2,1)S(1)} %convert_element_type.28), channel_id=1, source_target_pairs={{0,1},{1,2},{2,3},{3,0},{4,5},{5,6},{6,7},{7,4},{8,9},{9,10},{10,1... | collective-permute-start | bytes 1544 | tf_op jit(solution)/shard_map/ppermute | solution.py:149
  185.0 2.7 %collective-permute-done.3 = bf16[2,128]{1,0:T(2,128)(2,1)S(1)} collective-permute-done((bf16[2,128]{1,0:T(2,128)(2,1)S(1)}, bf16[2,128]{1,0:T(2,128)(2,1)S(1)}, u32[]{:S(2)}, u32[]{:S(2)}) %collective-permute-start.3) | collective-permute-done | bytes 544 | tf_op jit(solution)/shard_map/ppermute | solution.py:149
  188.7 0.7 reshape.169
  189.4 13.6 %all-to-all-start.1 = ((bf16[128,2,160]{2,1,0:T(2,128)(2,1)}), bf16[128,2,160]{2,1,0:T(2,128)(2,1)S(1)}, u32[]{:S(2)}, u32[]{:S(2)}) async-start(bf16[128,2,160]{2,1,0:T(2,128)(2,1)} %reshape.169), calls=%async_computation.1 | async-start | bytes 262144 | tf_op jit(solution)/shard_map/all_to_all | solution.py:304
  203.0 12.2 %all-to-all-done.1 = bf16[128,2,160]{2,1,0:T(2,128)(2,1)S(1)} async-done(((bf16[128,2,160]{2,1,0:T(2,128)(2,1)}), bf16[128,2,160]{2,1,0:T(2,128)(2,1)S(1)}, u32[]{:S(2)}, u32[]{:S(2)}) %all-to-all-start.1) | async-done | bytes 81952 | tf_op jit(solution)/shard_map/all_to_all | solution.py:304
  215.5 7.4 %select_reduce_fusion = f32[256,1024]{1,0:T(8,128)S(1)} fusion(f32[256,32]{1,0:T(8,128)S(1)} %fusion.1, s32[256,32]{1,0:T(8,128)S(1)} %copy.40), kind=kLoop, calls=%fused_computation.1 | loop fusion | flops 24903680 | bytes 1114112 | tf_op jit(solution)/shard_map/reduce_sum | solution.py:315
  222.9 1.8 convolution_multiply_fusion
  (82 shorter events, 6.1 us)
Async XLA Ops:
  16.0 18.6 %copy-start.2 = (s32[1,1,256,32]{2,3,1,0:T(8,128)S(1)}, s32[1,1,256,32]{2,3,1,0:T(8,128)}, u32[]{:S(2)}) copy-start(s32[1,1,256,32]{2,3,1,0:T(8,128)} %param.10) | copy-start | bytes 98308
  16.0 18.9 %copy-start.6 = (s32[1,1,256,1]{2,3,1,0:T(1,128)S(1)}, s32[1,1,256,1]{2,3,1,0:T(1,128)}, u32[]{:S(2)}) copy-start(s32[1,1,256,1]{2,3,1,0:T(1,128)} %param.9) | copy-start | bytes 3076
  16.0 20.5 %copy-start.8 = (s32[1,1,128]{2,1,0:T(1,128)S(1)}, s32[1,1,128]{2,1,0:T(1,128)}, u32[]{:S(2)}) copy-start(s32[1,1,128]{2,1,0:T(1,128)} %param.11) | copy-start | bytes 1540
  16.0 21.9 %copy-start = (bf16[1024,128]{1,0:T(8,128)(2,1)S(1)}, bf16[1024,128]{1,0:T(8,128)(2,1)}, u32[]{:S(2)}) copy-start(bf16[1024,128]{1,0:T(8,128)(2,1)} %param.6) | copy-start | bytes 786436
  16.0 90.7 %all-to-all-start = ((bf16[128,64,128]{2,1,0:T(8,128)(2,1)}), bf16[128,64,128]{2,1,0:T(8,128)(2,1)S(1)}, u32[]{:S(2)}, u32[]{:S(2)}) async-start(bf16[128,64,128]{2,1,0:T(8,128)(2,1)} %bitcast.61), calls=%async_computation | async-start | bytes 4194304 | tf_op jit(solution)/shard_map/all_to_all | solution.py:257
  34.8 71.9 %copy-start.4 = (f32[8,1024]{1,0:T(8,128)}, f32[8,1024]{1,0:T(8,128)S(1)}, u32[]{:S(2)}) copy-start(f32[8,1024]{1,0:T(8,128)S(1)} %mul.31.gw_ref) | copy-start | bytes 98308
  106.7 1.3 copy-start.1
  108.1 19.1 %copy-start.7 = (s32[1,1,128]{2,1,0:T(1,128)S(1)}, s32[1,1,128]{2,1,0:T(1,128)}, u32[]{:S(2)}) copy-start(s32[1,1,128]{2,1,0:T(1,128)} %param.8) | copy-start | bytes 1540
  116.8 10.6 %copy-start.3 = (s32[1,1,256,32]{2,3,1,0:T(8,128)S(1)}, s32[1,1,256,32]{2,3,1,0:T(8,128)}, u32[]{:S(2)}) copy-start(s32[1,1,256,32]{2,3,1,0:T(8,128)} %param.7) | copy-start | bytes 98308
  119.0 8.5 %collective-permute-start.2 = (f32[2,16512]{1,0:T(2,128)S(1)}, f32[2,16512]{1,0:T(2,128)S(1)}, u32[]{:S(2)}, u32[]{:S(2)}) collective-permute-start(f32[2,16512]{1,0:T(2,128)S(1)} %get-tuple-element.7), channel_id=1, source_target_pairs={{0,3},{1,0},{2,1},{3,2},{4,7},{5,4},{6,5},{7,6},{8,11},{9,8},{10,9... | collective-permute-start | bytes 396296 | tf_op jit(solution)/shard_map/ppermute | solution.py:139
  121.6 7.8 %collective-permute-start.1 = (f32[2,16512]{1,0:T(2,128)S(1)}, f32[2,16512]{1,0:T(2,128)S(1)}, u32[]{:S(2)}, u32[]{:S(2)}) collective-permute-start(f32[2,16512]{1,0:T(2,128)S(1)} %get-tuple-element.8), channel_id=1, source_target_pairs={{0,2},{1,3},{2,0},{3,1},{4,6},{5,7},{6,4},{7,5},{8,10},{9,11},{10,... | collective-permute-start | bytes 396296 | tf_op jit(solution)/shard_map/ppermute | solution.py:139
  124.8 6.9 %collective-permute-start = (f32[2,16512]{1,0:T(2,128)S(1)}, f32[2,16512]{1,0:T(2,128)S(1)}, u32[]{:S(2)}, u32[]{:S(2)}) collective-permute-start(f32[2,16512]{1,0:T(2,128)S(1)} %get-tuple-element.6), channel_id=1, source_target_pairs={{0,1},{1,2},{2,3},{3,0},{4,5},{5,6},{6,7},{7,4},{8,9},{9,10},{10,1... | collective-permute-start | bytes 396296 | tf_op jit(solution)/shard_map/ppermute | solution.py:139
  176.1 48.6 %copy-start.5 = (f32[2,1,128]{2,1,0:T(1,128)}, f32[2,1,128]{2,1,0:T(1,128)S(1)}, u32[]{:S(2)}) copy-start(f32[2,1,128]{2,1,0:T(1,128)S(1)} %fusion.2) | copy-start | bytes 3076
  176.1 8.9 %collective-permute-start.5 = (bf16[2,128]{1,0:T(2,128)(2,1)S(1)}, bf16[2,128]{1,0:T(2,128)(2,1)S(1)}, u32[]{:S(2)}, u32[]{:S(2)}) collective-permute-start(bf16[2,128]{1,0:T(2,128)(2,1)S(1)} %convert_element_type.28), channel_id=1, source_target_pairs={{0,3},{1,0},{2,1},{3,2},{4,7},{5,4},{6,5},{7,6},{8,11},{9,8},{10,9... | collective-permute-start | bytes 1544 | tf_op jit(solution)/shard_map/ppermute | solution.py:149
  178.7 6.2 %collective-permute-start.4 = (bf16[2,128]{1,0:T(2,128)(2,1)S(1)}, bf16[2,128]{1,0:T(2,128)(2,1)S(1)}, u32[]{:S(2)}, u32[]{:S(2)}) collective-permute-start(bf16[2,128]{1,0:T(2,128)(2,1)S(1)} %convert_element_type.28), channel_id=1, source_target_pairs={{0,2},{1,3},{2,0},{3,1},{4,6},{5,7},{6,4},{7,5},{8,10},{9,11},{10,... | collective-permute-start | bytes 1544 | tf_op jit(solution)/shard_map/ppermute | solution.py:149
  182.2 5.5 %collective-permute-start.3 = (bf16[2,128]{1,0:T(2,128)(2,1)S(1)}, bf16[2,128]{1,0:T(2,128)(2,1)S(1)}, u32[]{:S(2)}, u32[]{:S(2)}) collective-permute-start(bf16[2,128]{1,0:T(2,128)(2,1)S(1)} %convert_element_type.28), channel_id=1, source_target_pairs={{0,1},{1,2},{2,3},{3,0},{4,5},{5,6},{6,7},{7,4},{8,9},{9,10},{10,1... | collective-permute-start | bytes 1544 | tf_op jit(solution)/shard_map/ppermute | solution.py:149
  189.4 25.8 %all-to-all-start.1 = ((bf16[128,2,160]{2,1,0:T(2,128)(2,1)}), bf16[128,2,160]{2,1,0:T(2,128)(2,1)S(1)}, u32[]{:S(2)}, u32[]{:S(2)}) async-start(bf16[128,2,160]{2,1,0:T(2,128)(2,1)} %reshape.169), calls=%async_computation.1 | async-start | bytes 262144 | tf_op jit(solution)/shard_map/all_to_all | solution.py:304

commit v7 on v6

--- a/solution.py
+++ b/solution.py
@@ -129,27 +129,94 @@
     )(value)
 
 
+def rep_peers(n_rep):
+    me = lax.axis_index("rep")
+    return me, [(me + shift) % n_rep for shift in range(1, n_rep)]
+
+
+def scatter_kernel(n_rep, acc_ref, out_ref, recv, send_sem, recv_sem):
+    me, peers = rep_peers(n_rep)
+    ent = lax.axis_index("ent")
+    barrier = pltpu.get_barrier_semaphore()
+    for peer in peers:
+        pl.semaphore_signal(barrier, inc=1, device_id=(ent, peer), device_id_type=MESH_ID)
+    pl.semaphore_wait(barrier, n_rep - 1)
+    copies = []
+    for index, peer in enumerate(peers):
+        copy = pltpu.make_async_remote_copy(
+            src_ref=acc_ref.at[peer], dst_ref=recv.at[index], send_sem=send_sem.at[index],
+            recv_sem=recv_sem.at[index], device_id=(ent, peer), device_id_type=MESH_ID,
+        )
+        copy.start()
+        copies.append(copy)
+    total = acc_ref[me]
+    for index, copy in enumerate(copies):
+        copy.wait_recv()
+        total = total + recv[index]
+    for copy in copies:
+        copy.wait_send()
+    out_ref[...] = total
+
+
 def rep_scatter_sum(acc, n_rep, per_dev):
-    me = lax.axis_index("rep")
-    total = lax.dynamic_slice_in_dim(acc, me * per_dev, per_dev, 0)
-    for shift in range(1, n_rep):
-        dest = (me + shift) % n_rep
-        piece = lax.dynamic_slice_in_dim(acc, dest * per_dev, per_dev, 0)
-        pairs = [(i, (i + shift) % n_rep) for i in range(n_rep)]
-        total = total + lax.ppermute(piece, "rep", pairs)
+    blocks = acc.reshape(n_rep, per_dev, acc.shape[1])
+    total = pl.pallas_call(
+        functools.partial(scatter_kernel, n_rep),
+        out_shape=jax.ShapeDtypeStruct(blocks.shape[1:], acc.dtype),
+        in_specs=[pl.BlockSpec(memory_space=pltpu.VMEM)],
+        out_specs=pl.BlockSpec(memory_space=pltpu.VMEM),
+        scratch_shapes=[
+            pltpu.VMEM((n_rep - 1,) + blocks.shape[1:], acc.dtype),
+            pltpu.SemaphoreType.DMA((n_rep - 1,)),
+            pltpu.SemaphoreType.DMA((n_rep - 1,)),
+        ],
+        compiler_params=pltpu.CompilerParams(collective_id=1, has_side_effects=True),
+    )(blocks)
     width = acc.shape[1]
     return total[:, : width - 128], total[:, width - 128 :]
 
 
+def allgather_kernel(n_rep, val_ref, out_ref, gath, send_sem, recv_sem):
+    me, peers = rep_peers(n_rep)
+    ent = lax.axis_index("ent")
+    barrier = pltpu.get_barrier_semaphore()
+    for peer in peers:
+        pl.semaphore_signal(barrier, inc=1, device_id=(ent, peer), device_id_type=MESH_ID)
+    pl.semaphore_wait(barrier, n_rep - 1)
+    copies = []
+    for index, peer in enumerate(peers):
+        copy = pltpu.make_async_remote_copy(
+            src_ref=val_ref, dst_ref=gath.at[me], send_sem=send_sem.at[index],
+            recv_sem=recv_sem.at[me], device_id=(ent, peer), device_id_type=MESH_ID,
+        )
+        copy.start()
+        copies.append(copy)
+    gath[me] = val_ref[...]
+    for index in range(n_rep - 1):
+        source = peers[index]
+        pltpu.make_async_remote_copy(
+            src_ref=val_ref, dst_ref=gath.at[source], send_sem=send_sem.at[index],
+            recv_sem=recv_sem.at[source], device_id=(ent, source), device_id_type=MESH_ID,
+        ).wait_recv()
+    for copy in copies:
+        copy.wait_send()
+    out_ref[...] = gath[...]
+
+
 def rep_gather(value, n_rep):
-    me = lax.axis_index("rep")
-    got = [value]
-    for shift in range(1, n_rep):
-        pairs = [(i, (i + shift) % n_rep) for i in range(n_rep)]
-        got.append(lax.ppermute(value, "rep", pairs))
-    stacked = jnp.stack(got)
-    order = (me - jnp.arange(n_rep)) % n_rep
-    return jnp.take(stacked, order, axis=0).reshape(-1, value.shape[-1])
+    out = pl.pallas_call(
+        functools.partial(allgather_kernel, n_rep),
+        out_shape=jax.ShapeDtypeStruct((n_rep,) + value.shape, value.dtype),
+        in_specs=[pl.BlockSpec(memory_space=pltpu.VMEM)],
+        out_specs=pl.BlockSpec(memory_space=pltpu.VMEM),
+        scratch_shapes=[
+            pltpu.VMEM((n_rep,) + value.shape, value.dtype),
+            pltpu.SemaphoreType.DMA((n_rep - 1,)),
+            pltpu.SemaphoreType.DMA((n_rep,)),
+        ],
+        compiler_params=pltpu.CompilerParams(collective_id=2, has_side_effects=True),
+    )(value)
+    return out.reshape(-1, value.shape[-1])
 
 
 def gather_kernel(idx_ref, table_t_ref, out_ref):

time: 226 us -> 221 us (0.978)
  Pallas kernels: 84.8 us -> 102 us
  starting transfers between devices: 48.8 us -> 31.6 us
  waiting for transfers between devices: 19.1 us -> 12.2 us
    pallas_call x0 -> x2, Pallas kernels: none -> 17.4 us  [the longest x1 11.5 us: rep_scatter_sum(): pl.pallas_call(functools.partial(scatter_kernel, n_rep), out_shape=jax.Sh...]
    ppermute x6 -> x0, starting transfers between devices: 16.7 us -> none  [the longest x3 8.82 us: rep_gather(): got.append(lax.ppermute(value, 'rep', pairs))]
    ppermute x6 -> x0, waiting for transfers between devices: 6.91 us -> none  [the longest x3 4.17 us: rep_scatter_sum(): total = total + lax.ppermute(piece, 'rep', pairs)]
    unnamed x24 -> x23, local copies, waits for them, and re-layouts: 5.89 us -> 5.47 us
  transfers between devices with their start and end apart: 8 -> 2, of which waited for: 4 -> 1; matrix products, arithmetic and copies ran while one was open for 3% -> 3% of each run, Pallas kernels for 30% -> 30%
where the time goes in v7:
time: 221 us; the launch traced here: 220 us
  Pallas kernels  102 us (46%)
  other arithmetic  58 us (26%)
  starting transfers between devices  31.6 us (14%)
  waiting for transfers between devices  12.2 us (6%)
  local copies, waits for them, and re-layouts  10.8 us (5%)
  matrix products  4.15 us (2%)
    pallas_call x1, Pallas kernels, tree_sum(): pl.pallas_call(functools.partial(doubling_kernel, n_rep, low_bits, rounds...  66.2 us
    another operation x4, other arithmetic, solve_users(): lower = jnp.linalg.cholesky(gram)  23.6 us
    another operation x3, other arithmetic, solve_users(): lax.linalg.triangular_solve(lower, halfway, left_side=True, lower=True, t...  19.8 us
    all_to_all x1, starting transfers between devices, shards(): lax.all_to_all(picked.reshape(n_ent, slot_cap * tile_rows, rank_width), '...  18.6 us
    all_to_all x1, starting transfers between devices, shards(): lax.all_to_all(back_load.reshape(n_ent, slot_cap, -1), 'ent', split_axis=...  13 us
    all_to_all x1, waiting for transfers between devices, shards(): lax.all_to_all(back_load.reshape(n_ent, slot_cap, -1), 'ent', split_axis=...  12.2 us
    pallas_call x1, Pallas kernels, rep_scatter_sum(): pl.pallas_call(functools.partial(scatter_kernel, n_rep), out_shape=jax.Sh...  11.5 us
    pallas_call x1, Pallas kernels, gather_rows(): pl.pallas_call(gather_kernel, out_shape=jax.ShapeDtypeStruct((count, tabl...  9.66 us
  transfers between devices with their start and end apart: 2, of which 1 were waited for; matrix products, arithmetic and copies ran while one was open for 3% of the time, Pallas kernels for 30%

profile of v7, /device:TPU:1, one launch (start us, length us, event | category | flops | bytes accessed | tf_op | source)
XLA Modules:
  0.0 219.7 jit_solution(3743709808553167780)
XLA Ops:
  0.6 0.5 broadcast.147
  1.1 1.3 reduce.15
  3.0 0.9 copy.31
  3.9 1.8 copy.32
  5.7 0.6 broadcast_select_fusion.idx_ref
  6.3 9.7 %shard_map.77 = bf16[8192,128]{1,0:T(8,128)(2,1)} custom-call(s32[16,512]{1,0:T(8,128)} %broadcast_select_fusion.idx_ref, bf16[128,1024]{1,0:T(8,128)(2,1)} %bitcast.56), custom_call_target="tpu_custom_call" | custom-call | flops 2147483648 | bytes 2392064 | tf_op jit(solution)/shard_map/pallas_call | solution.py:233
  16.0 18.6 %all-to-all-start = ((bf16[128,64,128]{2,1,0:T(8,128)(2,1)}), bf16[128,64,128]{2,1,0:T(8,128)(2,1)S(1)}, u32[]{:S(2)}, u32[]{:S(2)}) async-start(bf16[128,64,128]{2,1,0:T(8,128)(2,1)} %bitcast.53), calls=%async_computation | async-start | bytes 4194304 | tf_op jit(solution)/shard_map/all_to_all | solution.py:324
  34.9 0.7 reduce.16
  35.7 0.7 broadcast_in_dim.70.user_ref
  36.4 0.7 reduce.17
  37.9 0.9 fusion.18.x_ref
  38.8 66.2 %shard_map.80 = f32[128,128]{1,0:T(8,128)} custom-call(f32[128,128]{1,0:T(8,128)} %fusion.18.x_ref), custom_call_target="tpu_custom_call" | custom-call | tf_op jit(solution)/shard_map/pallas_call | solution.py:111
  105.0 0.9 convert_add_fusion
  106.4 0.6 add_select_fusion.rw_ref
  107.0 1.3 copy-done.1
  108.3 8.7 %shard_map.78 = (f32[8,128,128]{2,1,0:T(8,128)}, f32[8,128]{1,0:T(8,128)}) custom-call(bf16[8192,128]{1,0:T(8,128)(2,1)} %bitcast.52, f32[8,1024]{1,0:T(8,128)} %copy-done.4, s32[8,1024]{1,0:T(8,128)} %broadcast_in_dim.70.user_ref, f32[8,1024]{1,0:T(8,128)} %add_select_fusion.rw_ref), custom_call_target="tpu_custom_call" | custom-call | flops 2684354560 | bytes 2723840 | tf_op jit(solution)/shard_map/pallas_call | solution.py:278
  117.1 1.4 concatenate.11
  118.4 1.7 pad_maximum_fusion.acc_ref
  120.2 11.5 %shard_map.79 = f32[2,16512]{1,0:T(2,128)} custom-call(f32[4,2,16512]{2,1,0:T(2,128)} %pad_maximum_fusion.acc_ref), custom_call_target="tpu_custom_call" | custom-call | tf_op jit(solution)/shard_map/pallas_call | solution.py:163
  131.7 0.9 slice_bitcast_fusion
  132.9 23.5 %custom-call.9 = f32[2,128,128]{2,1,0:T(8,128)S(1)} custom-call(f32[2,128,128]{2,1,0:T(8,128)S(1)} %fusion.5), custom_call_target="Cholesky" | custom-call | tf_op jit(solution)/shard_map/jit(cholesky)/cholesky | solution.py:21
  156.6 19.7 %custom-call.10 = f32[2,1,128,128]{2,3,1,0:T(8,128)S(1)} custom-call(f32[2,1,128,128]{3,2,1,0:T(8,128)S(1)} %select_bitcast_fusion), custom_call_target="InvertDiagBlocksLowerTriangular" | custom-call | tf_op jit(solution)/shard_map/triangular_solve | solution.py:23
  176.3 0.2 convolution_bitcast_fusion
  176.5 0.3 fusion.2
  176.8 0.5 convert_element_type.28.val_ref
  177.3 5.9 %shard_map.81 = bf16[4,2,128]{2,1,0:T(2,128)(2,1)} custom-call(bf16[2,128]{1,0:T(2,128)(2,1)} %convert_element_type.28.val_ref), custom_call_target="tpu_custom_call" | custom-call | tf_op jit(solution)/shard_map/pallas_call | solution.py:207
  183.2 0.9 convolution_convert_fusion
  184.3 0.7 reshape.117
  185.0 13.0 %all-to-all-start.1 = ((bf16[128,2,160]{2,1,0:T(2,128)(2,1)}), bf16[128,2,160]{2,1,0:T(2,128)(2,1)S(1)}, u32[]{:S(2)}, u32[]{:S(2)}) async-start(bf16[128,2,160]{2,1,0:T(2,128)(2,1)} %reshape.117), calls=%async_computation.1 | async-start | bytes 262144 | tf_op jit(solution)/shard_map/all_to_all | solution.py:371
  198.0 12.2 %all-to-all-done.1 = bf16[128,2,160]{2,1,0:T(2,128)(2,1)S(1)} async-done(((bf16[128,2,160]{2,1,0:T(2,128)(2,1)}), bf16[128,2,160]{2,1,0:T(2,128)(2,1)S(1)}, u32[]{:S(2)}, u32[]{:S(2)}) %all-to-all-start.1) | async-done | bytes 81952 | tf_op jit(solution)/shard_map/all_to_all | solution.py:371
  210.4 7.4 %select_reduce_fusion = f32[256,1024]{1,0:T(8,128)S(1)} fusion(f32[256,32]{1,0:T(8,128)S(1)} %fusion.1, s32[256,32]{1,0:T(8,128)S(1)} %copy.40), kind=kLoop, calls=%fused_computation | loop fusion | flops 24903680 | bytes 1114112 | tf_op jit(solution)/shard_map/reduce_sum | solution.py:382
  217.9 1.8 convolution_multiply_fusion
  (63 shorter events, 3.1 us)
Async XLA Ops:
  16.0 18.6 %copy-start.2 = (s32[1,1,256,32]{2,3,1,0:T(8,128)S(1)}, s32[1,1,256,32]{2,3,1,0:T(8,128)}, u32[]{:S(2)}) copy-start(s32[1,1,256,32]{2,3,1,0:T(8,128)} %param.10) | copy-start | bytes 98308
  16.0 18.8 %copy-start.5 = (s32[1,1,256,1]{2,3,1,0:T(1,128)S(1)}, s32[1,1,256,1]{2,3,1,0:T(1,128)}, u32[]{:S(2)}) copy-start(s32[1,1,256,1]{2,3,1,0:T(1,128)} %param.9) | copy-start | bytes 3076
  16.0 20.4 %copy-start.8 = (s32[1,1,128]{2,1,0:T(1,128)S(1)}, s32[1,1,128]{2,1,0:T(1,128)}, u32[]{:S(2)}) copy-start(s32[1,1,128]{2,1,0:T(1,128)} %param.11) | copy-start | bytes 1540
  16.0 21.9 %copy-start = (bf16[1024,128]{1,0:T(8,128)(2,1)S(1)}, bf16[1024,128]{1,0:T(8,128)(2,1)}, u32[]{:S(2)}) copy-start(bf16[1024,128]{1,0:T(8,128)(2,1)} %param.6) | copy-start | bytes 786436
  16.0 90.0 %copy-start.7 = (s32[1,1,128]{2,1,0:T(1,128)S(1)}, s32[1,1,128]{2,1,0:T(1,128)}, u32[]{:S(2)}) copy-start(s32[1,1,128]{2,1,0:T(1,128)} %param.8) | copy-start | bytes 1540
  16.0 90.2 %copy-start.3 = (s32[1,1,256,32]{2,3,1,0:T(8,128)S(1)}, s32[1,1,256,32]{2,3,1,0:T(8,128)}, u32[]{:S(2)}) copy-start(s32[1,1,256,32]{2,3,1,0:T(8,128)} %param.7) | copy-start | bytes 98308
  16.0 91.0 %all-to-all-start = ((bf16[128,64,128]{2,1,0:T(8,128)(2,1)}), bf16[128,64,128]{2,1,0:T(8,128)(2,1)S(1)}, u32[]{:S(2)}, u32[]{:S(2)}) async-start(bf16[128,64,128]{2,1,0:T(8,128)(2,1)} %bitcast.53), calls=%async_computation | async-start | bytes 4194304 | tf_op jit(solution)/shard_map/all_to_all | solution.py:324
  34.8 72.2 %copy-start.4 = (f32[8,1024]{1,0:T(8,128)}, f32[8,1024]{1,0:T(8,128)S(1)}, u32[]{:S(2)}) copy-start(f32[8,1024]{1,0:T(8,128)S(1)} %mul.19.gw_ref) | copy-start | bytes 98308
  107.0 1.4 copy-start.1
  131.7 44.6 %slice-start = ((f32[2,16512]{1,0:T(2,128)}), f32[2,128]{1,0:T(2,128)S(1)}, s32[]{:S(2)}) async-start(f32[2,16512]{1,0:T(2,128)} %shard_map.79), calls=%async_computation.2 | async-start | bytes 2048 | tf_op jit(solution)/shard_map/slice | solution.py:176
  176.8 42.9 %copy-start.6 = (f32[2,1,128]{2,1,0:T(1,128)}, f32[2,1,128]{2,1,0:T(1,128)S(1)}, u32[]{:S(2)}) copy-start(f32[2,1,128]{2,1,0:T(1,128)S(1)} %fusion.2) | copy-start | bytes 3076
  185.0 25.2 %all-to-all-start.1 = ((bf16[128,2,160]{2,1,0:T(2,128)(2,1)}), bf16[128,2,160]{2,1,0:T(2,128)(2,1)S(1)}, u32[]{:S(2)}, u32[]{:S(2)}) async-start(bf16[128,2,160]{2,1,0:T(2,128)(2,1)} %reshape.117), calls=%async_computation.1 | async-start | bytes 262144 | tf_op jit(solution)/shard_map/all_to_all | solution.py:371

commit v8 on v7

--- a/solution.py
+++ b/solution.py
@@ -17,13 +17,62 @@
 RHS_SCALE = 1.0 / 640.0
 
 
+def cholesky_kernel(gram_ref, rhs_ref, out_ref, a_s, l_s, y_s):
+    batch, n, _ = gram_ref.shape
+    a_s[...] = gram_ref[...]
+    y_s[...] = rhs_ref[...]
+    out_ref[...] = jnp.zeros_like(out_ref)
+    lane_m = lax.broadcasted_iota(jnp.int32, (n, n), 1)
+    sub_m = lax.broadcasted_iota(jnp.int32, (n, n), 0)
+    lane_v = lax.broadcasted_iota(jnp.int32, (1, n), 1)
+    sub_v = lax.broadcasted_iota(jnp.int32, (n, 1), 0)
+
+    def factor(j, carry):
+        for b in range(batch):
+            a = a_s[b]
+            row = jnp.sum(jnp.where(sub_m == j, a, 0.0), axis=0, keepdims=True)
+            col = jnp.sum(jnp.where(lane_m == j, a, 0.0), axis=1, keepdims=True)
+            diag = jnp.sum(jnp.where(lane_v == j, row, 0.0), axis=1, keepdims=True)
+            inv = 1.0 / jnp.sqrt(diag)
+            l_row = jnp.where(lane_v >= j, row, 0.0) * inv
+            l_col = jnp.where(sub_v >= j, col, 0.0) * inv
+            a_s[b] = a - l_col * l_row
+            l_s[b, pl.ds(j, 1), :] = l_row
+            y = y_s[pl.ds(b, 1), :]
+            y_j = jnp.sum(jnp.where(lane_v == j, y, 0.0), axis=1, keepdims=True) * inv
+            y_s[pl.ds(b, 1), :] = jnp.where(lane_v == j, y_j, y - y_j * l_row)
+        return carry
+
+    lax.fori_loop(0, n, factor, 0)
+
+    def back(t, carry):
+        j = n - 1 - t
+        for b in range(batch):
+            l_j = l_s[b, pl.ds(j, 1), :]
+            x = out_ref[pl.ds(b, 1), :]
+            y_j = jnp.sum(jnp.where(lane_v == j, y_s[pl.ds(b, 1), :], 0.0), axis=1, keepdims=True)
+            l_jj = jnp.sum(jnp.where(lane_v == j, l_j, 0.0), axis=1, keepdims=True)
+            known = jnp.sum(jnp.where(lane_v > j, l_j * x, 0.0), axis=1, keepdims=True)
+            out_ref[pl.ds(b, 1), :] = jnp.where(lane_v == j, (y_j - known) / l_jj, x)
+        return carry
+
+    lax.fori_loop(0, n, back, 0)
+
+
 def solve_users(gram, rhs):
-    lower = jnp.linalg.cholesky(gram)
-    halfway = lax.linalg.triangular_solve(lower, rhs[..., None], left_side=True, lower=True)
-    result = lax.linalg.triangular_solve(
-        lower, halfway, left_side=True, lower=True, transpose_a=True
-    )
-    return result[..., 0]
+    gram = (gram + jnp.swapaxes(gram, -1, -2)) / 2
+    batch, n, _ = gram.shape
+    return pl.pallas_call(
+        cholesky_kernel,
+        out_shape=jax.ShapeDtypeStruct((batch, n), jnp.float32),
+        in_specs=[pl.BlockSpec(memory_space=pltpu.VMEM)] * 2,
+        out_specs=pl.BlockSpec(memory_space=pltpu.VMEM),
+        scratch_shapes=[
+            pltpu.VMEM((batch, n, n), jnp.float32),
+            pltpu.VMEM((batch, n, n), jnp.float32),
+            pltpu.VMEM((batch, n), jnp.float32),
+        ],
+    )(gram, rhs)
 
 
 def flip_bits(value, mask, bits):

time: 221 us -> 209 us (0.946)
  other arithmetic: 58 us -> 15.9 us
  Pallas kernels: 102 us -> 132 us
    another operation x7 -> x0, other arithmetic: 43.4 us -> none  [the longest x4 23.6 us: solve_users(): lower = jnp.linalg.cholesky(gram)]
    pallas_call x0 -> x1, Pallas kernels: none -> 30.2 us  [solve_users(): pl.pallas_call(cholesky_kernel, out_shape=jax.ShapeDtypeStruct((batch, n)...]
    unnamed x23 -> x21, local copies, waits for them, and re-layouts: 5.47 us -> 5.46 us
  transfers between devices with their start and end apart: 2 -> 2, of which waited for: 1 -> 1; matrix products, arithmetic and copies ran while one was open for 3% -> 3% of each run, Pallas kernels for 30% -> 32%
where the time goes in v8:
time: 209 us; the launch traced here: 208 us
  Pallas kernels  132 us (63%)
  starting transfers between devices  31.5 us (15%)
  other arithmetic  15.9 us (8%)
  waiting for transfers between devices  12.2 us (6%)
  local copies, waits for them, and re-layouts  12 us (6%)
  matrix products  3.58 us (2%)
    pallas_call x1, Pallas kernels, tree_sum(): pl.pallas_call(functools.partial(doubling_kernel, n_rep, low_bits, rounds...  66.3 us
    pallas_call x1, Pallas kernels, solve_users(): pl.pallas_call(cholesky_kernel, out_shape=jax.ShapeDtypeStruct((batch, n)...  30.2 us
    all_to_all x1, starting transfers between devices, shards(): lax.all_to_all(picked.reshape(n_ent, slot_cap * tile_rows, rank_width), '...  18.6 us
    all_to_all x1, starting transfers between devices, shards(): lax.all_to_all(back_load.reshape(n_ent, slot_cap, -1), 'ent', split_axis=...  12.9 us
    all_to_all x1, waiting for transfers between devices, shards(): lax.all_to_all(back_load.reshape(n_ent, slot_cap, -1), 'ent', split_axis=...  12.2 us
    pallas_call x1, Pallas kernels, rep_scatter_sum(): pl.pallas_call(functools.partial(scatter_kernel, n_rep), out_shape=jax.Sh...  11.5 us
    pallas_call x1, Pallas kernels, gather_rows(): pl.pallas_call(gather_kernel, out_shape=jax.ShapeDtypeStruct((count, tabl...  9.64 us
    pallas_call x1, Pallas kernels, user_grams(): pl.pallas_call(functools.partial(gram_kernel, n_user), out_shape=(jax.Sha...  8.74 us
  transfers between devices with their start and end apart: 2, of which 1 were waited for; matrix products, arithmetic and copies ran while one was open for 3% of the time, Pallas kernels for 32%

profile of v8, /device:TPU:1, one launch (start us, length us, event | category | flops | bytes accessed | tf_op | source)
XLA Modules:
  0.0 208.3 jit_solution(9944883362975445166)
XLA Ops:
  0.6 0.5 broadcast.89
  1.1 1.3 reduce.9
  3.0 0.9 copy.31
  3.9 1.8 copy.32
  5.7 0.6 broadcast_select_fusion.idx_ref
  6.3 9.6 %shard_map.77 = bf16[8192,128]{1,0:T(8,128)(2,1)} custom-call(s32[16,512]{1,0:T(8,128)} %broadcast_select_fusion.idx_ref, bf16[128,1024]{1,0:T(8,128)(2,1)} %bitcast.35), custom_call_target="tpu_custom_call" | custom-call | flops 2147483648 | bytes 2392064 | tf_op jit(solution)/shard_map/pallas_call | solution.py:282
  16.0 18.6 %all-to-all-start = ((bf16[128,64,128]{2,1,0:T(8,128)(2,1)}), bf16[128,64,128]{2,1,0:T(8,128)(2,1)S(1)}, u32[]{:S(2)}, u32[]{:S(2)}) async-start(bf16[128,64,128]{2,1,0:T(8,128)(2,1)} %bitcast.33), calls=%async_computation | async-start | bytes 4194304 | tf_op jit(solution)/shard_map/all_to_all | solution.py:373
  34.8 0.7 reduce.10
  35.7 0.7 broadcast_in_dim.65.user_ref
  36.4 0.7 reduce.11
  37.9 0.9 fusion.15.x_ref
  38.8 66.3 %shard_map.80 = f32[128,128]{1,0:T(8,128)} custom-call(f32[128,128]{1,0:T(8,128)} %fusion.15.x_ref), custom_call_target="tpu_custom_call" | custom-call | tf_op jit(solution)/shard_map/pallas_call | solution.py:160
  105.1 0.9 convert_add_fusion
  106.1 0.1 reshape.96
  106.4 0.6 add_select_fusion.rw_ref
  107.0 1.3 copy-done.1
  108.3 8.7 %shard_map.78 = (f32[8,128,128]{2,1,0:T(8,128)}, f32[8,128]{1,0:T(8,128)}) custom-call(bf16[8192,128]{1,0:T(8,128)(2,1)} %bitcast.32, f32[8,1024]{1,0:T(8,128)} %copy-done.4, s32[8,1024]{1,0:T(8,128)} %broadcast_in_dim.65.user_ref, f32[8,1024]{1,0:T(8,128)} %add_select_fusion.rw_ref), custom_call_target="tpu_custom_call" | custom-call | flops 2684354560 | bytes 2723840 | tf_op jit(solution)/shard_map/pallas_call | solution.py:327
  117.1 1.4 concatenate.11
  118.4 1.7 pad_maximum_fusion.acc_ref
  120.1 11.5 %shard_map.79 = f32[2,16512]{1,0:T(2,128)} custom-call(f32[4,2,16512]{2,1,0:T(2,128)} %pad_maximum_fusion.acc_ref), custom_call_target="tpu_custom_call" | custom-call | tf_op jit(solution)/shard_map/pallas_call | solution.py:212
  131.6 0.9 slice_bitcast_fusion
  132.6 1.2 slice.13.rhs_ref
  134.0 0.7 fusion.2.gram_ref
  134.7 30.2 %shard_map.81 = f32[2,128]{1,0:T(2,128)} custom-call(f32[2,128,128]{2,1,0:T(8,128)} %fusion.2.gram_ref, f32[2,128]{1,0:T(2,128)} %slice.13.rhs_ref), custom_call_target="tpu_custom_call" | custom-call | tf_op jit(solution)/shard_map/pallas_call | solution.py:65
  164.9 1.2 convert_element_type.28.val_ref
  166.1 5.9 %shard_map.82 = bf16[4,2,128]{2,1,0:T(2,128)(2,1)} custom-call(bf16[2,128]{1,0:T(2,128)(2,1)} %convert_element_type.28.val_ref), custom_call_target="tpu_custom_call" | custom-call | tf_op jit(solution)/shard_map/pallas_call | solution.py:256
  172.0 0.9 convolution_convert_fusion
  173.0 0.7 reshape.98
  173.7 12.9 %all-to-all-start.1 = ((bf16[128,2,160]{2,1,0:T(2,128)(2,1)}), bf16[128,2,160]{2,1,0:T(2,128)(2,1)S(1)}, u32[]{:S(2)}, u32[]{:S(2)}) async-start(bf16[128,2,160]{2,1,0:T(2,128)(2,1)} %reshape.98), calls=%async_computation.1 | async-start | bytes 262144 | tf_op jit(solution)/shard_map/all_to_all | solution.py:420
  186.6 12.2 %all-to-all-done.1 = bf16[128,2,160]{2,1,0:T(2,128)(2,1)S(1)} async-done(((bf16[128,2,160]{2,1,0:T(2,128)(2,1)}), bf16[128,2,160]{2,1,0:T(2,128)(2,1)S(1)}, u32[]{:S(2)}, u32[]{:S(2)}) %all-to-all-start.1) | async-done | bytes 81952 | tf_op jit(solution)/shard_map/all_to_all | solution.py:420
  199.1 7.4 %select_reduce_fusion = f32[256,1024]{1,0:T(8,128)S(1)} fusion(f32[256,32]{1,0:T(8,128)S(1)} %fusion.1, s32[256,32]{1,0:T(8,128)S(1)} %copy.40), kind=kLoop, calls=%fused_computation | loop fusion | flops 24903680 | bytes 1114112 | tf_op jit(solution)/shard_map/reduce_sum | solution.py:431
  206.5 1.8 convolution_multiply_fusion
  (52 shorter events, 2.6 us)
Async XLA Ops:
  16.0 18.6 %copy-start.2 = (s32[1,1,256,32]{2,3,1,0:T(8,128)S(1)}, s32[1,1,256,32]{2,3,1,0:T(8,128)}, u32[]{:S(2)}) copy-start(s32[1,1,256,32]{2,3,1,0:T(8,128)} %param.10) | copy-start | bytes 98308
  16.0 18.8 %copy-start.5 = (s32[1,1,256,1]{2,3,1,0:T(1,128)S(1)}, s32[1,1,256,1]{2,3,1,0:T(1,128)}, u32[]{:S(2)}) copy-start(s32[1,1,256,1]{2,3,1,0:T(1,128)} %param.9) | copy-start | bytes 3076
  16.0 20.4 %copy-start.7 = (s32[1,1,128]{2,1,0:T(1,128)S(1)}, s32[1,1,128]{2,1,0:T(1,128)}, u32[]{:S(2)}) copy-start(s32[1,1,128]{2,1,0:T(1,128)} %param.11) | copy-start | bytes 1540
  16.0 21.9 %copy-start = (bf16[1024,128]{1,0:T(8,128)(2,1)S(1)}, bf16[1024,128]{1,0:T(8,128)(2,1)}, u32[]{:S(2)}) copy-start(bf16[1024,128]{1,0:T(8,128)(2,1)} %param.6) | copy-start | bytes 786436
  16.0 90.0 %copy-start.6 = (s32[1,1,128]{2,1,0:T(1,128)S(1)}, s32[1,1,128]{2,1,0:T(1,128)}, u32[]{:S(2)}) copy-start(s32[1,1,128]{2,1,0:T(1,128)} %param.8) | copy-start | bytes 1540
  16.0 90.3 %copy-start.3 = (s32[1,1,256,32]{2,3,1,0:T(8,128)S(1)}, s32[1,1,256,32]{2,3,1,0:T(8,128)}, u32[]{:S(2)}) copy-start(s32[1,1,256,32]{2,3,1,0:T(8,128)} %param.7) | copy-start | bytes 98308
  16.0 91.0 %all-to-all-start = ((bf16[128,64,128]{2,1,0:T(8,128)(2,1)}), bf16[128,64,128]{2,1,0:T(8,128)(2,1)S(1)}, u32[]{:S(2)}, u32[]{:S(2)}) async-start(bf16[128,64,128]{2,1,0:T(8,128)(2,1)} %bitcast.33), calls=%async_computation | async-start | bytes 4194304 | tf_op jit(solution)/shard_map/all_to_all | solution.py:373
  34.8 72.2 %copy-start.4 = (f32[8,1024]{1,0:T(8,128)}, f32[8,1024]{1,0:T(8,128)S(1)}, u32[]{:S(2)}) copy-start(f32[8,1024]{1,0:T(8,128)S(1)} %mul.19.gw_ref) | copy-start | bytes 98308
  107.0 1.3 copy-start.1
  173.7 25.1 %all-to-all-start.1 = ((bf16[128,2,160]{2,1,0:T(2,128)(2,1)}), bf16[128,2,160]{2,1,0:T(2,128)(2,1)S(1)}, u32[]{:S(2)}, u32[]{:S(2)}) async-start(bf16[128,2,160]{2,1,0:T(2,128)(2,1)} %reshape.98), calls=%async_computation.1 | async-start | bytes 262144 | tf_op jit(solution)/shard_map/all_to_all | solution.py:420

commit v9 on v8

--- a/solution.py
+++ b/solution.py
@@ -207,22 +207,22 @@
     out_ref[...] = total
 
 
-def rep_scatter_sum(acc, n_rep, per_dev):
-    blocks = acc.reshape(n_rep, per_dev, acc.shape[1])
+def rep_scatter_sum(blocks, n_rep, per_dev):
     total = pl.pallas_call(
         functools.partial(scatter_kernel, n_rep),
-        out_shape=jax.ShapeDtypeStruct(blocks.shape[1:], acc.dtype),
+        out_shape=jax.ShapeDtypeStruct(blocks.shape[1:], blocks.dtype),
         in_specs=[pl.BlockSpec(memory_space=pltpu.VMEM)],
         out_specs=pl.BlockSpec(memory_space=pltpu.VMEM),
         scratch_shapes=[
-            pltpu.VMEM((n_rep - 1,) + blocks.shape[1:], acc.dtype),
+            pltpu.VMEM((n_rep - 1,) + blocks.shape[1:], blocks.dtype),
             pltpu.SemaphoreType.DMA((n_rep - 1,)),
             pltpu.SemaphoreType.DMA((n_rep - 1,)),
         ],
         compiler_params=pltpu.CompilerParams(collective_id=1, has_side_effects=True),
     )(blocks)
-    width = acc.shape[1]
-    return total[:, : width - 128], total[:, width - 128 :]
+    width = blocks.shape[2]
+    grams = total[: per_dev * width].reshape(per_dev, width, width)
+    return grams, total[per_dev * width :]
 
 
 def allgather_kernel(n_rep, val_ref, out_ref, gath, send_sem, recv_sem):
@@ -296,13 +296,13 @@
     )(idx_lanes, table.T)
 
 
-def gram_kernel(n_user, rows_ref, gw_ref, user_ref, rw_ref, gram_ref, rhs_ref):
+def gram_kernel(n_user, per_dev, rows_ref, gw_ref, user_ref, rw_ref, out_ref):
     step = pl.program_id(0)
+    width = rows_ref.shape[1]
 
     @pl.when(step == 0)
     def _():
-        gram_ref[...] = jnp.zeros_like(gram_ref)
-        rhs_ref[...] = jnp.zeros_like(rhs_ref)
+        out_ref[...] = jnp.zeros_like(out_ref)
 
     rows = rows_ref[...]
     rows_t = rows.astype(jnp.float32).T
@@ -311,25 +311,30 @@
     zero = jnp.zeros((), jnp.bfloat16)
     for user in range(n_user):
         picked = jnp.where(users == user, weights_t, zero)
-        gram_ref[user] += jnp.dot(picked, rows, preferred_element_type=jnp.float32)
+        block, spot = user // per_dev, (user % per_dev) * width
+        out_ref[block, spot : spot + width, :] += jnp.dot(
+            picked, rows, preferred_element_type=jnp.float32
+        )
     slots = lax.broadcasted_iota(jnp.int32, (n_user, users.shape[1]), 0)
     per_user = jnp.where(users == slots, rw_ref[pl.ds(step, 1), :], 0.0)
     high = per_user.astype(jnp.bfloat16)
     low = (per_user - high.astype(jnp.float32)).astype(jnp.bfloat16)
-    rhs_ref[...] += jnp.dot(high, rows, preferred_element_type=jnp.float32) + jnp.dot(
+    rhs = jnp.dot(high, rows, preferred_element_type=jnp.float32) + jnp.dot(
         low, rows, preferred_element_type=jnp.float32
     )
-
-
-def user_grams(rows, gw_lanes, user_lanes, rw_lanes, n_user):
+    base = per_dev * width
+    for block in range(n_user // per_dev):
+        out_ref[block, base : base + per_dev, :] += rhs[block * per_dev : (block + 1) * per_dev]
+
+
+def user_grams(rows, gw_lanes, user_lanes, rw_lanes, n_user, per_dev):
     chunks, chunk = gw_lanes.shape
     width = rows.shape[1]
+    n_block = n_user // per_dev
+    block_rows = per_dev * width + per_dev
     return pl.pallas_call(
-        functools.partial(gram_kernel, n_user),
-        out_shape=(
-            jax.ShapeDtypeStruct((n_user, width, width), jnp.float32),
-            jax.ShapeDtypeStruct((n_user, width), jnp.float32),
-        ),
+        functools.partial(gram_kernel, n_user, per_dev),
+        out_shape=jax.ShapeDtypeStruct((n_block, block_rows, width), jnp.float32),
         grid=(chunks,),
         in_specs=[
             pl.BlockSpec((chunk, width), lambda i: (i, 0)),
@@ -337,17 +342,13 @@
             pl.BlockSpec((chunks, chunk), lambda i: (0, 0)),
             pl.BlockSpec((chunks, chunk), lambda i: (0, 0)),
         ],
-        out_specs=(
-            pl.BlockSpec((n_user, width, width), lambda i: (0, 0, 0)),
-            pl.BlockSpec((n_user, width), lambda i: (0, 0)),
-        ),
+        out_specs=pl.BlockSpec((n_block, block_rows, width), lambda i: (0, 0, 0)),
         cost_estimate=pl.CostEstimate(
             flops=2 * rows.shape[0] * width * width * (n_user + 2),
             transcendentals=0,
             bytes_accessed=rows.size * 2 + 12 * rows.shape[0] + n_user * width * (width + 1) * 4,
         ),
     )(rows, gw_lanes, user_lanes, rw_lanes)
-
 
 def shards(item_factors, tile_items, send_tiles, tile_users, tile_counts, recv_tiles):
     highest = lax.Precision.HIGHEST
@@ -389,20 +390,18 @@
     rows_all = incoming.reshape(tile_slots * tile_rows, rank_width)
     lane_chunk = 1024
     row_owner = jnp.repeat(owners, seg_length)
-    gram_acc, rhs_acc = user_grams(
+    gram_blocks = user_grams(
         rows_all,
         gram_weight.reshape(-1, lane_chunk),
         row_owner.reshape(-1, lane_chunk),
         rhs_weight.reshape(-1, lane_chunk),
         user_block,
-    )
-    gram_acc = gram_acc.reshape(user_block, rank_width * rank_width)
+        U_DEV,
+    )
     identity_mat = jnp.eye(rank_width, dtype=jnp.float32)
     added_term = tree_sum(partial_gram, n_ent * n_rep) + RIDGE * identity_mat
-    own_gram, own_rhs = rep_scatter_sum(
-        jnp.concatenate([gram_acc, rhs_acc], axis=1), n_rep, U_DEV
-    )
-    own_factors = solve_users(own_gram.reshape(-1, rank_width, rank_width) + added_term, own_rhs)
+    own_gram, own_rhs = rep_scatter_sum(gram_blocks, n_rep, U_DEV)
+    own_factors = solve_users(own_gram + added_term, own_rhs)
     solved = rep_gather(own_factors.astype(jnp.bfloat16), n_rep)
     run_factor = lax.dot_general(
         selector.astype(jnp.bfloat16),

time: 209 us -> 206 us (0.986)
    unnamed x21 -> x19, local copies, waits for them, and re-layouts: 5.46 us -> 4.54 us
where the time goes in v9:
time: 206 us
  Pallas kernels  132 us (64%)
  starting transfers between devices  31.5 us (15%)
  other arithmetic  14.3 us (7%)
  waiting for transfers between devices  12.2 us (6%)
  local copies, waits for them, and re-layouts  10.6 us (5%)
  matrix products  3.6 us (2%)
    pallas_call x1, Pallas kernels, tree_sum(): pl.pallas_call(functools.partial(doubling_kernel, n_rep, low_bits, rounds...  66.3 us
    pallas_call x1, Pallas kernels, solve_users(): pl.pallas_call(cholesky_kernel, out_shape=jax.ShapeDtypeStruct((batch, n)...  30.2 us
    all_to_all x1, starting transfers between devices, shards(): lax.all_to_all(picked.reshape(n_ent, slot_cap * tile_rows, rank_width), '...  18.6 us
    all_to_all x1, starting transfers between devices, shards(): lax.all_to_all(back_load.reshape(n_ent, slot_cap, -1), 'ent', split_axis=...  12.9 us
    all_to_all x1, waiting for transfers between devices, shards(): lax.all_to_all(back_load.reshape(n_ent, slot_cap, -1), 'ent', split_axis=...  12.2 us
    pallas_call x1, Pallas kernels, rep_scatter_sum(): pl.pallas_call(functools.partial(scatter_kernel, n_rep), out_shape=jax.Sh...  11.5 us
    pallas_call x1, Pallas kernels, gather_rows(): pl.pallas_call(gather_kernel, out_shape=jax.ShapeDtypeStruct((count, tabl...  9.71 us
    pallas_call x1, Pallas kernels, user_grams(): pl.pallas_call(functools.partial(gram_kernel, n_user, per_dev), out_shape...  8.81 us
  transfers between devices with their start and end apart: 2, of which 1 were waited for; matrix products, arithmetic and copies ran while one was open for 3% of the time, Pallas kernels for 32%

profile of v9, /device:TPU:1, one launch (start us, length us, event | category | flops | bytes accessed | tf_op | source)
XLA Modules:
  0.0 205.6 jit_solution(13158218149717583248)
XLA Ops:
  0.6 0.5 broadcast.89
  1.1 1.3 reduce.9
  3.0 0.9 copy.31
  3.9 1.8 copy.32
  5.7 0.6 broadcast_select_fusion.idx_ref
  6.3 9.7 %shard_map.77 = bf16[8192,128]{1,0:T(8,128)(2,1)} custom-call(s32[16,512]{1,0:T(8,128)} %broadcast_select_fusion.idx_ref, bf16[128,1024]{1,0:T(8,128)(2,1)} %bitcast.30), custom_call_target="tpu_custom_call" | custom-call | flops 2147483648 | bytes 2392064 | tf_op jit(solution)/shard_map/pallas_call | solution.py:282
  16.1 18.6 %all-to-all-start = ((bf16[128,64,128]{2,1,0:T(8,128)(2,1)}), bf16[128,64,128]{2,1,0:T(8,128)(2,1)S(1)}, u32[]{:S(2)}, u32[]{:S(2)}) async-start(bf16[128,64,128]{2,1,0:T(8,128)(2,1)} %bitcast.28), calls=%async_computation | async-start | bytes 4194304 | tf_op jit(solution)/shard_map/all_to_all | solution.py:374
  34.9 0.7 reduce.10
  35.8 0.7 broadcast_in_dim.65.user_ref
  36.5 0.7 reduce.11
  37.5 0.1 and.46
  37.8 0.1 gt.16
  38.0 0.9 fusion.15.x_ref
  38.9 66.3 %shard_map.80 = f32[128,128]{1,0:T(8,128)} custom-call(f32[128,128]{1,0:T(8,128)} %fusion.15.x_ref), custom_call_target="tpu_custom_call" | custom-call | tf_op jit(solution)/shard_map/pallas_call | solution.py:160
  105.2 0.9 convert_add_fusion
  106.2 0.1 reshape.91
  106.5 0.6 add_select_fusion.rw_ref
  107.1 1.3 copy-done.1
  108.5 8.8 %shard_map.78.acc_ref = f32[4,258,128]{2,1,0:T(8,128)} custom-call(bf16[8192,128]{1,0:T(8,128)(2,1)} %bitcast.27, f32[8,1024]{1,0:T(8,128)} %copy-done.4, s32[8,1024]{1,0:T(8,128)} %broadcast_in_dim.65.user_ref, f32[8,1024]{1,0:T(8,128)} %add_select_fusion.rw_ref), custom_call_target="tpu_custom_call" | custom-call | flops 2684354560 | bytes 2723840 | tf_op jit(solution)/shard_map/pallas_call | solution.py:335
  117.3 11.5 %shard_map.79 = f32[258,128]{1,0:T(8,128)} custom-call(f32[4,258,128]{2,1,0:T(8,128)} %shard_map.78.acc_ref), custom_call_target="tpu_custom_call" | custom-call | tf_op jit(solution)/shard_map/pallas_call | solution.py:211
  128.8 0.9 slice.12
  129.7 1.2 slice.13.rhs_ref
  131.2 0.7 fusion.2.gram_ref
  131.9 30.2 %shard_map.81 = f32[2,128]{1,0:T(2,128)} custom-call(f32[2,128,128]{2,1,0:T(8,128)} %fusion.2.gram_ref, f32[2,128]{1,0:T(2,128)} %slice.13.rhs_ref), custom_call_target="tpu_custom_call" | custom-call | tf_op jit(solution)/shard_map/pallas_call | solution.py:65
  162.1 1.2 convert_element_type.28.val_ref
  163.3 5.9 %shard_map.82 = bf16[4,2,128]{2,1,0:T(2,128)(2,1)} custom-call(bf16[2,128]{1,0:T(2,128)(2,1)} %convert_element_type.28.val_ref), custom_call_target="tpu_custom_call" | custom-call | tf_op jit(solution)/shard_map/pallas_call | solution.py:256
  169.2 0.9 convolution_convert_fusion
  170.2 0.7 reshape.93
  170.9 12.9 %all-to-all-start.1 = ((bf16[128,2,160]{2,1,0:T(2,128)(2,1)}), bf16[128,2,160]{2,1,0:T(2,128)(2,1)S(1)}, u32[]{:S(2)}, u32[]{:S(2)}) async-start(bf16[128,2,160]{2,1,0:T(2,128)(2,1)} %reshape.93), calls=%async_computation.1 | async-start | bytes 262144 | tf_op jit(solution)/shard_map/all_to_all | solution.py:419
  183.9 12.2 %all-to-all-done.1 = bf16[128,2,160]{2,1,0:T(2,128)(2,1)S(1)} async-done(((bf16[128,2,160]{2,1,0:T(2,128)(2,1)}), bf16[128,2,160]{2,1,0:T(2,128)(2,1)S(1)}, u32[]{:S(2)}, u32[]{:S(2)}) %all-to-all-start.1) | async-done | bytes 81952 | tf_op jit(solution)/shard_map/all_to_all | solution.py:419
  196.3 7.5 %select_reduce_fusion = f32[256,1024]{1,0:T(8,128)S(1)} fusion(f32[256,32]{1,0:T(8,128)S(1)} %fusion.1, s32[256,32]{1,0:T(8,128)S(1)} %copy.40), kind=kLoop, calls=%fused_computation | loop fusion | flops 24903680 | bytes 1114112 | tf_op jit(solution)/shard_map/reduce_sum | solution.py:430
  203.8 1.8 convolution_multiply_fusion
  (49 shorter events, 2.3 us)
Async XLA Ops:
  16.1 18.6 %copy-start.2 = (s32[1,1,256,32]{2,3,1,0:T(8,128)S(1)}, s32[1,1,256,32]{2,3,1,0:T(8,128)}, u32[]{:S(2)}) copy-start(s32[1,1,256,32]{2,3,1,0:T(8,128)} %param.10) | copy-start | bytes 98308
  16.1 18.8 %copy-start.5 = (s32[1,1,256,1]{2,3,1,0:T(1,128)S(1)}, s32[1,1,256,1]{2,3,1,0:T(1,128)}, u32[]{:S(2)}) copy-start(s32[1,1,256,1]{2,3,1,0:T(1,128)} %param.9) | copy-start | bytes 3076
  16.1 20.4 %copy-start.7 = (s32[1,1,128]{2,1,0:T(1,128)S(1)}, s32[1,1,128]{2,1,0:T(1,128)}, u32[]{:S(2)}) copy-start(s32[1,1,128]{2,1,0:T(1,128)} %param.11) | copy-start | bytes 1540
  16.1 21.9 %copy-start = (bf16[1024,128]{1,0:T(8,128)(2,1)S(1)}, bf16[1024,128]{1,0:T(8,128)(2,1)}, u32[]{:S(2)}) copy-start(bf16[1024,128]{1,0:T(8,128)(2,1)} %param.6) | copy-start | bytes 786436
  16.1 90.1 %copy-start.6 = (s32[1,1,128]{2,1,0:T(1,128)S(1)}, s32[1,1,128]{2,1,0:T(1,128)}, u32[]{:S(2)}) copy-start(s32[1,1,128]{2,1,0:T(1,128)} %param.8) | copy-start | bytes 1540
  16.1 90.3 %copy-start.3 = (s32[1,1,256,32]{2,3,1,0:T(8,128)S(1)}, s32[1,1,256,32]{2,3,1,0:T(8,128)}, u32[]{:S(2)}) copy-start(s32[1,1,256,32]{2,3,1,0:T(8,128)} %param.7) | copy-start | bytes 98308
  16.1 91.0 %all-to-all-start = ((bf16[128,64,128]{2,1,0:T(8,128)(2,1)}), bf16[128,64,128]{2,1,0:T(8,128)(2,1)S(1)}, u32[]{:S(2)}, u32[]{:S(2)}) async-start(bf16[128,64,128]{2,1,0:T(8,128)(2,1)} %bitcast.28), calls=%async_computation | async-start | bytes 4194304 | tf_op jit(solution)/shard_map/all_to_all | solution.py:374
  34.9 72.2 %copy-start.4 = (f32[8,1024]{1,0:T(8,128)}, f32[8,1024]{1,0:T(8,128)S(1)}, u32[]{:S(2)}) copy-start(f32[8,1024]{1,0:T(8,128)S(1)} %mul.19.gw_ref) | copy-start | bytes 98308
  107.1 1.3 copy-start.1
  170.9 25.1 %all-to-all-start.1 = ((bf16[128,2,160]{2,1,0:T(2,128)(2,1)}), bf16[128,2,160]{2,1,0:T(2,128)(2,1)S(1)}, u32[]{:S(2)}, u32[]{:S(2)}) async-start(bf16[128,2,160]{2,1,0:T(2,128)(2,1)} %reshape.93), calls=%async_computation.1 | async-start | bytes 262144 | tf_op jit(solution)/shard_map/all_to_all | solution.py:419

commit v10 on v9

--- a/solution.py
+++ b/solution.py
@@ -22,28 +22,32 @@
     a_s[...] = gram_ref[...]
     y_s[...] = rhs_ref[...]
     out_ref[...] = jnp.zeros_like(out_ref)
-    lane_m = lax.broadcasted_iota(jnp.int32, (n, n), 1)
-    sub_m = lax.broadcasted_iota(jnp.int32, (n, n), 0)
     lane_v = lax.broadcasted_iota(jnp.int32, (1, n), 1)
-    sub_v = lax.broadcasted_iota(jnp.int32, (n, 1), 0)
-
-    def factor(j, carry):
+
+    def factor(top, j, carry):
+        span = n - top
+        lane_m = lax.broadcasted_iota(jnp.int32, (span, n), 1)
+        sub_m = lax.broadcasted_iota(jnp.int32, (span, n), 0) + top
+        sub_v = lax.broadcasted_iota(jnp.int32, (span, 1), 0) + top
         for b in range(batch):
-            a = a_s[b]
+            a = a_s[b, top:, :]
             row = jnp.sum(jnp.where(sub_m == j, a, 0.0), axis=0, keepdims=True)
             col = jnp.sum(jnp.where(lane_m == j, a, 0.0), axis=1, keepdims=True)
             diag = jnp.sum(jnp.where(lane_v == j, row, 0.0), axis=1, keepdims=True)
             inv = 1.0 / jnp.sqrt(diag)
             l_row = jnp.where(lane_v >= j, row, 0.0) * inv
             l_col = jnp.where(sub_v >= j, col, 0.0) * inv
-            a_s[b] = a - l_col * l_row
+            a_s[b, top:, :] = a - l_col * l_row
             l_s[b, pl.ds(j, 1), :] = l_row
             y = y_s[pl.ds(b, 1), :]
             y_j = jnp.sum(jnp.where(lane_v == j, y, 0.0), axis=1, keepdims=True) * inv
             y_s[pl.ds(b, 1), :] = jnp.where(lane_v == j, y_j, y - y_j * l_row)
         return carry
 
-    lax.fori_loop(0, n, factor, 0)
+    quarter = n // 4
+    for part in range(4):
+        top = part * quarter
+        lax.fori_loop(top, top + quarter, functools.partial(factor, top), 0)
 
     def back(t, carry):
         j = n - 1 - t

time: 206 us -> 205 us (level)
  no operation moved by 1% of the time
where the time goes in v10:
time: 205 us; the launch traced here: 204 us
  Pallas kernels  131 us (64%)
  starting transfers between devices  31.5 us (15%)
  other arithmetic  14.3 us (7%)
  waiting for transfers between devices  12.2 us (6%)
  local copies, waits for them, and re-layouts  10.6 us (5%)
  matrix products  3.61 us (2%)
    pallas_call x1, Pallas kernels, tree_sum(): pl.pallas_call(functools.partial(doubling_kernel, n_rep, low_bits, rounds...  66.3 us
    pallas_call x1, Pallas kernels, solve_users(): pl.pallas_call(cholesky_kernel, out_shape=jax.ShapeDtypeStruct((batch, n)...  29 us
    all_to_all x1, starting transfers between devices, shards(): lax.all_to_all(picked.reshape(n_ent, slot_cap * tile_rows, rank_width), '...  18.6 us
    all_to_all x1, starting transfers between devices, shards(): lax.all_to_all(back_load.reshape(n_ent, slot_cap, -1), 'ent', split_axis=...  12.9 us
    all_to_all x1, waiting for transfers between devices, shards(): lax.all_to_all(back_load.reshape(n_ent, slot_cap, -1), 'ent', split_axis=...  12.2 us
    pallas_call x1, Pallas kernels, rep_scatter_sum(): pl.pallas_call(functools.partial(scatter_kernel, n_rep), out_shape=jax.Sh...  11.5 us
    pallas_call x1, Pallas kernels, gather_rows(): pl.pallas_call(gather_kernel, out_shape=jax.ShapeDtypeStruct((count, tabl...  9.71 us
    pallas_call x1, Pallas kernels, user_grams(): pl.pallas_call(functools.partial(gram_kernel, n_user, per_dev), out_shape...  8.81 us
  transfers between devices with their start and end apart: 2, of which 1 were waited for; matrix products, arithmetic and copies ran while one was open for 3% of the time, Pallas kernels for 32%

profile of v10, /device:TPU:1, one launch (start us, length us, event | category | flops | bytes accessed | tf_op | source)
XLA Modules:
  0.0 204.4 jit_solution(7929044271708537281)
XLA Ops:
  0.6 0.5 broadcast.89
  1.1 1.3 reduce.9
  3.0 0.9 copy.31
  3.9 1.8 copy.32
  5.7 0.6 broadcast_select_fusion.idx_ref
  6.3 9.7 %shard_map.77 = bf16[8192,128]{1,0:T(8,128)(2,1)} custom-call(s32[16,512]{1,0:T(8,128)} %broadcast_select_fusion.idx_ref, bf16[128,1024]{1,0:T(8,128)(2,1)} %bitcast.30), custom_call_target="tpu_custom_call" | custom-call | flops 2147483648 | bytes 2392064 | tf_op jit(solution)/shard_map/pallas_call | solution.py:286
  16.1 18.6 %all-to-all-start = ((bf16[128,64,128]{2,1,0:T(8,128)(2,1)}), bf16[128,64,128]{2,1,0:T(8,128)(2,1)S(1)}, u32[]{:S(2)}, u32[]{:S(2)}) async-start(bf16[128,64,128]{2,1,0:T(8,128)(2,1)} %bitcast.28), calls=%async_computation | async-start | bytes 4194304 | tf_op jit(solution)/shard_map/all_to_all | solution.py:378
  34.9 0.7 reduce.10
  35.8 0.7 broadcast_in_dim.65.user_ref
  36.5 0.7 reduce.11
  37.5 0.1 and.46
  37.8 0.1 gt.16
  38.0 0.9 fusion.15.x_ref
  38.9 66.3 %shard_map.80 = f32[128,128]{1,0:T(8,128)} custom-call(f32[128,128]{1,0:T(8,128)} %fusion.15.x_ref), custom_call_target="tpu_custom_call" | custom-call | tf_op jit(solution)/shard_map/pallas_call | solution.py:164
  105.2 0.9 convert_add_fusion
  106.2 0.1 reshape.91
  106.5 0.6 add_select_fusion.rw_ref
  107.1 1.3 copy-done.1
  108.5 8.8 %shard_map.78.acc_ref = f32[4,258,128]{2,1,0:T(8,128)} custom-call(bf16[8192,128]{1,0:T(8,128)(2,1)} %bitcast.27, f32[8,1024]{1,0:T(8,128)} %copy-done.4, s32[8,1024]{1,0:T(8,128)} %broadcast_in_dim.65.user_ref, f32[8,1024]{1,0:T(8,128)} %add_select_fusion.rw_ref), custom_call_target="tpu_custom_call" | custom-call | flops 2684354560 | bytes 2723840 | tf_op jit(solution)/shard_map/pallas_call | solution.py:339
  117.3 11.5 %shard_map.79 = f32[258,128]{1,0:T(8,128)} custom-call(f32[4,258,128]{2,1,0:T(8,128)} %shard_map.78.acc_ref), custom_call_target="tpu_custom_call" | custom-call | tf_op jit(solution)/shard_map/pallas_call | solution.py:215
  128.8 0.9 slice.12
  129.7 1.2 slice.13.rhs_ref
  131.2 0.7 fusion.2.gram_ref
  131.9 29.0 %shard_map.81 = f32[2,128]{1,0:T(2,128)} custom-call(f32[2,128,128]{2,1,0:T(8,128)} %fusion.2.gram_ref, f32[2,128]{1,0:T(2,128)} %slice.13.rhs_ref), custom_call_target="tpu_custom_call" | custom-call | tf_op jit(solution)/shard_map/pallas_call | solution.py:69
  160.9 1.2 convert_element_type.28.val_ref
  162.1 5.9 %shard_map.82 = bf16[4,2,128]{2,1,0:T(2,128)(2,1)} custom-call(bf16[2,128]{1,0:T(2,128)(2,1)} %convert_element_type.28.val_ref), custom_call_target="tpu_custom_call" | custom-call | tf_op jit(solution)/shard_map/pallas_call | solution.py:260
  168.0 0.9 convolution_convert_fusion
  169.0 0.7 reshape.93
  169.7 12.9 %all-to-all-start.1 = ((bf16[128,2,160]{2,1,0:T(2,128)(2,1)}), bf16[128,2,160]{2,1,0:T(2,128)(2,1)S(1)}, u32[]{:S(2)}, u32[]{:S(2)}) async-start(bf16[128,2,160]{2,1,0:T(2,128)(2,1)} %reshape.93), calls=%async_computation.1 | async-start | bytes 262144 | tf_op jit(solution)/shard_map/all_to_all | solution.py:423
  182.7 12.2 %all-to-all-done.1 = bf16[128,2,160]{2,1,0:T(2,128)(2,1)S(1)} async-done(((bf16[128,2,160]{2,1,0:T(2,128)(2,1)}), bf16[128,2,160]{2,1,0:T(2,128)(2,1)S(1)}, u32[]{:S(2)}, u32[]{:S(2)}) %all-to-all-start.1) | async-done | bytes 81952 | tf_op jit(solution)/shard_map/all_to_all | solution.py:423
  195.1 7.5 %select_reduce_fusion = f32[256,1024]{1,0:T(8,128)S(1)} fusion(f32[256,32]{1,0:T(8,128)S(1)} %fusion.1, s32[256,32]{1,0:T(8,128)S(1)} %copy.40), kind=kLoop, calls=%fused_computation | loop fusion | flops 24903680 | bytes 1114112 | tf_op jit(solution)/shard_map/reduce_sum | solution.py:434
  202.6 1.8 convolution_multiply_fusion
  (49 shorter events, 2.3 us)
Async XLA Ops:
  16.1 18.6 %copy-start.2 = (s32[1,1,256,32]{2,3,1,0:T(8,128)S(1)}, s32[1,1,256,32]{2,3,1,0:T(8,128)}, u32[]{:S(2)}) copy-start(s32[1,1,256,32]{2,3,1,0:T(8,128)} %param.10) | copy-start | bytes 98308
  16.1 18.8 %copy-start.5 = (s32[1,1,256,1]{2,3,1,0:T(1,128)S(1)}, s32[1,1,256,1]{2,3,1,0:T(1,128)}, u32[]{:S(2)}) copy-start(s32[1,1,256,1]{2,3,1,0:T(1,128)} %param.9) | copy-start | bytes 3076
  16.1 20.4 %copy-start.7 = (s32[1,1,128]{2,1,0:T(1,128)S(1)}, s32[1,1,128]{2,1,0:T(1,128)}, u32[]{:S(2)}) copy-start(s32[1,1,128]{2,1,0:T(1,128)} %param.11) | copy-start | bytes 1540
  16.1 21.9 %copy-start = (bf16[1024,128]{1,0:T(8,128)(2,1)S(1)}, bf16[1024,128]{1,0:T(8,128)(2,1)}, u32[]{:S(2)}) copy-start(bf16[1024,128]{1,0:T(8,128)(2,1)} %param.6) | copy-start | bytes 786436
  16.1 90.1 %copy-start.6 = (s32[1,1,128]{2,1,0:T(1,128)S(1)}, s32[1,1,128]{2,1,0:T(1,128)}, u32[]{:S(2)}) copy-start(s32[1,1,128]{2,1,0:T(1,128)} %param.8) | copy-start | bytes 1540
  16.1 90.3 %copy-start.3 = (s32[1,1,256,32]{2,3,1,0:T(8,128)S(1)}, s32[1,1,256,32]{2,3,1,0:T(8,128)}, u32[]{:S(2)}) copy-start(s32[1,1,256,32]{2,3,1,0:T(8,128)} %param.7) | copy-start | bytes 98308
  16.1 91.0 %all-to-all-start = ((bf16[128,64,128]{2,1,0:T(8,128)(2,1)}), bf16[128,64,128]{2,1,0:T(8,128)(2,1)S(1)}, u32[]{:S(2)}, u32[]{:S(2)}) async-start(bf16[128,64,128]{2,1,0:T(8,128)(2,1)} %bitcast.28), calls=%async_computation | async-start | bytes 4194304 | tf_op jit(solution)/shard_map/all_to_all | solution.py:378
  34.9 72.2 %copy-start.4 = (f32[8,1024]{1,0:T(8,128)}, f32[8,1024]{1,0:T(8,128)S(1)}, u32[]{:S(2)}) copy-start(f32[8,1024]{1,0:T(8,128)S(1)} %mul.19.gw_ref) | copy-start | bytes 98308
  107.1 1.3 copy-start.1
  169.7 25.1 %all-to-all-start.1 = ((bf16[128,2,160]{2,1,0:T(2,128)(2,1)}), bf16[128,2,160]{2,1,0:T(2,128)(2,1)S(1)}, u32[]{:S(2)}, u32[]{:S(2)}) async-start(bf16[128,2,160]{2,1,0:T(2,128)(2,1)} %reshape.93), calls=%async_computation.1 | async-start | bytes 262144 | tf_op jit(solution)/shard_map/all_to_all | solution.py:423

commit v11 on v10

--- a/solution.py
+++ b/solution.py
@@ -17,10 +17,8 @@
 RHS_SCALE = 1.0 / 640.0
 
 
-def cholesky_kernel(gram_ref, rhs_ref, out_ref, a_s, l_s, y_s):
-    batch, n, _ = gram_ref.shape
-    a_s[...] = gram_ref[...]
-    y_s[...] = rhs_ref[...]
+def cholesky_solve(a_s, l_s, y_s, out_ref):
+    batch, n, _ = a_s.shape
     out_ref[...] = jnp.zeros_like(out_ref)
     lane_v = lax.broadcasted_iota(jnp.int32, (1, n), 1)
 
@@ -61,22 +59,6 @@
         return carry
 
     lax.fori_loop(0, n, back, 0)
-
-
-def solve_users(gram, rhs):
-    gram = (gram + jnp.swapaxes(gram, -1, -2)) / 2
-    batch, n, _ = gram.shape
-    return pl.pallas_call(
-        cholesky_kernel,
-        out_shape=jax.ShapeDtypeStruct((batch, n), jnp.float32),
-        in_specs=[pl.BlockSpec(memory_space=pltpu.VMEM)] * 2,
-        out_specs=pl.BlockSpec(memory_space=pltpu.VMEM),
-        scratch_shapes=[
-            pltpu.VMEM((batch, n, n), jnp.float32),
-            pltpu.VMEM((batch, n, n), jnp.float32),
-            pltpu.VMEM((batch, n), jnp.float32),
-        ],
-    )(gram, rhs)
 
 
 def flip_bits(value, mask, bits):
@@ -187,9 +169,11 @@
     return me, [(me + shift) % n_rep for shift in range(1, n_rep)]
 
 
-def scatter_kernel(n_rep, acc_ref, out_ref, recv, send_sem, recv_sem):
+def owner_kernel(n_rep, blocks_ref, base_ref, out_ref, x_s, recv, a_s, l_s, y_s, fac, gath,
+                 sem_a, sem_b, sem_c, sem_d):
     me, peers = rep_peers(n_rep)
     ent = lax.axis_index("ent")
+    batch, n, _ = a_s.shape
     barrier = pltpu.get_barrier_semaphore()
     for peer in peers:
         pl.semaphore_signal(barrier, inc=1, device_id=(ent, peer), device_id_type=MESH_ID)
@@ -197,79 +181,67 @@
     copies = []
     for index, peer in enumerate(peers):
         copy = pltpu.make_async_remote_copy(
-            src_ref=acc_ref.at[peer], dst_ref=recv.at[index], send_sem=send_sem.at[index],
-            recv_sem=recv_sem.at[index], device_id=(ent, peer), device_id_type=MESH_ID,
+            src_ref=blocks_ref.at[peer], dst_ref=recv.at[index], send_sem=sem_a.at[index],
+            recv_sem=sem_b.at[index], device_id=(ent, peer), device_id_type=MESH_ID,
         )
         copy.start()
         copies.append(copy)
-    total = acc_ref[me]
+    total = blocks_ref[me]
     for index, copy in enumerate(copies):
         copy.wait_recv()
         total = total + recv[index]
     for copy in copies:
         copy.wait_send()
-    out_ref[...] = total
-
-
-def rep_scatter_sum(blocks, n_rep, per_dev):
-    total = pl.pallas_call(
-        functools.partial(scatter_kernel, n_rep),
-        out_shape=jax.ShapeDtypeStruct(blocks.shape[1:], blocks.dtype),
-        in_specs=[pl.BlockSpec(memory_space=pltpu.VMEM)],
-        out_specs=pl.BlockSpec(memory_space=pltpu.VMEM),
+    base = base_ref[...]
+    for b in range(batch):
+        gram = total[b * n : (b + 1) * n] + base
+        a_s[b] = (gram + gram.T) / 2
+    y_s[...] = total[batch * n : batch * n + batch]
+    cholesky_solve(a_s, l_s, y_s, x_s)
+    fac[...] = x_s[...].astype(fac.dtype)
+    gath[me] = fac[...]
+    sends = []
+    for index, peer in enumerate(peers):
+        copy = pltpu.make_async_remote_copy(
+            src_ref=fac, dst_ref=gath.at[me], send_sem=sem_c.at[index],
+            recv_sem=sem_d.at[me], device_id=(ent, peer), device_id_type=MESH_ID,
+        )
+        copy.start()
+        sends.append(copy)
+    for index, source in enumerate(peers):
+        pltpu.make_async_remote_copy(
+            src_ref=fac, dst_ref=gath.at[source], send_sem=sem_c.at[index],
+            recv_sem=sem_d.at[source], device_id=(ent, source), device_id_type=MESH_ID,
+        ).wait_recv()
+    for copy in sends:
+        copy.wait_send()
+    out_ref[...] = gath[...]
+
+
+def solve_owned(blocks, base, n_rep, per_dev):
+    n = blocks.shape[2]
+    return pl.pallas_call(
+        functools.partial(owner_kernel, n_rep),
+        out_shape=(
+            jax.ShapeDtypeStruct((n_rep, per_dev, n), jnp.bfloat16),
+            jax.ShapeDtypeStruct((per_dev, n), jnp.float32),
+        ),
+        in_specs=[pl.BlockSpec(memory_space=pltpu.VMEM)] * 2,
+        out_specs=(pl.BlockSpec(memory_space=pltpu.VMEM), pl.BlockSpec(memory_space=pltpu.VMEM)),
         scratch_shapes=[
-            pltpu.VMEM((n_rep - 1,) + blocks.shape[1:], blocks.dtype),
+            pltpu.VMEM((n_rep - 1,) + blocks.shape[1:], jnp.float32),
+            pltpu.VMEM((per_dev, n, n), jnp.float32),
+            pltpu.VMEM((per_dev, n, n), jnp.float32),
+            pltpu.VMEM((per_dev, n), jnp.float32),
+            pltpu.VMEM((per_dev, n), jnp.bfloat16),
+            pltpu.VMEM((n_rep, per_dev, n), jnp.bfloat16),
             pltpu.SemaphoreType.DMA((n_rep - 1,)),
             pltpu.SemaphoreType.DMA((n_rep - 1,)),
-        ],
-        compiler_params=pltpu.CompilerParams(collective_id=1, has_side_effects=True),
-    )(blocks)
-    width = blocks.shape[2]
-    grams = total[: per_dev * width].reshape(per_dev, width, width)
-    return grams, total[per_dev * width :]
-
-
-def allgather_kernel(n_rep, val_ref, out_ref, gath, send_sem, recv_sem):
-    me, peers = rep_peers(n_rep)
-    ent = lax.axis_index("ent")
-    barrier = pltpu.get_barrier_semaphore()
-    for peer in peers:
-        pl.semaphore_signal(barrier, inc=1, device_id=(ent, peer), device_id_type=MESH_ID)
-    pl.semaphore_wait(barrier, n_rep - 1)
-    copies = []
-    for index, peer in enumerate(peers):
-        copy = pltpu.make_async_remote_copy(
-            src_ref=val_ref, dst_ref=gath.at[me], send_sem=send_sem.at[index],
-            recv_sem=recv_sem.at[me], device_id=(ent, peer), device_id_type=MESH_ID,
-        )
-        copy.start()
-        copies.append(copy)
-    gath[me] = val_ref[...]
-    for index in range(n_rep - 1):
-        source = peers[index]
-        pltpu.make_async_remote_copy(
-            src_ref=val_ref, dst_ref=gath.at[source], send_sem=send_sem.at[index],
-            recv_sem=recv_sem.at[source], device_id=(ent, source), device_id_type=MESH_ID,
-        ).wait_recv()
-    for copy in copies:
-        copy.wait_send()
-    out_ref[...] = gath[...]
-
-
-def rep_gather(value, n_rep):
-    out = pl.pallas_call(
-        functools.partial(allgather_kernel, n_rep),
-        out_shape=jax.ShapeDtypeStruct((n_rep,) + value.shape, value.dtype),
-        in_specs=[pl.BlockSpec(memory_space=pltpu.VMEM)],
-        out_specs=pl.BlockSpec(memory_space=pltpu.VMEM),
-        scratch_shapes=[
-            pltpu.VMEM((n_rep,) + value.shape, value.dtype),
             pltpu.SemaphoreType.DMA((n_rep - 1,)),
             pltpu.SemaphoreType.DMA((n_rep,)),
         ],
-        compiler_params=pltpu.CompilerParams(collective_id=2, has_side_effects=True),
-    )(value)
-    return out.reshape(-1, value.shape[-1])
+        compiler_params=pltpu.CompilerParams(collective_id=1, has_side_effects=True),
+    )(blocks, base)
 
 
 def gather_kernel(idx_ref, table_t_ref, out_ref):
@@ -404,9 +376,8 @@
     )
     identity_mat = jnp.eye(rank_width, dtype=jnp.float32)
     added_term = tree_sum(partial_gram, n_ent * n_rep) + RIDGE * identity_mat
-    own_gram, own_rhs = rep_scatter_sum(gram_blocks, n_rep, U_DEV)
-    own_factors = solve_users(own_gram + added_term, own_rhs)
-    solved = rep_gather(own_factors.astype(jnp.bfloat16), n_rep)
+    solved, own_factors = solve_owned(gram_blocks, added_term, n_rep, U_DEV)
+    solved = solved.reshape(user_block, rank_width)
     run_factor = lax.dot_general(
         selector.astype(jnp.bfloat16),
         solved,

time: 205 us -> 196 us (0.956)
  Pallas kernels: 131 us -> 126 us
    pallas_call x3 -> x1, Pallas kernels: 46.5 us -> 41 us  [solve_owned(): pl.pallas_call(functools.partial(owner_kernel, n_rep), out_shape=(jax.Sha...]
    slice x2 -> x0, local copies, waits for them, and re-layouts: 2.16 us -> none  [the longest x1 1.25 us: rep_scatter_sum(): return (grams, total[per_dev * width:])]
    unnamed x19 -> x22, local copies, waits for them, and re-layouts: 4.54 us -> 5.09 us
  transfers between devices with their start and end apart: 2 -> 2, of which waited for: 1 -> 1; matrix products, arithmetic and copies ran while one was open for 3% -> 3% of each run, Pallas kernels for 32% -> 34%
where the time goes in v11:
time: 196 us; the launch traced here: 195 us
  Pallas kernels  126 us (64%)
  starting transfers between devices  31.2 us (16%)
  other arithmetic  13 us (7%)
  waiting for transfers between devices  12.2 us (6%)
  local copies, waits for them, and re-layouts  8.77 us (4%)
  matrix products  3.6 us (2%)
    pallas_call x1, Pallas kernels, tree_sum(): pl.pallas_call(functools.partial(doubling_kernel, n_rep, low_bits, rounds...  66.3 us
    pallas_call x1, Pallas kernels, solve_owned(): pl.pallas_call(functools.partial(owner_kernel, n_rep), out_shape=(jax.Sha...  41 us
    all_to_all x1, starting transfers between devices, shards(): lax.all_to_all(picked.reshape(n_ent, slot_cap * tile_rows, rank_width), '...  18.6 us
    all_to_all x1, starting transfers between devices, shards(): lax.all_to_all(back_load.reshape(n_ent, slot_cap, -1), 'ent', split_axis=...  12.6 us
    all_to_all x1, waiting for transfers between devices, shards(): lax.all_to_all(back_load.reshape(n_ent, slot_cap, -1), 'ent', split_axis=...  12.2 us
    pallas_call x1, Pallas kernels, gather_rows(): pl.pallas_call(gather_kernel, out_shape=jax.ShapeDtypeStruct((count, tabl...  9.65 us
    pallas_call x1, Pallas kernels, user_grams(): pl.pallas_call(functools.partial(gram_kernel, n_user, per_dev), out_shape...  8.82 us
    reduce_sum x1, other arithmetic, shards(): jnp.sum(jnp.where(hot_runs, run_weight[:, :, None], 0.0), axis=1)  7.42 us
  transfers between devices with their start and end apart: 2, of which 1 were waited for; matrix products, arithmetic and copies ran while one was open for 3% of the time, Pallas kernels for 34%

profile of v11, /device:TPU:1, one launch (start us, length us, event | category | flops | bytes accessed | tf_op | source)
XLA Modules:
  0.0 195.4 jit_solution(9861747236820578682)
XLA Ops:
  0.6 0.5 broadcast.87
  1.1 1.3 reduce.9
  2.7 0.1 broadcast_in_dim.59
  2.8 0.1 broadcast_in_dim.60
  3.0 0.9 copy.26
  3.9 1.8 copy.27
  5.7 0.6 broadcast_select_fusion.idx_ref
  6.3 9.7 %shard_map.77 = bf16[8192,128]{1,0:T(8,128)(2,1)} custom-call(s32[16,512]{1,0:T(8,128)} %broadcast_select_fusion.idx_ref, bf16[128,1024]{1,0:T(8,128)(2,1)} %bitcast.24), custom_call_target="tpu_custom_call" | custom-call | flops 2147483648 | bytes 2392064 | tf_op jit(solution)/shard_map/pallas_call | solution.py:258
  16.0 18.6 %all-to-all-start = ((bf16[128,64,128]{2,1,0:T(8,128)(2,1)}), bf16[128,64,128]{2,1,0:T(8,128)(2,1)S(1)}, u32[]{:S(2)}, u32[]{:S(2)}) async-start(bf16[128,64,128]{2,1,0:T(8,128)(2,1)} %bitcast.23), calls=%async_computation | async-start | bytes 4194304 | tf_op jit(solution)/shard_map/all_to_all | solution.py:350
  34.9 0.7 reduce.10
  35.7 0.7 broadcast_in_dim.64.user_ref
  36.4 0.7 reduce.11
  37.4 0.1 and.45
  37.5 0.1 and.46
  37.6 0.1 copy.31
  37.8 0.1 gt.16
  37.9 0.9 fusion.14.x_ref
  38.8 66.3 %shard_map.79 = f32[128,128]{1,0:T(8,128)} custom-call(f32[128,128]{1,0:T(8,128)} %fusion.14.x_ref), custom_call_target="tpu_custom_call" | custom-call | tf_op jit(solution)/shard_map/pallas_call | solution.py:146
  105.2 0.1 reshape.86
  105.5 0.6 add_select_fusion.rw_ref
  106.1 1.5 convert_add_fusion.base_ref
  107.6 1.3 copy-done.1
  108.9 8.8 %shard_map.78.blocks_ref = f32[4,258,128]{2,1,0:T(8,128)} custom-call(bf16[8192,128]{1,0:T(8,128)(2,1)} %bitcast.22, f32[8,1024]{1,0:T(8,128)} %copy-done.4, s32[8,1024]{1,0:T(8,128)} %broadcast_in_dim.64.user_ref, f32[8,1024]{1,0:T(8,128)} %add_select_fusion.rw_ref), custom_call_target="tpu_custom_call" | custom-call | flops 2684354560 | bytes 2723840 | tf_op jit(solution)/shard_map/pallas_call | solution.py:311
  117.7 41.0 %shard_map.80 = (bf16[4,2,128]{2,1,0:T(2,128)(2,1)}, f32[2,128]{1,0:T(2,128)}) custom-call(f32[4,258,128]{2,1,0:T(8,128)} %shard_map.78.blocks_ref, f32[128,128]{1,0:T(8,128)} %convert_add_fusion.base_ref), custom_call_target="tpu_custom_call" | custom-call | tf_op jit(solution)/shard_map/pallas_call | solution.py:223
  158.8 0.9 convolution_convert_fusion
  159.8 0.7 reshape.88
  160.5 12.6 %all-to-all-start.1 = ((bf16[128,2,160]{2,1,0:T(2,128)(2,1)}), bf16[128,2,160]{2,1,0:T(2,128)(2,1)S(1)}, u32[]{:S(2)}, u32[]{:S(2)}) async-start(bf16[128,2,160]{2,1,0:T(2,128)(2,1)} %reshape.88), calls=%async_computation.1 | async-start | bytes 262144 | tf_op jit(solution)/shard_map/all_to_all | solution.py:394
  173.1 12.2 %all-to-all-done.1 = bf16[128,2,160]{2,1,0:T(2,128)(2,1)S(1)} async-done(((bf16[128,2,160]{2,1,0:T(2,128)(2,1)}), bf16[128,2,160]{2,1,0:T(2,128)(2,1)S(1)}, u32[]{:S(2)}, u32[]{:S(2)}) %all-to-all-start.1) | async-done | bytes 81952 | tf_op jit(solution)/shard_map/all_to_all | solution.py:394
  185.3 0.1 reshape.89
  185.6 7.4 %select_reduce_fusion = f32[256,1024]{1,0:T(8,128)S(1)} fusion(f32[256,32]{1,0:T(8,128)S(1)} %fusion.1, s32[256,32]{1,0:T(8,128)S(1)} %copy.32), kind=kLoop, calls=%fused_computation | loop fusion | flops 24903680 | bytes 1114112 | tf_op jit(solution)/shard_map/reduce_sum | solution.py:405
  193.0 1.8 convolution_multiply_fusion
  194.8 0.6 copy.35
  (42 shorter events, 1.4 us)
Async XLA Ops:
  16.0 18.6 %copy-start.2 = (s32[1,1,256,32]{2,3,1,0:T(8,128)S(1)}, s32[1,1,256,32]{2,3,1,0:T(8,128)}, u32[]{:S(2)}) copy-start(s32[1,1,256,32]{2,3,1,0:T(8,128)} %param.10) | copy-start | bytes 98308
  16.0 18.8 %copy-start.5 = (s32[1,1,256,1]{2,3,1,0:T(1,128)S(1)}, s32[1,1,256,1]{2,3,1,0:T(1,128)}, u32[]{:S(2)}) copy-start(s32[1,1,256,1]{2,3,1,0:T(1,128)} %param.9) | copy-start | bytes 3076
  16.0 20.4 %copy-start.8 = (s32[1,1,128]{2,1,0:T(1,128)S(1)}, s32[1,1,128]{2,1,0:T(1,128)}, u32[]{:S(2)}) copy-start(s32[1,1,128]{2,1,0:T(1,128)} %param.11) | copy-start | bytes 1540
  16.0 21.9 %copy-start = (bf16[1024,128]{1,0:T(8,128)(2,1)S(1)}, bf16[1024,128]{1,0:T(8,128)(2,1)}, u32[]{:S(2)}) copy-start(bf16[1024,128]{1,0:T(8,128)(2,1)} %param.6) | copy-start | bytes 786436
  16.0 89.1 %copy-start.7 = (s32[1,1,128]{2,1,0:T(1,128)S(1)}, s32[1,1,128]{2,1,0:T(1,128)}, u32[]{:S(2)}) copy-start(s32[1,1,128]{2,1,0:T(1,128)} %param.8) | copy-start | bytes 1540
  16.0 89.3 %copy-start.3 = (s32[1,1,256,32]{2,3,1,0:T(8,128)S(1)}, s32[1,1,256,32]{2,3,1,0:T(8,128)}, u32[]{:S(2)}) copy-start(s32[1,1,256,32]{2,3,1,0:T(8,128)} %param.7) | copy-start | bytes 98308
  16.0 91.5 %all-to-all-start = ((bf16[128,64,128]{2,1,0:T(8,128)(2,1)}), bf16[128,64,128]{2,1,0:T(8,128)(2,1)S(1)}, u32[]{:S(2)}, u32[]{:S(2)}) async-start(bf16[128,64,128]{2,1,0:T(8,128)(2,1)} %bitcast.23), calls=%async_computation | async-start | bytes 4194304 | tf_op jit(solution)/shard_map/all_to_all | solution.py:350
  34.9 72.7 %copy-start.4 = (f32[8,1024]{1,0:T(8,128)}, f32[8,1024]{1,0:T(8,128)S(1)}, u32[]{:S(2)}) copy-start(f32[8,1024]{1,0:T(8,128)S(1)} %mul.19.gw_ref) | copy-start | bytes 98308
  107.6 1.3 copy-start.1
  159.7 35.2 %copy-start.6 = (f32[2,128]{1,0:T(2,128)S(1)}, f32[2,128]{1,0:T(2,128)}, u32[]{:S(2)}) copy-start(f32[2,128]{1,0:T(2,128)} %get-tuple-element.8) | copy-start | bytes 3076
  160.5 24.8 %all-to-all-start.1 = ((bf16[128,2,160]{2,1,0:T(2,128)(2,1)}), bf16[128,2,160]{2,1,0:T(2,128)(2,1)S(1)}, u32[]{:S(2)}, u32[]{:S(2)}) async-start(bf16[128,2,160]{2,1,0:T(2,128)(2,1)} %reshape.88), calls=%async_computation.1 | async-start | bytes 262144 | tf_op jit(solution)/shard_map/all_to_all | solution.py:394

commit v12 on v11

--- a/solution.py
+++ b/solution.py
@@ -395,17 +395,26 @@
         back_load.reshape(n_ent, slot_cap, -1), "ent", split_axis=0, concat_axis=0, tiled=True
     ).reshape(tile_slots, -1)
     back_factor = back_load[:, : seg_count * rank_width]
-    back_counts = back_load[:, seg_count * rank_width :].astype(jnp.float32)
-    back_weight = jnp.where(
-        live_send[:, None] & (back_counts > 0), 1.0 + ALPHA * back_counts, jnp.float32(0.0)
-    )
-    item_hot = item_ids[:, :, None] == jnp.arange(item_count, dtype=jnp.int32)[None, None, :]
-    run_weight = back_weight.reshape(tile_slots * seg_count, seg_length)
-    hot_runs = item_hot.reshape(tile_slots * seg_count, seg_length, item_count)
-    spread_mat = jnp.sum(jnp.where(hot_runs, run_weight[:, :, None], 0.0), axis=1)
+    back_counts = back_load[:, seg_count * rank_width :].astype(jnp.int32)
+    back_weight = jnp.where(live_send[:, None] & (back_counts > 0), 1 + 40 * back_counts, 0)
+    run_count = tile_slots * seg_count
+    run_items = item_ids.reshape(run_count, seg_length)
+    run_weight = back_weight.reshape(run_count, seg_length)
+    minor = 32
+    major = item_count // minor
+    hot_major = (run_items[:, :, None] // minor == jnp.arange(major)[None, None, :]).astype(jnp.bfloat16)
+    hot_minor = (run_items[:, :, None] % minor == jnp.arange(minor)[None, None, :]).astype(jnp.bfloat16)
+    weight_top = (run_weight // 16) * 16
+    weight_hi = weight_top.astype(jnp.bfloat16)
+    weight_lo = (run_weight - weight_top).astype(jnp.bfloat16)
+    weighted_minor = jnp.concatenate(
+        [hot_minor * weight_hi[:, :, None], hot_minor * weight_lo[:, :, None]], axis=2
+    )
+    both = jnp.einsum("rla,rlc->rac", hot_major, weighted_minor, preferred_element_type=jnp.float32)
+    spread_mat = (both[:, :, :minor] + both[:, :, minor:]).reshape(run_count, item_count)
     item_rhs = lax.dot_general(
         spread_mat,
-        back_factor.reshape(tile_slots * seg_count, rank_width).astype(jnp.float32),
+        back_factor.reshape(run_count, rank_width).astype(jnp.float32),
         (((0,), (0,)), ((), ())),
         precision=highest,
         preferred_element_type=jnp.float32,

time: 196 us -> 202 us (1.031)
  local copies, waits for them, and re-layouts: 8.77 us -> 12.2 us
    reduce_sum x1 -> x0, other arithmetic: 7.42 us -> none  [shards(): jnp.sum(jnp.where(hot_runs, run_weight[:, :, None], 0.0), axis=1)]
    mul x0 -> x1, other arithmetic: none -> 3.85 us  [shards(): hot_minor * weight_hi[:, :, None]]
    add x0 -> x1, local copies, waits for them, and re-layouts: none -> 3.51 us  [shards(): both[:, :, :minor] + both[:, :, minor:]]
    add x0 -> x1, other arithmetic: none -> 3.09 us  [shards(): both[:, :, :minor] + both[:, :, minor:]]
    unnamed x22 -> x20, local copies, waits for them, and re-layouts: 5.09 us -> 5.1 us
  transfers between devices with their start and end apart: 2 -> 2, of which waited for: 1 -> 1; matrix products, arithmetic and copies ran while one was open for 3% -> 3% of each run, Pallas kernels for 34% -> 33%
where the time goes in v12:
time: 202 us; the launch traced here: 201 us
  Pallas kernels  127 us (63%)
  starting transfers between devices  31 us (15%)
  other arithmetic  12.7 us (6%)
  local copies, waits for them, and re-layouts  12.2 us (6%)
  waiting for transfers between devices  12.2 us (6%)
  matrix products  5.06 us (3%)
    pallas_call x1, Pallas kernels, tree_sum(): pl.pallas_call(functools.partial(doubling_kernel, n_rep, low_bits, rounds...  67.1 us
    pallas_call x1, Pallas kernels, solve_owned(): pl.pallas_call(functools.partial(owner_kernel, n_rep), out_shape=(jax.Sha...  41.3 us
    all_to_all x1, starting transfers between devices, shards(): lax.all_to_all(picked.reshape(n_ent, slot_cap * tile_rows, rank_width), '...  18.6 us
    all_to_all x1, starting transfers between devices, shards(): lax.all_to_all(back_load.reshape(n_ent, slot_cap, -1), 'ent', split_axis=...  12.4 us
    all_to_all x1, waiting for transfers between devices, shards(): lax.all_to_all(back_load.reshape(n_ent, slot_cap, -1), 'ent', split_axis=...  12.2 us
    pallas_call x1, Pallas kernels, gather_rows(): pl.pallas_call(gather_kernel, out_shape=jax.ShapeDtypeStruct((count, tabl...  9.67 us
    pallas_call x1, Pallas kernels, user_grams(): pl.pallas_call(functools.partial(gram_kernel, n_user, per_dev), out_shape...  8.8 us
    unnamed x20, local copies, waits for them, and re-layouts  5.1 us
  transfers between devices with their start and end apart: 2, of which 1 were waited for; matrix products, arithmetic and copies ran while one was open for 3% of the time, Pallas kernels for 33%

profile of v12, /device:TPU:1, one launch (start us, length us, event | category | flops | bytes accessed | tf_op | source)
XLA Modules:
  0.0 200.8 jit_solution(1691339778760323130)
XLA Ops:
  0.6 0.5 broadcast.176
  1.1 1.3 reduce.9
  3.0 0.9 copy.18
  3.9 1.8 copy.19
  5.7 0.6 broadcast_select_fusion.idx_ref
  6.3 9.7 %shard_map.77 = bf16[8192,128]{1,0:T(8,128)(2,1)} custom-call(s32[16,512]{1,0:T(8,128)} %broadcast_select_fusion.idx_ref, bf16[128,1024]{1,0:T(8,128)(2,1)} %bitcast.51), custom_call_target="tpu_custom_call" | custom-call | flops 2147483648 | bytes 2392064 | tf_op jit(solution)/shard_map/pallas_call | solution.py:258
  16.0 18.6 %all-to-all-start = ((bf16[128,64,128]{2,1,0:T(8,128)(2,1)}), bf16[128,64,128]{2,1,0:T(8,128)(2,1)S(1)}, u32[]{:S(2)}, u32[]{:S(2)}) async-start(bf16[128,64,128]{2,1,0:T(8,128)(2,1)} %bitcast.50), calls=%async_computation | async-start | bytes 4194304 | tf_op jit(solution)/shard_map/all_to_all | solution.py:350
  34.6 0.7 reduce.11
  35.3 0.7 reduce.10
  36.5 0.1 gt.11
  36.7 0.1 and.79
  36.9 0.1 reshape.176
  37.1 0.9 fusion.29.x_ref
  38.0 67.1 %shard_map.79 = f32[128,128]{1,0:T(8,128)} custom-call(f32[128,128]{1,0:T(8,128)} %fusion.29.x_ref), custom_call_target="tpu_custom_call" | custom-call | tf_op jit(solution)/shard_map/pallas_call | solution.py:146
  105.4 0.7 broadcast_in_dim.53.user_ref
  106.1 0.6 add_select_fusion.3.rw_ref
  106.7 1.5 convert_add_fusion.base_ref
  108.2 1.3 copy-done.1
  109.6 8.8 %shard_map.78.blocks_ref = f32[4,258,128]{2,1,0:T(8,128)} custom-call(bf16[8192,128]{1,0:T(8,128)(2,1)} %bitcast.49, f32[8,1024]{1,0:T(8,128)} %copy-done.3, s32[8,1024]{1,0:T(8,128)} %broadcast_in_dim.53.user_ref, f32[8,1024]{1,0:T(8,128)} %add_select_fusion.3.rw_ref), custom_call_target="tpu_custom_call" | custom-call | flops 2684354560 | bytes 2723840 | tf_op jit(solution)/shard_map/pallas_call | solution.py:311
  118.4 41.3 %shard_map.80 = (bf16[4,2,128]{2,1,0:T(2,128)(2,1)}, f32[2,128]{1,0:T(2,128)}) custom-call(f32[4,258,128]{2,1,0:T(8,128)} %shard_map.78.blocks_ref, f32[128,128]{1,0:T(8,128)} %convert_add_fusion.base_ref), custom_call_target="tpu_custom_call" | custom-call | tf_op jit(solution)/shard_map/pallas_call | solution.py:223
  159.7 0.9 convolution_convert_fusion
  160.7 0.7 reshape.178
  161.5 12.4 %all-to-all-start.1 = ((bf16[128,2,160]{2,1,0:T(2,128)(2,1)}), bf16[128,2,160]{2,1,0:T(2,128)(2,1)S(1)}, u32[]{:S(2)}, u32[]{:S(2)}) async-start(bf16[128,2,160]{2,1,0:T(2,128)(2,1)} %reshape.178), calls=%async_computation.1 | async-start | bytes 262144 | tf_op jit(solution)/shard_map/all_to_all | solution.py:394
  173.9 12.2 %all-to-all-done.1 = bf16[128,2,160]{2,1,0:T(2,128)(2,1)S(1)} async-done(((bf16[128,2,160]{2,1,0:T(2,128)(2,1)}), bf16[128,2,160]{2,1,0:T(2,128)(2,1)S(1)}, u32[]{:S(2)}, u32[]{:S(2)}) %all-to-all-start.1) | async-done | bytes 81952 | tf_op jit(solution)/shard_map/all_to_all | solution.py:394
  186.1 0.1 reshape.179
  186.2 0.3 add_select_fusion.2
  186.5 3.9 %fusion.1 = (bf16[256,32,32]{2,1,0:T(8,128)(2,1)S(1)}, bf16[256,32,32]{2,1,0:T(8,128)(2,1)S(1)}) fusion(s32[256,32]{1,0:T(8,128)S(1)} %get-tuple-element.9, bf16[256,32]{1,0:T(8,128)(2,1)S(1)} %get-tuple-element.13, bf16[256,32]{1,0:T(8,128)(2,1)S(1)} %get-tuple-element.12), kind=kLoop, calls=%fused_computation.3 | loop fusion | flops 786432 | bytes 1114112 | tf_op jit(solution)/shard_map/mul | solution.py:411
  190.4 1.9 fusion.2
  192.3 3.1 %slice_add_fusion = f32[256,32,32]{2,1,0:T(8,128)} fusion(f32[256,32,64]{2,1,0:T(8,128)S(1)} %fusion.2), kind=kLoop, calls=%fused_computation | loop fusion | flops 262144 | bytes 3145728 | tf_op jit(solution)/shard_map/add | solution.py:414
  195.4 3.5 %copy.26 = f32[256,32,32]{0,2,1:T(8,128)S(1)} copy(f32[256,32,32]{2,1,0:T(8,128)} %slice_add_fusion) | data formatting | bytes 2097152 | tf_op jit(solution)/shard_map/add | solution.py:414
  198.9 1.4 convolution_multiply_fusion
  200.3 0.6 copy.28
  (42 shorter events, 1.7 us)
Async XLA Ops:
  16.0 18.6 %copy-start.7 = (s32[1,1,128]{2,1,0:T(1,128)S(1)}, s32[1,1,128]{2,1,0:T(1,128)}, u32[]{:S(2)}) copy-start(s32[1,1,128]{2,1,0:T(1,128)} %param.11) | copy-start | bytes 1540
  16.0 19.3 %copy-start.4 = (s32[1,1,256,1]{2,3,1,0:T(1,128)S(1)}, s32[1,1,256,1]{2,3,1,0:T(1,128)}, u32[]{:S(2)}) copy-start(s32[1,1,256,1]{2,3,1,0:T(1,128)} %param.9) | copy-start | bytes 3076
  16.0 20.3 %copy-start.2 = (s32[1,1,256,32]{2,3,1,0:T(8,128)S(1)}, s32[1,1,256,32]{2,3,1,0:T(8,128)}, u32[]{:S(2)}) copy-start(s32[1,1,256,32]{2,3,1,0:T(8,128)} %param.10) | copy-start | bytes 98308
  16.0 20.8 %copy-start.6 = (s32[1,1,128]{2,1,0:T(1,128)S(1)}, s32[1,1,128]{2,1,0:T(1,128)}, u32[]{:S(2)}) copy-start(s32[1,1,128]{2,1,0:T(1,128)} %param.8) | copy-start | bytes 1540
  16.0 21.0 %copy-start = (bf16[1024,128]{1,0:T(8,128)(2,1)S(1)}, bf16[1024,128]{1,0:T(8,128)(2,1)}, u32[]{:S(2)}) copy-start(bf16[1024,128]{1,0:T(8,128)(2,1)} %param.6) | copy-start | bytes 786436
  16.0 92.2 %all-to-all-start = ((bf16[128,64,128]{2,1,0:T(8,128)(2,1)}), bf16[128,64,128]{2,1,0:T(8,128)(2,1)S(1)}, u32[]{:S(2)}, u32[]{:S(2)}) async-start(bf16[128,64,128]{2,1,0:T(8,128)(2,1)} %bitcast.50), calls=%async_computation | async-start | bytes 4194304 | tf_op jit(solution)/shard_map/all_to_all | solution.py:350
  105.3 2.9 %copy-start.3 = (f32[8,1024]{1,0:T(8,128)}, f32[8,1024]{1,0:T(8,128)S(1)}, u32[]{:S(2)}) copy-start(f32[8,1024]{1,0:T(8,128)S(1)} %mul.42.gw_ref) | copy-start | bytes 98308
  108.2 1.4 copy-start.1
  161.5 24.7 %all-to-all-start.1 = ((bf16[128,2,160]{2,1,0:T(2,128)(2,1)}), bf16[128,2,160]{2,1,0:T(2,128)(2,1)S(1)}, u32[]{:S(2)}, u32[]{:S(2)}) async-start(bf16[128,2,160]{2,1,0:T(2,128)(2,1)} %reshape.178), calls=%async_computation.1 | async-start | bytes 262144 | tf_op jit(solution)/shard_map/all_to_all | solution.py:394
  195.4 4.9 %copy-start.5 = (f32[2,128]{1,0:T(2,128)S(1)}, f32[2,128]{1,0:T(2,128)}, u32[]{:S(2)}) copy-start(f32[2,128]{1,0:T(2,128)} %get-tuple-element.16) | copy-start | bytes 3076

commit v13 on v11

--- a/solution.py
+++ b/solution.py
@@ -252,7 +252,7 @@
     out_ref[...] = rows_t.T.astype(out_ref.dtype)
 
 
-def gather_rows(table, idx, chunk=512):
+def gather_rows(table, idx, chunk=1024):
     count = idx.shape[0]
     idx_lanes = idx.reshape(count // chunk, chunk)
     return pl.pallas_call(

time: 196 us -> 193 us (0.985)
  Pallas kernels: 126 us -> 123 us
    pallas_call x1, Pallas kernels: 9.65 us -> 6.41 us  [gather_rows(): pl.pallas_call(gather_kernel, out_shape=jax.ShapeDtypeStruct((count, tabl...]
where the time goes in v13:
time: 193 us; the launch traced here: 192 us
  Pallas kernels  123 us (64%)
  starting transfers between devices  31.2 us (16%)
  other arithmetic  13 us (7%)
  waiting for transfers between devices  12.2 us (6%)
  local copies, waits for them, and re-layouts  8.78 us (5%)
  matrix products  3.6 us (2%)
    pallas_call x1, Pallas kernels, tree_sum(): pl.pallas_call(functools.partial(doubling_kernel, n_rep, low_bits, rounds...  66.3 us
    pallas_call x1, Pallas kernels, solve_owned(): pl.pallas_call(functools.partial(owner_kernel, n_rep), out_shape=(jax.Sha...  41 us
    all_to_all x1, starting transfers between devices, shards(): lax.all_to_all(picked.reshape(n_ent, slot_cap * tile_rows, rank_width), '...  18.6 us
    all_to_all x1, starting transfers between devices, shards(): lax.all_to_all(back_load.reshape(n_ent, slot_cap, -1), 'ent', split_axis=...  12.7 us
    all_to_all x1, waiting for transfers between devices, shards(): lax.all_to_all(back_load.reshape(n_ent, slot_cap, -1), 'ent', split_axis=...  12.2 us
    pallas_call x1, Pallas kernels, user_grams(): pl.pallas_call(functools.partial(gram_kernel, n_user, per_dev), out_shape...  8.83 us
    reduce_sum x1, other arithmetic, shards(): jnp.sum(jnp.where(hot_runs, run_weight[:, :, None], 0.0), axis=1)  7.42 us
    pallas_call x1, Pallas kernels, gather_rows(): pl.pallas_call(gather_kernel, out_shape=jax.ShapeDtypeStruct((count, tabl...  6.41 us
  transfers between devices with their start and end apart: 2, of which 1 were waited for; matrix products, arithmetic and copies ran while one was open for 3% of the time, Pallas kernels for 34%

profile of v13, /device:TPU:1, one launch (start us, length us, event | category | flops | bytes accessed | tf_op | source)
XLA Modules:
  0.0 192.2 jit_solution(16844412376435383512)
XLA Ops:
  0.6 0.5 broadcast.87
  1.1 1.3 reduce.9
  2.7 0.1 broadcast_in_dim.59
  2.8 0.1 broadcast_in_dim.60
  3.0 0.9 copy.26
  3.9 1.8 copy.27
  5.7 0.6 broadcast_select_fusion.idx_ref
  6.4 6.4 %shard_map.77 = bf16[8192,128]{1,0:T(8,128)(2,1)} custom-call(s32[8,1024]{1,0:T(8,128)} %broadcast_select_fusion.idx_ref, bf16[128,1024]{1,0:T(8,128)(2,1)} %bitcast.24), custom_call_target="tpu_custom_call" | custom-call | flops 2147483648 | bytes 2392064 | tf_op jit(solution)/shard_map/pallas_call | solution.py:258
  12.8 18.6 %all-to-all-start = ((bf16[128,64,128]{2,1,0:T(8,128)(2,1)}), bf16[128,64,128]{2,1,0:T(8,128)(2,1)S(1)}, u32[]{:S(2)}, u32[]{:S(2)}) async-start(bf16[128,64,128]{2,1,0:T(8,128)(2,1)} %bitcast.23), calls=%async_computation | async-start | bytes 4194304 | tf_op jit(solution)/shard_map/all_to_all | solution.py:350
  31.6 0.7 reduce.10
  32.5 0.7 broadcast_in_dim.64.user_ref
  33.2 0.7 reduce.11
  34.1 0.1 and.44
  34.2 0.1 and.45
  34.4 0.1 copy.31
  34.5 0.1 gt.16
  34.7 0.9 fusion.11.x_ref
  35.6 66.3 %shard_map.79 = f32[128,128]{1,0:T(8,128)} custom-call(f32[128,128]{1,0:T(8,128)} %fusion.11.x_ref), custom_call_target="tpu_custom_call" | custom-call | tf_op jit(solution)/shard_map/pallas_call | solution.py:146
  102.0 0.1 reshape.86
  102.2 0.6 add_select_fusion.rw_ref
  102.8 1.5 convert_add_fusion.base_ref
  104.3 1.3 copy-done.1
  105.7 8.8 %shard_map.78.blocks_ref = f32[4,258,128]{2,1,0:T(8,128)} custom-call(bf16[8192,128]{1,0:T(8,128)(2,1)} %bitcast.22, f32[8,1024]{1,0:T(8,128)} %copy-done.4, s32[8,1024]{1,0:T(8,128)} %broadcast_in_dim.64.user_ref, f32[8,1024]{1,0:T(8,128)} %add_select_fusion.rw_ref), custom_call_target="tpu_custom_call" | custom-call | flops 2684354560 | bytes 2723840 | tf_op jit(solution)/shard_map/pallas_call | solution.py:311
  114.5 41.0 %shard_map.80 = (bf16[4,2,128]{2,1,0:T(2,128)(2,1)}, f32[2,128]{1,0:T(2,128)}) custom-call(f32[4,258,128]{2,1,0:T(8,128)} %shard_map.78.blocks_ref, f32[128,128]{1,0:T(8,128)} %convert_add_fusion.base_ref), custom_call_target="tpu_custom_call" | custom-call | tf_op jit(solution)/shard_map/pallas_call | solution.py:223
  155.5 0.9 convolution_convert_fusion
  156.5 0.7 reshape.88
  157.2 12.7 %all-to-all-start.1 = ((bf16[128,2,160]{2,1,0:T(2,128)(2,1)}), bf16[128,2,160]{2,1,0:T(2,128)(2,1)S(1)}, u32[]{:S(2)}, u32[]{:S(2)}) async-start(bf16[128,2,160]{2,1,0:T(2,128)(2,1)} %reshape.88), calls=%async_computation.1 | async-start | bytes 262144 | tf_op jit(solution)/shard_map/all_to_all | solution.py:394
  169.9 12.2 %all-to-all-done.1 = bf16[128,2,160]{2,1,0:T(2,128)(2,1)S(1)} async-done(((bf16[128,2,160]{2,1,0:T(2,128)(2,1)}), bf16[128,2,160]{2,1,0:T(2,128)(2,1)S(1)}, u32[]{:S(2)}, u32[]{:S(2)}) %all-to-all-start.1) | async-done | bytes 81952 | tf_op jit(solution)/shard_map/all_to_all | solution.py:394
  182.1 0.1 reshape.89
  182.4 7.4 %select_reduce_fusion = f32[256,1024]{1,0:T(8,128)S(1)} fusion(f32[256,32]{1,0:T(8,128)S(1)} %fusion.1, s32[256,32]{1,0:T(8,128)S(1)} %copy.32), kind=kLoop, calls=%fused_computation | loop fusion | flops 24903680 | bytes 1114112 | tf_op jit(solution)/shard_map/reduce_sum | solution.py:405
  189.8 1.8 convolution_multiply_fusion
  191.6 0.6 copy.35
  (42 shorter events, 1.4 us)
Async XLA Ops:
  12.8 18.6 %copy-start.2 = (s32[1,1,256,32]{2,3,1,0:T(8,128)S(1)}, s32[1,1,256,32]{2,3,1,0:T(8,128)}, u32[]{:S(2)}) copy-start(s32[1,1,256,32]{2,3,1,0:T(8,128)} %param.10) | copy-start | bytes 98308
  12.8 18.8 %copy-start.5 = (s32[1,1,256,1]{2,3,1,0:T(1,128)S(1)}, s32[1,1,256,1]{2,3,1,0:T(1,128)}, u32[]{:S(2)}) copy-start(s32[1,1,256,1]{2,3,1,0:T(1,128)} %param.9) | copy-start | bytes 3076
  12.8 20.4 %copy-start.8 = (s32[1,1,128]{2,1,0:T(1,128)S(1)}, s32[1,1,128]{2,1,0:T(1,128)}, u32[]{:S(2)}) copy-start(s32[1,1,128]{2,1,0:T(1,128)} %param.11) | copy-start | bytes 1540
  12.8 21.9 %copy-start = (bf16[1024,128]{1,0:T(8,128)(2,1)S(1)}, bf16[1024,128]{1,0:T(8,128)(2,1)}, u32[]{:S(2)}) copy-start(bf16[1024,128]{1,0:T(8,128)(2,1)} %param.6) | copy-start | bytes 786436
  12.8 89.1 %copy-start.7 = (s32[1,1,128]{2,1,0:T(1,128)S(1)}, s32[1,1,128]{2,1,0:T(1,128)}, u32[]{:S(2)}) copy-start(s32[1,1,128]{2,1,0:T(1,128)} %param.8) | copy-start | bytes 1540
  12.8 89.3 %copy-start.3 = (s32[1,1,256,32]{2,3,1,0:T(8,128)S(1)}, s32[1,1,256,32]{2,3,1,0:T(8,128)}, u32[]{:S(2)}) copy-start(s32[1,1,256,32]{2,3,1,0:T(8,128)} %param.7) | copy-start | bytes 98308
  12.8 91.5 %all-to-all-start = ((bf16[128,64,128]{2,1,0:T(8,128)(2,1)}), bf16[128,64,128]{2,1,0:T(8,128)(2,1)S(1)}, u32[]{:S(2)}, u32[]{:S(2)}) async-start(bf16[128,64,128]{2,1,0:T(8,128)(2,1)} %bitcast.23), calls=%async_computation | async-start | bytes 4194304 | tf_op jit(solution)/shard_map/all_to_all | solution.py:350
  31.6 72.7 %copy-start.4 = (f32[8,1024]{1,0:T(8,128)}, f32[8,1024]{1,0:T(8,128)S(1)}, u32[]{:S(2)}) copy-start(f32[8,1024]{1,0:T(8,128)S(1)} %mul.19.gw_ref) | copy-start | bytes 98308
  104.3 1.3 copy-start.1
  156.4 35.2 %copy-start.6 = (f32[2,128]{1,0:T(2,128)S(1)}, f32[2,128]{1,0:T(2,128)}, u32[]{:S(2)}) copy-start(f32[2,128]{1,0:T(2,128)} %get-tuple-element.8) | copy-start | bytes 3076
  157.2 24.9 %all-to-all-start.1 = ((bf16[128,2,160]{2,1,0:T(2,128)(2,1)}), bf16[128,2,160]{2,1,0:T(2,128)(2,1)S(1)}, u32[]{:S(2)}, u32[]{:S(2)}) async-start(bf16[128,2,160]{2,1,0:T(2,128)(2,1)} %reshape.88), calls=%async_computation.1 | async-start | bytes 262144 | tf_op jit(solution)/shard_map/all_to_all | solution.py:394

commit v14 on v13

--- a/solution.py
+++ b/solution.py
@@ -252,7 +252,7 @@
     out_ref[...] = rows_t.T.astype(out_ref.dtype)
 
 
-def gather_rows(table, idx, chunk=1024):
+def gather_rows(table, idx, chunk=2048):
     count = idx.shape[0]
     idx_lanes = idx.reshape(count // chunk, chunk)
     return pl.pallas_call(
@@ -364,7 +364,7 @@
     selector = owners[None, :] == jnp.arange(user_block, dtype=jnp.int32)[:, None]
     selector_f = selector.astype(jnp.float32)
     rows_all = incoming.reshape(tile_slots * tile_rows, rank_width)
-    lane_chunk = 1024
+    lane_chunk = 2048
     row_owner = jnp.repeat(owners, seg_length)
     gram_blocks = user_grams(
         rows_all,

time: 193 us -> 191 us (0.990)
  Pallas kernels: 123 us -> 120 us
  transfers between devices with their start and end apart: 2 -> 2, of which waited for: 1 -> 1; matrix products, arithmetic and copies ran while one was open for 3% -> 3% of each run, Pallas kernels for 34% -> 35%
where the time goes in v14:
time: 191 us; the launch traced here: 190 us
  Pallas kernels  120 us (63%)
  starting transfers between devices  31.1 us (16%)
  other arithmetic  13 us (7%)
  waiting for transfers between devices  12.2 us (6%)
  local copies, waits for them, and re-layouts  8.87 us (5%)
  matrix products  3.6 us (2%)
    pallas_call x1, Pallas kernels, tree_sum(): pl.pallas_call(functools.partial(doubling_kernel, n_rep, low_bits, rounds...  66.4 us
    pallas_call x1, Pallas kernels, solve_owned(): pl.pallas_call(functools.partial(owner_kernel, n_rep), out_shape=(jax.Sha...  41 us
    all_to_all x1, starting transfers between devices, shards(): lax.all_to_all(picked.reshape(n_ent, slot_cap * tile_rows, rank_width), '...  18.6 us
    all_to_all x1, starting transfers between devices, shards(): lax.all_to_all(back_load.reshape(n_ent, slot_cap, -1), 'ent', split_axis=...  12.5 us
    all_to_all x1, waiting for transfers between devices, shards(): lax.all_to_all(back_load.reshape(n_ent, slot_cap, -1), 'ent', split_axis=...  12.2 us
    pallas_call x1, Pallas kernels, user_grams(): pl.pallas_call(functools.partial(gram_kernel, n_user, per_dev), out_shape...  7.65 us
    reduce_sum x1, other arithmetic, shards(): jnp.sum(jnp.where(hot_runs, run_weight[:, :, None], 0.0), axis=1)  7.42 us
    pallas_call x1, Pallas kernels, gather_rows(): pl.pallas_call(gather_kernel, out_shape=jax.ShapeDtypeStruct((count, tabl...  5.25 us
  transfers between devices with their start and end apart: 2, of which 1 were waited for; matrix products, arithmetic and copies ran while one was open for 3% of the time, Pallas kernels for 35%

profile of v14, /device:TPU:1, one launch (start us, length us, event | category | flops | bytes accessed | tf_op | source)
XLA Modules:
  0.0 189.9 jit_solution(12284308100603529439)
XLA Ops:
  0.6 0.5 broadcast.87
  1.1 1.3 reduce.9
  2.9 0.1 broadcast_in_dim.60
  3.0 0.9 copy.26
  3.9 0.1 reshape_reshape.4
  4.0 1.8 copy.27
  5.8 0.6 broadcast_select_fusion.idx_ref
  6.4 5.2 %shard_map.77 = bf16[8192,128]{1,0:T(8,128)(2,1)} custom-call(s32[4,2048]{1,0:T(4,128)} %broadcast_select_fusion.idx_ref, bf16[128,1024]{1,0:T(8,128)(2,1)} %bitcast.24), custom_call_target="tpu_custom_call" | custom-call | flops 2147483648 | bytes 2392064 | tf_op jit(solution)/shard_map/pallas_call | solution.py:258
  11.7 18.6 %all-to-all-start = ((bf16[128,64,128]{2,1,0:T(8,128)(2,1)}), bf16[128,64,128]{2,1,0:T(8,128)(2,1)S(1)}, u32[]{:S(2)}, u32[]{:S(2)}) async-start(bf16[128,64,128]{2,1,0:T(8,128)(2,1)} %bitcast.23), calls=%async_computation | async-start | bytes 4194304 | tf_op jit(solution)/shard_map/all_to_all | solution.py:350
  30.4 0.1 mul.19.gw_ref
  30.5 0.7 reduce.10
  31.4 0.7 broadcast_in_dim.64.user_ref
  32.1 0.7 reduce.11
  33.2 0.1 and.45
  33.3 0.1 copy.31
  33.5 0.1 gt.16
  33.6 0.9 fusion.11.x_ref
  34.5 66.4 %shard_map.79 = f32[128,128]{1,0:T(8,128)} custom-call(f32[128,128]{1,0:T(8,128)} %fusion.11.x_ref), custom_call_target="tpu_custom_call" | custom-call | tf_op jit(solution)/shard_map/pallas_call | solution.py:146
  101.0 0.1 reshape.86
  101.3 1.5 convert_add_fusion.base_ref
  102.7 0.6 add_select_fusion.1.rw_ref
  103.4 1.3 copy-done.1
  104.7 7.6 %shard_map.78.blocks_ref = f32[4,258,128]{2,1,0:T(8,128)} custom-call(bf16[8192,128]{1,0:T(8,128)(2,1)} %bitcast.22, f32[4,2048]{1,0:T(4,128)} %copy-done.4, s32[4,2048]{1,0:T(4,128)} %broadcast_in_dim.64.user_ref, f32[4,2048]{1,0:T(4,128)} %add_select_fusion.1.rw_ref), custom_call_target="tpu_custom_call" | custom-call | flops 2684354560 | bytes 2723840 | tf_op jit(solution)/shard_map/pallas_call | solution.py:311
  112.3 41.0 %shard_map.80 = (bf16[4,2,128]{2,1,0:T(2,128)(2,1)}, f32[2,128]{1,0:T(2,128)}) custom-call(f32[4,258,128]{2,1,0:T(8,128)} %shard_map.78.blocks_ref, f32[128,128]{1,0:T(8,128)} %convert_add_fusion.base_ref), custom_call_target="tpu_custom_call" | custom-call | tf_op jit(solution)/shard_map/pallas_call | solution.py:223
  153.3 0.9 convolution_convert_fusion
  154.4 0.7 reshape.88
  155.1 12.5 %all-to-all-start.1 = ((bf16[128,2,160]{2,1,0:T(2,128)(2,1)}), bf16[128,2,160]{2,1,0:T(2,128)(2,1)S(1)}, u32[]{:S(2)}, u32[]{:S(2)}) async-start(bf16[128,2,160]{2,1,0:T(2,128)(2,1)} %reshape.88), calls=%async_computation.1 | async-start | bytes 262144 | tf_op jit(solution)/shard_map/all_to_all | solution.py:394
  167.7 12.2 %all-to-all-done.1 = bf16[128,2,160]{2,1,0:T(2,128)(2,1)S(1)} async-done(((bf16[128,2,160]{2,1,0:T(2,128)(2,1)}), bf16[128,2,160]{2,1,0:T(2,128)(2,1)S(1)}, u32[]{:S(2)}, u32[]{:S(2)}) %all-to-all-start.1) | async-done | bytes 81952 | tf_op jit(solution)/shard_map/all_to_all | solution.py:394
  179.9 0.1 reshape.89
  180.1 7.4 %select_reduce_fusion = f32[256,1024]{1,0:T(8,128)S(1)} fusion(f32[256,32]{1,0:T(8,128)S(1)} %fusion.1, s32[256,32]{1,0:T(8,128)S(1)} %copy.32), kind=kLoop, calls=%fused_computation | loop fusion | flops 24903680 | bytes 1114112 | tf_op jit(solution)/shard_map/reduce_sum | solution.py:405
  187.5 1.8 convolution_multiply_fusion
  189.3 0.6 copy.35
  (42 shorter events, 1.5 us)
Async XLA Ops:
  11.7 18.6 %copy-start.2 = (s32[1,1,256,32]{2,3,1,0:T(8,128)S(1)}, s32[1,1,256,32]{2,3,1,0:T(8,128)}, u32[]{:S(2)}) copy-start(s32[1,1,256,32]{2,3,1,0:T(8,128)} %param.10) | copy-start | bytes 98308
  11.7 18.8 %copy-start.5 = (s32[1,1,256,1]{2,3,1,0:T(1,128)S(1)}, s32[1,1,256,1]{2,3,1,0:T(1,128)}, u32[]{:S(2)}) copy-start(s32[1,1,256,1]{2,3,1,0:T(1,128)} %param.9) | copy-start | bytes 3076
  11.7 20.5 %copy-start.8 = (s32[1,1,128]{2,1,0:T(1,128)S(1)}, s32[1,1,128]{2,1,0:T(1,128)}, u32[]{:S(2)}) copy-start(s32[1,1,128]{2,1,0:T(1,128)} %param.11) | copy-start | bytes 1540
  11.7 21.9 %copy-start = (bf16[1024,128]{1,0:T(8,128)(2,1)S(1)}, bf16[1024,128]{1,0:T(8,128)(2,1)}, u32[]{:S(2)}) copy-start(bf16[1024,128]{1,0:T(8,128)(2,1)} %param.6) | copy-start | bytes 786436
  11.7 89.2 %copy-start.7 = (s32[1,1,128]{2,1,0:T(1,128)S(1)}, s32[1,1,128]{2,1,0:T(1,128)}, u32[]{:S(2)}) copy-start(s32[1,1,128]{2,1,0:T(1,128)} %param.8) | copy-start | bytes 1540
  11.7 89.5 %copy-start.3 = (s32[1,1,256,32]{2,3,1,0:T(8,128)S(1)}, s32[1,1,256,32]{2,3,1,0:T(8,128)}, u32[]{:S(2)}) copy-start(s32[1,1,256,32]{2,3,1,0:T(8,128)} %param.7) | copy-start | bytes 98308
  11.7 91.7 %all-to-all-start = ((bf16[128,64,128]{2,1,0:T(8,128)(2,1)}), bf16[128,64,128]{2,1,0:T(8,128)(2,1)S(1)}, u32[]{:S(2)}, u32[]{:S(2)}) async-start(bf16[128,64,128]{2,1,0:T(8,128)(2,1)} %bitcast.23), calls=%async_computation | async-start | bytes 4194304 | tf_op jit(solution)/shard_map/all_to_all | solution.py:350
  30.5 72.9 %copy-start.4 = (f32[4,2048]{1,0:T(4,128)}, f32[4,2048]{1,0:T(4,128)S(1)}, u32[]{:S(2)}) copy-start(f32[4,2048]{1,0:T(4,128)S(1)} %mul.19.gw_ref) | copy-start | bytes 98308
  103.4 1.3 copy-start.1
  154.2 35.1 %copy-start.6 = (f32[2,128]{1,0:T(2,128)S(1)}, f32[2,128]{1,0:T(2,128)}, u32[]{:S(2)}) copy-start(f32[2,128]{1,0:T(2,128)} %get-tuple-element.8) | copy-start | bytes 3076
  155.1 24.8 %all-to-all-start.1 = ((bf16[128,2,160]{2,1,0:T(2,128)(2,1)}), bf16[128,2,160]{2,1,0:T(2,128)(2,1)S(1)}, u32[]{:S(2)}, u32[]{:S(2)}) async-start(bf16[128,2,160]{2,1,0:T(2,128)(2,1)} %reshape.88), calls=%async_computation.1 | async-start | bytes 262144 | tf_op jit(solution)/shard_map/all_to_all | solution.py:394

commit v15 on v14

--- a/solution.py
+++ b/solution.py
@@ -45,7 +45,7 @@
     quarter = n // 4
     for part in range(4):
         top = part * quarter
-        lax.fori_loop(top, top + quarter, functools.partial(factor, top), 0)
+        lax.fori_loop(top, top + quarter, functools.partial(factor, top), 0, unroll=2)
 
     def back(t, carry):
         j = n - 1 - t
@@ -58,7 +58,7 @@
             out_ref[pl.ds(b, 1), :] = jnp.where(lane_v == j, (y_j - known) / l_jj, x)
         return carry
 
-    lax.fori_loop(0, n, back, 0)
+    lax.fori_loop(0, n, back, 0, unroll=2)
 
 
 def flip_bits(value, mask, bits):

time: 191 us -> 190 us (level)
  no operation moved by 1% of the time
where the time goes in v15:
time: 190 us; the launch traced here: 189 us
  Pallas kernels  119 us (63%)
  starting transfers between devices  31.1 us (16%)
  other arithmetic  13 us (7%)
  waiting for transfers between devices  12.2 us (6%)
  local copies, waits for them, and re-layouts  8.87 us (5%)
  matrix products  3.6 us (2%)
    pallas_call x1, Pallas kernels, tree_sum(): pl.pallas_call(functools.partial(doubling_kernel, n_rep, low_bits, rounds...  66.4 us
    pallas_call x1, Pallas kernels, solve_owned(): pl.pallas_call(functools.partial(owner_kernel, n_rep), out_shape=(jax.Sha...  40.1 us
    all_to_all x1, starting transfers between devices, shards(): lax.all_to_all(picked.reshape(n_ent, slot_cap * tile_rows, rank_width), '...  18.6 us
    all_to_all x1, starting transfers between devices, shards(): lax.all_to_all(back_load.reshape(n_ent, slot_cap, -1), 'ent', split_axis=...  12.5 us
    all_to_all x1, waiting for transfers between devices, shards(): lax.all_to_all(back_load.reshape(n_ent, slot_cap, -1), 'ent', split_axis=...  12.2 us
    pallas_call x1, Pallas kernels, user_grams(): pl.pallas_call(functools.partial(gram_kernel, n_user, per_dev), out_shape...  7.65 us
    reduce_sum x1, other arithmetic, shards(): jnp.sum(jnp.where(hot_runs, run_weight[:, :, None], 0.0), axis=1)  7.42 us
    pallas_call x1, Pallas kernels, gather_rows(): pl.pallas_call(gather_kernel, out_shape=jax.ShapeDtypeStruct((count, tabl...  5.25 us
  transfers between devices with their start and end apart: 2, of which 1 were waited for; matrix products, arithmetic and copies ran while one was open for 3% of the time, Pallas kernels for 35%

profile of v15, /device:TPU:1, one launch (start us, length us, event | category | flops | bytes accessed | tf_op | source)
XLA Modules:
  0.0 189.0 jit_solution(7131181900005853497)
XLA Ops:
  0.6 0.5 broadcast.87
  1.1 1.3 reduce.9
  2.9 0.1 broadcast_in_dim.60
  3.0 0.9 copy.26
  3.9 0.1 reshape_reshape.4
  4.0 1.8 copy.27
  5.8 0.6 broadcast_select_fusion.idx_ref
  6.4 5.2 %shard_map.77 = bf16[8192,128]{1,0:T(8,128)(2,1)} custom-call(s32[4,2048]{1,0:T(4,128)} %broadcast_select_fusion.idx_ref, bf16[128,1024]{1,0:T(8,128)(2,1)} %bitcast.24), custom_call_target="tpu_custom_call" | custom-call | flops 2147483648 | bytes 2392064 | tf_op jit(solution)/shard_map/pallas_call | solution.py:258
  11.7 18.6 %all-to-all-start = ((bf16[128,64,128]{2,1,0:T(8,128)(2,1)}), bf16[128,64,128]{2,1,0:T(8,128)(2,1)S(1)}, u32[]{:S(2)}, u32[]{:S(2)}) async-start(bf16[128,64,128]{2,1,0:T(8,128)(2,1)} %bitcast.23), calls=%async_computation | async-start | bytes 4194304 | tf_op jit(solution)/shard_map/all_to_all | solution.py:350
  30.4 0.1 mul.19.gw_ref
  30.5 0.7 reduce.10
  31.4 0.7 broadcast_in_dim.64.user_ref
  32.1 0.7 reduce.11
  33.2 0.1 and.45
  33.3 0.1 copy.31
  33.5 0.1 gt.16
  33.6 0.9 fusion.11.x_ref
  34.5 66.4 %shard_map.79 = f32[128,128]{1,0:T(8,128)} custom-call(f32[128,128]{1,0:T(8,128)} %fusion.11.x_ref), custom_call_target="tpu_custom_call" | custom-call | tf_op jit(solution)/shard_map/pallas_call | solution.py:146
  101.0 0.1 reshape.86
  101.3 1.5 convert_add_fusion.base_ref
  102.7 0.6 add_select_fusion.1.rw_ref
  103.4 1.3 copy-done.1
  104.7 7.6 %shard_map.78.blocks_ref = f32[4,258,128]{2,1,0:T(8,128)} custom-call(bf16[8192,128]{1,0:T(8,128)(2,1)} %bitcast.22, f32[4,2048]{1,0:T(4,128)} %copy-done.4, s32[4,2048]{1,0:T(4,128)} %broadcast_in_dim.64.user_ref, f32[4,2048]{1,0:T(4,128)} %add_select_fusion.1.rw_ref), custom_call_target="tpu_custom_call" | custom-call | flops 2684354560 | bytes 2723840 | tf_op jit(solution)/shard_map/pallas_call | solution.py:311
  112.3 40.1 %shard_map.80 = (bf16[4,2,128]{2,1,0:T(2,128)(2,1)}, f32[2,128]{1,0:T(2,128)}) custom-call(f32[4,258,128]{2,1,0:T(8,128)} %shard_map.78.blocks_ref, f32[128,128]{1,0:T(8,128)} %convert_add_fusion.base_ref), custom_call_target="tpu_custom_call" | custom-call | tf_op jit(solution)/shard_map/pallas_call | solution.py:223
  152.5 0.9 convolution_convert_fusion
  153.5 0.7 reshape.88
  154.2 12.5 %all-to-all-start.1 = ((bf16[128,2,160]{2,1,0:T(2,128)(2,1)}), bf16[128,2,160]{2,1,0:T(2,128)(2,1)S(1)}, u32[]{:S(2)}, u32[]{:S(2)}) async-start(bf16[128,2,160]{2,1,0:T(2,128)(2,1)} %reshape.88), calls=%async_computation.1 | async-start | bytes 262144 | tf_op jit(solution)/shard_map/all_to_all | solution.py:394
  166.8 12.2 %all-to-all-done.1 = bf16[128,2,160]{2,1,0:T(2,128)(2,1)S(1)} async-done(((bf16[128,2,160]{2,1,0:T(2,128)(2,1)}), bf16[128,2,160]{2,1,0:T(2,128)(2,1)S(1)}, u32[]{:S(2)}, u32[]{:S(2)}) %all-to-all-start.1) | async-done | bytes 81952 | tf_op jit(solution)/shard_map/all_to_all | solution.py:394
  179.0 0.1 reshape.89
  179.2 7.4 %select_reduce_fusion = f32[256,1024]{1,0:T(8,128)S(1)} fusion(f32[256,32]{1,0:T(8,128)S(1)} %fusion.1, s32[256,32]{1,0:T(8,128)S(1)} %copy.32), kind=kLoop, calls=%fused_computation | loop fusion | flops 24903680 | bytes 1114112 | tf_op jit(solution)/shard_map/reduce_sum | solution.py:405
  186.7 1.8 convolution_multiply_fusion
  188.5 0.6 copy.35
  (42 shorter events, 1.5 us)
Async XLA Ops:
  11.7 18.6 %copy-start.2 = (s32[1,1,256,32]{2,3,1,0:T(8,128)S(1)}, s32[1,1,256,32]{2,3,1,0:T(8,128)}, u32[]{:S(2)}) copy-start(s32[1,1,256,32]{2,3,1,0:T(8,128)} %param.10) | copy-start | bytes 98308
  11.7 18.8 %copy-start.5 = (s32[1,1,256,1]{2,3,1,0:T(1,128)S(1)}, s32[1,1,256,1]{2,3,1,0:T(1,128)}, u32[]{:S(2)}) copy-start(s32[1,1,256,1]{2,3,1,0:T(1,128)} %param.9) | copy-start | bytes 3076
  11.7 20.5 %copy-start.8 = (s32[1,1,128]{2,1,0:T(1,128)S(1)}, s32[1,1,128]{2,1,0:T(1,128)}, u32[]{:S(2)}) copy-start(s32[1,1,128]{2,1,0:T(1,128)} %param.11) | copy-start | bytes 1540
  11.7 21.9 %copy-start = (bf16[1024,128]{1,0:T(8,128)(2,1)S(1)}, bf16[1024,128]{1,0:T(8,128)(2,1)}, u32[]{:S(2)}) copy-start(bf16[1024,128]{1,0:T(8,128)(2,1)} %param.6) | copy-start | bytes 786436
  11.7 89.2 %copy-start.7 = (s32[1,1,128]{2,1,0:T(1,128)S(1)}, s32[1,1,128]{2,1,0:T(1,128)}, u32[]{:S(2)}) copy-start(s32[1,1,128]{2,1,0:T(1,128)} %param.8) | copy-start | bytes 1540
  11.7 89.5 %copy-start.3 = (s32[1,1,256,32]{2,3,1,0:T(8,128)S(1)}, s32[1,1,256,32]{2,3,1,0:T(8,128)}, u32[]{:S(2)}) copy-start(s32[1,1,256,32]{2,3,1,0:T(8,128)} %param.7) | copy-start | bytes 98308
  11.7 91.7 %all-to-all-start = ((bf16[128,64,128]{2,1,0:T(8,128)(2,1)}), bf16[128,64,128]{2,1,0:T(8,128)(2,1)S(1)}, u32[]{:S(2)}, u32[]{:S(2)}) async-start(bf16[128,64,128]{2,1,0:T(8,128)(2,1)} %bitcast.23), calls=%async_computation | async-start | bytes 4194304 | tf_op jit(solution)/shard_map/all_to_all | solution.py:350
  30.5 72.9 %copy-start.4 = (f32[4,2048]{1,0:T(4,128)}, f32[4,2048]{1,0:T(4,128)S(1)}, u32[]{:S(2)}) copy-start(f32[4,2048]{1,0:T(4,128)S(1)} %mul.19.gw_ref) | copy-start | bytes 98308
  103.4 1.3 copy-start.1
  153.4 35.1 %copy-start.6 = (f32[2,128]{1,0:T(2,128)S(1)}, f32[2,128]{1,0:T(2,128)}, u32[]{:S(2)}) copy-start(f32[2,128]{1,0:T(2,128)} %get-tuple-element.8) | copy-start | bytes 3076
  154.2 24.8 %all-to-all-start.1 = ((bf16[128,2,160]{2,1,0:T(2,128)(2,1)}), bf16[128,2,160]{2,1,0:T(2,128)(2,1)S(1)}, u32[]{:S(2)}, u32[]{:S(2)}) async-start(bf16[128,2,160]{2,1,0:T(2,128)(2,1)} %reshape.88), calls=%async_computation.1 | async-start | bytes 262144 | tf_op jit(solution)/shard_map/all_to_all | solution.py:394

commit v16 on v15

--- a/solution.py
+++ b/solution.py
@@ -45,7 +45,7 @@
     quarter = n // 4
     for part in range(4):
         top = part * quarter
-        lax.fori_loop(top, top + quarter, functools.partial(factor, top), 0, unroll=2)
+        lax.fori_loop(top, top + quarter, functools.partial(factor, top), 0, unroll=4)
 
     def back(t, carry):
         j = n - 1 - t
@@ -58,7 +58,7 @@
             out_ref[pl.ds(b, 1), :] = jnp.where(lane_v == j, (y_j - known) / l_jj, x)
         return carry
 
-    lax.fori_loop(0, n, back, 0, unroll=2)
+    lax.fori_loop(0, n, back, 0, unroll=4)
 
 
 def flip_bits(value, mask, bits):

time: 190 us -> 190 us (level)
  no operation moved by 1% of the time
where the time goes in v16:
time: 190 us
  Pallas kernels  120 us (63%)
  starting transfers between devices  31.1 us (16%)
  other arithmetic  13 us (7%)
  waiting for transfers between devices  12.2 us (6%)
  local copies, waits for them, and re-layouts  8.87 us (5%)
  matrix products  3.6 us (2%)
    pallas_call x1, Pallas kernels, tree_sum(): pl.pallas_call(functools.partial(doubling_kernel, n_rep, low_bits, rounds...  66.4 us
    pallas_call x1, Pallas kernels, solve_owned(): pl.pallas_call(functools.partial(owner_kernel, n_rep), out_shape=(jax.Sha...  40.6 us
    all_to_all x1, starting transfers between devices, shards(): lax.all_to_all(picked.reshape(n_ent, slot_cap * tile_rows, rank_width), '...  18.6 us
    all_to_all x1, starting transfers between devices, shards(): lax.all_to_all(back_load.reshape(n_ent, slot_cap, -1), 'ent', split_axis=...  12.5 us
    all_to_all x1, waiting for transfers between devices, shards(): lax.all_to_all(back_load.reshape(n_ent, slot_cap, -1), 'ent', split_axis=...  12.2 us
    pallas_call x1, Pallas kernels, user_grams(): pl.pallas_call(functools.partial(gram_kernel, n_user, per_dev), out_shape...  7.65 us
    reduce_sum x1, other arithmetic, shards(): jnp.sum(jnp.where(hot_runs, run_weight[:, :, None], 0.0), axis=1)  7.42 us
    pallas_call x1, Pallas kernels, gather_rows(): pl.pallas_call(gather_kernel, out_shape=jax.ShapeDtypeStruct((count, tabl...  5.25 us
  transfers between devices with their start and end apart: 2, of which 1 were waited for; matrix products, arithmetic and copies ran while one was open for 3% of the time, Pallas kernels for 35%

profile of v16, /device:TPU:1, one launch (start us, length us, event | category | flops | bytes accessed | tf_op | source)
XLA Modules:
  0.0 189.5 jit_solution(9435586169599341762)
XLA Ops:
  0.6 0.5 broadcast.87
  1.1 1.3 reduce.9
  2.9 0.1 broadcast_in_dim.60
  3.0 0.9 copy.26
  3.9 0.1 reshape_reshape.4
  4.0 1.8 copy.27
  5.8 0.6 broadcast_select_fusion.idx_ref
  6.4 5.2 %shard_map.77 = bf16[8192,128]{1,0:T(8,128)(2,1)} custom-call(s32[4,2048]{1,0:T(4,128)} %broadcast_select_fusion.idx_ref, bf16[128,1024]{1,0:T(8,128)(2,1)} %bitcast.24), custom_call_target="tpu_custom_call" | custom-call | flops 2147483648 | bytes 2392064 | tf_op jit(solution)/shard_map/pallas_call | solution.py:258
  11.7 18.6 %all-to-all-start = ((bf16[128,64,128]{2,1,0:T(8,128)(2,1)}), bf16[128,64,128]{2,1,0:T(8,128)(2,1)S(1)}, u32[]{:S(2)}, u32[]{:S(2)}) async-start(bf16[128,64,128]{2,1,0:T(8,128)(2,1)} %bitcast.23), calls=%async_computation | async-start | bytes 4194304 | tf_op jit(solution)/shard_map/all_to_all | solution.py:350
  30.4 0.1 mul.19.gw_ref
  30.5 0.7 reduce.10
  31.4 0.7 broadcast_in_dim.64.user_ref
  32.1 0.7 reduce.11
  33.2 0.1 and.45
  33.3 0.1 copy.31
  33.5 0.1 gt.16
  33.6 0.9 fusion.11.x_ref
  34.5 66.4 %shard_map.79 = f32[128,128]{1,0:T(8,128)} custom-call(f32[128,128]{1,0:T(8,128)} %fusion.11.x_ref), custom_call_target="tpu_custom_call" | custom-call | tf_op jit(solution)/shard_map/pallas_call | solution.py:146
  101.0 0.1 reshape.86
  101.3 1.5 convert_add_fusion.base_ref
  102.7 0.6 add_select_fusion.1.rw_ref
  103.4 1.3 copy-done.1
  104.7 7.6 %shard_map.78.blocks_ref = f32[4,258,128]{2,1,0:T(8,128)} custom-call(bf16[8192,128]{1,0:T(8,128)(2,1)} %bitcast.22, f32[4,2048]{1,0:T(4,128)} %copy-done.4, s32[4,2048]{1,0:T(4,128)} %broadcast_in_dim.64.user_ref, f32[4,2048]{1,0:T(4,128)} %add_select_fusion.1.rw_ref), custom_call_target="tpu_custom_call" | custom-call | flops 2684354560 | bytes 2723840 | tf_op jit(solution)/shard_map/pallas_call | solution.py:311
  112.3 40.6 %shard_map.80 = (bf16[4,2,128]{2,1,0:T(2,128)(2,1)}, f32[2,128]{1,0:T(2,128)}) custom-call(f32[4,258,128]{2,1,0:T(8,128)} %shard_map.78.blocks_ref, f32[128,128]{1,0:T(8,128)} %convert_add_fusion.base_ref), custom_call_target="tpu_custom_call" | custom-call | tf_op jit(solution)/shard_map/pallas_call | solution.py:223
  153.0 0.9 convolution_convert_fusion
  154.0 0.7 reshape.88
  154.7 12.5 %all-to-all-start.1 = ((bf16[128,2,160]{2,1,0:T(2,128)(2,1)}), bf16[128,2,160]{2,1,0:T(2,128)(2,1)S(1)}, u32[]{:S(2)}, u32[]{:S(2)}) async-start(bf16[128,2,160]{2,1,0:T(2,128)(2,1)} %reshape.88), calls=%async_computation.1 | async-start | bytes 262144 | tf_op jit(solution)/shard_map/all_to_all | solution.py:394
  167.3 12.2 %all-to-all-done.1 = bf16[128,2,160]{2,1,0:T(2,128)(2,1)S(1)} async-done(((bf16[128,2,160]{2,1,0:T(2,128)(2,1)}), bf16[128,2,160]{2,1,0:T(2,128)(2,1)S(1)}, u32[]{:S(2)}, u32[]{:S(2)}) %all-to-all-start.1) | async-done | bytes 81952 | tf_op jit(solution)/shard_map/all_to_all | solution.py:394
  179.5 0.1 reshape.89
  179.7 7.4 %select_reduce_fusion = f32[256,1024]{1,0:T(8,128)S(1)} fusion(f32[256,32]{1,0:T(8,128)S(1)} %fusion.1, s32[256,32]{1,0:T(8,128)S(1)} %copy.32), kind=kLoop, calls=%fused_computation | loop fusion | flops 24903680 | bytes 1114112 | tf_op jit(solution)/shard_map/reduce_sum | solution.py:405
  187.1 1.8 convolution_multiply_fusion
  189.0 0.6 copy.35
  (42 shorter events, 1.5 us)
Async XLA Ops:
  11.7 18.6 %copy-start.2 = (s32[1,1,256,32]{2,3,1,0:T(8,128)S(1)}, s32[1,1,256,32]{2,3,1,0:T(8,128)}, u32[]{:S(2)}) copy-start(s32[1,1,256,32]{2,3,1,0:T(8,128)} %param.10) | copy-start | bytes 98308
  11.7 18.8 %copy-start.5 = (s32[1,1,256,1]{2,3,1,0:T(1,128)S(1)}, s32[1,1,256,1]{2,3,1,0:T(1,128)}, u32[]{:S(2)}) copy-start(s32[1,1,256,1]{2,3,1,0:T(1,128)} %param.9) | copy-start | bytes 3076
  11.7 20.5 %copy-start.8 = (s32[1,1,128]{2,1,0:T(1,128)S(1)}, s32[1,1,128]{2,1,0:T(1,128)}, u32[]{:S(2)}) copy-start(s32[1,1,128]{2,1,0:T(1,128)} %param.11) | copy-start | bytes 1540
  11.7 21.9 %copy-start = (bf16[1024,128]{1,0:T(8,128)(2,1)S(1)}, bf16[1024,128]{1,0:T(8,128)(2,1)}, u32[]{:S(2)}) copy-start(bf16[1024,128]{1,0:T(8,128)(2,1)} %param.6) | copy-start | bytes 786436
  11.7 89.2 %copy-start.7 = (s32[1,1,128]{2,1,0:T(1,128)S(1)}, s32[1,1,128]{2,1,0:T(1,128)}, u32[]{:S(2)}) copy-start(s32[1,1,128]{2,1,0:T(1,128)} %param.8) | copy-start | bytes 1540
  11.7 89.5 %copy-start.3 = (s32[1,1,256,32]{2,3,1,0:T(8,128)S(1)}, s32[1,1,256,32]{2,3,1,0:T(8,128)}, u32[]{:S(2)}) copy-start(s32[1,1,256,32]{2,3,1,0:T(8,128)} %param.7) | copy-start | bytes 98308
  11.7 91.7 %all-to-all-start = ((bf16[128,64,128]{2,1,0:T(8,128)(2,1)}), bf16[128,64,128]{2,1,0:T(8,128)(2,1)S(1)}, u32[]{:S(2)}, u32[]{:S(2)}) async-start(bf16[128,64,128]{2,1,0:T(8,128)(2,1)} %bitcast.23), calls=%async_computation | async-start | bytes 4194304 | tf_op jit(solution)/shard_map/all_to_all | solution.py:350
  30.5 72.9 %copy-start.4 = (f32[4,2048]{1,0:T(4,128)}, f32[4,2048]{1,0:T(4,128)S(1)}, u32[]{:S(2)}) copy-start(f32[4,2048]{1,0:T(4,128)S(1)} %mul.19.gw_ref) | copy-start | bytes 98308
  103.4 1.3 copy-start.1
  153.9 35.1 %copy-start.6 = (f32[2,128]{1,0:T(2,128)S(1)}, f32[2,128]{1,0:T(2,128)}, u32[]{:S(2)}) copy-start(f32[2,128]{1,0:T(2,128)} %get-tuple-element.8) | copy-start | bytes 3076
  154.7 24.8 %all-to-all-start.1 = ((bf16[128,2,160]{2,1,0:T(2,128)(2,1)}), bf16[128,2,160]{2,1,0:T(2,128)(2,1)S(1)}, u32[]{:S(2)}, u32[]{:S(2)}) async-start(bf16[128,2,160]{2,1,0:T(2,128)(2,1)} %reshape.88), calls=%async_computation.1 | async-start | bytes 262144 | tf_op jit(solution)/shard_map/all_to_all | solution.py:394

commit v17 on v15

--- a/solution.py
+++ b/solution.py
@@ -384,21 +384,23 @@
         (((0,), (0,)), ((), ())),
         preferred_element_type=jnp.float32,
     ).astype(jnp.bfloat16)
-    back_load = jnp.concatenate(
-        [
-            run_factor.reshape(tile_slots, seg_count * rank_width),
-            counts_int.astype(jnp.bfloat16),
-        ],
-        axis=1,
-    )
-    back_load = lax.all_to_all(
-        back_load.reshape(n_ent, slot_cap, -1), "ent", split_axis=0, concat_axis=0, tiled=True
-    ).reshape(tile_slots, -1)
-    back_factor = back_load[:, : seg_count * rank_width]
-    back_counts = back_load[:, seg_count * rank_width :].astype(jnp.float32)
+    back_counts = lax.all_to_all(
+        counts_int.astype(jnp.bfloat16).reshape(n_ent, slot_cap, tile_rows),
+        "ent",
+        split_axis=0,
+        concat_axis=0,
+        tiled=True,
+    ).reshape(tile_slots, tile_rows).astype(jnp.float32)
     back_weight = jnp.where(
         live_send[:, None] & (back_counts > 0), 1.0 + ALPHA * back_counts, jnp.float32(0.0)
     )
+    back_factor = lax.all_to_all(
+        run_factor.reshape(n_ent, slot_cap, seg_count * rank_width),
+        "ent",
+        split_axis=0,
+        concat_axis=0,
+        tiled=True,
+    ).reshape(tile_slots, seg_count * rank_width)
     item_hot = item_ids[:, :, None] == jnp.arange(item_count, dtype=jnp.int32)[None, None, :]
     run_weight = back_weight.reshape(tile_slots * seg_count, seg_length)
     hot_runs = item_hot.reshape(tile_slots * seg_count, seg_length, item_count)

time: 190 us -> 197 us (1.037)
  starting transfers between devices: 31.1 us -> 44.3 us
  waiting for transfers between devices: 12.2 us -> 4.57 us
    all_to_all x1 -> x2, starting transfers between devices: 12.5 us -> 30.9 us  [the longest x1 18.4 us: shards(): lax.all_to_all(counts_int.astype(jnp.bfloat16).reshape(n_ent, slot_cap, t...]
    all_to_all x1 -> x2, waiting for transfers between devices: 12.2 us -> 4.56 us  [the longest x1 4.07 us: shards(): lax.all_to_all(run_factor.reshape(n_ent, slot_cap, seg_count * rank_width...]
    all_to_all x1, starting transfers between devices: 18.6 us -> 13.4 us  [shards(): lax.all_to_all(picked.reshape(n_ent, slot_cap * tile_rows, rank_width), '...]
  transfers between devices with their start and end apart: 2 -> 3, of which waited for: 1 -> 2; matrix products, arithmetic and copies ran while one was open for 3% -> 10% of each run, Pallas kernels for 35% -> 37%
where the time goes in v17:
time: 197 us; the launch traced here: 196 us
  Pallas kernels  119 us (60%)
  starting transfers between devices  44.3 us (22%)
  other arithmetic  13.8 us (7%)
  local copies, waits for them, and re-layouts  8.7 us (4%)
  waiting for transfers between devices  4.57 us (2%)
  matrix products  4.25 us (2%)
    pallas_call x1, Pallas kernels, tree_sum(): pl.pallas_call(functools.partial(doubling_kernel, n_rep, low_bits, rounds...  66.4 us
    pallas_call x1, Pallas kernels, solve_owned(): pl.pallas_call(functools.partial(owner_kernel, n_rep), out_shape=(jax.Sha...  40.1 us
    all_to_all x1, starting transfers between devices, shards(): lax.all_to_all(counts_int.astype(jnp.bfloat16).reshape(n_ent, slot_cap, t...  18.4 us
    all_to_all x1, starting transfers between devices, shards(): lax.all_to_all(picked.reshape(n_ent, slot_cap * tile_rows, rank_width), '...  13.4 us
    all_to_all x1, starting transfers between devices, shards(): lax.all_to_all(run_factor.reshape(n_ent, slot_cap, seg_count * rank_width...  12.5 us
    pallas_call x1, Pallas kernels, user_grams(): pl.pallas_call(functools.partial(gram_kernel, n_user, per_dev), out_shape...  7.64 us
    reduce_sum x1, other arithmetic, shards(): jnp.sum(jnp.where(hot_runs, run_weight[:, :, None], 0.0), axis=1)  7.37 us
    pallas_call x1, Pallas kernels, gather_rows(): pl.pallas_call(gather_kernel, out_shape=jax.ShapeDtypeStruct((count, tabl...  5.23 us
  transfers between devices with their start and end apart: 3, of which 2 were waited for; matrix products, arithmetic and copies ran while one was open for 10% of the time, Pallas kernels for 37%

profile of v17, /device:TPU:1, one launch (start us, length us, event | category | flops | bytes accessed | tf_op | source)
XLA Modules:
  0.0 196.0 jit_solution(374744422410760408)
XLA Ops:
  0.6 0.8 convert_element_type.31
  1.4 0.7 copy.33
  2.1 18.4 %all-to-all-start.1 = ((bf16[128,2,32]{2,1,0:T(2,128)(2,1)}), bf16[128,2,32]{2,1,0:T(2,128)(2,1)S(1)}, u32[]{:S(2)}, u32[]{:S(2)}) async-start(bf16[128,2,32]{2,1,0:T(2,128)(2,1)} %bitcast.7), calls=%async_computation.1 | async-start | bytes 131072 | tf_op jit(solution)/shard_map/all_to_all | solution.py:387
  20.6 0.5 broadcast.119
  21.1 1.3 reduce.9
  22.8 0.1 broadcast_in_dim.62
  22.9 0.9 copy.26
  23.9 1.8 copy.27
  25.7 0.6 broadcast_select_fusion.idx_ref
  26.3 5.2 %shard_map.77 = bf16[8192,128]{1,0:T(8,128)(2,1)} custom-call(s32[4,2048]{1,0:T(4,128)} %broadcast_select_fusion.idx_ref, bf16[128,1024]{1,0:T(8,128)(2,1)} %bitcast.29), custom_call_target="tpu_custom_call" | custom-call | flops 2147483648 | bytes 2392064 | tf_op jit(solution)/shard_map/pallas_call | solution.py:258
  31.6 0.5 all-to-all-done.1
  32.1 13.4 %all-to-all-start = ((bf16[128,64,128]{2,1,0:T(8,128)(2,1)}), bf16[128,64,128]{2,1,0:T(8,128)(2,1)S(1)}, u32[]{:S(2)}, u32[]{:S(2)}) async-start(bf16[128,64,128]{2,1,0:T(8,128)(2,1)} %bitcast.25), calls=%async_computation | async-start | bytes 4194304 | tf_op jit(solution)/shard_map/all_to_all | solution.py:350
  45.8 0.7 reduce.10
  46.6 0.7 broadcast_in_dim.66.user_ref
  47.4 0.7 reduce.11
  48.4 0.1 and.49
  48.6 0.1 copy.31
  48.7 0.1 gt.23
  48.8 0.9 fusion.8.x_ref
  49.8 66.4 %shard_map.79 = f32[128,128]{1,0:T(8,128)} custom-call(f32[128,128]{1,0:T(8,128)} %fusion.8.x_ref), custom_call_target="tpu_custom_call" | custom-call | tf_op jit(solution)/shard_map/pallas_call | solution.py:146
  116.2 0.1 reshape.119
  116.5 1.5 convert_add_fusion.base_ref
  118.0 0.6 add_select_fusion.1.rw_ref
  119.0 1.3 copy-done.1
  120.3 7.6 %shard_map.78.blocks_ref = f32[4,258,128]{2,1,0:T(8,128)} custom-call(bf16[8192,128]{1,0:T(8,128)(2,1)} %bitcast.26, f32[4,2048]{1,0:T(4,128)} %copy-done.4, s32[4,2048]{1,0:T(4,128)} %broadcast_in_dim.66.user_ref, f32[4,2048]{1,0:T(4,128)} %add_select_fusion.1.rw_ref), custom_call_target="tpu_custom_call" | custom-call | flops 2684354560 | bytes 2723840 | tf_op jit(solution)/shard_map/pallas_call | solution.py:311
  127.9 40.1 %shard_map.80 = (bf16[4,2,128]{2,1,0:T(2,128)(2,1)}, f32[2,128]{1,0:T(2,128)}) custom-call(f32[4,258,128]{2,1,0:T(8,128)} %shard_map.78.blocks_ref, f32[128,128]{1,0:T(8,128)} %convert_add_fusion.base_ref), custom_call_target="tpu_custom_call" | custom-call | tf_op jit(solution)/shard_map/pallas_call | solution.py:223
  168.1 1.5 convolution_convert_fusion
  169.7 12.5 %all-to-all-start.2 = ((bf16[128,2,128]{2,1,0:T(2,128)(2,1)}), bf16[128,2,128]{2,1,0:T(2,128)(2,1)S(1)}, u32[]{:S(2)}, u32[]{:S(2)}) async-start(bf16[128,2,128]{2,1,0:T(2,128)(2,1)} %bitcast.11), calls=%async_computation.2 | async-start | bytes 131072 | tf_op jit(solution)/shard_map/all_to_all | solution.py:397
  182.2 7.4 %select_reduce_fusion = f32[256,1024]{1,0:T(8,128)S(1)} fusion(f32[256,32]{1,0:T(8,128)S(1)} %and_select_fusion, s32[256,32]{1,0:T(8,128)S(1)} %copy.32), kind=kLoop, calls=%fused_computation | loop fusion | flops 24903680 | bytes 1114112 | tf_op jit(solution)/shard_map/reduce_sum | solution.py:407
  189.6 4.1 %all-to-all-done.2 = bf16[128,2,128]{2,1,0:T(2,128)(2,1)S(1)} async-done(((bf16[128,2,128]{2,1,0:T(2,128)(2,1)}), bf16[128,2,128]{2,1,0:T(2,128)(2,1)S(1)}, u32[]{:S(2)}, u32[]{:S(2)}) %all-to-all-start.2) | async-done | bytes 65568 | tf_op jit(solution)/shard_map/all_to_all | solution.py:397
  193.6 1.8 convolution_multiply_fusion
  195.4 0.6 copy.35
  (44 shorter events, 1.9 us)
Async XLA Ops:
  2.1 29.9 %all-to-all-start.1 = ((bf16[128,2,32]{2,1,0:T(2,128)(2,1)}), bf16[128,2,32]{2,1,0:T(2,128)(2,1)S(1)}, u32[]{:S(2)}, u32[]{:S(2)}) async-start(bf16[128,2,32]{2,1,0:T(2,128)(2,1)} %bitcast.7), calls=%async_computation.1 | async-start | bytes 131072 | tf_op jit(solution)/shard_map/all_to_all | solution.py:387
  32.1 13.4 %copy-start.2 = (s32[1,1,256,32]{2,3,1,0:T(8,128)S(1)}, s32[1,1,256,32]{2,3,1,0:T(8,128)}, u32[]{:S(2)}) copy-start(s32[1,1,256,32]{2,3,1,0:T(8,128)} %param.10) | copy-start | bytes 98308
  32.1 13.7 %copy-start.5 = (s32[1,1,256,1]{2,3,1,0:T(1,128)S(1)}, s32[1,1,256,1]{2,3,1,0:T(1,128)}, u32[]{:S(2)}) copy-start(s32[1,1,256,1]{2,3,1,0:T(1,128)} %param.9) | copy-start | bytes 3076
  32.1 15.3 %copy-start.8 = (s32[1,1,128]{2,1,0:T(1,128)S(1)}, s32[1,1,128]{2,1,0:T(1,128)}, u32[]{:S(2)}) copy-start(s32[1,1,128]{2,1,0:T(1,128)} %param.11) | copy-start | bytes 1540
  32.1 16.8 %copy-start = (bf16[1024,128]{1,0:T(8,128)(2,1)S(1)}, bf16[1024,128]{1,0:T(8,128)(2,1)}, u32[]{:S(2)}) copy-start(bf16[1024,128]{1,0:T(8,128)(2,1)} %param.6) | copy-start | bytes 786436
  32.1 84.1 %copy-start.7 = (s32[1,1,128]{2,1,0:T(1,128)S(1)}, s32[1,1,128]{2,1,0:T(1,128)}, u32[]{:S(2)}) copy-start(s32[1,1,128]{2,1,0:T(1,128)} %param.8) | copy-start | bytes 1540
  32.1 84.3 %copy-start.3 = (s32[1,1,256,32]{2,3,1,0:T(8,128)S(1)}, s32[1,1,256,32]{2,3,1,0:T(8,128)}, u32[]{:S(2)}) copy-start(s32[1,1,256,32]{2,3,1,0:T(8,128)} %param.7) | copy-start | bytes 98308
  32.1 86.9 %all-to-all-start = ((bf16[128,64,128]{2,1,0:T(8,128)(2,1)}), bf16[128,64,128]{2,1,0:T(8,128)(2,1)S(1)}, u32[]{:S(2)}, u32[]{:S(2)}) async-start(bf16[128,64,128]{2,1,0:T(8,128)(2,1)} %bitcast.25), calls=%async_computation | async-start | bytes 4194304 | tf_op jit(solution)/shard_map/all_to_all | solution.py:350
  45.8 73.2 %copy-start.4 = (f32[4,2048]{1,0:T(4,128)}, f32[4,2048]{1,0:T(4,128)S(1)}, u32[]{:S(2)}) copy-start(f32[4,2048]{1,0:T(4,128)S(1)} %mul.24.gw_ref) | copy-start | bytes 98308
  119.0 1.3 copy-start.1
  168.1 27.3 %copy-start.6 = (f32[2,128]{1,0:T(2,128)S(1)}, f32[2,128]{1,0:T(2,128)}, u32[]{:S(2)}) copy-start(f32[2,128]{1,0:T(2,128)} %get-tuple-element.8) | copy-start | bytes 3076
  169.7 24.0 %all-to-all-start.2 = ((bf16[128,2,128]{2,1,0:T(2,128)(2,1)}), bf16[128,2,128]{2,1,0:T(2,128)(2,1)S(1)}, u32[]{:S(2)}, u32[]{:S(2)}) async-start(bf16[128,2,128]{2,1,0:T(2,128)(2,1)} %bitcast.11), calls=%async_computation.2 | async-start | bytes 131072 | tf_op jit(solution)/shard_map/all_to_all | solution.py:397

commit v18 on v15

--- a/solution.py
+++ b/solution.py
@@ -252,7 +252,7 @@
     out_ref[...] = rows_t.T.astype(out_ref.dtype)
 
 
-def gather_rows(table, idx, chunk=2048):
+def gather_rows(table, idx, chunk=4096):
     count = idx.shape[0]
     idx_lanes = idx.reshape(count // chunk, chunk)
     return pl.pallas_call(

time: 190 us -> 190 us (level)
  no operation moved by 1% of the time
where the time goes in v18:
time: 190 us; the launch traced here: 189 us
  Pallas kernels  120 us (63%)
  starting transfers between devices  31.1 us (16%)
  other arithmetic  13 us (7%)
  waiting for transfers between devices  12.2 us (6%)
  local copies, waits for them, and re-layouts  8.9 us (5%)
  matrix products  3.6 us (2%)
    pallas_call x1, Pallas kernels, tree_sum(): pl.pallas_call(functools.partial(doubling_kernel, n_rep, low_bits, rounds...  66.4 us
    pallas_call x1, Pallas kernels, solve_owned(): pl.pallas_call(functools.partial(owner_kernel, n_rep), out_shape=(jax.Sha...  40.1 us
    all_to_all x1, starting transfers between devices, shards(): lax.all_to_all(picked.reshape(n_ent, slot_cap * tile_rows, rank_width), '...  18.6 us
    all_to_all x1, starting transfers between devices, shards(): lax.all_to_all(back_load.reshape(n_ent, slot_cap, -1), 'ent', split_axis=...  12.5 us
    all_to_all x1, waiting for transfers between devices, shards(): lax.all_to_all(back_load.reshape(n_ent, slot_cap, -1), 'ent', split_axis=...  12.2 us
    pallas_call x1, Pallas kernels, user_grams(): pl.pallas_call(functools.partial(gram_kernel, n_user, per_dev), out_shape...  7.65 us
    reduce_sum x1, other arithmetic, shards(): jnp.sum(jnp.where(hot_runs, run_weight[:, :, None], 0.0), axis=1)  7.42 us
    pallas_call x1, Pallas kernels, gather_rows(): pl.pallas_call(gather_kernel, out_shape=jax.ShapeDtypeStruct((count, tabl...  5.34 us
  transfers between devices with their start and end apart: 2, of which 1 were waited for; matrix products, arithmetic and copies ran while one was open for 3% of the time, Pallas kernels for 35%

profile of v18, /device:TPU:1, one launch (start us, length us, event | category | flops | bytes accessed | tf_op | source)
XLA Modules:
  0.0 189.2 jit_solution(7924314587657384329)
XLA Ops:
  0.6 0.5 broadcast.87
  1.1 1.3 reduce.9
  2.6 0.1 broadcast_in_dim.58
  2.9 0.1 broadcast_in_dim.60
  3.0 0.9 copy.22
  3.9 0.1 reshape_reshape.4
  4.0 1.8 copy.23
  5.8 0.6 broadcast_select_fusion.idx_ref
  6.4 5.3 %shard_map.77 = bf16[8192,128]{1,0:T(8,128)(2,1)} custom-call(s32[2,4096]{1,0:T(2,128)} %broadcast_select_fusion.idx_ref, bf16[128,1024]{1,0:T(8,128)(2,1)} %bitcast.23), custom_call_target="tpu_custom_call" | custom-call | flops 2147483648 | bytes 2392064 | tf_op jit(solution)/shard_map/pallas_call | solution.py:258
  11.8 18.6 %all-to-all-start = ((bf16[128,64,128]{2,1,0:T(8,128)(2,1)}), bf16[128,64,128]{2,1,0:T(8,128)(2,1)S(1)}, u32[]{:S(2)}, u32[]{:S(2)}) async-start(bf16[128,64,128]{2,1,0:T(8,128)(2,1)} %bitcast.22), calls=%async_computation | async-start | bytes 4194304 | tf_op jit(solution)/shard_map/all_to_all | solution.py:350
  30.7 0.7 reduce.10
  31.5 0.7 broadcast_in_dim.64.user_ref
  32.2 0.7 reduce.11
  33.3 0.1 and.46
  33.5 0.1 copy.27
  33.6 0.1 gt.16
  33.7 0.9 fusion.11.x_ref
  34.6 66.4 %shard_map.79 = f32[128,128]{1,0:T(8,128)} custom-call(f32[128,128]{1,0:T(8,128)} %fusion.11.x_ref), custom_call_target="tpu_custom_call" | custom-call | tf_op jit(solution)/shard_map/pallas_call | solution.py:146
  101.1 0.1 reshape.86
  101.4 1.5 convert_add_fusion.base_ref
  102.9 0.6 add_select_fusion.1.rw_ref
  103.5 1.3 copy-done.1
  104.9 7.6 %shard_map.78.blocks_ref = f32[4,258,128]{2,1,0:T(8,128)} custom-call(bf16[8192,128]{1,0:T(8,128)(2,1)} %bitcast.21, f32[4,2048]{1,0:T(4,128)} %copy-done.4, s32[4,2048]{1,0:T(4,128)} %broadcast_in_dim.64.user_ref, f32[4,2048]{1,0:T(4,128)} %add_select_fusion.1.rw_ref), custom_call_target="tpu_custom_call" | custom-call | flops 2684354560 | bytes 2723840 | tf_op jit(solution)/shard_map/pallas_call | solution.py:311
  112.5 40.1 %shard_map.80 = (bf16[4,2,128]{2,1,0:T(2,128)(2,1)}, f32[2,128]{1,0:T(2,128)}) custom-call(f32[4,258,128]{2,1,0:T(8,128)} %shard_map.78.blocks_ref, f32[128,128]{1,0:T(8,128)} %convert_add_fusion.base_ref), custom_call_target="tpu_custom_call" | custom-call | tf_op jit(solution)/shard_map/pallas_call | solution.py:223
  152.7 0.9 convolution_convert_fusion
  153.7 0.7 reshape.88
  154.4 12.5 %all-to-all-start.1 = ((bf16[128,2,160]{2,1,0:T(2,128)(2,1)}), bf16[128,2,160]{2,1,0:T(2,128)(2,1)S(1)}, u32[]{:S(2)}, u32[]{:S(2)}) async-start(bf16[128,2,160]{2,1,0:T(2,128)(2,1)} %reshape.88), calls=%async_computation.1 | async-start | bytes 262144 | tf_op jit(solution)/shard_map/all_to_all | solution.py:394
  166.9 12.2 %all-to-all-done.1 = bf16[128,2,160]{2,1,0:T(2,128)(2,1)S(1)} async-done(((bf16[128,2,160]{2,1,0:T(2,128)(2,1)}), bf16[128,2,160]{2,1,0:T(2,128)(2,1)S(1)}, u32[]{:S(2)}, u32[]{:S(2)}) %all-to-all-start.1) | async-done | bytes 81952 | tf_op jit(solution)/shard_map/all_to_all | solution.py:394
  179.1 0.1 reshape.89
  179.4 7.4 %select_reduce_fusion = f32[256,1024]{1,0:T(8,128)S(1)} fusion(f32[256,32]{1,0:T(8,128)S(1)} %fusion.1, s32[256,32]{1,0:T(8,128)S(1)} %copy.28), kind=kLoop, calls=%fused_computation | loop fusion | flops 24903680 | bytes 1114112 | tf_op jit(solution)/shard_map/reduce_sum | solution.py:405
  186.8 1.8 convolution_multiply_fusion
  188.6 0.6 copy.31
  (41 shorter events, 1.5 us)
Async XLA Ops:
  11.8 18.6 %copy-start.2 = (s32[1,1,256,32]{2,3,1,0:T(8,128)S(1)}, s32[1,1,256,32]{2,3,1,0:T(8,128)}, u32[]{:S(2)}) copy-start(s32[1,1,256,32]{2,3,1,0:T(8,128)} %param.10) | copy-start | bytes 98308
  11.8 18.9 %copy-start.5 = (s32[1,1,256,1]{2,3,1,0:T(1,128)S(1)}, s32[1,1,256,1]{2,3,1,0:T(1,128)}, u32[]{:S(2)}) copy-start(s32[1,1,256,1]{2,3,1,0:T(1,128)} %param.9) | copy-start | bytes 3076
  11.8 20.5 %copy-start.8 = (s32[1,1,128]{2,1,0:T(1,128)S(1)}, s32[1,1,128]{2,1,0:T(1,128)}, u32[]{:S(2)}) copy-start(s32[1,1,128]{2,1,0:T(1,128)} %param.11) | copy-start | bytes 1540
  11.8 21.9 %copy-start = (bf16[1024,128]{1,0:T(8,128)(2,1)S(1)}, bf16[1024,128]{1,0:T(8,128)(2,1)}, u32[]{:S(2)}) copy-start(bf16[1024,128]{1,0:T(8,128)(2,1)} %param.6) | copy-start | bytes 786436
  11.8 89.3 %copy-start.7 = (s32[1,1,128]{2,1,0:T(1,128)S(1)}, s32[1,1,128]{2,1,0:T(1,128)}, u32[]{:S(2)}) copy-start(s32[1,1,128]{2,1,0:T(1,128)} %param.8) | copy-start | bytes 1540
  11.8 89.5 %copy-start.3 = (s32[1,1,256,32]{2,3,1,0:T(8,128)S(1)}, s32[1,1,256,32]{2,3,1,0:T(8,128)}, u32[]{:S(2)}) copy-start(s32[1,1,256,32]{2,3,1,0:T(8,128)} %param.7) | copy-start | bytes 98308
  11.8 91.7 %all-to-all-start = ((bf16[128,64,128]{2,1,0:T(8,128)(2,1)}), bf16[128,64,128]{2,1,0:T(8,128)(2,1)S(1)}, u32[]{:S(2)}, u32[]{:S(2)}) async-start(bf16[128,64,128]{2,1,0:T(8,128)(2,1)} %bitcast.22), calls=%async_computation | async-start | bytes 4194304 | tf_op jit(solution)/shard_map/all_to_all | solution.py:350
  30.6 72.9 %copy-start.4 = (f32[4,2048]{1,0:T(4,128)}, f32[4,2048]{1,0:T(4,128)S(1)}, u32[]{:S(2)}) copy-start(f32[4,2048]{1,0:T(4,128)S(1)} %mul.19.gw_ref) | copy-start | bytes 98308
  103.5 1.3 copy-start.1
  153.5 35.1 %copy-start.6 = (f32[2,128]{1,0:T(2,128)S(1)}, f32[2,128]{1,0:T(2,128)}, u32[]{:S(2)}) copy-start(f32[2,128]{1,0:T(2,128)} %get-tuple-element.8) | copy-start | bytes 3076
  154.4 24.7 %all-to-all-start.1 = ((bf16[128,2,160]{2,1,0:T(2,128)(2,1)}), bf16[128,2,160]{2,1,0:T(2,128)(2,1)S(1)}, u32[]{:S(2)}, u32[]{:S(2)}) async-start(bf16[128,2,160]{2,1,0:T(2,128)(2,1)} %reshape.88), calls=%async_computation.1 | async-start | bytes 262144 | tf_op jit(solution)/shard_map/all_to_all | solution.py:394

commit v19 on v18

--- a/solution.py
+++ b/solution.py
@@ -364,7 +364,7 @@
     selector = owners[None, :] == jnp.arange(user_block, dtype=jnp.int32)[:, None]
     selector_f = selector.astype(jnp.float32)
     rows_all = incoming.reshape(tile_slots * tile_rows, rank_width)
-    lane_chunk = 2048
+    lane_chunk = 4096
     row_owner = jnp.repeat(owners, seg_length)
     gram_blocks = user_grams(
         rows_all,

time: 190 us -> 190 us (level)
  no operation moved by 1% of the time
where the time goes in v19:
time: 190 us; the launch traced here: 189 us
  Pallas kernels  120 us (63%)
  starting transfers between devices  31.2 us (16%)
  other arithmetic  12.3 us (6%)
  waiting for transfers between devices  12.2 us (6%)
  local copies, waits for them, and re-layouts  8.85 us (5%)
  matrix products  3.62 us (2%)
    pallas_call x1, Pallas kernels, tree_sum(): pl.pallas_call(functools.partial(doubling_kernel, n_rep, low_bits, rounds...  66.9 us
    pallas_call x1, Pallas kernels, solve_owned(): pl.pallas_call(functools.partial(owner_kernel, n_rep), out_shape=(jax.Sha...  40.3 us
    all_to_all x1, starting transfers between devices, shards(): lax.all_to_all(picked.reshape(n_ent, slot_cap * tile_rows, rank_width), '...  18.6 us
    all_to_all x1, starting transfers between devices, shards(): lax.all_to_all(back_load.reshape(n_ent, slot_cap, -1), 'ent', split_axis=...  12.6 us
    all_to_all x1, waiting for transfers between devices, shards(): lax.all_to_all(back_load.reshape(n_ent, slot_cap, -1), 'ent', split_axis=...  12.2 us
    pallas_call x1, Pallas kernels, user_grams(): pl.pallas_call(functools.partial(gram_kernel, n_user, per_dev), out_shape...  7.69 us
    reduce_sum x1, other arithmetic, shards(): jnp.sum(jnp.where(hot_runs, run_weight[:, :, None], 0.0), axis=1)  7.42 us
    pallas_call x1, Pallas kernels, gather_rows(): pl.pallas_call(gather_kernel, out_shape=jax.ShapeDtypeStruct((count, tabl...  5.37 us
  transfers between devices with their start and end apart: 2, of which 1 were waited for; matrix products, arithmetic and copies ran while one was open for 3% of the time, Pallas kernels for 35%

profile of v19, /device:TPU:1, one launch (start us, length us, event | category | flops | bytes accessed | tf_op | source)
XLA Modules:
  0.0 189.3 jit_solution(15103609915505519650)
XLA Ops:
  0.6 0.5 broadcast.84
  1.1 1.3 reduce.6
  2.6 0.1 broadcast_in_dim.58
  2.9 0.1 broadcast_in_dim.60
  3.0 0.9 copy.20
  3.9 0.1 reshape_reshape.4
  4.0 1.8 copy.21
  5.8 0.6 broadcast_select_fusion.idx_ref
  6.4 5.4 %shard_map.77 = bf16[8192,128]{1,0:T(8,128)(2,1)} custom-call(s32[2,4096]{1,0:T(2,128)} %broadcast_select_fusion.idx_ref, bf16[128,1024]{1,0:T(8,128)(2,1)} %bitcast.22), custom_call_target="tpu_custom_call" | custom-call | flops 2147483648 | bytes 2392064 | tf_op jit(solution)/shard_map/pallas_call | solution.py:258
  11.8 18.6 %all-to-all-start = ((bf16[128,64,128]{2,1,0:T(8,128)(2,1)}), bf16[128,64,128]{2,1,0:T(8,128)(2,1)S(1)}, u32[]{:S(2)}, u32[]{:S(2)}) async-start(bf16[128,64,128]{2,1,0:T(8,128)(2,1)} %bitcast.21), calls=%async_computation | async-start | bytes 4194304 | tf_op jit(solution)/shard_map/all_to_all | solution.py:350
  30.8 0.7 broadcast_in_dim.64.user_ref
  31.5 0.7 reduce.7
  32.3 0.1 broadcast_in_dim.67
  32.6 0.1 and.45
  32.7 0.1 copy.23
  32.9 0.1 gt.16
  33.0 0.9 fusion.8.x_ref
  33.9 66.9 %shard_map.79 = f32[128,128]{1,0:T(8,128)} custom-call(f32[128,128]{1,0:T(8,128)} %fusion.8.x_ref), custom_call_target="tpu_custom_call" | custom-call | tf_op jit(solution)/shard_map/pallas_call | solution.py:146
  100.9 0.1 reshape.86
  101.1 1.5 convert_add_fusion.base_ref
  102.6 0.7 and_select_fusion.rw_ref
  103.3 1.3 copy-done.1
  104.6 7.7 %shard_map.78.blocks_ref = f32[4,258,128]{2,1,0:T(8,128)} custom-call(bf16[8192,128]{1,0:T(8,128)(2,1)} %bitcast.20, f32[2,4096]{1,0:T(2,128)} %copy-done.4, s32[2,4096]{1,0:T(2,128)} %broadcast_in_dim.64.user_ref, f32[2,4096]{1,0:T(2,128)} %and_select_fusion.rw_ref), custom_call_target="tpu_custom_call" | custom-call | flops 2684354560 | bytes 2723840 | tf_op jit(solution)/shard_map/pallas_call | solution.py:311
  112.3 40.3 %shard_map.80 = (bf16[4,2,128]{2,1,0:T(2,128)(2,1)}, f32[2,128]{1,0:T(2,128)}) custom-call(f32[4,258,128]{2,1,0:T(8,128)} %shard_map.78.blocks_ref, f32[128,128]{1,0:T(8,128)} %convert_add_fusion.base_ref), custom_call_target="tpu_custom_call" | custom-call | tf_op jit(solution)/shard_map/pallas_call | solution.py:223
  152.6 0.9 convolution_convert_fusion
  153.6 0.7 reshape.88
  154.4 12.6 %all-to-all-start.1 = ((bf16[128,2,160]{2,1,0:T(2,128)(2,1)}), bf16[128,2,160]{2,1,0:T(2,128)(2,1)S(1)}, u32[]{:S(2)}, u32[]{:S(2)}) async-start(bf16[128,2,160]{2,1,0:T(2,128)(2,1)} %reshape.88), calls=%async_computation.1 | async-start | bytes 262144 | tf_op jit(solution)/shard_map/all_to_all | solution.py:394
  167.0 12.2 %all-to-all-done.1 = bf16[128,2,160]{2,1,0:T(2,128)(2,1)S(1)} async-done(((bf16[128,2,160]{2,1,0:T(2,128)(2,1)}), bf16[128,2,160]{2,1,0:T(2,128)(2,1)S(1)}, u32[]{:S(2)}, u32[]{:S(2)}) %all-to-all-start.1) | async-done | bytes 81952 | tf_op jit(solution)/shard_map/all_to_all | solution.py:394
  179.2 0.1 reshape.89
  179.4 7.4 %select_reduce_fusion = f32[256,1024]{1,0:T(8,128)S(1)} fusion(f32[256,32]{1,0:T(8,128)S(1)} %fusion.1, s32[256,32]{1,0:T(8,128)S(1)} %copy.24), kind=kLoop, calls=%fused_computation | loop fusion | flops 24903680 | bytes 1114112 | tf_op jit(solution)/shard_map/reduce_sum | solution.py:405
  186.9 1.8 convolution_multiply_fusion
  188.7 0.6 copy.27
  (38 shorter events, 1.3 us)
Async XLA Ops:
  11.8 18.6 %copy-start.2 = (s32[1,1,256,32]{2,3,1,0:T(8,128)S(1)}, s32[1,1,256,32]{2,3,1,0:T(8,128)}, u32[]{:S(2)}) copy-start(s32[1,1,256,32]{2,3,1,0:T(8,128)} %param.10) | copy-start | bytes 98308
  11.8 18.9 %copy-start.5 = (s32[1,1,256,1]{2,3,1,0:T(1,128)S(1)}, s32[1,1,256,1]{2,3,1,0:T(1,128)}, u32[]{:S(2)}) copy-start(s32[1,1,256,1]{2,3,1,0:T(1,128)} %param.9) | copy-start | bytes 3076
  11.8 19.7 %copy-start.8 = (s32[1,1,128]{2,1,0:T(1,128)S(1)}, s32[1,1,128]{2,1,0:T(1,128)}, u32[]{:S(2)}) copy-start(s32[1,1,128]{2,1,0:T(1,128)} %param.11) | copy-start | bytes 1540
  11.8 21.2 %copy-start = (bf16[1024,128]{1,0:T(8,128)(2,1)S(1)}, bf16[1024,128]{1,0:T(8,128)(2,1)}, u32[]{:S(2)}) copy-start(bf16[1024,128]{1,0:T(8,128)(2,1)} %param.6) | copy-start | bytes 786436
  11.8 89.0 %copy-start.7 = (s32[1,1,128]{2,1,0:T(1,128)S(1)}, s32[1,1,128]{2,1,0:T(1,128)}, u32[]{:S(2)}) copy-start(s32[1,1,128]{2,1,0:T(1,128)} %param.8) | copy-start | bytes 1540
  11.8 89.2 %copy-start.3 = (s32[1,1,256,32]{2,3,1,0:T(8,128)S(1)}, s32[1,1,256,32]{2,3,1,0:T(8,128)}, u32[]{:S(2)}) copy-start(s32[1,1,256,32]{2,3,1,0:T(8,128)} %param.7) | copy-start | bytes 98308
  11.8 91.4 %all-to-all-start = ((bf16[128,64,128]{2,1,0:T(8,128)(2,1)}), bf16[128,64,128]{2,1,0:T(8,128)(2,1)S(1)}, u32[]{:S(2)}, u32[]{:S(2)}) async-start(bf16[128,64,128]{2,1,0:T(8,128)(2,1)} %bitcast.21), calls=%async_computation | async-start | bytes 4194304 | tf_op jit(solution)/shard_map/all_to_all | solution.py:350
  30.6 72.6 %copy-start.4 = (f32[2,4096]{1,0:T(2,128)}, f32[2,4096]{1,0:T(2,128)S(1)}, u32[]{:S(2)}) copy-start(f32[2,4096]{1,0:T(2,128)S(1)} %mul.19.gw_ref) | copy-start | bytes 98308
  103.3 1.3 copy-start.1
  153.5 35.2 %copy-start.6 = (f32[2,128]{1,0:T(2,128)S(1)}, f32[2,128]{1,0:T(2,128)}, u32[]{:S(2)}) copy-start(f32[2,128]{1,0:T(2,128)} %get-tuple-element.8) | copy-start | bytes 3076
  154.4 24.8 %all-to-all-start.1 = ((bf16[128,2,160]{2,1,0:T(2,128)(2,1)}), bf16[128,2,160]{2,1,0:T(2,128)(2,1)S(1)}, u32[]{:S(2)}, u32[]{:S(2)}) async-start(bf16[128,2,160]{2,1,0:T(2,128)(2,1)} %reshape.88), calls=%async_computation.1 | async-start | bytes 262144 | tf_op jit(solution)/shard_map/all_to_all | solution.py:394

commit v20 on v18

--- a/solution.py
+++ b/solution.py
@@ -24,13 +24,12 @@
 
     def factor(top, j, carry):
         span = n - top
-        lane_m = lax.broadcasted_iota(jnp.int32, (span, n), 1)
         sub_m = lax.broadcasted_iota(jnp.int32, (span, n), 0) + top
         sub_v = lax.broadcasted_iota(jnp.int32, (span, 1), 0) + top
         for b in range(batch):
             a = a_s[b, top:, :]
             row = jnp.sum(jnp.where(sub_m == j, a, 0.0), axis=0, keepdims=True)
-            col = jnp.sum(jnp.where(lane_m == j, a, 0.0), axis=1, keepdims=True)
+            col = jnp.transpose(jnp.broadcast_to(row, (8, n)))[top:, 0:1]
             diag = jnp.sum(jnp.where(lane_v == j, row, 0.0), axis=1, keepdims=True)
             inv = 1.0 / jnp.sqrt(diag)
             l_row = jnp.where(lane_v >= j, row, 0.0) * inv

time: 190 us -> 208 us (1.095)
  Pallas kernels: 120 us -> 137 us
    pallas_call x1, Pallas kernels: 40.1 us -> 57.9 us  [solve_owned(): pl.pallas_call(functools.partial(owner_kernel, n_rep), out_shape=(jax.Sha...]
  transfers between devices with their start and end apart: 2 -> 2, of which waited for: 1 -> 1; matrix products, arithmetic and copies ran while one was open for 3% -> 3% of each run, Pallas kernels for 35% -> 32%
where the time goes in v20:
time: 208 us; the launch traced here: 207 us
  Pallas kernels  137 us (66%)
  starting transfers between devices  31.1 us (15%)
  other arithmetic  13 us (6%)
  waiting for transfers between devices  12.2 us (6%)
  local copies, waits for them, and re-layouts  8.9 us (4%)
  matrix products  3.6 us (2%)
    pallas_call x1, Pallas kernels, tree_sum(): pl.pallas_call(functools.partial(doubling_kernel, n_rep, low_bits, rounds...  66.4 us
    pallas_call x1, Pallas kernels, solve_owned(): pl.pallas_call(functools.partial(owner_kernel, n_rep), out_shape=(jax.Sha...  57.9 us
    all_to_all x1, starting transfers between devices, shards(): lax.all_to_all(picked.reshape(n_ent, slot_cap * tile_rows, rank_width), '...  18.6 us
    all_to_all x1, starting transfers between devices, shards(): lax.all_to_all(back_load.reshape(n_ent, slot_cap, -1), 'ent', split_axis=...  12.5 us
    all_to_all x1, waiting for transfers between devices, shards(): lax.all_to_all(back_load.reshape(n_ent, slot_cap, -1), 'ent', split_axis=...  12.2 us
    pallas_call x1, Pallas kernels, user_grams(): pl.pallas_call(functools.partial(gram_kernel, n_user, per_dev), out_shape...  7.65 us
    reduce_sum x1, other arithmetic, shards(): jnp.sum(jnp.where(hot_runs, run_weight[:, :, None], 0.0), axis=1)  7.42 us
    pallas_call x1, Pallas kernels, gather_rows(): pl.pallas_call(gather_kernel, out_shape=jax.ShapeDtypeStruct((count, tabl...  5.34 us
  transfers between devices with their start and end apart: 2, of which 1 were waited for; matrix products, arithmetic and copies ran while one was open for 3% of the time, Pallas kernels for 32%

profile of v20, /device:TPU:1, one launch (start us, length us, event | category | flops | bytes accessed | tf_op | source)
XLA Modules:
  0.0 207.0 jit_solution(15792031101690176164)
XLA Ops:
  0.6 0.5 broadcast.87
  1.1 1.3 reduce.9
  2.6 0.1 broadcast_in_dim.58
  2.9 0.1 broadcast_in_dim.60
  3.0 0.9 copy.22
  3.9 0.1 reshape_reshape.4
  4.0 1.8 copy.23
  5.8 0.6 broadcast_select_fusion.idx_ref
  6.4 5.3 %shard_map.77 = bf16[8192,128]{1,0:T(8,128)(2,1)} custom-call(s32[2,4096]{1,0:T(2,128)} %broadcast_select_fusion.idx_ref, bf16[128,1024]{1,0:T(8,128)(2,1)} %bitcast.23), custom_call_target="tpu_custom_call" | custom-call | flops 2147483648 | bytes 2392064 | tf_op jit(solution)/shard_map/pallas_call | solution.py:257
  11.8 18.6 %all-to-all-start = ((bf16[128,64,128]{2,1,0:T(8,128)(2,1)}), bf16[128,64,128]{2,1,0:T(8,128)(2,1)S(1)}, u32[]{:S(2)}, u32[]{:S(2)}) async-start(bf16[128,64,128]{2,1,0:T(8,128)(2,1)} %bitcast.22), calls=%async_computation | async-start | bytes 4194304 | tf_op jit(solution)/shard_map/all_to_all | solution.py:349
  30.7 0.7 reduce.10
  31.5 0.7 broadcast_in_dim.64.user_ref
  32.2 0.7 reduce.11
  33.3 0.1 and.46
  33.5 0.1 copy.27
  33.6 0.1 gt.16
  33.7 0.9 fusion.11.x_ref
  34.6 66.4 %shard_map.79 = f32[128,128]{1,0:T(8,128)} custom-call(f32[128,128]{1,0:T(8,128)} %fusion.11.x_ref), custom_call_target="tpu_custom_call" | custom-call | tf_op jit(solution)/shard_map/pallas_call | solution.py:145
  101.1 0.1 reshape.86
  101.4 1.5 convert_add_fusion.base_ref
  102.9 0.6 add_select_fusion.1.rw_ref
  103.5 1.3 copy-done.1
  104.9 7.6 %shard_map.78.blocks_ref = f32[4,258,128]{2,1,0:T(8,128)} custom-call(bf16[8192,128]{1,0:T(8,128)(2,1)} %bitcast.21, f32[4,2048]{1,0:T(4,128)} %copy-done.4, s32[4,2048]{1,0:T(4,128)} %broadcast_in_dim.64.user_ref, f32[4,2048]{1,0:T(4,128)} %add_select_fusion.1.rw_ref), custom_call_target="tpu_custom_call" | custom-call | flops 2684354560 | bytes 2723840 | tf_op jit(solution)/shard_map/pallas_call | solution.py:310
  112.5 57.9 %shard_map.80 = (bf16[4,2,128]{2,1,0:T(2,128)(2,1)}, f32[2,128]{1,0:T(2,128)}) custom-call(f32[4,258,128]{2,1,0:T(8,128)} %shard_map.78.blocks_ref, f32[128,128]{1,0:T(8,128)} %convert_add_fusion.base_ref), custom_call_target="tpu_custom_call" | custom-call | tf_op jit(solution)/shard_map/pallas_call | solution.py:222
  170.4 0.9 convolution_convert_fusion
  171.4 0.7 reshape.88
  172.2 12.5 %all-to-all-start.1 = ((bf16[128,2,160]{2,1,0:T(2,128)(2,1)}), bf16[128,2,160]{2,1,0:T(2,128)(2,1)S(1)}, u32[]{:S(2)}, u32[]{:S(2)}) async-start(bf16[128,2,160]{2,1,0:T(2,128)(2,1)} %reshape.88), calls=%async_computation.1 | async-start | bytes 262144 | tf_op jit(solution)/shard_map/all_to_all | solution.py:393
  184.7 12.2 %all-to-all-done.1 = bf16[128,2,160]{2,1,0:T(2,128)(2,1)S(1)} async-done(((bf16[128,2,160]{2,1,0:T(2,128)(2,1)}), bf16[128,2,160]{2,1,0:T(2,128)(2,1)S(1)}, u32[]{:S(2)}, u32[]{:S(2)}) %all-to-all-start.1) | async-done | bytes 81952 | tf_op jit(solution)/shard_map/all_to_all | solution.py:393
  196.9 0.1 reshape.89
  197.1 7.4 %select_reduce_fusion = f32[256,1024]{1,0:T(8,128)S(1)} fusion(f32[256,32]{1,0:T(8,128)S(1)} %fusion.1, s32[256,32]{1,0:T(8,128)S(1)} %copy.28), kind=kLoop, calls=%fused_computation | loop fusion | flops 24903680 | bytes 1114112 | tf_op jit(solution)/shard_map/reduce_sum | solution.py:404
  204.6 1.8 convolution_multiply_fusion
  206.4 0.6 copy.31
  (41 shorter events, 1.5 us)
Async XLA Ops:
  11.8 18.6 %copy-start.2 = (s32[1,1,256,32]{2,3,1,0:T(8,128)S(1)}, s32[1,1,256,32]{2,3,1,0:T(8,128)}, u32[]{:S(2)}) copy-start(s32[1,1,256,32]{2,3,1,0:T(8,128)} %param.10) | copy-start | bytes 98308
  11.8 18.9 %copy-start.5 = (s32[1,1,256,1]{2,3,1,0:T(1,128)S(1)}, s32[1,1,256,1]{2,3,1,0:T(1,128)}, u32[]{:S(2)}) copy-start(s32[1,1,256,1]{2,3,1,0:T(1,128)} %param.9) | copy-start | bytes 3076
  11.8 20.5 %copy-start.8 = (s32[1,1,128]{2,1,0:T(1,128)S(1)}, s32[1,1,128]{2,1,0:T(1,128)}, u32[]{:S(2)}) copy-start(s32[1,1,128]{2,1,0:T(1,128)} %param.11) | copy-start | bytes 1540
  11.8 21.9 %copy-start = (bf16[1024,128]{1,0:T(8,128)(2,1)S(1)}, bf16[1024,128]{1,0:T(8,128)(2,1)}, u32[]{:S(2)}) copy-start(bf16[1024,128]{1,0:T(8,128)(2,1)} %param.6) | copy-start | bytes 786436
  11.8 89.3 %copy-start.7 = (s32[1,1,128]{2,1,0:T(1,128)S(1)}, s32[1,1,128]{2,1,0:T(1,128)}, u32[]{:S(2)}) copy-start(s32[1,1,128]{2,1,0:T(1,128)} %param.8) | copy-start | bytes 1540
  11.8 89.5 %copy-start.3 = (s32[1,1,256,32]{2,3,1,0:T(8,128)S(1)}, s32[1,1,256,32]{2,3,1,0:T(8,128)}, u32[]{:S(2)}) copy-start(s32[1,1,256,32]{2,3,1,0:T(8,128)} %param.7) | copy-start | bytes 98308
  11.8 91.7 %all-to-all-start = ((bf16[128,64,128]{2,1,0:T(8,128)(2,1)}), bf16[128,64,128]{2,1,0:T(8,128)(2,1)S(1)}, u32[]{:S(2)}, u32[]{:S(2)}) async-start(bf16[128,64,128]{2,1,0:T(8,128)(2,1)} %bitcast.22), calls=%async_computation | async-start | bytes 4194304 | tf_op jit(solution)/shard_map/all_to_all | solution.py:349
  30.6 72.9 %copy-start.4 = (f32[4,2048]{1,0:T(4,128)}, f32[4,2048]{1,0:T(4,128)S(1)}, u32[]{:S(2)}) copy-start(f32[4,2048]{1,0:T(4,128)S(1)} %mul.19.gw_ref) | copy-start | bytes 98308
  103.5 1.3 copy-start.1
  171.3 35.1 %copy-start.6 = (f32[2,128]{1,0:T(2,128)S(1)}, f32[2,128]{1,0:T(2,128)}, u32[]{:S(2)}) copy-start(f32[2,128]{1,0:T(2,128)} %get-tuple-element.8) | copy-start | bytes 3076
  172.2 24.7 %all-to-all-start.1 = ((bf16[128,2,160]{2,1,0:T(2,128)(2,1)}), bf16[128,2,160]{2,1,0:T(2,128)(2,1)S(1)}, u32[]{:S(2)}, u32[]{:S(2)}) async-start(bf16[128,2,160]{2,1,0:T(2,128)(2,1)} %reshape.88), calls=%async_computation.1 | async-start | bytes 262144 | tf_op jit(solution)/shard_map/all_to_all | solution.py:393

commit v21 on v18

--- a/solution.py
+++ b/solution.py
@@ -42,8 +42,9 @@
             y_s[pl.ds(b, 1), :] = jnp.where(lane_v == j, y_j, y - y_j * l_row)
         return carry
 
-    quarter = n // 4
-    for part in range(4):
+    parts = 8
+    quarter = n // parts
+    for part in range(parts):
         top = part * quarter
         lax.fori_loop(top, top + quarter, functools.partial(factor, top), 0, unroll=2)
 

time: 190 us -> 190 us (level)
  no operation moved by 1% of the time
where the time goes in v21:
time: 190 us; the launch traced here: 189 us
  Pallas kernels  119 us (63%)
  starting transfers between devices  31.1 us (16%)
  other arithmetic  13 us (7%)
  waiting for transfers between devices  12.2 us (6%)
  local copies, waits for them, and re-layouts  8.9 us (5%)
  matrix products  3.6 us (2%)
    pallas_call x1, Pallas kernels, tree_sum(): pl.pallas_call(functools.partial(doubling_kernel, n_rep, low_bits, rounds...  66.4 us
    pallas_call x1, Pallas kernels, solve_owned(): pl.pallas_call(functools.partial(owner_kernel, n_rep), out_shape=(jax.Sha...  39.9 us
    all_to_all x1, starting transfers between devices, shards(): lax.all_to_all(picked.reshape(n_ent, slot_cap * tile_rows, rank_width), '...  18.6 us
    all_to_all x1, starting transfers between devices, shards(): lax.all_to_all(back_load.reshape(n_ent, slot_cap, -1), 'ent', split_axis=...  12.5 us
    all_to_all x1, waiting for transfers between devices, shards(): lax.all_to_all(back_load.reshape(n_ent, slot_cap, -1), 'ent', split_axis=...  12.2 us
    pallas_call x1, Pallas kernels, user_grams(): pl.pallas_call(functools.partial(gram_kernel, n_user, per_dev), out_shape...  7.65 us
    reduce_sum x1, other arithmetic, shards(): jnp.sum(jnp.where(hot_runs, run_weight[:, :, None], 0.0), axis=1)  7.42 us
    pallas_call x1, Pallas kernels, gather_rows(): pl.pallas_call(gather_kernel, out_shape=jax.ShapeDtypeStruct((count, tabl...  5.34 us
  transfers between devices with their start and end apart: 2, of which 1 were waited for; matrix products, arithmetic and copies ran while one was open for 3% of the time, Pallas kernels for 35%

profile of v21, /device:TPU:1, one launch (start us, length us, event | category | flops | bytes accessed | tf_op | source)
XLA Modules:
  0.0 188.9 jit_solution(17017971104904893638)
XLA Ops:
  0.6 0.5 broadcast.87
  1.1 1.3 reduce.9
  2.6 0.1 broadcast_in_dim.58
  2.9 0.1 broadcast_in_dim.60
  3.0 0.9 copy.22
  3.9 0.1 reshape_reshape.4
  4.0 1.8 copy.23
  5.8 0.6 broadcast_select_fusion.idx_ref
  6.4 5.3 %shard_map.77 = bf16[8192,128]{1,0:T(8,128)(2,1)} custom-call(s32[2,4096]{1,0:T(2,128)} %broadcast_select_fusion.idx_ref, bf16[128,1024]{1,0:T(8,128)(2,1)} %bitcast.23), custom_call_target="tpu_custom_call" | custom-call | flops 2147483648 | bytes 2392064 | tf_op jit(solution)/shard_map/pallas_call | solution.py:259
  11.8 18.6 %all-to-all-start = ((bf16[128,64,128]{2,1,0:T(8,128)(2,1)}), bf16[128,64,128]{2,1,0:T(8,128)(2,1)S(1)}, u32[]{:S(2)}, u32[]{:S(2)}) async-start(bf16[128,64,128]{2,1,0:T(8,128)(2,1)} %bitcast.22), calls=%async_computation | async-start | bytes 4194304 | tf_op jit(solution)/shard_map/all_to_all | solution.py:351
  30.7 0.7 reduce.10
  31.5 0.7 broadcast_in_dim.64.user_ref
  32.2 0.7 reduce.11
  33.3 0.1 and.46
  33.5 0.1 copy.27
  33.6 0.1 gt.16
  33.7 0.9 fusion.11.x_ref
  34.6 66.4 %shard_map.79 = f32[128,128]{1,0:T(8,128)} custom-call(f32[128,128]{1,0:T(8,128)} %fusion.11.x_ref), custom_call_target="tpu_custom_call" | custom-call | tf_op jit(solution)/shard_map/pallas_call | solution.py:147
  101.1 0.1 reshape.86
  101.4 1.5 convert_add_fusion.base_ref
  102.9 0.6 add_select_fusion.1.rw_ref
  103.5 1.3 copy-done.1
  104.9 7.6 %shard_map.78.blocks_ref = f32[4,258,128]{2,1,0:T(8,128)} custom-call(bf16[8192,128]{1,0:T(8,128)(2,1)} %bitcast.21, f32[4,2048]{1,0:T(4,128)} %copy-done.4, s32[4,2048]{1,0:T(4,128)} %broadcast_in_dim.64.user_ref, f32[4,2048]{1,0:T(4,128)} %add_select_fusion.1.rw_ref), custom_call_target="tpu_custom_call" | custom-call | flops 2684354560 | bytes 2723840 | tf_op jit(solution)/shard_map/pallas_call | solution.py:312
  112.5 39.9 %shard_map.80 = (bf16[4,2,128]{2,1,0:T(2,128)(2,1)}, f32[2,128]{1,0:T(2,128)}) custom-call(f32[4,258,128]{2,1,0:T(8,128)} %shard_map.78.blocks_ref, f32[128,128]{1,0:T(8,128)} %convert_add_fusion.base_ref), custom_call_target="tpu_custom_call" | custom-call | tf_op jit(solution)/shard_map/pallas_call | solution.py:224
  152.4 0.9 convolution_convert_fusion
  153.4 0.7 reshape.88
  154.1 12.5 %all-to-all-start.1 = ((bf16[128,2,160]{2,1,0:T(2,128)(2,1)}), bf16[128,2,160]{2,1,0:T(2,128)(2,1)S(1)}, u32[]{:S(2)}, u32[]{:S(2)}) async-start(bf16[128,2,160]{2,1,0:T(2,128)(2,1)} %reshape.88), calls=%async_computation.1 | async-start | bytes 262144 | tf_op jit(solution)/shard_map/all_to_all | solution.py:395
  166.7 12.2 %all-to-all-done.1 = bf16[128,2,160]{2,1,0:T(2,128)(2,1)S(1)} async-done(((bf16[128,2,160]{2,1,0:T(2,128)(2,1)}), bf16[128,2,160]{2,1,0:T(2,128)(2,1)S(1)}, u32[]{:S(2)}, u32[]{:S(2)}) %all-to-all-start.1) | async-done | bytes 81952 | tf_op jit(solution)/shard_map/all_to_all | solution.py:395
  178.9 0.1 reshape.89
  179.1 7.4 %select_reduce_fusion = f32[256,1024]{1,0:T(8,128)S(1)} fusion(f32[256,32]{1,0:T(8,128)S(1)} %fusion.1, s32[256,32]{1,0:T(8,128)S(1)} %copy.28), kind=kLoop, calls=%fused_computation | loop fusion | flops 24903680 | bytes 1114112 | tf_op jit(solution)/shard_map/reduce_sum | solution.py:406
  186.5 1.8 convolution_multiply_fusion
  188.3 0.6 copy.31
  (41 shorter events, 1.5 us)
Async XLA Ops:
  11.8 18.6 %copy-start.2 = (s32[1,1,256,32]{2,3,1,0:T(8,128)S(1)}, s32[1,1,256,32]{2,3,1,0:T(8,128)}, u32[]{:S(2)}) copy-start(s32[1,1,256,32]{2,3,1,0:T(8,128)} %param.10) | copy-start | bytes 98308
  11.8 18.9 %copy-start.5 = (s32[1,1,256,1]{2,3,1,0:T(1,128)S(1)}, s32[1,1,256,1]{2,3,1,0:T(1,128)}, u32[]{:S(2)}) copy-start(s32[1,1,256,1]{2,3,1,0:T(1,128)} %param.9) | copy-start | bytes 3076
  11.8 20.5 %copy-start.8 = (s32[1,1,128]{2,1,0:T(1,128)S(1)}, s32[1,1,128]{2,1,0:T(1,128)}, u32[]{:S(2)}) copy-start(s32[1,1,128]{2,1,0:T(1,128)} %param.11) | copy-start | bytes 1540
  11.8 21.9 %copy-start = (bf16[1024,128]{1,0:T(8,128)(2,1)S(1)}, bf16[1024,128]{1,0:T(8,128)(2,1)}, u32[]{:S(2)}) copy-start(bf16[1024,128]{1,0:T(8,128)(2,1)} %param.6) | copy-start | bytes 786436
  11.8 89.3 %copy-start.7 = (s32[1,1,128]{2,1,0:T(1,128)S(1)}, s32[1,1,128]{2,1,0:T(1,128)}, u32[]{:S(2)}) copy-start(s32[1,1,128]{2,1,0:T(1,128)} %param.8) | copy-start | bytes 1540
  11.8 89.5 %copy-start.3 = (s32[1,1,256,32]{2,3,1,0:T(8,128)S(1)}, s32[1,1,256,32]{2,3,1,0:T(8,128)}, u32[]{:S(2)}) copy-start(s32[1,1,256,32]{2,3,1,0:T(8,128)} %param.7) | copy-start | bytes 98308
  11.8 91.7 %all-to-all-start = ((bf16[128,64,128]{2,1,0:T(8,128)(2,1)}), bf16[128,64,128]{2,1,0:T(8,128)(2,1)S(1)}, u32[]{:S(2)}, u32[]{:S(2)}) async-start(bf16[128,64,128]{2,1,0:T(8,128)(2,1)} %bitcast.22), calls=%async_computation | async-start | bytes 4194304 | tf_op jit(solution)/shard_map/all_to_all | solution.py:351
  30.6 72.9 %copy-start.4 = (f32[4,2048]{1,0:T(4,128)}, f32[4,2048]{1,0:T(4,128)S(1)}, u32[]{:S(2)}) copy-start(f32[4,2048]{1,0:T(4,128)S(1)} %mul.19.gw_ref) | copy-start | bytes 98308
  103.5 1.3 copy-start.1
  153.3 35.1 %copy-start.6 = (f32[2,128]{1,0:T(2,128)S(1)}, f32[2,128]{1,0:T(2,128)}, u32[]{:S(2)}) copy-start(f32[2,128]{1,0:T(2,128)} %get-tuple-element.8) | copy-start | bytes 3076
  154.1 24.7 %all-to-all-start.1 = ((bf16[128,2,160]{2,1,0:T(2,128)(2,1)}), bf16[128,2,160]{2,1,0:T(2,128)(2,1)S(1)}, u32[]{:S(2)}, u32[]{:S(2)}) async-start(bf16[128,2,160]{2,1,0:T(2,128)(2,1)} %reshape.88), calls=%async_computation.1 | async-start | bytes 262144 | tf_op jit(solution)/shard_map/all_to_all | solution.py:395

commit v22 on v18

--- a/solution.py
+++ b/solution.py
@@ -285,12 +285,13 @@
     weights_t = (rows_t * gw_ref[pl.ds(step, 1), :]).astype(jnp.bfloat16)
     users = user_ref[pl.ds(step, 1), :]
     zero = jnp.zeros((), jnp.bfloat16)
+    picked = jnp.concatenate(
+        [jnp.where(users == user, weights_t, zero) for user in range(n_user)], axis=0
+    )
+    grams = jnp.dot(picked, rows, preferred_element_type=jnp.float32)
     for user in range(n_user):
-        picked = jnp.where(users == user, weights_t, zero)
         block, spot = user // per_dev, (user % per_dev) * width
-        out_ref[block, spot : spot + width, :] += jnp.dot(
-            picked, rows, preferred_element_type=jnp.float32
-        )
+        out_ref[block, spot : spot + width, :] += grams[user * width : (user + 1) * width]
     slots = lax.broadcasted_iota(jnp.int32, (n_user, users.shape[1]), 0)
     per_user = jnp.where(users == slots, rw_ref[pl.ds(step, 1), :], 0.0)
     high = per_user.astype(jnp.bfloat16)

time: 190 us -> 190 us (level)
  no operation moved by 1% of the time
where the time goes in v22:
time: 190 us; the launch traced here: 189 us
  Pallas kernels  119 us (63%)
  starting transfers between devices  31.1 us (16%)
  other arithmetic  13 us (7%)
  waiting for transfers between devices  12.2 us (6%)
  local copies, waits for them, and re-layouts  8.9 us (5%)
  matrix products  3.6 us (2%)
    pallas_call x1, Pallas kernels, tree_sum(): pl.pallas_call(functools.partial(doubling_kernel, n_rep, low_bits, rounds...  66.4 us
    pallas_call x1, Pallas kernels, solve_owned(): pl.pallas_call(functools.partial(owner_kernel, n_rep), out_shape=(jax.Sha...  40.1 us
    all_to_all x1, starting transfers between devices, shards(): lax.all_to_all(picked.reshape(n_ent, slot_cap * tile_rows, rank_width), '...  18.6 us
    all_to_all x1, starting transfers between devices, shards(): lax.all_to_all(back_load.reshape(n_ent, slot_cap, -1), 'ent', split_axis=...  12.5 us
    all_to_all x1, waiting for transfers between devices, shards(): lax.all_to_all(back_load.reshape(n_ent, slot_cap, -1), 'ent', split_axis=...  12.2 us
    pallas_call x1, Pallas kernels, user_grams(): pl.pallas_call(functools.partial(gram_kernel, n_user, per_dev), out_shape...  7.62 us
    reduce_sum x1, other arithmetic, shards(): jnp.sum(jnp.where(hot_runs, run_weight[:, :, None], 0.0), axis=1)  7.42 us
    pallas_call x1, Pallas kernels, gather_rows(): pl.pallas_call(gather_kernel, out_shape=jax.ShapeDtypeStruct((count, tabl...  5.34 us
  transfers between devices with their start and end apart: 2, of which 1 were waited for; matrix products, arithmetic and copies ran while one was open for 3% of the time, Pallas kernels for 35%

profile of v22, /device:TPU:1, one launch (start us, length us, event | category | flops | bytes accessed | tf_op | source)
XLA Modules:
  0.0 189.2 jit_solution(2853742888053372838)
XLA Ops:
  0.6 0.5 broadcast.87
  1.1 1.3 reduce.9
  2.6 0.1 broadcast_in_dim.58
  2.9 0.1 broadcast_in_dim.60
  3.0 0.9 copy.22
  3.9 0.1 reshape_reshape.4
  4.0 1.8 copy.23
  5.8 0.6 broadcast_select_fusion.idx_ref
  6.4 5.3 %shard_map.77 = bf16[8192,128]{1,0:T(8,128)(2,1)} custom-call(s32[2,4096]{1,0:T(2,128)} %broadcast_select_fusion.idx_ref, bf16[128,1024]{1,0:T(8,128)(2,1)} %bitcast.23), custom_call_target="tpu_custom_call" | custom-call | flops 2147483648 | bytes 2392064 | tf_op jit(solution)/shard_map/pallas_call | solution.py:258
  11.8 18.6 %all-to-all-start = ((bf16[128,64,128]{2,1,0:T(8,128)(2,1)}), bf16[128,64,128]{2,1,0:T(8,128)(2,1)S(1)}, u32[]{:S(2)}, u32[]{:S(2)}) async-start(bf16[128,64,128]{2,1,0:T(8,128)(2,1)} %bitcast.22), calls=%async_computation | async-start | bytes 4194304 | tf_op jit(solution)/shard_map/all_to_all | solution.py:351
  30.7 0.7 reduce.10
  31.5 0.7 broadcast_in_dim.64.user_ref
  32.2 0.7 reduce.11
  33.3 0.1 and.46
  33.5 0.1 copy.27
  33.6 0.1 gt.16
  33.7 0.9 fusion.11.x_ref
  34.6 66.4 %shard_map.79 = f32[128,128]{1,0:T(8,128)} custom-call(f32[128,128]{1,0:T(8,128)} %fusion.11.x_ref), custom_call_target="tpu_custom_call" | custom-call | tf_op jit(solution)/shard_map/pallas_call | solution.py:146
  101.1 0.1 reshape.86
  101.4 1.5 convert_add_fusion.base_ref
  102.9 0.6 add_select_fusion.1.rw_ref
  103.5 1.3 copy-done.1
  104.9 7.6 %shard_map.78.blocks_ref = f32[4,258,128]{2,1,0:T(8,128)} custom-call(bf16[8192,128]{1,0:T(8,128)(2,1)} %bitcast.21, f32[4,2048]{1,0:T(4,128)} %copy-done.4, s32[4,2048]{1,0:T(4,128)} %broadcast_in_dim.64.user_ref, f32[4,2048]{1,0:T(4,128)} %add_select_fusion.1.rw_ref), custom_call_target="tpu_custom_call" | custom-call | flops 2684354560 | bytes 2723840 | tf_op jit(solution)/shard_map/pallas_call | solution.py:312
  112.5 40.1 %shard_map.80 = (bf16[4,2,128]{2,1,0:T(2,128)(2,1)}, f32[2,128]{1,0:T(2,128)}) custom-call(f32[4,258,128]{2,1,0:T(8,128)} %shard_map.78.blocks_ref, f32[128,128]{1,0:T(8,128)} %convert_add_fusion.base_ref), custom_call_target="tpu_custom_call" | custom-call | tf_op jit(solution)/shard_map/pallas_call | solution.py:223
  152.6 0.9 convolution_convert_fusion
  153.6 0.7 reshape.88
  154.4 12.5 %all-to-all-start.1 = ((bf16[128,2,160]{2,1,0:T(2,128)(2,1)}), bf16[128,2,160]{2,1,0:T(2,128)(2,1)S(1)}, u32[]{:S(2)}, u32[]{:S(2)}) async-start(bf16[128,2,160]{2,1,0:T(2,128)(2,1)} %reshape.88), calls=%async_computation.1 | async-start | bytes 262144 | tf_op jit(solution)/shard_map/all_to_all | solution.py:395
  166.9 12.2 %all-to-all-done.1 = bf16[128,2,160]{2,1,0:T(2,128)(2,1)S(1)} async-done(((bf16[128,2,160]{2,1,0:T(2,128)(2,1)}), bf16[128,2,160]{2,1,0:T(2,128)(2,1)S(1)}, u32[]{:S(2)}, u32[]{:S(2)}) %all-to-all-start.1) | async-done | bytes 81952 | tf_op jit(solution)/shard_map/all_to_all | solution.py:395
  179.1 0.1 reshape.89
  179.4 7.4 %select_reduce_fusion = f32[256,1024]{1,0:T(8,128)S(1)} fusion(f32[256,32]{1,0:T(8,128)S(1)} %fusion.1, s32[256,32]{1,0:T(8,128)S(1)} %copy.28), kind=kLoop, calls=%fused_computation | loop fusion | flops 24903680 | bytes 1114112 | tf_op jit(solution)/shard_map/reduce_sum | solution.py:406
  186.8 1.8 convolution_multiply_fusion
  188.6 0.6 copy.31
  (41 shorter events, 1.5 us)
Async XLA Ops:
  11.8 18.6 %copy-start.2 = (s32[1,1,256,32]{2,3,1,0:T(8,128)S(1)}, s32[1,1,256,32]{2,3,1,0:T(8,128)}, u32[]{:S(2)}) copy-start(s32[1,1,256,32]{2,3,1,0:T(8,128)} %param.10) | copy-start | bytes 98308
  11.8 18.9 %copy-start.5 = (s32[1,1,256,1]{2,3,1,0:T(1,128)S(1)}, s32[1,1,256,1]{2,3,1,0:T(1,128)}, u32[]{:S(2)}) copy-start(s32[1,1,256,1]{2,3,1,0:T(1,128)} %param.9) | copy-start | bytes 3076
  11.8 20.5 %copy-start.8 = (s32[1,1,128]{2,1,0:T(1,128)S(1)}, s32[1,1,128]{2,1,0:T(1,128)}, u32[]{:S(2)}) copy-start(s32[1,1,128]{2,1,0:T(1,128)} %param.11) | copy-start | bytes 1540
  11.8 21.9 %copy-start = (bf16[1024,128]{1,0:T(8,128)(2,1)S(1)}, bf16[1024,128]{1,0:T(8,128)(2,1)}, u32[]{:S(2)}) copy-start(bf16[1024,128]{1,0:T(8,128)(2,1)} %param.6) | copy-start | bytes 786436
  11.8 89.3 %copy-start.7 = (s32[1,1,128]{2,1,0:T(1,128)S(1)}, s32[1,1,128]{2,1,0:T(1,128)}, u32[]{:S(2)}) copy-start(s32[1,1,128]{2,1,0:T(1,128)} %param.8) | copy-start | bytes 1540
  11.8 89.5 %copy-start.3 = (s32[1,1,256,32]{2,3,1,0:T(8,128)S(1)}, s32[1,1,256,32]{2,3,1,0:T(8,128)}, u32[]{:S(2)}) copy-start(s32[1,1,256,32]{2,3,1,0:T(8,128)} %param.7) | copy-start | bytes 98308
  11.8 91.7 %all-to-all-start = ((bf16[128,64,128]{2,1,0:T(8,128)(2,1)}), bf16[128,64,128]{2,1,0:T(8,128)(2,1)S(1)}, u32[]{:S(2)}, u32[]{:S(2)}) async-start(bf16[128,64,128]{2,1,0:T(8,128)(2,1)} %bitcast.22), calls=%async_computation | async-start | bytes 4194304 | tf_op jit(solution)/shard_map/all_to_all | solution.py:351
  30.6 72.9 %copy-start.4 = (f32[4,2048]{1,0:T(4,128)}, f32[4,2048]{1,0:T(4,128)S(1)}, u32[]{:S(2)}) copy-start(f32[4,2048]{1,0:T(4,128)S(1)} %mul.19.gw_ref) | copy-start | bytes 98308
  103.5 1.3 copy-start.1
  153.5 35.1 %copy-start.6 = (f32[2,128]{1,0:T(2,128)S(1)}, f32[2,128]{1,0:T(2,128)}, u32[]{:S(2)}) copy-start(f32[2,128]{1,0:T(2,128)} %get-tuple-element.8) | copy-start | bytes 3076
  154.4 24.8 %all-to-all-start.1 = ((bf16[128,2,160]{2,1,0:T(2,128)(2,1)}), bf16[128,2,160]{2,1,0:T(2,128)(2,1)S(1)}, u32[]{:S(2)}, u32[]{:S(2)}) async-start(bf16[128,2,160]{2,1,0:T(2,128)(2,1)} %reshape.88), calls=%async_computation.1 | async-start | bytes 262144 | tf_op jit(solution)/shard_map/all_to_all | solution.py:395

commit v23 on v18

--- a/solution.py
+++ b/solution.py
@@ -252,7 +252,7 @@
     out_ref[...] = rows_t.T.astype(out_ref.dtype)
 
 
-def gather_rows(table, idx, chunk=4096):
+def gather_rows(table, idx, chunk=8192):
     count = idx.shape[0]
     idx_lanes = idx.reshape(count // chunk, chunk)
     return pl.pallas_call(

time: 190 us -> 188 us (0.989)
    unnamed x22 -> x20, local copies, waits for them, and re-layouts: 5.09 us -> 5.08 us
  transfers between devices with their start and end apart: 2 -> 2, of which waited for: 1 -> 1; matrix products, arithmetic and copies ran while one was open for 3% -> 4% of each run, Pallas kernels for 35% -> 35%
where the time goes in v23:
time: 188 us
  Pallas kernels  119 us (63%)
  starting transfers between devices  31.1 us (17%)
  waiting for transfers between devices  12.1 us (6%)
  other arithmetic  11.7 us (6%)
  local copies, waits for them, and re-layouts  9.21 us (5%)
  matrix products  3.6 us (2%)
    pallas_call x1, Pallas kernels, tree_sum(): pl.pallas_call(functools.partial(doubling_kernel, n_rep, low_bits, rounds...  65.7 us
    pallas_call x1, Pallas kernels, solve_owned(): pl.pallas_call(functools.partial(owner_kernel, n_rep), out_shape=(jax.Sha...  40.3 us
    all_to_all x1, starting transfers between devices, shards(): lax.all_to_all(picked.reshape(n_ent, slot_cap * tile_rows, rank_width), '...  18.5 us
    all_to_all x1, starting transfers between devices, shards(): lax.all_to_all(back_load.reshape(n_ent, slot_cap, -1), 'ent', split_axis=...  12.6 us
    all_to_all x1, waiting for transfers between devices, shards(): lax.all_to_all(back_load.reshape(n_ent, slot_cap, -1), 'ent', split_axis=...  12.1 us
    pallas_call x1, Pallas kernels, user_grams(): pl.pallas_call(functools.partial(gram_kernel, n_user, per_dev), out_shape...  7.65 us
    reduce_sum x1, other arithmetic, shards(): jnp.sum(jnp.where(hot_runs, run_weight[:, :, None], 0.0), axis=1)  7.42 us
    pallas_call x1, Pallas kernels, gather_rows(): pl.pallas_call(gather_kernel, out_shape=jax.ShapeDtypeStruct((count, tabl...  5.52 us
  transfers between devices with their start and end apart: 2, of which 1 were waited for; matrix products, arithmetic and copies ran while one was open for 4% of the time, Pallas kernels for 35%

profile of v23, /device:TPU:1, one launch (start us, length us, event | category | flops | bytes accessed | tf_op | source)
XLA Modules:
  0.0 187.7 jit_solution(5735097571844345976)
XLA Ops:
  0.6 0.7 broadcast_in_dim.48
  1.4 0.1 reshape.94
  1.6 0.1 reshape.95
  1.7 0.9 copy.22
  2.6 0.1 reshape_reshape.4
  2.7 1.8 copy.23
  4.5 0.7 broadcast_select_fusion.idx_ref
  5.2 5.5 %shard_map.77 = bf16[8192,128]{1,0:T(8,128)(2,1)} custom-call(s32[1,8192]{1,0:T(1,128)} %broadcast_select_fusion.idx_ref, bf16[128,1024]{1,0:T(8,128)(2,1)} %bitcast.23), custom_call_target="tpu_custom_call" | custom-call | flops 2147483648 | bytes 2392064 | tf_op jit(solution)/shard_map/pallas_call | solution.py:258
  10.7 18.5 %all-to-all-start = ((bf16[128,64,128]{2,1,0:T(8,128)(2,1)}), bf16[128,64,128]{2,1,0:T(8,128)(2,1)S(1)}, u32[]{:S(2)}, u32[]{:S(2)}) async-start(bf16[128,64,128]{2,1,0:T(8,128)(2,1)} %bitcast.22), calls=%async_computation | async-start | bytes 4194304 | tf_op jit(solution)/shard_map/all_to_all | solution.py:350
  29.4 0.1 mul.19.gw_ref
  29.5 0.5 broadcast.82
  30.0 0.7 reduce.6
  30.9 0.7 broadcast_in_dim.53.user_ref
  31.6 0.7 reduce.7
  32.7 0.1 and.40
  32.8 0.1 copy.27
  33.0 0.1 gt.16
  33.1 0.9 fusion.10.x_ref
  34.0 65.7 %shard_map.79 = f32[128,128]{1,0:T(8,128)} custom-call(f32[128,128]{1,0:T(8,128)} %fusion.10.x_ref), custom_call_target="tpu_custom_call" | custom-call | tf_op jit(solution)/shard_map/pallas_call | solution.py:146
  99.7 1.5 convert_add_fusion.base_ref
  101.2 0.6 add_select_fusion.1.rw_ref
  101.8 1.3 copy-done.1
  103.2 7.7 %shard_map.78.blocks_ref = f32[4,258,128]{2,1,0:T(8,128)} custom-call(bf16[8192,128]{1,0:T(8,128)(2,1)} %bitcast.21, f32[4,2048]{1,0:T(4,128)} %copy-done.4, s32[4,2048]{1,0:T(4,128)} %broadcast_in_dim.53.user_ref, f32[4,2048]{1,0:T(4,128)} %add_select_fusion.1.rw_ref), custom_call_target="tpu_custom_call" | custom-call | flops 2684354560 | bytes 2723840 | tf_op jit(solution)/shard_map/pallas_call | solution.py:311
  110.8 40.3 %shard_map.80 = (bf16[4,2,128]{2,1,0:T(2,128)(2,1)}, f32[2,128]{1,0:T(2,128)}) custom-call(f32[4,258,128]{2,1,0:T(8,128)} %shard_map.78.blocks_ref, f32[128,128]{1,0:T(8,128)} %convert_add_fusion.base_ref), custom_call_target="tpu_custom_call" | custom-call | tf_op jit(solution)/shard_map/pallas_call | solution.py:223
  151.1 0.9 convolution_convert_fusion
  152.1 0.7 reshape.99
  152.8 12.6 %all-to-all-start.1 = ((bf16[128,2,160]{2,1,0:T(2,128)(2,1)}), bf16[128,2,160]{2,1,0:T(2,128)(2,1)S(1)}, u32[]{:S(2)}, u32[]{:S(2)}) async-start(bf16[128,2,160]{2,1,0:T(2,128)(2,1)} %reshape.99), calls=%async_computation.1 | async-start | bytes 262144 | tf_op jit(solution)/shard_map/all_to_all | solution.py:394
  165.6 12.1 %all-to-all-done.1 = bf16[128,2,160]{2,1,0:T(2,128)(2,1)S(1)} async-done(((bf16[128,2,160]{2,1,0:T(2,128)(2,1)}), bf16[128,2,160]{2,1,0:T(2,128)(2,1)S(1)}, u32[]{:S(2)}, u32[]{:S(2)}) %all-to-all-start.1) | async-done | bytes 81952 | tf_op jit(solution)/shard_map/all_to_all | solution.py:394
  177.7 0.1 reshape.100
  177.9 7.4 %select_reduce_fusion = f32[256,1024]{1,0:T(8,128)S(1)} fusion(f32[256,32]{1,0:T(8,128)S(1)} %fusion.1, s32[256,32]{1,0:T(8,128)S(1)} %copy.28), kind=kLoop, calls=%fused_computation | loop fusion | flops 24903680 | bytes 1114112 | tf_op jit(solution)/shard_map/reduce_sum | solution.py:405
  185.3 1.8 convolution_multiply_fusion
  187.2 0.6 copy.31
  (34 shorter events, 1.1 us)
Async XLA Ops:
  10.7 18.5 %copy-start.2 = (s32[1,1,256,32]{2,3,1,0:T(8,128)S(1)}, s32[1,1,256,32]{2,3,1,0:T(8,128)}, u32[]{:S(2)}) copy-start(s32[1,1,256,32]{2,3,1,0:T(8,128)} %param.10) | copy-start | bytes 98308
  10.7 19.3 %copy-start.5 = (s32[1,1,256,1]{2,3,1,0:T(1,128)S(1)}, s32[1,1,256,1]{2,3,1,0:T(1,128)}, u32[]{:S(2)}) copy-start(s32[1,1,256,1]{2,3,1,0:T(1,128)} %param.9) | copy-start | bytes 3076
  10.7 20.9 %copy-start.7 = (s32[1,1,128]{2,1,0:T(1,128)S(1)}, s32[1,1,128]{2,1,0:T(1,128)}, u32[]{:S(2)}) copy-start(s32[1,1,128]{2,1,0:T(1,128)} %param.11) | copy-start | bytes 1540
  10.7 22.4 %copy-start = (bf16[1024,128]{1,0:T(8,128)(2,1)S(1)}, bf16[1024,128]{1,0:T(8,128)(2,1)}, u32[]{:S(2)}) copy-start(bf16[1024,128]{1,0:T(8,128)(2,1)} %param.6) | copy-start | bytes 786436
  10.7 91.1 %all-to-all-start = ((bf16[128,64,128]{2,1,0:T(8,128)(2,1)}), bf16[128,64,128]{2,1,0:T(8,128)(2,1)S(1)}, u32[]{:S(2)}, u32[]{:S(2)}) async-start(bf16[128,64,128]{2,1,0:T(8,128)(2,1)} %bitcast.22), calls=%async_computation | async-start | bytes 4194304 | tf_op jit(solution)/shard_map/all_to_all | solution.py:350
  29.5 72.3 %copy-start.4 = (f32[4,2048]{1,0:T(4,128)}, f32[4,2048]{1,0:T(4,128)S(1)}, u32[]{:S(2)}) copy-start(f32[4,2048]{1,0:T(4,128)S(1)} %mul.19.gw_ref) | copy-start | bytes 98308
  101.8 1.3 copy-start.1
  103.2 62.3 %copy-start.3 = (s32[1,1,256,32]{2,3,1,0:T(8,128)S(1)}, s32[1,1,256,32]{2,3,1,0:T(8,128)}, u32[]{:S(2)}) copy-start(s32[1,1,256,32]{2,3,1,0:T(8,128)} %param.7) | copy-start | bytes 98308
  152.1 35.1 %copy-start.6 = (f32[2,128]{1,0:T(2,128)S(1)}, f32[2,128]{1,0:T(2,128)}, u32[]{:S(2)}) copy-start(f32[2,128]{1,0:T(2,128)} %get-tuple-element.8) | copy-start | bytes 3076
  152.8 24.8 %all-to-all-start.1 = ((bf16[128,2,160]{2,1,0:T(2,128)(2,1)}), bf16[128,2,160]{2,1,0:T(2,128)(2,1)S(1)}, u32[]{:S(2)}, u32[]{:S(2)}) async-start(bf16[128,2,160]{2,1,0:T(2,128)(2,1)} %reshape.99), calls=%async_computation.1 | async-start | bytes 262144 | tf_op jit(solution)/shard_map/all_to_all | solution.py:394

commit v24 on v23

--- a/solution.py
+++ b/solution.py
@@ -364,7 +364,7 @@
     selector = owners[None, :] == jnp.arange(user_block, dtype=jnp.int32)[:, None]
     selector_f = selector.astype(jnp.float32)
     rows_all = incoming.reshape(tile_slots * tile_rows, rank_width)
-    lane_chunk = 2048
+    lane_chunk = 8192
     row_owner = jnp.repeat(owners, seg_length)
     gram_blocks = user_grams(
         rows_all,

time: 188 us -> 189 us (level)
  Pallas kernels: 119 us -> 121 us
    pallas_call x1, Pallas kernels: 65.7 us -> 67.7 us  [tree_sum(): pl.pallas_call(functools.partial(doubling_kernel, n_rep, low_bits, rounds...]
    unnamed x20 -> x19, local copies, waits for them, and re-layouts: 5.08 us -> 4.57 us
  transfers between devices with their start and end apart: 2 -> 2, of which waited for: 1 -> 1; matrix products, arithmetic and copies ran while one was open for 4% -> 3% of each run, Pallas kernels for 35% -> 36%
where the time goes in v24:
time: 189 us; the launch traced here: 188 us
  Pallas kernels  121 us (64%)
  starting transfers between devices  31.3 us (17%)
  waiting for transfers between devices  12.1 us (6%)
  other arithmetic  10.4 us (6%)
  local copies, waits for them, and re-layouts  8.54 us (5%)
  matrix products  3.6 us (2%)
    pallas_call x1, Pallas kernels, tree_sum(): pl.pallas_call(functools.partial(doubling_kernel, n_rep, low_bits, rounds...  67.7 us
    pallas_call x1, Pallas kernels, solve_owned(): pl.pallas_call(functools.partial(owner_kernel, n_rep), out_shape=(jax.Sha...  40.2 us
    all_to_all x1, starting transfers between devices, shards(): lax.all_to_all(picked.reshape(n_ent, slot_cap * tile_rows, rank_width), '...  18.6 us
    all_to_all x1, starting transfers between devices, shards(): lax.all_to_all(back_load.reshape(n_ent, slot_cap, -1), 'ent', split_axis=...  12.7 us
    all_to_all x1, waiting for transfers between devices, shards(): lax.all_to_all(back_load.reshape(n_ent, slot_cap, -1), 'ent', split_axis=...  12.1 us
    pallas_call x1, Pallas kernels, user_grams(): pl.pallas_call(functools.partial(gram_kernel, n_user, per_dev), out_shape...  7.82 us
    reduce_sum x1, other arithmetic, shards(): jnp.sum(jnp.where(hot_runs, run_weight[:, :, None], 0.0), axis=1)  7.42 us
    pallas_call x1, Pallas kernels, gather_rows(): pl.pallas_call(gather_kernel, out_shape=jax.ShapeDtypeStruct((count, tabl...  5.48 us
  transfers between devices with their start and end apart: 2, of which 1 were waited for; matrix products, arithmetic and copies ran while one was open for 3% of the time, Pallas kernels for 36%

profile of v24, /device:TPU:1, one launch (start us, length us, event | category | flops | bytes accessed | tf_op | source)
XLA Modules:
  0.0 188.0 jit_solution(7072895743898114174)
XLA Ops:
  0.6 0.7 broadcast_in_dim.40
  1.4 0.1 reshape.133
  1.5 0.1 broadcast_in_dim.41
  1.6 0.1 reshape.134
  1.7 0.9 copy.20
  2.6 0.1 reshape_reshape.6
  2.7 1.8 copy.21
  4.5 0.7 broadcast_select_fusion.idx_ref
  5.2 5.5 %shard_map.77 = bf16[8192,128]{1,0:T(8,128)(2,1)} custom-call(s32[1,8192]{1,0:T(1,128)} %broadcast_select_fusion.idx_ref, bf16[128,1024]{1,0:T(8,128)(2,1)} %bitcast.22), custom_call_target="tpu_custom_call" | custom-call | flops 2147483648 | bytes 2392064 | tf_op jit(solution)/shard_map/pallas_call | solution.py:258
  10.7 18.6 %all-to-all-start = ((bf16[128,64,128]{2,1,0:T(8,128)(2,1)}), bf16[128,64,128]{2,1,0:T(8,128)(2,1)S(1)}, u32[]{:S(2)}, u32[]{:S(2)}) async-start(bf16[128,64,128]{2,1,0:T(8,128)(2,1)} %bitcast.21), calls=%async_computation | async-start | bytes 4194304 | tf_op jit(solution)/shard_map/all_to_all | solution.py:350
  29.4 0.1 mul.28.gw_ref
  29.7 0.1 reshape.139
  29.8 0.1 and.44
  29.9 0.1 and.45
  30.1 0.1 copy.23
  30.2 0.1 gt.22
  30.4 0.7 reshape_reshape.7.user_ref
  31.2 0.9 fusion.7.x_ref
  32.1 67.7 %shard_map.79 = f32[128,128]{1,0:T(8,128)} custom-call(f32[128,128]{1,0:T(8,128)} %fusion.7.x_ref), custom_call_target="tpu_custom_call" | custom-call | tf_op jit(solution)/shard_map/pallas_call | solution.py:146
  99.7 1.5 convert_add_fusion.base_ref
  101.2 0.7 and_select_fusion.rw_ref
  101.9 1.3 copy-done.1
  103.2 7.8 %shard_map.78.blocks_ref = f32[4,258,128]{2,1,0:T(8,128)} custom-call(bf16[8192,128]{1,0:T(8,128)(2,1)} %bitcast.20, f32[1,8192]{1,0:T(1,128)} %copy-done.4, s32[1,8192]{1,0:T(1,128)} %reshape_reshape.7.user_ref, f32[1,8192]{1,0:T(1,128)} %and_select_fusion.rw_ref), custom_call_target="tpu_custom_call" | custom-call | flops 2684354560 | bytes 2723840 | tf_op jit(solution)/shard_map/pallas_call | solution.py:311
  111.0 40.2 %shard_map.80 = (bf16[4,2,128]{2,1,0:T(2,128)(2,1)}, f32[2,128]{1,0:T(2,128)}) custom-call(f32[4,258,128]{2,1,0:T(8,128)} %shard_map.78.blocks_ref, f32[128,128]{1,0:T(8,128)} %convert_add_fusion.base_ref), custom_call_target="tpu_custom_call" | custom-call | tf_op jit(solution)/shard_map/pallas_call | solution.py:223
  151.3 0.9 convolution_convert_fusion
  152.3 0.7 reshape.141
  153.0 12.7 %all-to-all-start.1 = ((bf16[128,2,160]{2,1,0:T(2,128)(2,1)}), bf16[128,2,160]{2,1,0:T(2,128)(2,1)S(1)}, u32[]{:S(2)}, u32[]{:S(2)}) async-start(bf16[128,2,160]{2,1,0:T(2,128)(2,1)} %reshape.141), calls=%async_computation.1 | async-start | bytes 262144 | tf_op jit(solution)/shard_map/all_to_all | solution.py:394
  165.8 12.1 %all-to-all-done.1 = bf16[128,2,160]{2,1,0:T(2,128)(2,1)S(1)} async-done(((bf16[128,2,160]{2,1,0:T(2,128)(2,1)}), bf16[128,2,160]{2,1,0:T(2,128)(2,1)S(1)}, u32[]{:S(2)}, u32[]{:S(2)}) %all-to-all-start.1) | async-done | bytes 81952 | tf_op jit(solution)/shard_map/all_to_all | solution.py:394
  177.9 0.1 reshape.142
  178.1 7.4 %select_reduce_fusion = f32[256,1024]{1,0:T(8,128)S(1)} fusion(f32[256,32]{1,0:T(8,128)S(1)} %fusion.1, s32[256,32]{1,0:T(8,128)S(1)} %copy.24), kind=kLoop, calls=%fused_computation | loop fusion | flops 24903680 | bytes 1114112 | tf_op jit(solution)/shard_map/reduce_sum | solution.py:405
  185.6 1.8 convolution_multiply_fusion
  187.4 0.6 copy.27
  (28 shorter events, 0.6 us)
Async XLA Ops:
  10.7 18.6 %copy-start.2 = (s32[1,1,256,32]{2,3,1,0:T(8,128)S(1)}, s32[1,1,256,32]{2,3,1,0:T(8,128)}, u32[]{:S(2)}) copy-start(s32[1,1,256,32]{2,3,1,0:T(8,128)} %param.10) | copy-start | bytes 98308
  10.7 18.9 %copy-start.7 = (s32[1,1,128]{2,1,0:T(1,128)S(1)}, s32[1,1,128]{2,1,0:T(1,128)}, u32[]{:S(2)}) copy-start(s32[1,1,128]{2,1,0:T(1,128)} %param.11) | copy-start | bytes 1540
  10.7 19.6 %copy-start.5 = (s32[1,1,256,1]{2,3,1,0:T(1,128)S(1)}, s32[1,1,256,1]{2,3,1,0:T(1,128)}, u32[]{:S(2)}) copy-start(s32[1,1,256,1]{2,3,1,0:T(1,128)} %param.9) | copy-start | bytes 3076
  10.7 20.5 %copy-start = (bf16[1024,128]{1,0:T(8,128)(2,1)S(1)}, bf16[1024,128]{1,0:T(8,128)(2,1)}, u32[]{:S(2)}) copy-start(bf16[1024,128]{1,0:T(8,128)(2,1)} %param.6) | copy-start | bytes 786436
  10.7 91.2 %all-to-all-start = ((bf16[128,64,128]{2,1,0:T(8,128)(2,1)}), bf16[128,64,128]{2,1,0:T(8,128)(2,1)S(1)}, u32[]{:S(2)}, u32[]{:S(2)}) async-start(bf16[128,64,128]{2,1,0:T(8,128)(2,1)} %bitcast.21), calls=%async_computation | async-start | bytes 4194304 | tf_op jit(solution)/shard_map/all_to_all | solution.py:350
  29.6 72.3 %copy-start.4 = (f32[1,8192]{1,0:T(1,128)}, f32[1,8192]{1,0:T(1,128)S(1)}, u32[]{:S(2)}) copy-start(f32[1,8192]{1,0:T(1,128)S(1)} %mul.28.gw_ref) | copy-start | bytes 98308
  101.9 1.3 copy-start.1
  103.2 62.5 %copy-start.3 = (s32[1,1,256,32]{2,3,1,0:T(8,128)S(1)}, s32[1,1,256,32]{2,3,1,0:T(8,128)}, u32[]{:S(2)}) copy-start(s32[1,1,256,32]{2,3,1,0:T(8,128)} %param.7) | copy-start | bytes 98308
  152.3 35.1 %copy-start.6 = (f32[2,128]{1,0:T(2,128)S(1)}, f32[2,128]{1,0:T(2,128)}, u32[]{:S(2)}) copy-start(f32[2,128]{1,0:T(2,128)} %get-tuple-element.8) | copy-start | bytes 3076
  153.0 24.9 %all-to-all-start.1 = ((bf16[128,2,160]{2,1,0:T(2,128)(2,1)}), bf16[128,2,160]{2,1,0:T(2,128)(2,1)S(1)}, u32[]{:S(2)}, u32[]{:S(2)}) async-start(bf16[128,2,160]{2,1,0:T(2,128)(2,1)} %reshape.141), calls=%async_computation.1 | async-start | bytes 262144 | tf_op jit(solution)/shard_map/all_to_all | solution.py:394
